TPU v7x, 512 devices: a whole 4x8x8 slice. The times are simulated.
512 devices in a mesh: context: 8 (over z), expert: 32 (over x, y), dp: 2 (over core).
Axes of the slice: x: 4, y: 8, z: 8, core: 2. Of those that a mesh axis runs over, the one named last changes fastest.
Arguments:
- residual: bfloat16 [32768, 1024], P(('dp', 'expert', 'context')), parts along dimension 0, may hold values from -6 to 6
- queries: bfloat16 [32768, 2048], P(('dp', 'expert', 'context')), parts along dimension 0, may hold values from -4.6 to 4.6
- key_vectors: bfloat16 [32768, 256], P(('dp', 'expert', 'context')), parts along dimension 0, may hold values from -5 to 5
- value_vectors: bfloat16 [32768, 256], P(('dp', 'expert', 'context')), parts along dimension 0, may hold values from -5 to 5
- output_weight: bfloat16 [2048, 1024], P('context'), may hold values from -0.875 to 0.875
- norm_gain: float32 [1024], replicated, may hold values from 0.1 to 1.9
- routes: int32 [32768, 8], P(('dp', 'expert', 'context')), parts along dimension 0, may hold values from 0 to 127, all different within a row; in each aligned block of 64 rows (0 to 63, 64 to 127, ...) at most 5 rows name the same one
- gate_levels: int32 [32768, 8], P(('dp', 'expert', 'context')), parts along dimension 0, may hold values from 16 to 96
- expert_in: bfloat16 [256, 1024, 384], P(('context', 'expert')), may hold values from -0.1875 to 0.1875
- expert_out: bfloat16 [256, 192, 1024], P(('context', 'expert')), may hold values from -0.3125 to 0.3125
Outputs:
- layer_out: float32 [32768, 1024], P(('dp', 'expert', 'context')), parts along dimension 0
There are 2 independent parts, one for each index of `dp`. A program takes and returns all parts, laid end to end along the dimension named above; an argument that names none is the same for every part. Nothing has to cross between parts.
Inputs may be any that keep to these rules, and one draw needn't show every extreme that they name: `routes`: in the rows of one device no expert is named more than 5 times, and in every draw some expert reaches 5 in some device's rows; each row names 8 different experts.
All inputs are finite; a program needn't handle non-finite values.
Results may differ from a plain program's by a relative error of at most 0.022.
Values may be sent and summed in bfloat16 or wider, within the bound.
No kernel may reach another device: no remote copies, remote signals or barrier semaphores. Data moves between devices by JAX's collectives and lax.ppermute only.
A program may use at most 192 MiB of HBM per device.

v0:
```python
import math

import jax
import jax.numpy as jnp
import numpy as np
from jax import lax
from jax.sharding import PartitionSpec as P

HD = 128


def expert_apply(gathered, weight_in, weight_out):
    projection = jnp.dot(gathered, weight_in, preferred_element_type=jnp.float32)
    inner_half = weight_in.shape[1] // 2
    activated = (jax.nn.silu(projection[:, :inner_half]) * projection[:, inner_half:]).astype(
        jnp.bfloat16
    )
    return jnp.dot(activated, weight_out, preferred_element_type=jnp.float32).astype(jnp.bfloat16)


def local(
    residual,
    queries,
    key_vectors,
    value_vectors,
    output_weight,
    norm_gain,
    routes,
    gate_levels,
    expert_in,
    expert_out,
):
    context_size = lax.axis_size("context")
    expert_size = lax.axis_size("expert")
    tok_rows, width = residual.shape
    head_count = queries.shape[1] // HD
    key_head_count = key_vectors.shape[1] // HD
    group_size = head_count // key_head_count
    heads_here = head_count // context_size
    keys_here = max(1, heads_here // group_size)
    queries_per_key = min(heads_here, group_size)
    group_rows = tok_rows * context_size
    weight_in = expert_in[0]
    weight_out = expert_out[0]
    head_table = (
        (
            np.arange(context_size)[:, None] * heads_here // group_size
            + np.arange(keys_here)[None, :]
        )
        .reshape(-1)
        .astype(np.int32)
    )
    key_select = key_vectors.reshape(tok_rows, key_head_count, HD)[:, head_table].reshape(
        tok_rows, context_size * keys_here * HD
    )
    value_select = value_vectors.reshape(tok_rows, key_head_count, HD)[:, head_table].reshape(
        tok_rows, context_size * keys_here * HD
    )
    query_local, key_local, value_local = (
        lax.all_to_all(queries, "context", split_axis=1, concat_axis=0, tiled=True),
        lax.all_to_all(key_select, "context", split_axis=1, concat_axis=0, tiled=True),
        lax.all_to_all(value_select, "context", split_axis=1, concat_axis=0, tiled=True),
    )
    own_block = lax.axis_index("expert")
    scaling = 1.0 / math.sqrt(HD)
    to_count = query_local.shape[0]
    query_sets = [
        (
            query_local.reshape(to_count, keys_here, queries_per_key, HD)
            .transpose(1, 0, 2, 3)
            .reshape(keys_here, to_count * queries_per_key, HD),
            own_block * group_rows
            + jnp.arange(group_rows * queries_per_key, dtype=jnp.int32) // queries_per_key,
            (own_block + 1) * group_rows,
        )
    ]
    set_counts = [group_rows]
    initial = tuple(
        (
            (
                jnp.full((keys_here, count * queries_per_key), -1e30, jnp.float32),
                jnp.zeros((keys_here, count * queries_per_key), jnp.float32),
                jnp.zeros((keys_here, count * queries_per_key, HD), jnp.float32),
            )
            for count in set_counts
        )
    )
    start = jnp.int32(0)
    key_piece = lax.all_gather(key_local, "expert", axis=0, tiled=True)
    value_piece = lax.all_gather(value_local, "expert", axis=0, tiled=True)
    piece_rows = key_piece.shape[0]
    key_heads = key_piece.reshape(piece_rows, keys_here, HD).transpose(1, 0, 2)
    value_heads = value_piece.reshape(piece_rows, keys_here, HD).transpose(1, 0, 2)
    key_position = jnp.arange(piece_rows, dtype=jnp.int32)
    updated = []
    for query_set, state in zip(query_sets, initial):
        query_rows, query_position, key_limit = query_set

        def update(inner, query_rows=query_rows, query_position=query_position):
            run_max, run_total, accum = inner
            allowed = (key_position[None, :] <= query_position[:, None])[None]
            scores = (
                jnp.einsum(
                    "grd,gnd->grn", query_rows, key_heads, preferred_element_type=jnp.float32
                )
                * scaling
            )
            masked = jnp.where(allowed, scores, -1e30)
            new_max = jnp.maximum(run_max, jnp.max(masked, axis=2))
            weights = jnp.where(allowed, jnp.exp(masked - new_max[:, :, None]), 0.0)
            run_total = jnp.sum(weights, axis=2)
            accum = jnp.einsum(
                "grn,gnd->grd",
                weights.astype(jnp.bfloat16),
                value_heads,
                preferred_element_type=jnp.float32,
            )
            return (new_max, run_total, accum)

        def unchanged(inner):
            return inner

        updated.append(lax.cond(start < key_limit, update, unchanged, state))
    states = tuple(updated)
    run_max, run_total, accum = states[0]
    result = (accum / run_total[:, :, None]).astype(jnp.bfloat16)
    attention = (
        result.reshape(keys_here, group_rows, queries_per_key, HD)
        .transpose(1, 0, 2, 3)
        .reshape(group_rows, heads_here * HD)
    )
    projected = lax.psum_scatter(
        jnp.dot(attention, output_weight, preferred_element_type=jnp.float32).astype(jnp.bfloat16),
        "context",
        scatter_dimension=0,
        tiled=True,
    ).astype(jnp.float32)
    hidden_state = residual.astype(jnp.float32) + projected
    mean_square = jnp.mean(hidden_state * hidden_state, axis=1, keepdims=True)
    normed = (hidden_state * lax.rsqrt(mean_square + 1e-06) * norm_gain).astype(jnp.bfloat16)
    top_count = routes.shape[1]
    expert_count = expert_size * context_size // 2
    group_experts = expert_size // 2
    capacity = min(tok_rows, max(2, 5 * tok_rows * top_count // (4 * expert_count)))
    slot_count = expert_count * capacity
    flat_routes = routes.reshape(-1)
    expert_hits = (
        flat_routes[:, None] == jnp.arange(expert_count, dtype=jnp.int32)[None, :]
    ).astype(jnp.int32)
    earlier = jnp.cumsum(expert_hits, axis=0) - expert_hits
    target_slot = flat_routes * capacity + jnp.sum(earlier * expert_hits, axis=1)
    placement = (
        target_slot.reshape(tok_rows, top_count)[:, :, None]
        == jnp.arange(slot_count, dtype=jnp.int32)[None, None, :]
    )
    sending = jnp.any(placement, axis=1).astype(jnp.bfloat16)
    outgoing = lax.dot_general(
        sending, normed, (((0,), (0,)), ((), ())), preferred_element_type=jnp.float32
    ).astype(jnp.bfloat16)
    gate_shares = jnp.sum(
        jnp.where(placement, gate_levels[:, :, None].astype(jnp.float32) / 256.0, 0.0), axis=1
    ).astype(jnp.bfloat16)
    arrived = lax.all_to_all(
        outgoing.reshape(context_size, group_experts, capacity, width),
        "context",
        split_axis=0,
        concat_axis=0,
        tiled=True,
    )
    item_count = arrived.shape[2]
    copies = jnp.broadcast_to(
        arrived.transpose(1, 0, 2, 3)[:, None], (group_experts, 2, context_size, item_count, width)
    ).reshape(expert_size, context_size, item_count, width)
    rows_in = lax.all_to_all(copies, "expert", split_axis=0, concat_axis=0, tiled=True)
    partial_out = expert_apply(rows_in.reshape(-1, width), weight_in, weight_out).reshape(
        rows_in.shape
    )
    came_back = lax.all_to_all(partial_out, "expert", split_axis=0, concat_axis=0, tiled=True)
    summed = (
        came_back.reshape(group_experts, 2, context_size, item_count, width)
        .astype(jnp.float32)
        .sum(axis=1)
        .astype(jnp.bfloat16)
    )
    result = summed.transpose(1, 0, 2, 3)
    answers = lax.all_to_all(result, "context", split_axis=0, concat_axis=0, tiled=True)
    moe_sum = jnp.dot(
        gate_shares, answers.reshape(slot_count, width), preferred_element_type=jnp.float32
    )
    return hidden_state + moe_sum


def solution(mesh):
    return jax.shard_map(
        local,
        mesh=mesh,
        in_specs=(
            P(("dp", "expert", "context"), None),
            P(("dp", "expert", "context"), None),
            P(("dp", "expert", "context"), None),
            P(("dp", "expert", "context"), None),
            P("context", None),
            P(),
            P(("dp", "expert", "context"), None),
            P(("dp", "expert", "context"), None),
            P(("context", "expert"), None, None),
            P(("context", "expert"), None, None),
        ),
        out_specs=P(("dp", "expert", "context"), None),
        check_vma=False,
    )
```

profile of v0, /device:TPU:8, one launch (start us, length us, event | category | flops | bytes accessed | tf_op | source)
XLA Modules:
  0.0 555.0 jit_solution(13816407835851833400)
XLA Ops:
  8.6 19.3 %all_to_all.68 = bf16[64,8,128]{2,0,1:T(8,128)(2,1)} all-to-all(bf16[64,8,128]{2,0,1:T(8,128)(2,1)S(1)} %bitcast.70), channel_id=1, replica_groups=mesh['context'=8,'expert'=32,'dp'=2] {'context'}, dimensions={1} | all-to-all | bytes 262144 | tf_op jit(solution)/shard_map/all_to_all | solution.py:61
  29.3 12.1 %all_to_all.69 = bf16[64,8,128]{2,0,1:T(8,128)(2,1)} all-to-all(bf16[64,8,128]{2,0,1:T(8,128)(2,1)S(1)} %bitcast.69), channel_id=1, replica_groups=mesh['context'=8,'expert'=32,'dp'=2] {'context'}, dimensions={1} | all-to-all | bytes 262144 | tf_op jit(solution)/shard_map/all_to_all | solution.py:62
  43.2 3.4 all-to-all-start
  46.6 10.3 %all-to-all-done = bf16[64,8,256]{2,0,1:T(8,128)(2,1)S(1)} async-done(((bf16[64,8,256]{2,0,1:T(8,128)(2,1)}), bf16[64,8,256]{2,0,1:T(8,128)(2,1)S(1)}, u32[]{:S(2)}, u32[]{:S(2)}) %all-to-all-start) | async-done | bytes 262176 | tf_op jit(solution)/shard_map/all_to_all | solution.py:60
  57.0 54.5 %all-gather.3.cloned.1.call-done = bf16[16384,128]{1,0:T(8,128)(2,1)} async-done(((bf16[512,128]{1,0:T(8,128)(2,1)}), bf16[16384,128]{1,0:T(8,128)(2,1)}) %all-gather.3.cloned.1.call-update) | async-done | bytes 4194320 | tf_op jit(solution)/shard_map/all_gather | solution.py:89
  111.5 87.7 %all-gather.5.cloned.1.call-done = bf16[16384,128]{1,0:T(8,128)(2,1)} async-done(((bf16[512,128]{1,0:T(8,128)(2,1)}), bf16[16384,128]{1,0:T(8,128)(2,1)}) %all-gather.5.cloned.1.call-update) | async-done | bytes 4194320 | tf_op jit(solution)/shard_map/all_gather | solution.py:90
  199.3 74.4 %conditional.1 = (f32[1,1024]{1,0:T(1,128)S(1)}, f32[1,1024,128]{2,1,0:T(8,128)S(1)}) conditional(s32[]{:T(128)} %convert_element_type.51, () %tuple.19, (s32[16384]{0:T(1024)S(1)}, s32[]{:T(128)}, s32[1024]{0:T(1024)S(1)}, bf16[8,64,256]{2,1,0:T(8,128)(2,1)S(1)}, bf16[16384,128]{1,0:T(8,128)(2,1)}, /*index=5*/bf16[16384,128]{1,0:T(8,128)(2,1)}) %tuple.32), branch_computations={%region_0.1_spmd, %region_1.4_spmd} | conditional | flops 8858378240 | bytes 211267616 | solution.py:123
  199.4 25.7 %fusion = (f32[1024]{0:T(1024)S(1)}, f32[1024,16384]{1,0:T(8,128)}) fusion(s32[16384]{0:T(1024)S(1)} %get-tuple-element.90, s32[1024]{0:T(1024)S(1)} %fusion.8, bf16[1024,128]{1,0:T(8,128)(2,1)S(1)} %reshape.111, bf16[16384,128]{1,0:T(8,128)(2,1)} %get-tuple-element.94), kind=kOutput, calls=%fused_computation.4 | convolution fusion | flops 4362075136 | bytes 71639040 | tf_op jit(solution)/shard_map/cond/branch_1_fun/grd,gnd->grn/dot_general | solution.py:103
  225.2 26.5 %fusion.5 = f32[1,1024,128]{2,1,0:T(8,128)S(1)} fusion(bf16[16384,128]{1,0:T(8,128)(2,1)} %get-tuple-element.95, f32[1024,16384]{1,0:T(8,128)} %get-tuple-element.113, f32[1024]{0:T(1024)S(1)} %broadcast_maximum_fusion, s32[16384]{0:T(1024)S(1)} %get-tuple-element.90, s32[1024]{0:T(1024)S(1)} %fusion.8), kind=kOutput, calls=%fused_computation.8 | convolution fusion | flops 4395630592 | bytes 71901184 | tf_op jit(solution)/shard_map/cond/branch_1_fun/grn,gnd->grd/dot_general | solution.py:112
  251.6 22.1 %fusion.2 = f32[1024]{0:T(1024)S(1)} fusion(f32[1024,16384]{1,0:T(8,128)} %get-tuple-element.113, f32[1024]{0:T(1024)S(1)} %broadcast_maximum_fusion, s32[16384]{0:T(1024)S(1)} %get-tuple-element.90, s32[1024]{0:T(1024)S(1)} %fusion.8), kind=kLoop, calls=%fused_computation.6 | loop fusion | flops 100662272 | bytes 67186688 | tf_op jit(solution)/shard_map/cond/branch_1_fun/reduce_sum | solution.py:111
  277.2 37.8 %reduce-scatter.2.cloned.1.call-done = bf16[64,1024]{1,0:T(8,128)(2,1)} async-done(((bf16[512,1024]{1,0:T(8,128)(2,1)}), bf16[64,1024]{1,0:T(8,128)(2,1)}) %reduce-scatter.2.cloned.1.call-update) | async-done | bytes 131088 | tf_op jit(solution)/shard_map/reduce_scatter | solution.py:132
  316.1 2.5 convolution_convert_fusion.1
  318.7 2.6 reshape.124
  322.2 34.2 %all_to_all.70 = bf16[8,16,5,1024]{3,1,2,0:T(8,128)(2,1)S(1)} all-to-all(bf16[8,16,5,1024]{3,1,2,0:T(8,128)(2,1)S(1)} %copy.81), channel_id=1, replica_groups=mesh['context'=8,'expert'=32,'dp'=2] {'context'}, dimensions={0} | all-to-all | bytes 2621440 | tf_op jit(solution)/shard_map/all_to_all | solution.py:163
  357.4 66.3 %all_to_all.71 = bf16[32,8,5,1024]{3,1,2,0:T(8,128)(2,1)S(1)} all-to-all(bf16[32,8,5,1024]{3,1,2,0:T(8,128)(2,1)S(1)} %bitcast.61), channel_id=1, replica_groups=mesh['context'=8,'expert'=32,'dp'=2] {'expert'}, dimensions={0} | all-to-all | bytes 5242880 | tf_op jit(solution)/shard_map/all_to_all | solution.py:174
  423.7 4.0 copy.83
  427.7 4.9 reshape.126
  434.8 2.9 reshape.127
  437.7 4.9 copy.84
  442.6 61.2 %all_to_all.72 = bf16[32,8,5,1024]{3,1,2,0:T(8,128)(2,1)S(1)} all-to-all(bf16[32,8,5,1024]{3,1,2,0:T(8,128)(2,1)S(1)} %copy.84), channel_id=1, replica_groups=mesh['context'=8,'expert'=32,'dp'=2] {'expert'}, dimensions={0} | all-to-all | bytes 5242880 | tf_op jit(solution)/shard_map/all_to_all | solution.py:178
  506.2 6.4 %all-to-all-start.6 = ((bf16[8,16,5,1024]{3,1,2,0:T(8,128)(2,1)}), bf16[8,16,5,1024]{3,1,2,0:T(8,128)(2,1)}, u32[]{:S(2)}, u32[]{:S(2)}) async-start(bf16[8,16,5,1024]{3,1,2,0:T(8,128)(2,1)} %copy.86), calls=%async_computation.7 | async-start | bytes 2621440 | tf_op jit(solution)/shard_map/all_to_all | solution.py:186
  513.2 29.2 %all-to-all-done.6 = bf16[8,16,5,1024]{3,1,2,0:T(8,128)(2,1)} async-done(((bf16[8,16,5,1024]{3,1,2,0:T(8,128)(2,1)}), bf16[8,16,5,1024]{3,1,2,0:T(8,128)(2,1)}, u32[]{:S(2)}, u32[]{:S(2)}) %all-to-all-start.6) | async-done | bytes 1310752 | tf_op jit(solution)/shard_map/all_to_all | solution.py:186
  542.4 2.2 copy.87
  546.1 2.4 convolution_add_fusion
  (70 shorter events, 18.3 us)
Async XLA Ops:
  6.5 426.1 %copy-start = (bf16[1,1024,384]{2,1,0:T(8,128)(2,1)S(1)}, bf16[1,1024,384]{2,1,0:T(8,128)(2,1)}, u32[]{:S(2)}) copy-start(bf16[1,1024,384]{2,1,0:T(8,128)(2,1)} %param.23) | copy-start | bytes 2359300
  6.5 105.0 %all-gather.3.cloned.1.call-start = ((), (), s32[]{:S(2)}) async-start(), calls=%async_computation.8 | async-start | bytes 4325376 | tf_op jit(solution)/shard_map/all_gather | solution.py:89
  28.0 171.3 %all-gather.5.cloned.1.call-start = ((), (), s32[]{:S(2)}) async-start(), calls=%async_computation.9 | async-start | bytes 4325376 | tf_op jit(solution)/shard_map/all_gather | solution.py:90
  43.2 13.8 %all-to-all-start = ((bf16[64,8,256]{2,0,1:T(8,128)(2,1)}), bf16[64,8,256]{2,0,1:T(8,128)(2,1)S(1)}, u32[]{:S(2)}, u32[]{:S(2)}) async-start(bf16[64,8,256]{2,0,1:T(8,128)(2,1)} %bitcast.57), calls=%async_computation | async-start | bytes 524288 | tf_op jit(solution)/shard_map/all_to_all | solution.py:60
  46.6 268.4 %reduce-scatter.2.cloned.1.call-start = ((), (), s32[]{:S(2)}) async-start(), calls=%async_computation.10 | async-start | bytes 1179648 | tf_op jit(solution)/shard_map/reduce_scatter | solution.py:132
  199.3 74.8 %copy-start.3 = (bf16[256,1024]{1,0:T(8,128)(2,1)S(1)}, bf16[256,1024]{1,0:T(8,128)(2,1)}, u32[]{:S(2)}) copy-start(bf16[256,1024]{1,0:T(8,128)(2,1)} %param.19) | copy-start | bytes 1572868
  273.7 1.8 copy-start.6
  273.7 41.3 %copy-start.1 = (bf16[64,1024]{1,0:T(8,128)(2,1)S(1)}, bf16[64,1024]{1,0:T(8,128)(2,1)}, u32[]{:S(2)}) copy-start(bf16[64,1024]{1,0:T(8,128)(2,1)} %param.15) | copy-start | bytes 393220
  273.7 42.4 %copy-start.7 = (f32[1024]{0:T(1024)S(1)}, f32[1024]{0:T(1024)}, u32[]{:S(2)}) copy-start(f32[1024]{0:T(1024)} %param.20) | copy-start | bytes 12292
  276.7 39.4 %copy-start.4 = (s32[64,8]{1,0:T(8,128)}, s32[64,8]{1,0:T(8,128)S(1)}, u32[]{:S(2)}) copy-start(s32[64,8]{1,0:T(8,128)S(1)} %copy.79) | copy-start | bytes 6148
  432.6 1.3 copy-start.9
  503.8 8.8 %copy-start.8 = (s32[64,8]{0,1:T(8,128)S(1)}, s32[64,8]{0,1:T(8,128)}, u32[]{:S(2)}) copy-start(s32[64,8]{0,1:T(8,128)} %param.22) | copy-start | bytes 6148
  503.8 8.9 %copy-start.5 = (s32[64,8]{1,0:T(8,128)S(1)}, s32[64,8]{1,0:T(8,128)}, u32[]{:S(2)}) copy-start(s32[64,8]{1,0:T(8,128)} %copy-done.4) | copy-start | bytes 6148
  506.2 39.9 %copy-start.2 = (bf16[64,1024]{1,0:T(8,128)(2,1)S(1)}, bf16[64,1024]{1,0:T(8,128)(2,1)}, u32[]{:S(2)}) copy-start(bf16[64,1024]{1,0:T(8,128)(2,1)} %reduce-scatter.2.cloned.1.call-done) | copy-start | bytes 393220
  506.2 36.2 %all-to-all-start.6 = ((bf16[8,16,5,1024]{3,1,2,0:T(8,128)(2,1)}), bf16[8,16,5,1024]{3,1,2,0:T(8,128)(2,1)}, u32[]{:S(2)}, u32[]{:S(2)}) async-start(bf16[8,16,5,1024]{3,1,2,0:T(8,128)(2,1)} %copy.86), calls=%async_computation.7 | async-start | bytes 2621440 | tf_op jit(solution)/shard_map/all_to_all | solution.py:186
Sparse Core Ops, SparseCore 0:
  28.1 83.4 all-gather.2
  114.7 84.5 all-gather.4
  275.7 39.3 reduce-scatter.1
where the time goes:
time: 556 us; the launch traced here: 555 us
  waiting for transfers between devices  220 us (40%)
  blocking collectives  193 us (35%)
  matrix products  60.7 us (11%)
  local copies, waits for them, and re-layouts  32 us (6%)
  other arithmetic  26.1 us (5%)
  between operations  13.4 us (2%)
  starting transfers between devices  9.92 us (2%)
    all_gather x1, waiting for transfers between devices, local(): value_piece = lax.all_gather(value_local, 'expert', axis=0, tiled=True)  87.7 us
    all_to_all x1, blocking collectives, local(): lax.all_to_all(copies, 'expert', split_axis=0, concat_axis=0, tiled=True)  66.3 us
    all_to_all x1, blocking collectives, local(): lax.all_to_all(partial_out, 'expert', split_axis=0, concat_axis=0, tiled=...  61.2 us
    all_gather x1, waiting for transfers between devices, local(): key_piece = lax.all_gather(key_local, 'expert', axis=0, tiled=True)  54.5 us
    reduce_scatter x1, waiting for transfers between devices, local(): lax.psum_scatter(jnp.dot(attention, output_weight, preferred_element_type...  37.8 us
    all_to_all x1, blocking collectives, local(): lax.all_to_all(outgoing.reshape(context_size, group_experts, capacity, wi...  34.2 us
    all_to_all x1, waiting for transfers between devices, local(): lax.all_to_all(result, 'context', split_axis=0, concat_axis=0, tiled=True)  29.2 us
    dot_general x1, matrix products, update(): jnp.einsum('grn,gnd->grd', weights.astype(jnp.bfloat16), value_heads, pre...  26.5 us
  transfers between devices with their start and end apart: 5, of which 5 were waited for; matrix products, arithmetic and copies ran while one was open for 1% of the time, Pallas kernels for 0%

commit v1 on v0

v1 whole, which is shorter than its diff:
```python
import math

import jax
import jax.numpy as jnp
from jax import lax
from jax.experimental import pallas as pl
from jax.experimental.pallas import tpu as pltpu
from jax.sharding import Mesh
from jax.sharding import PartitionSpec as P

HD = 128
CAP = 5
LOG2E = 1.4426950408889634
BF = jnp.bfloat16
F32 = jnp.float32
NEG = -1e30
STAT = 8


def flash_kernel(pos_ref, q_ref, kv_ref, o_ref, vt_ref, m_ref, acc_ref):
    block = pl.program_id(0)
    own_x = pos_ref[0]
    own_y = pos_ref[1]
    nz = q_ref.shape[1]
    cols = nz * 128
    scale = LOG2E / math.sqrt(HD)

    @pl.when((block == 0) & (pl.program_id(1) == 0))
    def _():
        for c in range(8):
            v = kv_ref[4 * (c % 2) : 4 * (c % 2) + 4, c // 2, :, 128:256].reshape(512, HD)
            vt_ref[c, 0:HD, :] = v.astype(F32).T.astype(BF)
            vt_ref[c, HD : HD + 16, :] = jnp.ones((16, 512), BF)

    tiles = block * 8 + own_y
    chunk_count = tiles // 4
    q_raw = q_ref[0]
    q = jnp.concatenate([q_raw[:, :, 0:HD], q_raw[:, :, HD : 2 * HD]], axis=1).reshape(cols, HD)
    group = 256
    groups = [(g * group, q[g * group : (g + 1) * group]) for g in range(cols // group)]

    def keys(c):
        return kv_ref[pl.ds(4 * (c % 2), 4), c // 2, :, 0:HD].reshape(512, HD)

    def scores(k, q_group):
        return lax.dot_general(
            k, q_group, (((1,), (1,)), ((), ())), preferred_element_type=F32
        )

    last_keys = keys(chunk_count)
    last_values = vt_ref[chunk_count]
    row = lax.broadcasted_iota(jnp.int32, (512, group), 0)
    col = lax.broadcasted_iota(jnp.int32, (512, group), 1)
    inner = row % 128
    key_pos = (4 * chunk_count + row // 128) * 512 + (inner // 16) * 64 + inner % 16 + 16 * own_x
    for start, q_group in groups:
        z_first = pl.program_id(1) * nz + start // 128
        q_pos = tiles * 512 + (z_first + col // 128) * 64 + col % 64
        allowed = key_pos <= q_pos
        s = jnp.where(allowed, scores(last_keys, q_group), NEG)
        m = jnp.max(s, axis=0, keepdims=True)
        p = jnp.where(allowed, jnp.exp2((s - m) * scale), 0.0).astype(BF)
        m_ref[:, start : start + group] = m
        acc_ref[:, start : start + group] = jnp.dot(last_values, p, preferred_element_type=F32)

    def step(c, carry):
        k = keys(c)
        values = vt_ref[c]
        for start, q_group in groups:
            s = scores(k, q_group)
            m_old = m_ref[:, start : start + group]
            m = jnp.maximum(m_old, jnp.max(s, axis=0, keepdims=True))
            p = jnp.exp2((s - m) * scale).astype(BF)
            alpha = jnp.exp2((m_old - m) * scale)
            m_ref[:, start : start + group] = m
            acc_ref[:, start : start + group] = acc_ref[
                :, start : start + group
            ] * alpha + jnp.dot(values, p, preferred_element_type=F32)
        return carry

    lax.fori_loop(0, chunk_count, step, 0)
    total = acc_ref[HD : HD + 1, :]
    seen = total > 0.0
    safe = jnp.where(seen, total, 1.0)
    out = (acc_ref[0:HD, :] * (1.0 / safe)).astype(BF)
    level = jnp.where(seen, m_ref[...] * scale + jnp.log(safe) * LOG2E, NEG)
    first = level.astype(BF).astype(F32)
    second = (level - first).astype(BF).astype(F32)
    third = level - first - second
    pick = lax.broadcasted_iota(jnp.int32, (STAT, cols), 0)
    stats = jnp.where(pick == 0, first, jnp.where(pick == 1, second, jnp.where(pick == 2, third, 0.0)))
    stats = stats.astype(BF)
    for i in range(nz):
        o_ref[0, i, 0:HD, :] = out[:, i * 128 : (i + 1) * 128]
        o_ref[0, i, HD : HD + STAT, :] = stats[:, i * 128 : (i + 1) * 128]


def flash(position, queries, key_values):
    nz = 4
    return pl.pallas_call(
        flash_kernel,
        grid_spec=pltpu.PrefetchScalarGridSpec(
            num_scalar_prefetch=1,
            grid=(4, 8 // nz),
            in_specs=[
                pl.BlockSpec((1, nz, 64, 256), lambda i, j, s: (i, j, 0, 0)),
                pl.BlockSpec((8, 4, 128, 256), lambda i, j, s: (0, 0, 0, 0)),
            ],
            out_specs=pl.BlockSpec((1, nz, HD + STAT, 128), lambda i, j, s: (i, j, 0, 0)),
            scratch_shapes=[
                pltpu.VMEM((8, HD + 16, 512), BF),
                pltpu.VMEM((1, nz * 128), F32),
                pltpu.VMEM((HD + 16, nz * 128), F32),
            ],
        ),
        out_shape=jax.ShapeDtypeStruct((4, 8, HD + STAT, 128), BF),
        compiler_params=pltpu.CompilerParams(vmem_limit_bytes=40 * 1024 * 1024),
        name="flash",
    )(position, queries, key_values)


def merge_kernel(parts_ref, w_ref, res_ref, gain_ref, hidden_ref, normed_ref, acc_ref):
    c = pl.program_id(0)
    levels = []
    for x in range(4):
        st = parts_ref[x, 0, HD : HD + STAT, :].astype(F32)
        levels.append(st[0:1] + st[1:2] + st[2:3])
    top = jnp.maximum(jnp.maximum(levels[0], levels[1]), jnp.maximum(levels[2], levels[3]))
    shares = [jnp.exp2(level - top) for level in levels]
    inverse = 1.0 / (shares[0] + shares[1] + shares[2] + shares[3])
    mixed = parts_ref[0, 0, 0:HD, :].astype(F32) * (shares[0] * inverse)
    for x in range(1, 4):
        mixed = mixed + parts_ref[x, 0, 0:HD, :].astype(F32) * (shares[x] * inverse)
    rows = mixed.T.astype(BF)
    attention = jnp.concatenate([rows[0:64], rows[64:128]], axis=1)
    part = jnp.dot(attention, w_ref[...], preferred_element_type=F32)

    @pl.when(c == 0)
    def _():
        acc_ref[...] = res_ref[...].astype(F32) + part

    @pl.when(c > 0)
    def _():
        acc_ref[...] = acc_ref[...] + part

    @pl.when(c == 7)
    def _():
        hidden = acc_ref[...]
        hidden_ref[...] = hidden
        mean_square = jnp.mean(hidden * hidden, axis=1, keepdims=True)
        normed_ref[...] = (hidden * lax.rsqrt(mean_square + 1e-6) * gain_ref[...]).astype(BF)


def merge(parts, weight, residual, gain):
    tokens, width = residual.shape
    return pl.pallas_call(
        merge_kernel,
        grid=(8,),
        in_specs=[
            pl.BlockSpec((4, 1, HD + STAT, 128), lambda c: (0, c, 0, 0)),
            pl.BlockSpec((256, width), lambda c: (c, 0)),
            pl.BlockSpec((tokens, width), lambda c: (0, 0)),
            pl.BlockSpec((1, width), lambda c: (0, 0)),
        ],
        out_specs=[
            pl.BlockSpec((tokens, width), lambda c: (0, 0)),
            pl.BlockSpec((tokens, width), lambda c: (0, 0)),
        ],
        out_shape=[
            jax.ShapeDtypeStruct((tokens, width), F32),
            jax.ShapeDtypeStruct((tokens, width), BF),
        ],
        scratch_shapes=[pltpu.VMEM((tokens, width), F32)],
        name="merge",
    )(parts, weight, residual, gain)


def select_kernel(sel_ref, x_ref, o_ref, tmp_ref):
    count = sel_ref.shape[0]
    sel = sel_ref[...]
    for j in range(0, 8, 2):
        got = jnp.dot(sel, x_ref[:, j * 128 : (j + 2) * 128], preferred_element_type=F32)
        tmp_ref[pl.ds(j, count, stride=8), :] = got[:, 0:128]
        tmp_ref[pl.ds(j + 1, count, stride=8), :] = got[:, 128:256]
    o_ref[...] = tmp_ref[...].astype(BF)


def select(chosen, tokens):
    count = chosen.shape[0]
    return pl.pallas_call(
        select_kernel,
        out_shape=jax.ShapeDtypeStruct((count * 8, 128), BF),
        scratch_shapes=[pltpu.VMEM((count * 8, 128), F32)],
        compiler_params=pltpu.CompilerParams(vmem_limit_bytes=40 * 1024 * 1024),
        name="select",
    )(chosen, tokens)


def expert_kernel(x_ref, win_ref, wout_ref, o_ref, tmp_ref):
    rows = x_ref.shape[0] // 8
    inner = wout_ref.shape[0]
    tmp_ref[...] = x_ref[...].astype(F32)
    x = jnp.concatenate(
        [tmp_ref[pl.ds(j, rows, stride=8), :].astype(BF) for j in range(8)], axis=1
    )
    projection = jnp.dot(x, win_ref[...], preferred_element_type=F32)
    gate = projection[:, 0:inner]
    activated = (gate / (1.0 + jnp.exp(-gate)) * projection[:, inner:]).astype(BF)
    out = jnp.dot(activated, wout_ref[...], preferred_element_type=F32)
    for j in range(8):
        tmp_ref[pl.ds(j, rows, stride=8), :] = out[:, j * 128 : (j + 1) * 128]
    o_ref[...] = tmp_ref[...].astype(BF)


def expert(rows_in, weight_in, weight_out):
    total = rows_in.shape[0]
    block = total // 4
    return pl.pallas_call(
        expert_kernel,
        grid=(4,),
        in_specs=[
            pl.BlockSpec((block, 128), lambda i: (i, 0)),
            pl.BlockSpec(weight_in.shape, lambda i: (0, 0)),
            pl.BlockSpec(weight_out.shape, lambda i: (0, 0)),
        ],
        out_specs=pl.BlockSpec((block, 128), lambda i: (i, 0)),
        out_shape=jax.ShapeDtypeStruct((total, 128), BF),
        scratch_shapes=[pltpu.VMEM((block, 128), F32)],
        compiler_params=pltpu.CompilerParams(vmem_limit_bytes=40 * 1024 * 1024),
        name="expert",
    )(rows_in, weight_in, weight_out)


def gather_kernel(gates_ref, x_ref, o_ref, tmp_ref):
    count = gates_ref.shape[1]
    gates = gates_ref[...]
    tmp_ref[...] = x_ref[...].astype(F32)
    for j in range(0, 8, 2):
        x = jnp.concatenate(
            [
                tmp_ref[pl.ds(j, count, stride=8), :].astype(BF),
                tmp_ref[pl.ds(j + 1, count, stride=8), :].astype(BF),
            ],
            axis=1,
        )
        o_ref[:, j * 128 : (j + 2) * 128] = jnp.dot(
            gates, x, preferred_element_type=F32
        ).astype(BF)


def gather(gates, rows):
    count = gates.shape[1]
    return pl.pallas_call(
        gather_kernel,
        out_shape=jax.ShapeDtypeStruct((gates.shape[0], 1024), BF),
        scratch_shapes=[pltpu.VMEM((count * 8, 128), F32)],
        compiler_params=pltpu.CompilerParams(vmem_limit_bytes=40 * 1024 * 1024),
        name="gather",
    )(gates, rows)


def local(
    residual,
    queries,
    key_vectors,
    value_vectors,
    output_weight,
    norm_gain,
    routes,
    gate_levels,
    expert_in,
    expert_out,
):
    tokens, width = residual.shape
    own_x = lax.axis_index("x")
    own_y = lax.axis_index("y2") * 2 + lax.axis_index("y1")

    key_value = jnp.concatenate(
        [key_vectors.reshape(4, 16, 2, HD), value_vectors.reshape(4, 16, 2, HD)], axis=3
    ).transpose(0, 2, 1, 3)
    key_value = jnp.broadcast_to(key_value[:, :, None], (4, 2, 4, 16, 2 * HD)).reshape(
        32, 16, 2 * HD
    )
    key_value = lax.all_to_all(key_value, ("x", "z"), split_axis=0, concat_axis=0, tiled=True)
    key_values = lax.all_gather(
        key_value.reshape(512, 2 * HD), ("y2", "y1"), axis=0, tiled=True
    ).reshape(8, 4, 128, 2 * HD)

    query = queries.reshape(tokens, 8, 2 * HD).transpose(1, 0, 2)
    query = jnp.broadcast_to(query[None], (4, 8, tokens, 2 * HD)).reshape(32, tokens, 2 * HD)
    query, _ = lax.optimization_barrier((query, key_value))
    query = lax.all_to_all(query, ("x", "z"), split_axis=0, concat_axis=0, tiled=True).reshape(
        4, 8, tokens, 2 * HD
    )

    listing = jnp.concatenate([routes, gate_levels], axis=1)
    listing = jnp.broadcast_to(listing[None], (4, tokens, 16))
    listing, _ = lax.optimization_barrier((listing, query))
    listing = lax.all_to_all(listing, "x", split_axis=0, concat_axis=0, tiled=True)
    named, levels = listing[:, :, 0:8], listing[:, :, 8:16]
    local_expert = jnp.arange(32, dtype=jnp.int32)
    wanted = (local_expert // 4) * 16 + own_x * 4 + local_expert % 4
    match = named[:, :, :, None] == wanted
    hits = jnp.any(match, axis=2)
    gates = jnp.sum(jnp.where(match, levels[:, :, :, None], 0), axis=2).astype(F32) / 256.0
    before = jnp.tril(jnp.ones((tokens, tokens), BF), -1)
    ranks = jnp.einsum(
        "ab,sbq->saq", before, hits.astype(BF), preferred_element_type=F32
    ).astype(jnp.int32)
    ranks = jnp.where(hits, ranks, -1)
    slots = jnp.arange(CAP, dtype=jnp.int32)
    same = jnp.eye(4, dtype=jnp.bool_)
    placed = (ranks.transpose(2, 0, 1)[:, None, None, :, :] == slots[None, None, :, None, None]) & (
        same[None, :, None, :, None]
    )
    chosen = placed.astype(BF).reshape(32 * 4 * CAP, 4 * tokens)
    back = (ranks[:, :, :, None, None] == slots) & same[:, None, None, :, None]
    shares = jnp.where(back, gates[:, :, :, None, None], 0.0).astype(BF)
    shares = shares.reshape(4 * tokens, 32 * 4 * CAP)

    swap = [(0, 1), (1, 0)]
    own_in, own_out, _ = lax.optimization_barrier((expert_in[0], expert_out[0], query))
    other_in = lax.ppermute(own_in, "y1", swap)
    other_out = lax.ppermute(own_out, "y1", swap)
    half = own_in.shape[1] // 2
    weight_in = jnp.concatenate(
        [own_in[:, :half], other_in[:, :half], own_in[:, half:], other_in[:, half:]], axis=1
    )
    weight_out = jnp.concatenate([own_out, other_out], axis=0)

    output_weight, _ = lax.optimization_barrier((output_weight, key_values))
    whole_weight = lax.all_gather(output_weight, "z", axis=0, tiled=True)

    position = jnp.stack([own_x, own_y]).astype(jnp.int32)
    parts = flash(position, query, key_values)
    parts = lax.all_to_all(
        parts.reshape(32, HD + STAT, 128), ("x", "z"), split_axis=0, concat_axis=0, tiled=True
    ).reshape(4, 8, HD + STAT, 128)
    hidden, normed = merge(parts, whole_weight, residual, norm_gain.reshape(1, width))

    spread = jnp.broadcast_to(normed[None], (4, tokens, width))
    spread = lax.all_to_all(spread, "x", split_axis=0, concat_axis=0, tiled=True)
    outgoing = select(chosen, spread.reshape(4 * tokens, width))
    arrived = lax.all_to_all(
        outgoing.reshape(32, 4 * CAP * 8, 128), ("z", "y2"), split_axis=0, concat_axis=0, tiled=True
    )
    done = expert(arrived.reshape(-1, 128), weight_in, weight_out)
    answers = lax.all_to_all(
        done.reshape(32, 4 * CAP * 8, 128), ("z", "y2"), split_axis=0, concat_axis=0, tiled=True
    )
    sums = gather(shares, answers.reshape(-1, 128))
    sums = lax.all_to_all(
        sums.reshape(4, tokens, width), "x", split_axis=0, concat_axis=0, tiled=True
    )
    return hidden + jnp.sum(sums.astype(F32), axis=0)


def solution(mesh):
    fine = Mesh(mesh.devices.reshape(8, 4, 4, 2, 2), ("z", "x", "y2", "y1", "dp"))
    rows = P(("dp", "x", "y2", "y1", "z"), None)
    halves = P(("z", "x", "y2", "y1"), None, None)
    return jax.shard_map(
        local,
        mesh=fine,
        in_specs=(rows, rows, rows, rows, P("z", None), P(), rows, rows, halves, halves),
        out_specs=rows,
        check_vma=False,
    )
```

time: 556 us -> 334 us (0.60)
  the two profiles are of different devices: /device:TPU:8 before, /device:TPU:16 now
where the time goes in v1:
time: 334 us; the launch traced here: 333 us
  waiting for transfers between devices  163 us (49%)
  starting transfers between devices  58.9 us (18%)
  Pallas kernels  45.6 us (14%)
  blocking collectives  36 us (11%)
  between operations  13.8 us (4%)
  local copies, waits for them, and re-layouts  10.9 us (3%)
  other arithmetic  4.68 us (1%)
    all_gather x1, waiting for transfers between devices, local(): lax.all_gather(key_value.reshape(512, 2 * HD), ('y2', 'y1'), axis=0, tile...  38.5 us
    ppermute x1, waiting for transfers between devices, local(): other_out = lax.ppermute(own_out, 'y1', swap)  33.2 us
    all_to_all x1, waiting for transfers between devices, local(): lax.all_to_all(query, ('x', 'z'), split_axis=0, concat_axis=0, tiled=True)  33.1 us
    pallas_call x1, Pallas kernels, flash(): pl.pallas_call(flash_kernel, grid_spec=pltpu.PrefetchScalarGridSpec(num_s...  32.3 us
    all_to_all x1, waiting for transfers between devices, local(): lax.all_to_all(done.reshape(32, 4 * CAP * 8, 128), ('z', 'y2'), split_axi...  32 us
    all_to_all x1, blocking collectives, local(): lax.all_to_all(key_value, ('x', 'z'), split_axis=0, concat_axis=0, tiled=...  25.5 us
    all_to_all x1, waiting for transfers between devices, local(): lax.all_to_all(parts.reshape(32, HD + STAT, 128), ('x', 'z'), split_axis=...  19 us
    all_to_all x1, starting transfers between devices, local(): lax.all_to_all(outgoing.reshape(32, 4 * CAP * 8, 128), ('z', 'y2'), split...  14.1 us
  transfers between devices with their start and end apart: 10, of which 6 were waited for; matrix products, arithmetic and copies ran while one was open for 2% of the time, Pallas kernels for 10%

profile of v1, /device:TPU:16, one launch (start us, length us, event | category | flops | bytes accessed | tf_op | source)
XLA Modules:
  0.0 333.1 jit_solution(5540480952537882687)
XLA Ops:
  8.2 25.5 %all_to_all.40 = bf16[32,16,256]{2,1,0:T(8,128)(2,1)} all-to-all(bf16[32,16,256]{2,1,0:T(8,128)(2,1)S(1)} %bitcast.51), channel_id=1, replica_groups=mesh['z'=8,'x'=4,'y2'=4,'y1'=2,'dp'=2] {'x','z'}, dimensions={0} | all-to-all | bytes 524288 | tf_op jit(solution)/shard_map/all_to_all | solution.py:284
  33.8 38.5 %all-gather.3.cloned.1.call-done = bf16[4096,256]{1,0:T(8,128)(2,1)} async-done(((bf16[512,256]{1,0:T(8,128)(2,1)}), bf16[4096,256]{1,0:T(8,128)(2,1)}) %all-gather.3.cloned.1.call-update) | async-done | bytes 2097168 | tf_op jit(solution)/shard_map/all_gather | solution.py:285
  72.5 1.1 broadcast_in_dim.44
  73.6 10.2 %all-to-all-start.1 = ((bf16[32,64,256]{2,1,0:T(8,128)(2,1)}), bf16[32,64,256]{2,1,0:T(8,128)(2,1)S(1)}, u32[]{:S(2)}, u32[]{:S(2)}) async-start(bf16[32,64,256]{2,1,0:T(8,128)(2,1)} %bitcast.48), calls=%async_computation.1 | async-start | bytes 2097152 | tf_op jit(solution)/shard_map/all_to_all | solution.py:292
  83.8 33.1 %all-to-all-done.1 = bf16[32,64,256]{2,1,0:T(8,128)(2,1)S(1)} async-done(((bf16[32,64,256]{2,1,0:T(8,128)(2,1)}), bf16[32,64,256]{2,1,0:T(8,128)(2,1)S(1)}, u32[]{:S(2)}, u32[]{:S(2)}) %all-to-all-start.1) | async-done | bytes 1048608 | tf_op jit(solution)/shard_map/all_to_all | solution.py:292
  117.6 4.1 %all-to-all-start.3 = ((s32[4,1,1024]{2,1,0:T(1,128)}), s32[4,1,1024]{2,1,0:T(1,128)S(1)}, u32[]{:S(2)}, u32[]{:S(2)}) async-start(s32[4,1,1024]{2,1,0:T(1,128)} %reshape.148), calls=%async_computation.3 | async-start | bytes 32768 | tf_op jit(solution)/shard_map/all_to_all | solution.py:299
  121.8 32.3 %flash.1 = bf16[4,8,136,128]{3,2,1,0:T(8,128)(2,1)} custom-call(s32[2]{0:T(128)S(1)} %pad_add_fusion.1.pos_ref, bf16[4,8,64,256]{3,2,1,0:T(8,128)(2,1)S(1)} %bitcast.43, bf16[8,4,128,256]{3,2,1,0:T(8,128)(2,1)S(1)} %bitcast.44), custom_call_target="tpu_custom_call" | custom-call | tf_op jit(solution)/shard_map/flash/pallas_call | solution.py:100
  154.2 7.8 %all-to-all-start.2 = ((bf16[32,136,128]{2,1,0:T(8,128)(2,1)}), bf16[32,136,128]{2,1,0:T(8,128)(2,1)S(1)}, u32[]{:S(2)}, u32[]{:S(2)}) async-start(bf16[32,136,128]{2,1,0:T(8,128)(2,1)} %bitcast.9), calls=%async_computation.2 | async-start | bytes 2228224 | tf_op jit(solution)/shard_map/all_to_all | solution.py:336
  163.9 19.0 %all-to-all-done.2 = bf16[32,136,128]{2,1,0:T(8,128)(2,1)S(1)} async-done(((bf16[32,136,128]{2,1,0:T(8,128)(2,1)}), bf16[32,136,128]{2,1,0:T(8,128)(2,1)S(1)}, u32[]{:S(2)}, u32[]{:S(2)}) %all-to-all-start.2) | async-done | bytes 1114144 | tf_op jit(solution)/shard_map/all_to_all | solution.py:336
  183.9 7.1 %merge.1 = (f32[64,1024]{1,0:T(8,128)}, bf16[64,1024]{1,0:T(8,128)(2,1)}) custom-call(bf16[4,8,136,128]{3,2,1,0:T(8,128)(2,1)} %bitcast.47, bf16[2048,1024]{1,0:T(8,128)(2,1)} %all-gather.5.cloned.1.call-done.w_ref, bf16[64,1024]{1,0:T(8,128)(2,1)} %res_ref.1, f32[1,1024]{1,0:T(1,128)} %bitcast.59), custom_call_target="tpu_custom_call" | custom-call | tf_op jit(solution)/shard_map/merge/pallas_call | solution.py:156
  191.0 1.8 broadcast_in_dim.82
  192.8 3.5 %all-to-all-start.4 = ((bf16[4,64,1024]{2,1,0:T(8,128)(2,1)}), bf16[4,64,1024]{2,1,0:T(8,128)(2,1)S(1)}, u32[]{:S(2)}, u32[]{:S(2)}) async-start(bf16[4,64,1024]{2,1,0:T(8,128)(2,1)} %broadcast_in_dim.82), calls=%async_computation.4 | async-start | bytes 1048576 | tf_op jit(solution)/shard_map/all_to_all | solution.py:342
  197.1 7.2 %all-to-all-done.4 = bf16[4,64,1024]{2,1,0:T(8,128)(2,1)S(1)} async-done(((bf16[4,64,1024]{2,1,0:T(8,128)(2,1)}), bf16[4,64,1024]{2,1,0:T(8,128)(2,1)S(1)}, u32[]{:S(2)}, u32[]{:S(2)}) %all-to-all-start.4) | async-done | bytes 524320 | tf_op jit(solution)/shard_map/all_to_all | solution.py:342
  204.3 1.8 select.11
  206.1 14.1 %all-to-all-start.5 = ((bf16[32,160,128]{2,1,0:T(8,128)(2,1)}), bf16[32,160,128]{2,1,0:T(8,128)(2,1)S(1)}, u32[]{:S(2)}, u32[]{:S(2)}) async-start(bf16[32,160,128]{2,1,0:T(8,128)(2,1)} %bitcast.17), calls=%async_computation.5 | async-start | bytes 2621440 | tf_op jit(solution)/shard_map/all_to_all | solution.py:344
  220.2 1.9 collective-permute-start
  222.1 3.9 %collective-permute-start.1 = (bf16[192,1024]{1,0:T(8,128)(2,1)S(1)}, bf16[192,1024]{1,0:T(8,128)(2,1)S(1)}, u32[]{:S(2)}, u32[]{:S(2)}) collective-permute-start(bf16[192,1024]{1,0:T(8,128)(2,1)S(1)} %bitcast.54), channel_id=1, source_target_pairs={{0,2},{2,0},{1,3},{3,1},{4,6},{6,4},{5,7},{7,5},{8,10},{10,8},{9,1... | collective-permute-start | bytes 1179656 | tf_op jit(solution)/shard_map/ppermute | solution.py:324
  226.3 33.2 %collective-permute-done.1 = bf16[192,1024]{1,0:T(8,128)(2,1)S(1)} collective-permute-done((bf16[192,1024]{1,0:T(8,128)(2,1)S(1)}, bf16[192,1024]{1,0:T(8,128)(2,1)S(1)}, u32[]{:S(2)}, u32[]{:S(2)}) %collective-permute-start.1) | collective-permute-done | bytes 393248 | tf_op jit(solution)/shard_map/ppermute | solution.py:324
  261.6 1.1 copy-done.1
  262.7 3.6 %expert.1 = bf16[5120,128]{1,0:T(8,128)(2,1)S(1)} custom-call(bf16[5120,128]{1,0:T(8,128)(2,1)S(1)} %bitcast.41, bf16[1024,768]{1,0:T(8,128)(2,1)S(1)} %pad_maximum_fusion.win_ref, bf16[384,1024]{1,0:T(8,128)(2,1)S(1)} %copy-done.1), custom_call_target="tpu_custom_call" | custom-call | tf_op jit(solution)/shard_map/expert/pallas_call | solution.py:218
  266.4 1.1 copy-done
  267.4 13.3 %all-to-all-start.6 = ((bf16[32,160,128]{2,1,0:T(8,128)(2,1)}), bf16[32,160,128]{2,1,0:T(8,128)(2,1)S(1)}, u32[]{:S(2)}, u32[]{:S(2)}) async-start(bf16[32,160,128]{2,1,0:T(8,128)(2,1)} %bitcast.42), calls=%async_computation.6 | async-start | bytes 2621440 | tf_op jit(solution)/shard_map/all_to_all | solution.py:348
  282.1 32.0 %all-to-all-done.6 = bf16[32,160,128]{2,1,0:T(8,128)(2,1)S(1)} async-done(((bf16[32,160,128]{2,1,0:T(8,128)(2,1)}), bf16[32,160,128]{2,1,0:T(8,128)(2,1)S(1)}, u32[]{:S(2)}, u32[]{:S(2)}) %all-to-all-start.6) | async-done | bytes 1310752 | tf_op jit(solution)/shard_map/all_to_all | solution.py:348
  314.9 10.5 %all_to_all.41 = bf16[4,64,1024]{2,1,0:T(8,128)(2,1)S(1)} all-to-all(bf16[4,64,1024]{2,1,0:T(8,128)(2,1)S(1)} %bitcast.46), channel_id=1, replica_groups=mesh['z'=8,'x'=4,'y2'=4,'y1'=2,'dp'=2] {'x'}, dimensions={0} | all-to-all | bytes 1048576 | tf_op jit(solution)/shard_map/all_to_all | solution.py:352
  (67 shorter events, 11.6 us)
Async XLA Ops:
  6.5 65.8 %copy-start.7 = (bf16[64,2048]{1,0:T(8,128)(2,1)S(1)}, bf16[64,2048]{1,0:T(8,128)(2,1)}, u32[]{:S(2)}) copy-start(bf16[64,2048]{1,0:T(8,128)(2,1)} %param.11) | copy-start | bytes 786436
  6.5 65.8 %all-gather.3.cloned.1.call-start = ((), (), s32[]{:S(2)}) async-start(), calls=%async_computation.8 | async-start | bytes 2359296 | tf_op jit(solution)/shard_map/all_gather | solution.py:285
  33.8 149.1 %all-gather.5.cloned.1.call-start = ((), (), s32[]{:S(2)}) async-start(), calls=%async_computation.9 | async-start | bytes 4718592 | tf_op jit(solution)/shard_map/all_gather | solution.py:332
  72.5 11.3 %copy-start.8 = (s32[64,8]{0,1:T(8,128)S(1)}, s32[64,8]{0,1:T(8,128)}, u32[]{:S(2)}) copy-start(s32[64,8]{0,1:T(8,128)} %param.17) | copy-start | bytes 6148
  72.5 11.3 %copy-start.9 = (s32[64,8]{0,1:T(8,128)S(1)}, s32[64,8]{0,1:T(8,128)}, u32[]{:S(2)}) copy-start(s32[64,8]{0,1:T(8,128)} %param.16) | copy-start | bytes 6148
  72.5 49.3 %copy-start.2 = (bf16[4096,256]{1,0:T(8,128)(2,1)S(1)}, bf16[4096,256]{1,0:T(8,128)(2,1)}, u32[]{:S(2)}) copy-start(bf16[4096,256]{1,0:T(8,128)(2,1)} %all-gather.3.cloned.1.call-done) | copy-start | bytes 6291460
  73.6 43.3 %all-to-all-start.1 = ((bf16[32,64,256]{2,1,0:T(8,128)(2,1)}), bf16[32,64,256]{2,1,0:T(8,128)(2,1)S(1)}, u32[]{:S(2)}, u32[]{:S(2)}) async-start(bf16[32,64,256]{2,1,0:T(8,128)(2,1)} %bitcast.48), calls=%async_computation.1 | async-start | bytes 2097152 | tf_op jit(solution)/shard_map/all_to_all | solution.py:292
  117.6 36.6 %all-to-all-start.3 = ((s32[4,1,1024]{2,1,0:T(1,128)}), s32[4,1,1024]{2,1,0:T(1,128)S(1)}, u32[]{:S(2)}, u32[]{:S(2)}) async-start(s32[4,1,1024]{2,1,0:T(1,128)} %reshape.148), calls=%async_computation.3 | async-start | bytes 32768 | tf_op jit(solution)/shard_map/all_to_all | solution.py:299
  154.2 28.7 %all-to-all-start.2 = ((bf16[32,136,128]{2,1,0:T(8,128)(2,1)}), bf16[32,136,128]{2,1,0:T(8,128)(2,1)S(1)}, u32[]{:S(2)}, u32[]{:S(2)}) async-start(bf16[32,136,128]{2,1,0:T(8,128)(2,1)} %bitcast.9), calls=%async_computation.2 | async-start | bytes 2228224 | tf_op jit(solution)/shard_map/all_to_all | solution.py:336
  182.9 1.0 copy-start.3
  192.8 11.5 %all-to-all-start.4 = ((bf16[4,64,1024]{2,1,0:T(8,128)(2,1)}), bf16[4,64,1024]{2,1,0:T(8,128)(2,1)S(1)}, u32[]{:S(2)}, u32[]{:S(2)}) async-start(bf16[4,64,1024]{2,1,0:T(8,128)(2,1)} %broadcast_in_dim.82), calls=%async_computation.4 | async-start | bytes 1048576 | tf_op jit(solution)/shard_map/all_to_all | solution.py:342
  206.1 14.1 %copy-start.4 = (bf16[1,1024,384]{2,1,0:T(8,128)(2,1)S(1)}, bf16[1,1024,384]{2,1,0:T(8,128)(2,1)}, u32[]{:S(2)}) copy-start(bf16[1,1024,384]{2,1,0:T(8,128)(2,1)} %param.18) | copy-start | bytes 2359300
  206.1 16.1 %copy-start.5 = (bf16[1,192,1024]{2,1,0:T(8,128)(2,1)S(1)}, bf16[1,192,1024]{2,1,0:T(8,128)(2,1)}, u32[]{:S(2)}) copy-start(bf16[1,192,1024]{2,1,0:T(8,128)(2,1)} %param.19) | copy-start | bytes 1179652
  206.1 55.5 %all-to-all-start.5 = ((bf16[32,160,128]{2,1,0:T(8,128)(2,1)}), bf16[32,160,128]{2,1,0:T(8,128)(2,1)S(1)}, u32[]{:S(2)}, u32[]{:S(2)}) async-start(bf16[32,160,128]{2,1,0:T(8,128)(2,1)} %bitcast.17), calls=%async_computation.5 | async-start | bytes 2621440 | tf_op jit(solution)/shard_map/all_to_all | solution.py:344
  220.2 40.3 %collective-permute-start = (bf16[1024,384]{1,0:T(8,128)(2,1)S(1)}, bf16[1024,384]{1,0:T(8,128)(2,1)S(1)}, u32[]{:S(2)}, u32[]{:S(2)}) collective-permute-start(bf16[1024,384]{1,0:T(8,128)(2,1)S(1)} %bitcast.49), channel_id=1, source_target_pairs={{0,2},{2,0},{1,3},{3,1},{4,6},{6,4},{5,7},{7,5},{8,10},{10,8},{9,1... | collective-permute-start | bytes 2359304 | tf_op jit(solution)/shard_map/ppermute | solution.py:323
  222.1 37.4 %collective-permute-start.1 = (bf16[192,1024]{1,0:T(8,128)(2,1)S(1)}, bf16[192,1024]{1,0:T(8,128)(2,1)S(1)}, u32[]{:S(2)}, u32[]{:S(2)}) collective-permute-start(bf16[192,1024]{1,0:T(8,128)(2,1)S(1)} %bitcast.54), channel_id=1, source_target_pairs={{0,2},{2,0},{1,3},{3,1},{4,6},{6,4},{5,7},{7,5},{8,10},{10,8},{9,1... | collective-permute-start | bytes 1179656 | tf_op jit(solution)/shard_map/ppermute | solution.py:324
  261.6 1.1 copy-start.1
  266.3 1.1 copy-start
  267.4 46.7 %all-to-all-start.6 = ((bf16[32,160,128]{2,1,0:T(8,128)(2,1)}), bf16[32,160,128]{2,1,0:T(8,128)(2,1)S(1)}, u32[]{:S(2)}, u32[]{:S(2)}) async-start(bf16[32,160,128]{2,1,0:T(8,128)(2,1)} %bitcast.42), calls=%async_computation.6 | async-start | bytes 2621440 | tf_op jit(solution)/shard_map/all_to_all | solution.py:348
  314.1 11.4 %copy-start.6 = (f32[64,1024]{1,0:T(8,128)S(1)}, f32[64,1024]{1,0:T(8,128)}, u32[]{:S(2)}) copy-start(f32[64,1024]{1,0:T(8,128)} %get-tuple-element.14) | copy-start | bytes 786436
Sparse Core Ops, SparseCore 0:
  33.9 38.3 all-gather.2
  74.4 71.8 all-gather.4

commit v2 on v1

--- a/solution.py
+++ b/solution.py
@@ -115,11 +115,14 @@
         ),
         out_shape=jax.ShapeDtypeStruct((4, 8, HD + STAT, 128), BF),
         compiler_params=pltpu.CompilerParams(vmem_limit_bytes=40 * 1024 * 1024),
+        cost_estimate=pl.CostEstimate(
+            flops=4 * 4096 * 2560 * HD, bytes_accessed=5 << 20, transcendentals=4096 * 2560
+        ),
         name="flash",
     )(position, queries, key_values)
 
 
-def merge_kernel(parts_ref, w_ref, res_ref, gain_ref, hidden_ref, normed_ref, acc_ref):
+def merge_kernel(pos_ref, parts_ref, w_ref, v_ref, res_ref, gain_ref, hidden_ref, normed_ref, acc_ref):
     c = pl.program_id(0)
     levels = []
     for x in range(4):
@@ -132,8 +135,13 @@
     for x in range(1, 4):
         mixed = mixed + parts_ref[x, 0, 0:HD, :].astype(F32) * (shares[x] * inverse)
     rows = mixed.T.astype(BF)
-    attention = jnp.concatenate([rows[0:64], rows[64:128]], axis=1)
-    part = jnp.dot(attention, w_ref[...], preferred_element_type=F32)
+    first = pos_ref[2] == 0
+    attention = jnp.concatenate(
+        [jnp.where(first, rows[0:64], rows[64:128]), jnp.where(first, rows[64:128], rows[0:64])],
+        axis=1,
+    )
+    weight = jnp.concatenate([w_ref[...], v_ref[...]], axis=0)
+    part = jnp.dot(attention, weight, preferred_element_type=F32)
 
     @pl.when(c == 0)
     def _():
@@ -151,28 +159,32 @@
         normed_ref[...] = (hidden * lax.rsqrt(mean_square + 1e-6) * gain_ref[...]).astype(BF)
 
 
-def merge(parts, weight, residual, gain):
+def merge(position, parts, weight, weight_other, residual, gain):
     tokens, width = residual.shape
     return pl.pallas_call(
         merge_kernel,
-        grid=(8,),
-        in_specs=[
-            pl.BlockSpec((4, 1, HD + STAT, 128), lambda c: (0, c, 0, 0)),
-            pl.BlockSpec((256, width), lambda c: (c, 0)),
-            pl.BlockSpec((tokens, width), lambda c: (0, 0)),
-            pl.BlockSpec((1, width), lambda c: (0, 0)),
-        ],
-        out_specs=[
-            pl.BlockSpec((tokens, width), lambda c: (0, 0)),
-            pl.BlockSpec((tokens, width), lambda c: (0, 0)),
-        ],
+        grid_spec=pltpu.PrefetchScalarGridSpec(
+            num_scalar_prefetch=1,
+            grid=(8,),
+            in_specs=[
+                pl.BlockSpec((4, 1, HD + STAT, 128), lambda c, s: (0, c, 0, 0)),
+                pl.BlockSpec((128, width), lambda c, s: (c, 0)),
+                pl.BlockSpec((128, width), lambda c, s: (c, 0)),
+                pl.BlockSpec((tokens, width), lambda c, s: (0, 0)),
+                pl.BlockSpec((1, width), lambda c, s: (0, 0)),
+            ],
+            out_specs=[
+                pl.BlockSpec((tokens, width), lambda c, s: (0, 0)),
+                pl.BlockSpec((tokens, width), lambda c, s: (0, 0)),
+            ],
+            scratch_shapes=[pltpu.VMEM((tokens, width), F32)],
+        ),
         out_shape=[
             jax.ShapeDtypeStruct((tokens, width), F32),
             jax.ShapeDtypeStruct((tokens, width), BF),
         ],
-        scratch_shapes=[pltpu.VMEM((tokens, width), F32)],
         name="merge",
-    )(parts, weight, residual, gain)
+    )(position, parts, weight, weight_other, residual, gain)
 
 
 def select_kernel(sel_ref, x_ref, o_ref, tmp_ref):
@@ -273,7 +285,10 @@
 ):
     tokens, width = residual.shape
     own_x = lax.axis_index("x")
-    own_y = lax.axis_index("y2") * 2 + lax.axis_index("y1")
+    own_y2 = lax.axis_index("y2")
+    own_y = own_y2 * 2 + lax.axis_index("y1")
+    own_core = lax.axis_index("dp")
+    position = jnp.stack([own_x, own_y, own_core]).astype(jnp.int32)
 
     key_value = jnp.concatenate(
         [key_vectors.reshape(4, 16, 2, HD), value_vectors.reshape(4, 16, 2, HD)], axis=3
@@ -296,10 +311,10 @@
     listing = jnp.concatenate([routes, gate_levels], axis=1)
     listing = jnp.broadcast_to(listing[None], (4, tokens, 16))
     listing, _ = lax.optimization_barrier((listing, query))
-    listing = lax.all_to_all(listing, "x", split_axis=0, concat_axis=0, tiled=True)
+    listing = lax.all_to_all(listing, "y2", split_axis=0, concat_axis=0, tiled=True)
     named, levels = listing[:, :, 0:8], listing[:, :, 8:16]
     local_expert = jnp.arange(32, dtype=jnp.int32)
-    wanted = (local_expert // 4) * 16 + own_x * 4 + local_expert % 4
+    wanted = (local_expert % 8) * 16 + (local_expert // 8) * 4 + own_y2
     match = named[:, :, :, None] == wanted
     hits = jnp.any(match, axis=2)
     gates = jnp.sum(jnp.where(match, levels[:, :, :, None], 0), axis=2).astype(F32) / 256.0
@@ -322,35 +337,38 @@
     own_in, own_out, _ = lax.optimization_barrier((expert_in[0], expert_out[0], query))
     other_in = lax.ppermute(own_in, "y1", swap)
     other_out = lax.ppermute(own_out, "y1", swap)
+    head_weight = lax.dynamic_slice_in_dim(output_weight, own_core * HD, HD, 0)
+    head_weight, _ = lax.optimization_barrier((head_weight, query))
+    gathered = lax.all_gather(head_weight, "z", axis=0, tiled=True)
+    gathered_other = lax.ppermute(gathered, "dp", swap)
+
+    parts = flash(position, query, key_values)
+    parts, other_in, other_out = lax.optimization_barrier((parts, other_in, other_out))
+    parts = lax.all_to_all(
+        parts.reshape(32, HD + STAT, 128), ("x", "z"), split_axis=0, concat_axis=0, tiled=True
+    ).reshape(4, 8, HD + STAT, 128)
     half = own_in.shape[1] // 2
     weight_in = jnp.concatenate(
         [own_in[:, :half], other_in[:, :half], own_in[:, half:], other_in[:, half:]], axis=1
     )
     weight_out = jnp.concatenate([own_out, other_out], axis=0)
-
-    output_weight, _ = lax.optimization_barrier((output_weight, key_values))
-    whole_weight = lax.all_gather(output_weight, "z", axis=0, tiled=True)
-
-    position = jnp.stack([own_x, own_y]).astype(jnp.int32)
-    parts = flash(position, query, key_values)
-    parts = lax.all_to_all(
-        parts.reshape(32, HD + STAT, 128), ("x", "z"), split_axis=0, concat_axis=0, tiled=True
-    ).reshape(4, 8, HD + STAT, 128)
-    hidden, normed = merge(parts, whole_weight, residual, norm_gain.reshape(1, width))
+    hidden, normed = merge(
+        position, parts, gathered, gathered_other, residual, norm_gain.reshape(1, width)
+    )
 
     spread = jnp.broadcast_to(normed[None], (4, tokens, width))
-    spread = lax.all_to_all(spread, "x", split_axis=0, concat_axis=0, tiled=True)
+    spread = lax.all_to_all(spread, "y2", split_axis=0, concat_axis=0, tiled=True)
     outgoing = select(chosen, spread.reshape(4 * tokens, width))
     arrived = lax.all_to_all(
-        outgoing.reshape(32, 4 * CAP * 8, 128), ("z", "y2"), split_axis=0, concat_axis=0, tiled=True
+        outgoing.reshape(32, 4 * CAP * 8, 128), ("x", "z"), split_axis=0, concat_axis=0, tiled=True
     )
     done = expert(arrived.reshape(-1, 128), weight_in, weight_out)
     answers = lax.all_to_all(
-        done.reshape(32, 4 * CAP * 8, 128), ("z", "y2"), split_axis=0, concat_axis=0, tiled=True
+        done.reshape(32, 4 * CAP * 8, 128), ("x", "z"), split_axis=0, concat_axis=0, tiled=True
     )
     sums = gather(shares, answers.reshape(-1, 128))
     sums = lax.all_to_all(
-        sums.reshape(4, tokens, width), "x", split_axis=0, concat_axis=0, tiled=True
+        sums.reshape(4, tokens, width), "y2", split_axis=0, concat_axis=0, tiled=True
     )
     return hidden + jnp.sum(sums.astype(F32), axis=0)
 

time: 334 us -> 297 us (0.89)
  the two profiles are of different devices: /device:TPU:16 before, /device:TPU:64 now
where the time goes in v2:
time: 297 us; the launch traced here: 296 us
  waiting for transfers between devices  123 us (41%)
  starting transfers between devices  49.9 us (17%)
  Pallas kernels  47.1 us (16%)
  blocking collectives  42.3 us (14%)
  local copies, waits for them, and re-layouts  14.9 us (5%)
  between operations  13.8 us (5%)
  other arithmetic  4.66 us (2%)
    pallas_call x1, Pallas kernels, flash(): pl.pallas_call(flash_kernel, grid_spec=pltpu.PrefetchScalarGridSpec(num_s...  32.4 us
    all_to_all x1, waiting for transfers between devices, local(): lax.all_to_all(done.reshape(32, 4 * CAP * 8, 128), ('x', 'z'), split_axis...  30.8 us
    all_to_all x1, waiting for transfers between devices, local(): lax.all_to_all(outgoing.reshape(32, 4 * CAP * 8, 128), ('x', 'z'), split_...  28.5 us
    all_to_all x1, waiting for transfers between devices, local(): lax.all_to_all(query, ('x', 'z'), split_axis=0, concat_axis=0, tiled=True)  26.9 us
    all_to_all x1, blocking collectives, local(): lax.all_to_all(key_value, ('x', 'z'), split_axis=0, concat_axis=0, tiled=...  24.8 us
    all_to_all x1, waiting for transfers between devices, local(): lax.all_to_all(parts.reshape(32, HD + STAT, 128), ('x', 'z'), split_axis=...  24.6 us
    all_to_all x1, blocking collectives, local(): lax.all_to_all(sums.reshape(4, tokens, width), 'y2', split_axis=0, concat...  17.5 us
    all_to_all x1, starting transfers between devices, local(): lax.all_to_all(spread, 'y2', split_axis=0, concat_axis=0, tiled=True)  14.5 us
  transfers between devices with their start and end apart: 11, of which 5 were waited for; matrix products, arithmetic and copies ran while one was open for 3% of the time, Pallas kernels for 11%

profile of v2, /device:TPU:64, one launch (start us, length us, event | category | flops | bytes accessed | tf_op | source)
XLA Modules:
  0.0 295.6 jit_solution(8203051283914021604)
XLA Ops:
  8.3 24.8 %all_to_all.40 = bf16[32,16,256]{2,1,0:T(8,128)(2,1)} all-to-all(bf16[32,16,256]{2,1,0:T(8,128)(2,1)S(1)} %bitcast.50), channel_id=1, replica_groups=mesh['z'=8,'x'=4,'y2'=4,'y1'=2,'dp'=2] {'x','z'}, dimensions={0} | all-to-all | bytes 524288 | tf_op jit(solution)/shard_map/all_to_all | solution.py:299
  33.2 1.1 broadcast_in_dim.44
  34.4 4.7 %all-to-all-start.1 = ((bf16[32,64,256]{2,1,0:T(8,128)(2,1)}), bf16[32,64,256]{2,1,0:T(8,128)(2,1)S(1)}, u32[]{:S(2)}, u32[]{:S(2)}) async-start(bf16[32,64,256]{2,1,0:T(8,128)(2,1)} %bitcast.4), calls=%async_computation.1 | async-start | bytes 2097152 | tf_op jit(solution)/shard_map/all_to_all | solution.py:307
  39.9 26.9 %all-to-all-done.1 = bf16[32,64,256]{2,1,0:T(8,128)(2,1)S(1)} async-done(((bf16[32,64,256]{2,1,0:T(8,128)(2,1)}), bf16[32,64,256]{2,1,0:T(8,128)(2,1)S(1)}, u32[]{:S(2)}, u32[]{:S(2)}) %all-to-all-start.1) | async-done | bytes 1048608 | tf_op jit(solution)/shard_map/all_to_all | solution.py:307
  66.8 3.5 %collective-permute-start = (bf16[1024,384]{1,0:T(8,128)(2,1)S(1)}, bf16[1024,384]{1,0:T(8,128)(2,1)}, u32[]{:S(2)}, u32[]{:S(2)}) collective-permute-start(bf16[1024,384]{1,0:T(8,128)(2,1)S(1)} %bitcast.48), channel_id=1, source_target_pairs={{0,2},{2,0},{1,3},{3,1},{4,6},{6,4},{5,7},{7,5},{8,10},{10,8},{9,1... | collective-permute-start | bytes 2359304 | tf_op jit(solution)/shard_map/ppermute | solution.py:338
  70.4 2.4 collective-permute-start.1
  73.5 7.1 %all-to-all-start.3 = ((s32[4,1,1024]{2,1,0:T(1,128)}), s32[4,1,1024]{2,1,0:T(1,128)S(1)}, u32[]{:S(2)}, u32[]{:S(2)}) async-start(s32[4,1,1024]{2,1,0:T(1,128)} %reshape.149), calls=%async_computation.3 | async-start | bytes 32768 | tf_op jit(solution)/shard_map/all_to_all | solution.py:314
  80.6 1.6 copy-done.3
  82.2 32.4 %flash.1 = bf16[4,8,136,128]{3,2,1,0:T(8,128)(2,1)} custom-call(s32[3]{0:T(128)S(1)} %pad_add_fusion.1.pos_ref, bf16[4,8,64,256]{3,2,1,0:T(8,128)(2,1)S(1)} %bitcast.45, bf16[8,4,128,256]{3,2,1,0:T(8,128)(2,1)S(1)} %bitcast.46), custom_call_target="tpu_custom_call" | custom-call | flops 5368709120 | bytes 5242880 | tf_op jit(solution)/shard_map/flash/pallas_call | solution.py:100
  115.3 5.4 %all-to-all-start.2 = ((bf16[32,136,128]{2,1,0:T(8,128)(2,1)}), bf16[32,136,128]{2,1,0:T(8,128)(2,1)S(1)}, u32[]{:S(2)}, u32[]{:S(2)}) async-start(bf16[32,136,128]{2,1,0:T(8,128)(2,1)} %bitcast.12), calls=%async_computation.2 | async-start | bytes 2228224 | tf_op jit(solution)/shard_map/all_to_all | solution.py:347
  120.8 1.9 collective-permute-start.2
  124.3 24.6 %all-to-all-done.2 = bf16[32,136,128]{2,1,0:T(8,128)(2,1)S(1)} async-done(((bf16[32,136,128]{2,1,0:T(8,128)(2,1)}), bf16[32,136,128]{2,1,0:T(8,128)(2,1)S(1)}, u32[]{:S(2)}, u32[]{:S(2)}) %all-to-all-start.2) | async-done | bytes 1114144 | tf_op jit(solution)/shard_map/all_to_all | solution.py:347
  149.9 7.8 %merge.1 = (f32[64,1024]{1,0:T(8,128)}, bf16[64,1024]{1,0:T(8,128)(2,1)}) custom-call(s32[3]{0:T(128)} %copy-done.2, bf16[4,8,136,128]{3,2,1,0:T(8,128)(2,1)} %bitcast.47, bf16[1024,1024]{1,0:T(8,128)(2,1)} %all-gather.5.cloned.1.call-done.w_ref, bf16[1024,1024]{1,0:T(8,128)(2,1)} %collective-permute-done.2.v_ref, bf16[64,1024]{1,0:T(8,128)(2,1)} %res_ref.1, ...), custom_call_target="tpu_custom_call" | custom-call | tf_op jit(solution)/shard_map/merge/pallas_call | solution.py:164
  157.7 1.8 broadcast_in_dim.82
  159.4 14.5 %all-to-all-start.4 = ((bf16[4,64,1024]{2,1,0:T(8,128)(2,1)}), bf16[4,64,1024]{2,1,0:T(8,128)(2,1)S(1)}, u32[]{:S(2)}, u32[]{:S(2)}) async-start(bf16[4,64,1024]{2,1,0:T(8,128)(2,1)} %broadcast_in_dim.82), calls=%async_computation.4 | async-start | bytes 1048576 | tf_op jit(solution)/shard_map/all_to_all | solution.py:360
  175.1 11.9 %all-to-all-done.4 = bf16[4,64,1024]{2,1,0:T(8,128)(2,1)S(1)} async-done(((bf16[4,64,1024]{2,1,0:T(8,128)(2,1)}), bf16[4,64,1024]{2,1,0:T(8,128)(2,1)S(1)}, u32[]{:S(2)}, u32[]{:S(2)}) %all-to-all-start.4) | async-done | bytes 524320 | tf_op jit(solution)/shard_map/all_to_all | solution.py:360
  187.0 1.8 select.11
  188.8 5.0 %all-to-all-start.5 = ((bf16[32,160,128]{2,1,0:T(8,128)(2,1)}), bf16[32,160,128]{2,1,0:T(8,128)(2,1)S(1)}, u32[]{:S(2)}, u32[]{:S(2)}) async-start(bf16[32,160,128]{2,1,0:T(8,128)(2,1)} %bitcast.20), calls=%async_computation.5 | async-start | bytes 2621440 | tf_op jit(solution)/shard_map/all_to_all | solution.py:362
  195.7 1.5 fusion.14
  197.9 28.5 %all-to-all-done.5 = bf16[32,160,128]{2,1,0:T(8,128)(2,1)S(1)} async-done(((bf16[32,160,128]{2,1,0:T(8,128)(2,1)}), bf16[32,160,128]{2,1,0:T(8,128)(2,1)S(1)}, u32[]{:S(2)}, u32[]{:S(2)}) %all-to-all-start.5) | async-done | bytes 1310752 | tf_op jit(solution)/shard_map/all_to_all | solution.py:362
  227.6 4.4 %expert.1 = bf16[5120,128]{1,0:T(8,128)(2,1)} custom-call(bf16[5120,128]{1,0:T(8,128)(2,1)S(1)} %bitcast.42, bf16[1024,768]{1,0:T(8,128)(2,1)S(1)} %pad_maximum_fusion.win_ref, bf16[384,1024]{1,0:T(8,128)(2,1)S(1)} %copy-done.1), custom_call_target="tpu_custom_call" | custom-call | tf_op jit(solution)/shard_map/expert/pallas_call | solution.py:230
  231.9 5.4 %all-to-all-start.6 = ((bf16[32,160,128]{2,1,0:T(8,128)(2,1)}), bf16[32,160,128]{2,1,0:T(8,128)(2,1)S(1)}, u32[]{:S(2)}, u32[]{:S(2)}) async-start(bf16[32,160,128]{2,1,0:T(8,128)(2,1)} %bitcast.22), calls=%async_computation.6 | async-start | bytes 2621440 | tf_op jit(solution)/shard_map/all_to_all | solution.py:366
  238.8 30.8 %all-to-all-done.6 = bf16[32,160,128]{2,1,0:T(8,128)(2,1)S(1)} async-done(((bf16[32,160,128]{2,1,0:T(8,128)(2,1)}), bf16[32,160,128]{2,1,0:T(8,128)(2,1)S(1)}, u32[]{:S(2)}, u32[]{:S(2)}) %all-to-all-start.6) | async-done | bytes 1310752 | tf_op jit(solution)/shard_map/all_to_all | solution.py:366
  270.4 17.5 %all_to_all.41 = bf16[4,64,1024]{2,1,0:T(8,128)(2,1)S(1)} all-to-all(bf16[4,64,1024]{2,1,0:T(8,128)(2,1)S(1)} %bitcast.44), channel_id=1, replica_groups=mesh['z'=8,'x'=4,'y2'=4,'y1'=2,'dp'=2] {'y2'}, dimensions={0} | all-to-all | bytes 1048576 | tf_op jit(solution)/shard_map/all_to_all | solution.py:370
  (76 shorter events, 14.7 us)
Async XLA Ops:
  6.5 32.6 %copy-start = (bf16[256,1024]{1,0:T(8,128)(2,1)S(1)}, bf16[256,1024]{1,0:T(8,128)(2,1)}, u32[]{:S(2)}) copy-start(bf16[256,1024]{1,0:T(8,128)(2,1)} %param.14) | copy-start | bytes 1572868
  6.5 26.5 %copy-start.10 = (bf16[64,2048]{1,0:T(8,128)(2,1)S(1)}, bf16[64,2048]{1,0:T(8,128)(2,1)}, u32[]{:S(2)}) copy-start(bf16[64,2048]{1,0:T(8,128)(2,1)} %param.11) | copy-start | bytes 786436
  6.5 74.0 %all-gather.3.cloned.1.call-start = ((), (), s32[]{:S(2)}) async-start(), calls=%async_computation.8 | async-start | bytes 2359296 | tf_op jit(solution)/shard_map/all_gather | solution.py:300
  34.3 32.5 %copy-start.5 = (bf16[1,1024,384]{2,1,0:T(8,128)(2,1)S(1)}, bf16[1,1024,384]{2,1,0:T(8,128)(2,1)}, u32[]{:S(2)}) copy-start(bf16[1,1024,384]{2,1,0:T(8,128)(2,1)} %param.18) | copy-start | bytes 2359300
  34.3 36.1 %copy-start.11 = (s32[64,8]{0,1:T(8,128)S(1)}, s32[64,8]{0,1:T(8,128)}, u32[]{:S(2)}) copy-start(s32[64,8]{0,1:T(8,128)} %param.17) | copy-start | bytes 6148
  34.3 36.1 %copy-start.12 = (s32[64,8]{0,1:T(8,128)S(1)}, s32[64,8]{0,1:T(8,128)}, u32[]{:S(2)}) copy-start(s32[64,8]{0,1:T(8,128)} %param.16) | copy-start | bytes 6148
  34.4 36.1 %copy-start.6 = (bf16[1,192,1024]{2,1,0:T(8,128)(2,1)S(1)}, bf16[1,192,1024]{2,1,0:T(8,128)(2,1)}, u32[]{:S(2)}) copy-start(bf16[1,192,1024]{2,1,0:T(8,128)(2,1)} %param.19) | copy-start | bytes 1179652
  34.4 32.4 %all-to-all-start.1 = ((bf16[32,64,256]{2,1,0:T(8,128)(2,1)}), bf16[32,64,256]{2,1,0:T(8,128)(2,1)S(1)}, u32[]{:S(2)}, u32[]{:S(2)}) async-start(bf16[32,64,256]{2,1,0:T(8,128)(2,1)} %bitcast.4), calls=%async_computation.1 | async-start | bytes 2097152 | tf_op jit(solution)/shard_map/all_to_all | solution.py:307
  39.1 81.7 %all-gather.5.cloned.1.call-start = ((), (), s32[]{:S(2)}) async-start(), calls=%async_computation.9 | async-start | bytes 2359296 | tf_op jit(solution)/shard_map/all_gather | solution.py:342
  66.8 47.7 %collective-permute-start = (bf16[1024,384]{1,0:T(8,128)(2,1)S(1)}, bf16[1024,384]{1,0:T(8,128)(2,1)}, u32[]{:S(2)}, u32[]{:S(2)}) collective-permute-start(bf16[1024,384]{1,0:T(8,128)(2,1)S(1)} %bitcast.48), channel_id=1, source_target_pairs={{0,2},{2,0},{1,3},{3,1},{4,6},{6,4},{5,7},{7,5},{8,10},{10,8},{9,1... | collective-permute-start | bytes 2359304 | tf_op jit(solution)/shard_map/ppermute | solution.py:338
  70.4 44.1 %copy-start.2 = (s32[3]{0:T(128)}, s32[3]{0:T(128)S(1)}, u32[]{:S(2)}) copy-start(s32[3]{0:T(128)S(1)} %pad_add_fusion.1.pos_ref) | copy-start | bytes 40
  70.4 44.1 %collective-permute-start.1 = (bf16[192,1024]{1,0:T(8,128)(2,1)S(1)}, bf16[192,1024]{1,0:T(8,128)(2,1)S(1)}, u32[]{:S(2)}, u32[]{:S(2)}) collective-permute-start(bf16[192,1024]{1,0:T(8,128)(2,1)S(1)} %bitcast.53), channel_id=1, source_target_pairs={{0,2},{2,0},{1,3},{3,1},{4,6},{6,4},{5,7},{7,5},{8,10},{10,8},{9,1... | collective-permute-start | bytes 1179656 | tf_op jit(solution)/shard_map/ppermute | solution.py:339
  73.5 41.1 %all-to-all-start.3 = ((s32[4,1,1024]{2,1,0:T(1,128)}), s32[4,1,1024]{2,1,0:T(1,128)S(1)}, u32[]{:S(2)}, u32[]{:S(2)}) async-start(s32[4,1,1024]{2,1,0:T(1,128)} %reshape.149), calls=%async_computation.3 | async-start | bytes 32768 | tf_op jit(solution)/shard_map/all_to_all | solution.py:314
  80.6 1.6 copy-start.3
  114.5 0.8 copy-start.7
  115.3 33.5 %all-to-all-start.2 = ((bf16[32,136,128]{2,1,0:T(8,128)(2,1)}), bf16[32,136,128]{2,1,0:T(8,128)(2,1)S(1)}, u32[]{:S(2)}, u32[]{:S(2)}) async-start(bf16[32,136,128]{2,1,0:T(8,128)(2,1)} %bitcast.12), calls=%async_computation.2 | async-start | bytes 2228224 | tf_op jit(solution)/shard_map/all_to_all | solution.py:347
  120.8 28.1 %collective-permute-start.2 = (bf16[1024,1024]{1,0:T(8,128)(2,1)}, bf16[1024,1024]{1,0:T(8,128)(2,1)}, u32[]{:S(2)}, u32[]{:S(2)}) collective-permute-start(bf16[1024,1024]{1,0:T(8,128)(2,1)} %all-gather.5.cloned.1.call-done.w_ref), channel_id=1, source_target_pairs={{0,1},{1,0},{2,3},{3,2},{4,5},{5,4},{6,7},{7,6},{8,9},{9,8},{10,11... | collective-permute-start | bytes 6291464 | tf_op jit(solution)/shard_map/ppermute | solution.py:343
  148.8 1.0 copy-start.4
  159.4 27.6 %all-to-all-start.4 = ((bf16[4,64,1024]{2,1,0:T(8,128)(2,1)}), bf16[4,64,1024]{2,1,0:T(8,128)(2,1)S(1)}, u32[]{:S(2)}, u32[]{:S(2)}) async-start(bf16[4,64,1024]{2,1,0:T(8,128)(2,1)} %broadcast_in_dim.82), calls=%async_computation.4 | async-start | bytes 1048576 | tf_op jit(solution)/shard_map/all_to_all | solution.py:360
  188.8 37.6 %all-to-all-start.5 = ((bf16[32,160,128]{2,1,0:T(8,128)(2,1)}), bf16[32,160,128]{2,1,0:T(8,128)(2,1)S(1)}, u32[]{:S(2)}, u32[]{:S(2)}) async-start(bf16[32,160,128]{2,1,0:T(8,128)(2,1)} %bitcast.20), calls=%async_computation.5 | async-start | bytes 2621440 | tf_op jit(solution)/shard_map/all_to_all | solution.py:362
  193.8 1.0 copy-start.8
  226.4 1.1 copy-start.1
  231.9 37.6 %all-to-all-start.6 = ((bf16[32,160,128]{2,1,0:T(8,128)(2,1)}), bf16[32,160,128]{2,1,0:T(8,128)(2,1)S(1)}, u32[]{:S(2)}, u32[]{:S(2)}) async-start(bf16[32,160,128]{2,1,0:T(8,128)(2,1)} %bitcast.22), calls=%async_computation.6 | async-start | bytes 2621440 | tf_op jit(solution)/shard_map/all_to_all | solution.py:366
  269.6 18.4 %copy-start.9 = (f32[64,1024]{1,0:T(8,128)S(1)}, f32[64,1024]{1,0:T(8,128)}, u32[]{:S(2)}) copy-start(f32[64,1024]{1,0:T(8,128)} %get-tuple-element.20) | copy-start | bytes 786436
Sparse Core Ops, SparseCore 0:
  33.2 39.6 all-gather.2
  75.0 44.4 all-gather.4

commit v3 on v2

--- a/solution.py
+++ b/solution.py
@@ -14,71 +14,111 @@
 BF = jnp.bfloat16
 F32 = jnp.float32
 NEG = -1e30
+LOW = -1e29
 STAT = 8
-
-
-def flash_kernel(pos_ref, q_ref, kv_ref, o_ref, vt_ref, m_ref, acc_ref):
+SWAP = [(0, 1), (1, 0)]
+
+
+def flash_kernel(pos_ref, q_ref, kv_ref, o_ref, vt_ref, bias_ref, acc_ref, m_ref, top_ref):
     block = pl.program_id(0)
     own_x = pos_ref[0]
     own_y = pos_ref[1]
-    nz = q_ref.shape[1]
-    cols = nz * 128
+    cols = 1024
     scale = LOG2E / math.sqrt(HD)
 
-    @pl.when((block == 0) & (pl.program_id(1) == 0))
-    def _():
+    def keys(c):
+        return kv_ref[pl.ds(4 * (c % 2), 4), c // 2, :, 0:HD].reshape(512, HD)
+
+    @pl.when(block == 0)
+    def _():
+        eye = (
+            lax.broadcasted_iota(jnp.int32, (HD, HD), 0)
+            == lax.broadcasted_iota(jnp.int32, (HD, HD), 1)
+        ).astype(BF)
         for c in range(8):
-            v = kv_ref[4 * (c % 2) : 4 * (c % 2) + 4, c // 2, :, 128:256].reshape(512, HD)
-            vt_ref[c, 0:HD, :] = v.astype(F32).T.astype(BF)
+            v = kv_ref[4 * (c % 2) : 4 * (c % 2) + 4, c // 2, :, HD : 2 * HD].reshape(512, HD)
+            turned = lax.dot_general(eye, v, (((1,), (1,)), ((), ())), preferred_element_type=F32)
+            vt_ref[c, 0:HD, :] = turned.astype(BF)
             vt_ref[c, HD : HD + 16, :] = jnp.ones((16, 512), BF)
+        row = lax.broadcasted_iota(jnp.int32, (512, 128), 0)
+        col = lax.broadcasted_iota(jnp.int32, (512, 128), 1)
+        inner = row % 128
+        key_pos = (
+            (row // 128 - own_y % 4) * 512 + (inner // 16) * 64 + inner % 16 + 16 * own_x - col % 64
+        )
+        for z in range(8):
+            bias_ref[:, z * 128 : (z + 1) * 128] = jnp.where(key_pos <= z * 64, 0.0, NEG)
 
     tiles = block * 8 + own_y
     chunk_count = tiles // 4
     q_raw = q_ref[0]
     q = jnp.concatenate([q_raw[:, :, 0:HD], q_raw[:, :, HD : 2 * HD]], axis=1).reshape(cols, HD)
-    group = 256
+    group = 1024
     groups = [(g * group, q[g * group : (g + 1) * group]) for g in range(cols // group)]
 
-    def keys(c):
-        return kv_ref[pl.ds(4 * (c % 2), 4), c // 2, :, 0:HD].reshape(512, HD)
-
     def scores(k, q_group):
-        return lax.dot_general(
-            k, q_group, (((1,), (1,)), ((), ())), preferred_element_type=F32
-        )
-
-    last_keys = keys(chunk_count)
-    last_values = vt_ref[chunk_count]
-    row = lax.broadcasted_iota(jnp.int32, (512, group), 0)
-    col = lax.broadcasted_iota(jnp.int32, (512, group), 1)
-    inner = row % 128
-    key_pos = (4 * chunk_count + row // 128) * 512 + (inner // 16) * 64 + inner % 16 + 16 * own_x
+        return lax.dot_general(k, q_group, (((1,), (1,)), ((), ())), preferred_element_type=F32)
+
+    first_keys = kv_ref[0, 0, :, 0:HD]
+    hide = jnp.where(tiles == 0, 1.0, 0.0)
     for start, q_group in groups:
-        z_first = pl.program_id(1) * nz + start // 128
-        q_pos = tiles * 512 + (z_first + col // 128) * 64 + col % 64
-        allowed = key_pos <= q_pos
-        s = jnp.where(allowed, scores(last_keys, q_group), NEG)
-        m = jnp.max(s, axis=0, keepdims=True)
-        p = jnp.where(allowed, jnp.exp2((s - m) * scale), 0.0).astype(BF)
-        m_ref[:, start : start + group] = m
-        acc_ref[:, start : start + group] = jnp.dot(last_values, p, preferred_element_type=F32)
-
-    def step(c, carry):
+        part = slice(start, start + group)
+        s = scores(first_keys, q_group) + bias_ref[0:128, part] * hide
+        m_ref[:, part] = jnp.maximum(jnp.max(s, axis=0, keepdims=True), LOW)
+        top_ref[:, part] = jnp.max(s.reshape(16, 8, group), axis=0)
+        acc_ref[:, part] = jnp.zeros((HD + 16, group), F32)
+
+    def quick(c, masked):
+        k = keys(c)
+        values = vt_ref[c]
+        found = [scores(k, q_group) for _, q_group in groups]
+        for (start, _), s in zip(groups, found):
+            part = slice(start, start + group)
+            if masked:
+                s = s + bias_ref[:, part]
+            p = jnp.exp2(s * scale - m_ref[:, part] * scale).astype(BF)
+            top_ref[:, part] = jnp.maximum(
+                top_ref[:, part], jnp.max(s.reshape(64, 8, group), axis=0)
+            )
+            acc_ref[:, part] = acc_ref[:, part] + jnp.dot(values, p, preferred_element_type=F32)
+
+    def quick_step(c, carry):
+        quick(c, False)
+        return carry
+
+    lax.fori_loop(0, chunk_count, quick_step, 0)
+    quick(chunk_count, True)
+
+    def careful(c, masked):
         k = keys(c)
         values = vt_ref[c]
         for start, q_group in groups:
+            part = slice(start, start + group)
             s = scores(k, q_group)
-            m_old = m_ref[:, start : start + group]
+            if masked:
+                s = s + bias_ref[:, part]
+            m_old = m_ref[:, part]
             m = jnp.maximum(m_old, jnp.max(s, axis=0, keepdims=True))
             p = jnp.exp2((s - m) * scale).astype(BF)
             alpha = jnp.exp2((m_old - m) * scale)
-            m_ref[:, start : start + group] = m
-            acc_ref[:, start : start + group] = acc_ref[
-                :, start : start + group
-            ] * alpha + jnp.dot(values, p, preferred_element_type=F32)
+            m_ref[:, part] = m
+            acc_ref[:, part] = acc_ref[:, part] * alpha + jnp.dot(
+                values, p, preferred_element_type=F32
+            )
+
+    def careful_step(c, carry):
+        careful(c, False)
         return carry
 
-    lax.fori_loop(0, chunk_count, step, 0)
+    rise = jnp.max((top_ref[...] - m_ref[...]) * scale)
+
+    @pl.when(rise > 64.0)
+    def _():
+        m_ref[...] = jnp.full((1, cols), LOW, F32)
+        acc_ref[...] = jnp.zeros((HD + 16, cols), F32)
+        lax.fori_loop(0, chunk_count, careful_step, 0)
+        careful(chunk_count, True)
+
     total = acc_ref[HD : HD + 1, :]
     seen = total > 0.0
     safe = jnp.where(seen, total, 1.0)
@@ -90,27 +130,28 @@
     pick = lax.broadcasted_iota(jnp.int32, (STAT, cols), 0)
     stats = jnp.where(pick == 0, first, jnp.where(pick == 1, second, jnp.where(pick == 2, third, 0.0)))
     stats = stats.astype(BF)
-    for i in range(nz):
+    for i in range(8):
         o_ref[0, i, 0:HD, :] = out[:, i * 128 : (i + 1) * 128]
         o_ref[0, i, HD : HD + STAT, :] = stats[:, i * 128 : (i + 1) * 128]
 
 
 def flash(position, queries, key_values):
-    nz = 4
     return pl.pallas_call(
         flash_kernel,
         grid_spec=pltpu.PrefetchScalarGridSpec(
             num_scalar_prefetch=1,
-            grid=(4, 8 // nz),
+            grid=(4,),
             in_specs=[
-                pl.BlockSpec((1, nz, 64, 256), lambda i, j, s: (i, j, 0, 0)),
-                pl.BlockSpec((8, 4, 128, 256), lambda i, j, s: (0, 0, 0, 0)),
+                pl.BlockSpec((1, 8, 64, 256), lambda i, s: (i, 0, 0, 0)),
+                pl.BlockSpec((8, 4, 128, 256), lambda i, s: (0, 0, 0, 0)),
             ],
-            out_specs=pl.BlockSpec((1, nz, HD + STAT, 128), lambda i, j, s: (i, j, 0, 0)),
+            out_specs=pl.BlockSpec((1, 8, HD + STAT, 128), lambda i, s: (i, 0, 0, 0)),
             scratch_shapes=[
                 pltpu.VMEM((8, HD + 16, 512), BF),
-                pltpu.VMEM((1, nz * 128), F32),
-                pltpu.VMEM((HD + 16, nz * 128), F32),
+                pltpu.VMEM((512, 1024), F32),
+                pltpu.VMEM((HD + 16, 1024), F32),
+                pltpu.VMEM((1, 1024), F32),
+                pltpu.VMEM((8, 1024), F32),
             ],
         ),
         out_shape=jax.ShapeDtypeStruct((4, 8, HD + STAT, 128), BF),
@@ -122,69 +163,91 @@
     )(position, queries, key_values)
 
 
-def merge_kernel(pos_ref, parts_ref, w_ref, v_ref, res_ref, gain_ref, hidden_ref, normed_ref, acc_ref):
-    c = pl.program_id(0)
-    levels = []
-    for x in range(4):
-        st = parts_ref[x, 0, HD : HD + STAT, :].astype(F32)
-        levels.append(st[0:1] + st[1:2] + st[2:3])
-    top = jnp.maximum(jnp.maximum(levels[0], levels[1]), jnp.maximum(levels[2], levels[3]))
-    shares = [jnp.exp2(level - top) for level in levels]
-    inverse = 1.0 / (shares[0] + shares[1] + shares[2] + shares[3])
-    mixed = parts_ref[0, 0, 0:HD, :].astype(F32) * (shares[0] * inverse)
-    for x in range(1, 4):
-        mixed = mixed + parts_ref[x, 0, 0:HD, :].astype(F32) * (shares[x] * inverse)
-    rows = mixed.T.astype(BF)
-    first = pos_ref[2] == 0
-    attention = jnp.concatenate(
-        [jnp.where(first, rows[0:64], rows[64:128]), jnp.where(first, rows[64:128], rows[0:64])],
-        axis=1,
-    )
-    weight = jnp.concatenate([w_ref[...], v_ref[...]], axis=0)
-    part = jnp.dot(attention, weight, preferred_element_type=F32)
-
-    @pl.when(c == 0)
-    def _():
-        acc_ref[...] = res_ref[...].astype(F32) + part
-
-    @pl.when(c > 0)
-    def _():
-        acc_ref[...] = acc_ref[...] + part
-
-    @pl.when(c == 7)
-    def _():
-        hidden = acc_ref[...]
-        hidden_ref[...] = hidden
+def merged_heads(pos_ref, parts_ref, second):
+    found = []
+    for c in range(2):
+        levels = []
+        for x in range(4):
+            st = parts_ref[x, c, HD : HD + STAT, :].astype(F32)
+            levels.append(st[0:1] + st[1:2] + st[2:3])
+        top = jnp.maximum(jnp.maximum(levels[0], levels[1]), jnp.maximum(levels[2], levels[3]))
+        shares = [jnp.exp2(level - top) for level in levels]
+        inverse = 1.0 / (shares[0] + shares[1] + shares[2] + shares[3])
+        mixed = parts_ref[0, c, 0:HD, :].astype(F32) * (shares[0] * inverse)
+        for x in range(1, 4):
+            mixed = mixed + parts_ref[x, c, 0:HD, :].astype(F32) * (shares[x] * inverse)
+        rows = mixed.T.astype(BF)
+        found.append(jnp.where((pos_ref[2] == 0) != second, rows[0:64], rows[64:128]))
+    return jnp.concatenate(found, axis=1)
+
+
+def merge_own_kernel(pos_ref, parts_ref, w_ref, res_ref, o_ref):
+    part = jnp.dot(merged_heads(pos_ref, parts_ref, False), w_ref[...], preferred_element_type=F32)
+
+    @pl.when(pl.program_id(0) == 0)
+    def _():
+        o_ref[...] = res_ref[...].astype(F32) + part
+
+    @pl.when(pl.program_id(0) > 0)
+    def _():
+        o_ref[...] = o_ref[...] + part
+
+
+def merge_other_kernel(pos_ref, parts_ref, w_ref, sum_ref, gain_ref, hidden_ref, normed_ref):
+    step = pl.program_id(0)
+    part = jnp.dot(merged_heads(pos_ref, parts_ref, True), w_ref[...], preferred_element_type=F32)
+
+    @pl.when(step == 0)
+    def _():
+        hidden_ref[...] = sum_ref[...] + part
+
+    @pl.when(step > 0)
+    def _():
+        hidden_ref[...] = hidden_ref[...] + part
+
+    @pl.when(step == 3)
+    def _():
+        hidden = hidden_ref[...]
         mean_square = jnp.mean(hidden * hidden, axis=1, keepdims=True)
         normed_ref[...] = (hidden * lax.rsqrt(mean_square + 1e-6) * gain_ref[...]).astype(BF)
 
 
+def merge_specs(tokens, width):
+    return [
+        pl.BlockSpec((4, 2, HD + STAT, 128), lambda c, s: (0, c, 0, 0)),
+        pl.BlockSpec((256, width), lambda c, s: (c, 0)),
+        pl.BlockSpec((tokens, width), lambda c, s: (0, 0)),
+    ]
+
+
 def merge(position, parts, weight, weight_other, residual, gain):
     tokens, width = residual.shape
-    return pl.pallas_call(
-        merge_kernel,
+    whole = pl.BlockSpec((tokens, width), lambda c, s: (0, 0))
+    half_sum = pl.pallas_call(
+        merge_own_kernel,
         grid_spec=pltpu.PrefetchScalarGridSpec(
             num_scalar_prefetch=1,
-            grid=(8,),
-            in_specs=[
-                pl.BlockSpec((4, 1, HD + STAT, 128), lambda c, s: (0, c, 0, 0)),
-                pl.BlockSpec((128, width), lambda c, s: (c, 0)),
-                pl.BlockSpec((128, width), lambda c, s: (c, 0)),
-                pl.BlockSpec((tokens, width), lambda c, s: (0, 0)),
-                pl.BlockSpec((1, width), lambda c, s: (0, 0)),
-            ],
-            out_specs=[
-                pl.BlockSpec((tokens, width), lambda c, s: (0, 0)),
-                pl.BlockSpec((tokens, width), lambda c, s: (0, 0)),
-            ],
-            scratch_shapes=[pltpu.VMEM((tokens, width), F32)],
+            grid=(4,),
+            in_specs=merge_specs(tokens, width),
+            out_specs=whole,
+        ),
+        out_shape=jax.ShapeDtypeStruct((tokens, width), F32),
+        name="merge_own",
+    )(position, parts, weight, residual)
+    return pl.pallas_call(
+        merge_other_kernel,
+        grid_spec=pltpu.PrefetchScalarGridSpec(
+            num_scalar_prefetch=1,
+            grid=(4,),
+            in_specs=merge_specs(tokens, width) + [pl.BlockSpec((1, width), lambda c, s: (0, 0))],
+            out_specs=[whole, whole],
         ),
         out_shape=[
             jax.ShapeDtypeStruct((tokens, width), F32),
             jax.ShapeDtypeStruct((tokens, width), BF),
         ],
-        name="merge",
-    )(position, parts, weight, weight_other, residual, gain)
+        name="merge_other",
+    )(position, parts, weight_other, half_sum, gain)
 
 
 def select_kernel(sel_ref, x_ref, o_ref, tmp_ref):
@@ -308,9 +371,23 @@
         4, 8, tokens, 2 * HD
     )
 
+    head_weight = lax.dynamic_slice_in_dim(output_weight, own_core * HD, HD, 0)
+    head_weight, _ = lax.optimization_barrier((head_weight, query))
+    gathered = lax.all_gather(head_weight, "z", axis=0, tiled=True)
+    gathered_other = lax.ppermute(gathered, "dp", SWAP)
+
+    own_in, own_out, _ = lax.optimization_barrier((expert_in[0], expert_out[0], query))
+    other_in = lax.ppermute(own_in, "y1", SWAP)
+    other_out = lax.ppermute(own_out, "y1", SWAP)
+
+    shards = flash(position, query, key_values)
+    shards, other_in, other_out = lax.optimization_barrier((shards, other_in, other_out))
+    parts = lax.all_to_all(
+        shards.reshape(32, HD + STAT, 128), ("x", "z"), split_axis=0, concat_axis=0, tiled=True
+    ).reshape(4, 8, HD + STAT, 128)
     listing = jnp.concatenate([routes, gate_levels], axis=1)
     listing = jnp.broadcast_to(listing[None], (4, tokens, 16))
-    listing, _ = lax.optimization_barrier((listing, query))
+    listing, _ = lax.optimization_barrier((listing, shards))
     listing = lax.all_to_all(listing, "y2", split_axis=0, concat_axis=0, tiled=True)
     named, levels = listing[:, :, 0:8], listing[:, :, 8:16]
     local_expert = jnp.arange(32, dtype=jnp.int32)
@@ -333,20 +410,6 @@
     shares = jnp.where(back, gates[:, :, :, None, None], 0.0).astype(BF)
     shares = shares.reshape(4 * tokens, 32 * 4 * CAP)
 
-    swap = [(0, 1), (1, 0)]
-    own_in, own_out, _ = lax.optimization_barrier((expert_in[0], expert_out[0], query))
-    other_in = lax.ppermute(own_in, "y1", swap)
-    other_out = lax.ppermute(own_out, "y1", swap)
-    head_weight = lax.dynamic_slice_in_dim(output_weight, own_core * HD, HD, 0)
-    head_weight, _ = lax.optimization_barrier((head_weight, query))
-    gathered = lax.all_gather(head_weight, "z", axis=0, tiled=True)
-    gathered_other = lax.ppermute(gathered, "dp", swap)
-
-    parts = flash(position, query, key_values)
-    parts, other_in, other_out = lax.optimization_barrier((parts, other_in, other_out))
-    parts = lax.all_to_all(
-        parts.reshape(32, HD + STAT, 128), ("x", "z"), split_axis=0, concat_axis=0, tiled=True
-    ).reshape(4, 8, HD + STAT, 128)
     half = own_in.shape[1] // 2
     weight_in = jnp.concatenate(
         [own_in[:, :half], other_in[:, :half], own_in[:, half:], other_in[:, half:]], axis=1

time: 297 us -> 281 us (0.946)
  blocking collectives: 42.3 us -> 63.3 us
  waiting for transfers between devices: 123 us -> 105 us
  starting transfers between devices: 49.9 us -> 33.7 us
    all_to_all x0 -> x1, blocking collectives: none -> 22.2 us  [local(): lax.all_to_all(listing, 'y2', split_axis=0, concat_axis=0, tiled=True)]
    all_to_all x1, starting transfers between devices: 14.5 us -> 3.47 us  [local(): lax.all_to_all(spread, 'y2', split_axis=0, concat_axis=0, tiled=True)]
    all_to_all x1, waiting for transfers between devices: 28.5 us -> 22.3 us  [local(): lax.all_to_all(outgoing.reshape(32, 4 * CAP * 8, 128), ('x', 'z'), split_...]
    all_to_all x1, waiting for transfers between devices: 30.8 us -> 24.9 us  [local(): lax.all_to_all(done.reshape(32, 4 * CAP * 8, 128), ('x', 'z'), split_axis...]
    all_to_all x2 -> x1, starting transfers between devices: 12.5 us -> 7.42 us  [local(): lax.all_to_all(shards.reshape(32, HD + STAT, 128), ('x', 'z'), split_axis...]
    all_to_all x2 -> x1, waiting for transfers between devices: 24.6 us -> 20.6 us  [local(): lax.all_to_all(shards.reshape(32, HD + STAT, 128), ('x', 'z'), split_axis...]
    pallas_call x1, Pallas kernels: 32.4 us -> 29.2 us  [flash(): pl.pallas_call(flash_kernel, grid_spec=pltpu.PrefetchScalarGridSpec(num_s...]
    pallas_call x1 -> x2, Pallas kernels: 7.77 us -> 9.77 us  [the longest x1 5.01 us: merge(): pl.pallas_call(merge_other_kernel, grid_spec=pltpu.PrefetchScalarGridSpec...]
  transfers between devices with their start and end apart: 11 -> 10, of which waited for: 5 -> 6; matrix products, arithmetic and copies ran while one was open for 3% -> 3% of each run, Pallas kernels for 11% -> 12%
where the time goes in v3:
time: 281 us; the launch traced here: 280 us
  waiting for transfers between devices  105 us (37%)
  blocking collectives  63.3 us (23%)
  Pallas kernels  45.9 us (16%)
  starting transfers between devices  33.7 us (12%)
  between operations  13.8 us (5%)
  local copies, waits for them, and re-layouts  13.5 us (5%)
  other arithmetic  4.67 us (2%)
    pallas_call x1, Pallas kernels, flash(): pl.pallas_call(flash_kernel, grid_spec=pltpu.PrefetchScalarGridSpec(num_s...  29.2 us
    all_to_all x1, waiting for transfers between devices, local(): lax.all_to_all(query, ('x', 'z'), split_axis=0, concat_axis=0, tiled=True)  26.9 us
    all_to_all x1, waiting for transfers between devices, local(): lax.all_to_all(done.reshape(32, 4 * CAP * 8, 128), ('x', 'z'), split_axis...  24.9 us
    all_to_all x1, blocking collectives, local(): lax.all_to_all(key_value, ('x', 'z'), split_axis=0, concat_axis=0, tiled=...  24.8 us
    all_to_all x1, waiting for transfers between devices, local(): lax.all_to_all(outgoing.reshape(32, 4 * CAP * 8, 128), ('x', 'z'), split_...  22.3 us
    all_to_all x1, blocking collectives, local(): lax.all_to_all(listing, 'y2', split_axis=0, concat_axis=0, tiled=True)  22.2 us
    all_to_all x1, waiting for transfers between devices, local(): lax.all_to_all(shards.reshape(32, HD + STAT, 128), ('x', 'z'), split_axis...  20.6 us
    all_to_all x1, blocking collectives, local(): lax.all_to_all(sums.reshape(4, tokens, width), 'y2', split_axis=0, concat...  16.3 us
  transfers between devices with their start and end apart: 10, of which 6 were waited for; matrix products, arithmetic and copies ran while one was open for 3% of the time, Pallas kernels for 12%

profile of v3, /device:TPU:64, one launch (start us, length us, event | category | flops | bytes accessed | tf_op | source)
XLA Modules:
  0.0 280.2 jit_solution(16900491563572760454)
XLA Ops:
  8.3 24.8 %all_to_all.40 = bf16[32,16,256]{2,1,0:T(8,128)(2,1)} all-to-all(bf16[32,16,256]{2,1,0:T(8,128)(2,1)S(1)} %bitcast.51), channel_id=1, replica_groups=mesh['z'=8,'x'=4,'y2'=4,'y1'=2,'dp'=2] {'x','z'}, dimensions={0} | all-to-all | bytes 524288 | tf_op jit(solution)/shard_map/all_to_all | solution.py:362
  34.3 4.7 %all-to-all-start.1 = ((bf16[32,64,256]{2,1,0:T(8,128)(2,1)}), bf16[32,64,256]{2,1,0:T(8,128)(2,1)S(1)}, u32[]{:S(2)}, u32[]{:S(2)}) async-start(bf16[32,64,256]{2,1,0:T(8,128)(2,1)} %bitcast.4), calls=%async_computation.1 | async-start | bytes 2097152 | tf_op jit(solution)/shard_map/all_to_all | solution.py:370
  39.9 26.9 %all-to-all-done.1 = bf16[32,64,256]{2,1,0:T(8,128)(2,1)S(1)} async-done(((bf16[32,64,256]{2,1,0:T(8,128)(2,1)}), bf16[32,64,256]{2,1,0:T(8,128)(2,1)S(1)}, u32[]{:S(2)}, u32[]{:S(2)}) %all-to-all-start.1) | async-done | bytes 1048608 | tf_op jit(solution)/shard_map/all_to_all | solution.py:370
  66.8 3.5 %collective-permute-start = (bf16[1024,384]{1,0:T(8,128)(2,1)S(1)}, bf16[1024,384]{1,0:T(8,128)(2,1)}, u32[]{:S(2)}, u32[]{:S(2)}) collective-permute-start(bf16[1024,384]{1,0:T(8,128)(2,1)S(1)} %bitcast.49), channel_id=1, source_target_pairs={{0,2},{2,0},{1,3},{3,1},{4,6},{6,4},{5,7},{7,5},{8,10},{10,8},{9,1... | collective-permute-start | bytes 2359304 | tf_op jit(solution)/shard_map/ppermute | solution.py:380
  70.4 2.4 collective-permute-start.1
  72.9 1.6 copy-done.3
  74.5 29.2 %flash.1 = bf16[4,8,136,128]{3,2,1,0:T(8,128)(2,1)} custom-call(s32[3]{0:T(128)S(1)} %pad_add_fusion.1.pos_ref, bf16[4,8,64,256]{3,2,1,0:T(8,128)(2,1)S(1)} %bitcast.45, bf16[8,4,128,256]{3,2,1,0:T(8,128)(2,1)S(1)} %bitcast.46), custom_call_target="tpu_custom_call" | custom-call | flops 5368709120 | bytes 5242880 | tf_op jit(solution)/shard_map/flash/pallas_call | solution.py:139
  103.9 22.2 %all_to_all.41 = s32[4,1,1024]{2,1,0:T(1,128)S(1)} all-to-all(s32[4,1,1024]{2,1,0:T(1,128)S(1)} %reshape.149), channel_id=1, replica_groups=mesh['z'=8,'x'=4,'y2'=4,'y1'=2,'dp'=2] {'y2'}, dimensions={0} | all-to-all | bytes 32768 | tf_op jit(solution)/shard_map/all_to_all | solution.py:391
  126.1 7.4 %all-to-all-start.2 = ((bf16[32,136,128]{2,1,0:T(8,128)(2,1)}), bf16[32,136,128]{2,1,0:T(8,128)(2,1)S(1)}, u32[]{:S(2)}, u32[]{:S(2)}) async-start(bf16[32,136,128]{2,1,0:T(8,128)(2,1)} %bitcast.12), calls=%async_computation.2 | async-start | bytes 2228224 | tf_op jit(solution)/shard_map/all_to_all | solution.py:385
  133.5 1.9 collective-permute-start.2
  137.0 20.6 %all-to-all-done.2 = bf16[32,136,128]{2,1,0:T(8,128)(2,1)S(1)} async-done(((bf16[32,136,128]{2,1,0:T(8,128)(2,1)}), bf16[32,136,128]{2,1,0:T(8,128)(2,1)S(1)}, u32[]{:S(2)}, u32[]{:S(2)}) %all-to-all-start.2) | async-done | bytes 1114144 | tf_op jit(solution)/shard_map/all_to_all | solution.py:385
  158.7 4.8 %merge_own.1.sum_ref = f32[64,1024]{1,0:T(8,128)} custom-call(s32[3]{0:T(128)} %copy-done.2, bf16[4,8,136,128]{3,2,1,0:T(8,128)(2,1)} %bitcast.47, bf16[1024,1024]{1,0:T(8,128)(2,1)} %all-gather.5.cloned.1.call-done.w_ref, bf16[64,1024]{1,0:T(8,128)(2,1)} %res_ref.1), custom_call_target="tpu_custom_call" | custom-call | tf_op jit(solution)/shard_map/merge_own/pallas_call | solution.py:226
  163.4 5.0 %merge_other.1 = (f32[64,1024]{1,0:T(8,128)}, bf16[64,1024]{1,0:T(8,128)(2,1)}) custom-call(s32[3]{0:T(128)} %copy-done.2, bf16[4,8,136,128]{3,2,1,0:T(8,128)(2,1)} %bitcast.48, bf16[1024,1024]{1,0:T(8,128)(2,1)} %collective-permute-done.2.w_ref, f32[64,1024]{1,0:T(8,128)} %merge_own.1.sum_ref, f32[1,1024]{1,0:T(1,128)} %bitcast.59), custom_call_target="tpu_custom_call" | custom-call | tf_op jit(solution)/shard_map/merge_other/pallas_call | solution.py:237
  168.4 1.8 broadcast_in_dim.82
  170.2 3.5 %all-to-all-start.4 = ((bf16[4,64,1024]{2,1,0:T(8,128)(2,1)}), bf16[4,64,1024]{2,1,0:T(8,128)(2,1)S(1)}, u32[]{:S(2)}, u32[]{:S(2)}) async-start(bf16[4,64,1024]{2,1,0:T(8,128)(2,1)} %broadcast_in_dim.82), calls=%async_computation.4 | async-start | bytes 1048576 | tf_op jit(solution)/shard_map/all_to_all | solution.py:423
  174.8 10.3 %all-to-all-done.4 = bf16[4,64,1024]{2,1,0:T(8,128)(2,1)S(1)} async-done(((bf16[4,64,1024]{2,1,0:T(8,128)(2,1)}), bf16[4,64,1024]{2,1,0:T(8,128)(2,1)S(1)}, u32[]{:S(2)}, u32[]{:S(2)}) %all-to-all-start.4) | async-done | bytes 524320 | tf_op jit(solution)/shard_map/all_to_all | solution.py:423
  185.1 1.8 select.11
  186.9 5.1 %all-to-all-start.5 = ((bf16[32,160,128]{2,1,0:T(8,128)(2,1)}), bf16[32,160,128]{2,1,0:T(8,128)(2,1)S(1)}, u32[]{:S(2)}, u32[]{:S(2)}) async-start(bf16[32,160,128]{2,1,0:T(8,128)(2,1)} %bitcast.20), calls=%async_computation.5 | async-start | bytes 2621440 | tf_op jit(solution)/shard_map/all_to_all | solution.py:425
  193.9 1.5 fusion.14
  196.1 22.3 %all-to-all-done.5 = bf16[32,160,128]{2,1,0:T(8,128)(2,1)S(1)} async-done(((bf16[32,160,128]{2,1,0:T(8,128)(2,1)}), bf16[32,160,128]{2,1,0:T(8,128)(2,1)S(1)}, u32[]{:S(2)}, u32[]{:S(2)}) %all-to-all-start.5) | async-done | bytes 1310752 | tf_op jit(solution)/shard_map/all_to_all | solution.py:425
  219.5 4.4 %expert.1 = bf16[5120,128]{1,0:T(8,128)(2,1)} custom-call(bf16[5120,128]{1,0:T(8,128)(2,1)S(1)} %bitcast.42, bf16[1024,768]{1,0:T(8,128)(2,1)S(1)} %pad_maximum_fusion.win_ref, bf16[384,1024]{1,0:T(8,128)(2,1)S(1)} %copy-done.1), custom_call_target="tpu_custom_call" | custom-call | tf_op jit(solution)/shard_map/expert/pallas_call | solution.py:293
  223.9 5.2 %all-to-all-start.6 = ((bf16[32,160,128]{2,1,0:T(8,128)(2,1)}), bf16[32,160,128]{2,1,0:T(8,128)(2,1)S(1)}, u32[]{:S(2)}, u32[]{:S(2)}) async-start(bf16[32,160,128]{2,1,0:T(8,128)(2,1)} %bitcast.22), calls=%async_computation.6 | async-start | bytes 2621440 | tf_op jit(solution)/shard_map/all_to_all | solution.py:429
  230.6 24.9 %all-to-all-done.6 = bf16[32,160,128]{2,1,0:T(8,128)(2,1)S(1)} async-done(((bf16[32,160,128]{2,1,0:T(8,128)(2,1)}), bf16[32,160,128]{2,1,0:T(8,128)(2,1)S(1)}, u32[]{:S(2)}, u32[]{:S(2)}) %all-to-all-start.6) | async-done | bytes 1310752 | tf_op jit(solution)/shard_map/all_to_all | solution.py:429
  256.2 16.3 %all_to_all.42 = bf16[4,64,1024]{2,1,0:T(8,128)(2,1)S(1)} all-to-all(bf16[4,64,1024]{2,1,0:T(8,128)(2,1)S(1)} %bitcast.44), channel_id=1, replica_groups=mesh['z'=8,'x'=4,'y2'=4,'y1'=2,'dp'=2] {'y2'}, dimensions={0} | all-to-all | bytes 1048576 | tf_op jit(solution)/shard_map/all_to_all | solution.py:433
  (76 shorter events, 14.7 us)
Async XLA Ops:
  6.5 32.6 %copy-start = (bf16[256,1024]{1,0:T(8,128)(2,1)S(1)}, bf16[256,1024]{1,0:T(8,128)(2,1)}, u32[]{:S(2)}) copy-start(bf16[256,1024]{1,0:T(8,128)(2,1)} %param.14) | copy-start | bytes 1572868
  6.5 26.5 %copy-start.10 = (bf16[64,2048]{1,0:T(8,128)(2,1)S(1)}, bf16[64,2048]{1,0:T(8,128)(2,1)}, u32[]{:S(2)}) copy-start(bf16[64,2048]{1,0:T(8,128)(2,1)} %param.11) | copy-start | bytes 786436
  6.5 66.4 %all-gather.3.cloned.1.call-start = ((), (), s32[]{:S(2)}) async-start(), calls=%async_computation.8 | async-start | bytes 2359296 | tf_op jit(solution)/shard_map/all_gather | solution.py:363
  34.3 32.5 %copy-start.5 = (bf16[1,1024,384]{2,1,0:T(8,128)(2,1)S(1)}, bf16[1,1024,384]{2,1,0:T(8,128)(2,1)}, u32[]{:S(2)}) copy-start(bf16[1,1024,384]{2,1,0:T(8,128)(2,1)} %param.18) | copy-start | bytes 2359300
  34.3 36.1 %copy-start.11 = (s32[64,8]{0,1:T(8,128)S(1)}, s32[64,8]{0,1:T(8,128)}, u32[]{:S(2)}) copy-start(s32[64,8]{0,1:T(8,128)} %param.17) | copy-start | bytes 6148
  34.3 36.1 %copy-start.12 = (s32[64,8]{0,1:T(8,128)S(1)}, s32[64,8]{0,1:T(8,128)}, u32[]{:S(2)}) copy-start(s32[64,8]{0,1:T(8,128)} %param.16) | copy-start | bytes 6148
  34.3 36.1 %copy-start.6 = (bf16[1,192,1024]{2,1,0:T(8,128)(2,1)S(1)}, bf16[1,192,1024]{2,1,0:T(8,128)(2,1)}, u32[]{:S(2)}) copy-start(bf16[1,192,1024]{2,1,0:T(8,128)(2,1)} %param.19) | copy-start | bytes 1179652
  34.3 32.4 %all-to-all-start.1 = ((bf16[32,64,256]{2,1,0:T(8,128)(2,1)}), bf16[32,64,256]{2,1,0:T(8,128)(2,1)S(1)}, u32[]{:S(2)}, u32[]{:S(2)}) async-start(bf16[32,64,256]{2,1,0:T(8,128)(2,1)} %bitcast.4), calls=%async_computation.1 | async-start | bytes 2097152 | tf_op jit(solution)/shard_map/all_to_all | solution.py:370
  39.1 94.5 %all-gather.5.cloned.1.call-start = ((), (), s32[]{:S(2)}) async-start(), calls=%async_computation.9 | async-start | bytes 2359296 | tf_op jit(solution)/shard_map/all_gather | solution.py:376
  66.8 37.0 %collective-permute-start = (bf16[1024,384]{1,0:T(8,128)(2,1)S(1)}, bf16[1024,384]{1,0:T(8,128)(2,1)}, u32[]{:S(2)}, u32[]{:S(2)}) collective-permute-start(bf16[1024,384]{1,0:T(8,128)(2,1)S(1)} %bitcast.49), channel_id=1, source_target_pairs={{0,2},{2,0},{1,3},{3,1},{4,6},{6,4},{5,7},{7,5},{8,10},{10,8},{9,1... | collective-permute-start | bytes 2359304 | tf_op jit(solution)/shard_map/ppermute | solution.py:380
  70.4 33.4 %copy-start.2 = (s32[3]{0:T(128)}, s32[3]{0:T(128)S(1)}, u32[]{:S(2)}) copy-start(s32[3]{0:T(128)S(1)} %pad_add_fusion.1.pos_ref) | copy-start | bytes 40
  70.4 33.3 %collective-permute-start.1 = (bf16[192,1024]{1,0:T(8,128)(2,1)S(1)}, bf16[192,1024]{1,0:T(8,128)(2,1)S(1)}, u32[]{:S(2)}, u32[]{:S(2)}) collective-permute-start(bf16[192,1024]{1,0:T(8,128)(2,1)S(1)} %bitcast.54), channel_id=1, source_target_pairs={{0,2},{2,0},{1,3},{3,1},{4,6},{6,4},{5,7},{7,5},{8,10},{10,8},{9,1... | collective-permute-start | bytes 1179656 | tf_op jit(solution)/shard_map/ppermute | solution.py:381
  72.9 1.6 copy-start.3
  103.8 22.3 %copy-start.7 = (bf16[192,1024]{1,0:T(8,128)(2,1)}, bf16[192,1024]{1,0:T(8,128)(2,1)S(1)}, u32[]{:S(2)}) copy-start(bf16[192,1024]{1,0:T(8,128)(2,1)S(1)} %collective-permute-done.1) | copy-start | bytes 1179652
  126.1 31.6 %all-to-all-start.2 = ((bf16[32,136,128]{2,1,0:T(8,128)(2,1)}), bf16[32,136,128]{2,1,0:T(8,128)(2,1)S(1)}, u32[]{:S(2)}, u32[]{:S(2)}) async-start(bf16[32,136,128]{2,1,0:T(8,128)(2,1)} %bitcast.12), calls=%async_computation.2 | async-start | bytes 2228224 | tf_op jit(solution)/shard_map/all_to_all | solution.py:385
  133.5 29.9 %collective-permute-start.2 = (bf16[1024,1024]{1,0:T(8,128)(2,1)}, bf16[1024,1024]{1,0:T(8,128)(2,1)}, u32[]{:S(2)}, u32[]{:S(2)}) collective-permute-start(bf16[1024,1024]{1,0:T(8,128)(2,1)} %all-gather.5.cloned.1.call-done.w_ref), channel_id=1, source_target_pairs={{0,1},{1,0},{2,3},{3,2},{4,5},{5,4},{6,7},{7,6},{8,9},{9,8},{10,11... | collective-permute-start | bytes 6291464 | tf_op jit(solution)/shard_map/ppermute | solution.py:377
  157.6 1.0 copy-start.4
  170.2 14.9 %all-to-all-start.4 = ((bf16[4,64,1024]{2,1,0:T(8,128)(2,1)}), bf16[4,64,1024]{2,1,0:T(8,128)(2,1)S(1)}, u32[]{:S(2)}, u32[]{:S(2)}) async-start(bf16[4,64,1024]{2,1,0:T(8,128)(2,1)} %broadcast_in_dim.82), calls=%async_computation.4 | async-start | bytes 1048576 | tf_op jit(solution)/shard_map/all_to_all | solution.py:423
  186.9 31.5 %all-to-all-start.5 = ((bf16[32,160,128]{2,1,0:T(8,128)(2,1)}), bf16[32,160,128]{2,1,0:T(8,128)(2,1)S(1)}, u32[]{:S(2)}, u32[]{:S(2)}) async-start(bf16[32,160,128]{2,1,0:T(8,128)(2,1)} %bitcast.20), calls=%async_computation.5 | async-start | bytes 2621440 | tf_op jit(solution)/shard_map/all_to_all | solution.py:425
  192.0 1.0 copy-start.8
  218.4 1.1 copy-start.1
  223.9 31.5 %all-to-all-start.6 = ((bf16[32,160,128]{2,1,0:T(8,128)(2,1)}), bf16[32,160,128]{2,1,0:T(8,128)(2,1)S(1)}, u32[]{:S(2)}, u32[]{:S(2)}) async-start(bf16[32,160,128]{2,1,0:T(8,128)(2,1)} %bitcast.22), calls=%async_computation.6 | async-start | bytes 2621440 | tf_op jit(solution)/shard_map/all_to_all | solution.py:429
  255.4 17.2 %copy-start.9 = (f32[64,1024]{1,0:T(8,128)S(1)}, f32[64,1024]{1,0:T(8,128)}, u32[]{:S(2)}) copy-start(f32[64,1024]{1,0:T(8,128)} %get-tuple-element.20) | copy-start | bytes 786436
Sparse Core Ops, SparseCore 0:
  33.2 39.6 all-gather.2
  75.0 43.9 all-gather.4

commit v4 on v3

--- a/solution.py
+++ b/solution.py
@@ -209,7 +209,9 @@
     def _():
         hidden = hidden_ref[...]
         mean_square = jnp.mean(hidden * hidden, axis=1, keepdims=True)
-        normed_ref[...] = (hidden * lax.rsqrt(mean_square + 1e-6) * gain_ref[...]).astype(BF)
+        normed = (hidden * lax.rsqrt(mean_square + 1e-6) * gain_ref[...]).astype(BF)
+        for x in range(4):
+            normed_ref[x] = normed
 
 
 def merge_specs(tokens, width):
@@ -240,11 +242,11 @@
             num_scalar_prefetch=1,
             grid=(4,),
             in_specs=merge_specs(tokens, width) + [pl.BlockSpec((1, width), lambda c, s: (0, 0))],
-            out_specs=[whole, whole],
+            out_specs=[whole, pl.BlockSpec((4, tokens, width), lambda c, s: (0, 0, 0))],
         ),
         out_shape=[
             jax.ShapeDtypeStruct((tokens, width), F32),
-            jax.ShapeDtypeStruct((tokens, width), BF),
+            jax.ShapeDtypeStruct((4, tokens, width), BF),
         ],
         name="merge_other",
     )(position, parts, weight_other, half_sum, gain)
@@ -334,6 +336,11 @@
     )(gates, rows)
 
 
+def after(value, other):
+    first = other[(0,) * other.ndim]
+    return value + jnp.where(first > 1 << 30, 1, 0).astype(value.dtype)
+
+
 def local(
     residual,
     queries,
@@ -348,14 +355,19 @@
 ):
     tokens, width = residual.shape
     own_x = lax.axis_index("x")
-    own_y2 = lax.axis_index("y2")
-    own_y = own_y2 * 2 + lax.axis_index("y1")
+    own_y = lax.axis_index("y2") * 2 + lax.axis_index("y1")
     own_core = lax.axis_index("dp")
     position = jnp.stack([own_x, own_y, own_core]).astype(jnp.int32)
 
-    key_value = jnp.concatenate(
-        [key_vectors.reshape(4, 16, 2, HD), value_vectors.reshape(4, 16, 2, HD)], axis=3
-    ).transpose(0, 2, 1, 3)
+    key_value = jnp.stack(
+        [
+            jnp.concatenate(
+                [key_vectors[:, g : g + HD], value_vectors[:, g : g + HD]], axis=1
+            ).reshape(4, 16, 2 * HD)
+            for g in (0, HD)
+        ],
+        axis=1,
+    )
     key_value = jnp.broadcast_to(key_value[:, :, None], (4, 2, 4, 16, 2 * HD)).reshape(
         32, 16, 2 * HD
     )
@@ -374,24 +386,22 @@
     head_weight = lax.dynamic_slice_in_dim(output_weight, own_core * HD, HD, 0)
     head_weight, _ = lax.optimization_barrier((head_weight, query))
     gathered = lax.all_gather(head_weight, "z", axis=0, tiled=True)
-    gathered_other = lax.ppermute(gathered, "dp", SWAP)
 
     own_in, own_out, _ = lax.optimization_barrier((expert_in[0], expert_out[0], query))
     other_in = lax.ppermute(own_in, "y1", SWAP)
     other_out = lax.ppermute(own_out, "y1", SWAP)
 
     shards = flash(position, query, key_values)
-    shards, other_in, other_out = lax.optimization_barrier((shards, other_in, other_out))
     parts = lax.all_to_all(
         shards.reshape(32, HD + STAT, 128), ("x", "z"), split_axis=0, concat_axis=0, tiled=True
     ).reshape(4, 8, HD + STAT, 128)
-    listing = jnp.concatenate([routes, gate_levels], axis=1)
-    listing = jnp.broadcast_to(listing[None], (4, tokens, 16))
-    listing, _ = lax.optimization_barrier((listing, shards))
-    listing = lax.all_to_all(listing, "y2", split_axis=0, concat_axis=0, tiled=True)
+    gathered, other_in, other_out = lax.optimization_barrier((gathered, other_in, other_out))
+    gathered_other = lax.ppermute(gathered, "dp", SWAP)
+    listing = after(jnp.concatenate([routes, gate_levels], axis=1), other_out)
+    listing = lax.all_gather(listing, "x", axis=0, tiled=True).reshape(4, tokens, 16)
     named, levels = listing[:, :, 0:8], listing[:, :, 8:16]
     local_expert = jnp.arange(32, dtype=jnp.int32)
-    wanted = (local_expert % 8) * 16 + (local_expert // 8) * 4 + own_y2
+    wanted = (local_expert // 4) * 16 + own_x * 4 + local_expert % 4
     match = named[:, :, :, None] == wanted
     hits = jnp.any(match, axis=2)
     gates = jnp.sum(jnp.where(match, levels[:, :, :, None], 0), axis=2).astype(F32) / 256.0
@@ -415,23 +425,22 @@
         [own_in[:, :half], other_in[:, :half], own_in[:, half:], other_in[:, half:]], axis=1
     )
     weight_out = jnp.concatenate([own_out, other_out], axis=0)
-    hidden, normed = merge(
+    hidden, spread = merge(
         position, parts, gathered, gathered_other, residual, norm_gain.reshape(1, width)
     )
 
-    spread = jnp.broadcast_to(normed[None], (4, tokens, width))
-    spread = lax.all_to_all(spread, "y2", split_axis=0, concat_axis=0, tiled=True)
+    spread = lax.all_to_all(spread, "x", split_axis=0, concat_axis=0, tiled=True)
     outgoing = select(chosen, spread.reshape(4 * tokens, width))
     arrived = lax.all_to_all(
-        outgoing.reshape(32, 4 * CAP * 8, 128), ("x", "z"), split_axis=0, concat_axis=0, tiled=True
+        outgoing.reshape(32, 4 * CAP * 8, 128), ("z", "y2"), split_axis=0, concat_axis=0, tiled=True
     )
     done = expert(arrived.reshape(-1, 128), weight_in, weight_out)
     answers = lax.all_to_all(
-        done.reshape(32, 4 * CAP * 8, 128), ("x", "z"), split_axis=0, concat_axis=0, tiled=True
+        done.reshape(32, 4 * CAP * 8, 128), ("z", "y2"), split_axis=0, concat_axis=0, tiled=True
     )
     sums = gather(shares, answers.reshape(-1, 128))
     sums = lax.all_to_all(
-        sums.reshape(4, tokens, width), "y2", split_axis=0, concat_axis=0, tiled=True
+        sums.reshape(4, tokens, width), "x", split_axis=0, concat_axis=0, tiled=True
     )
     return hidden + jnp.sum(sums.astype(F32), axis=0)
 

time: 281 us -> 288 us (1.025)
  the two profiles are of different devices: /device:TPU:64 before, /device:TPU:24 now
where the time goes in v4:
time: 288 us; the launch traced here: 286 us
  waiting for transfers between devices  115 us (40%)
  blocking collectives  54.8 us (19%)
  Pallas kernels  47.1 us (16%)
  starting transfers between devices  39.7 us (14%)
  between operations  14.4 us (5%)
  local copies, waits for them, and re-layouts  11.5 us (4%)
  other arithmetic  3.94 us (1%)
    all_to_all x1, waiting for transfers between devices, local(): lax.all_to_all(done.reshape(32, 4 * CAP * 8, 128), ('z', 'y2'), split_axi...  34.2 us
    pallas_call x1, Pallas kernels, flash(): pl.pallas_call(flash_kernel, grid_spec=pltpu.PrefetchScalarGridSpec(num_s...  30.2 us
    all_to_all x1, waiting for transfers between devices, local(): lax.all_to_all(outgoing.reshape(32, 4 * CAP * 8, 128), ('z', 'y2'), split...  28.7 us
    all_to_all x1, waiting for transfers between devices, local(): lax.all_to_all(query, ('x', 'z'), split_axis=0, concat_axis=0, tiled=True)  27.2 us
    all_to_all x1, blocking collectives, local(): lax.all_to_all(key_value, ('x', 'z'), split_axis=0, concat_axis=0, tiled=...  25.5 us
    all_gather x1, waiting for transfers between devices, local(): gathered = lax.all_gather(head_weight, 'z', axis=0, tiled=True)  17.3 us
    all_to_all x1, blocking collectives, local(): lax.all_to_all(sums.reshape(4, tokens, width), 'x', split_axis=0, concat_...  17.2 us
    all_gather x1, blocking collectives, local(): lax.all_gather(listing, 'x', axis=0, tiled=True).reshape(4, tokens, 16)  12.1 us
  transfers between devices with their start and end apart: 10, of which 5 were waited for; matrix products, arithmetic and copies ran while one was open for 3% of the time, Pallas kernels for 12%

profile of v4, /device:TPU:24, one launch (start us, length us, event | category | flops | bytes accessed | tf_op | source)
XLA Modules:
  0.0 286.5 jit_solution(12722780618656031587)
XLA Ops:
  8.2 25.5 %all_to_all.35 = bf16[32,16,256]{2,1,0:T(8,128)(2,1)} all-to-all(bf16[32,16,256]{2,1,0:T(8,128)(2,1)S(1)} %bitcast.52), channel_id=1, replica_groups=mesh['z'=8,'x'=4,'y2'=4,'y1'=2,'dp'=2] {'x','z'}, dimensions={0} | all-to-all | bytes 524288 | tf_op jit(solution)/shard_map/all_to_all | solution.py:374
  35.0 4.5 %all-to-all-start.1 = ((bf16[32,64,256]{2,1,0:T(8,128)(2,1)}), bf16[32,64,256]{2,1,0:T(8,128)(2,1)S(1)}, u32[]{:S(2)}, u32[]{:S(2)}) async-start(bf16[32,64,256]{2,1,0:T(8,128)(2,1)} %bitcast.4), calls=%async_computation.1 | async-start | bytes 2097152 | tf_op jit(solution)/shard_map/all_to_all | solution.py:382
  40.3 27.2 %all-to-all-done.1 = bf16[32,64,256]{2,1,0:T(8,128)(2,1)S(1)} async-done(((bf16[32,64,256]{2,1,0:T(8,128)(2,1)}), bf16[32,64,256]{2,1,0:T(8,128)(2,1)S(1)}, u32[]{:S(2)}, u32[]{:S(2)}) %all-to-all-start.1) | async-done | bytes 1048608 | tf_op jit(solution)/shard_map/all_to_all | solution.py:382
  67.5 2.4 collective-permute-start
  70.0 3.5 %collective-permute-start.1 = (bf16[192,1024]{1,0:T(8,128)(2,1)S(1)}, bf16[192,1024]{1,0:T(8,128)(2,1)S(1)}, u32[]{:S(2)}, u32[]{:S(2)}) collective-permute-start(bf16[192,1024]{1,0:T(8,128)(2,1)S(1)} %bitcast.55), channel_id=1, source_target_pairs={{0,2},{2,0},{1,3},{3,1},{4,6},{6,4},{5,7},{7,5},{8,10},{10,8},{9,1... | collective-permute-start | bytes 1179656 | tf_op jit(solution)/shard_map/ppermute | solution.py:392
  73.5 1.6 copy-done.3
  75.1 30.2 %flash.1 = bf16[4,8,136,128]{3,2,1,0:T(8,128)(2,1)} custom-call(s32[3]{0:T(128)S(1)} %pad_add_fusion.pos_ref, bf16[4,8,64,256]{3,2,1,0:T(8,128)(2,1)S(1)} %bitcast.46, bf16[8,4,128,256]{3,2,1,0:T(8,128)(2,1)S(1)} %bitcast.47), custom_call_target="tpu_custom_call" | custom-call | flops 5368709120 | bytes 5242880 | tf_op jit(solution)/shard_map/flash/pallas_call | solution.py:139
  105.3 8.4 %all-to-all-start.2 = ((bf16[32,136,128]{2,1,0:T(8,128)(2,1)}), bf16[32,136,128]{2,1,0:T(8,128)(2,1)S(1)}, u32[]{:S(2)}, u32[]{:S(2)}) async-start(bf16[32,136,128]{2,1,0:T(8,128)(2,1)} %bitcast.11), calls=%async_computation.2 | async-start | bytes 2228224 | tf_op jit(solution)/shard_map/all_to_all | solution.py:395
  113.8 17.3 %all-gather.6.cloned.1.call-done.w_ref = bf16[1024,1024]{1,0:T(8,128)(2,1)} async-done(((bf16[128,1024]{1,0:T(8,128)(2,1)}), bf16[1024,1024]{1,0:T(8,128)(2,1)}) %all-gather.6.cloned.1.call-update) | async-done | bytes 2097168 | tf_op jit(solution)/shard_map/all_gather | solution.py:388
  131.1 1.9 collective-permute-start.2
  134.3 12.1 %all-gather = s32[4,64,16]{1,2,0:T(8,128)S(1)} all-gather(s32[1,64,16]{1,2,0:T(8,128)S(1)} %fusion.5), channel_id=1, replica_groups=mesh['z'=8,'x'=4,'y2'=4,'y1'=2,'dp'=2] {'x'}, dimensions={0}, use_global_device_ids=true | all-gather | bytes 20480 | tf_op jit(solution)/shard_map/all_gather | solution.py:401
  147.9 4.8 %merge_own.1.sum_ref = f32[64,1024]{1,0:T(8,128)} custom-call(s32[3]{0:T(128)} %copy-done.2, bf16[4,8,136,128]{3,2,1,0:T(8,128)(2,1)} %bitcast.48, bf16[1024,1024]{1,0:T(8,128)(2,1)} %all-gather.6.cloned.1.call-done.w_ref, bf16[64,1024]{1,0:T(8,128)(2,1)} %res_ref.1), custom_call_target="tpu_custom_call" | custom-call | tf_op jit(solution)/shard_map/merge_own/pallas_call | solution.py:228
  152.7 5.2 %merge_other.1 = (f32[64,1024]{1,0:T(8,128)}, bf16[4,64,1024]{2,1,0:T(8,128)(2,1)}) custom-call(s32[3]{0:T(128)} %copy-done.2, bf16[4,8,136,128]{3,2,1,0:T(8,128)(2,1)} %bitcast.49, bf16[1024,1024]{1,0:T(8,128)(2,1)} %collective-permute-done.2.w_ref, f32[64,1024]{1,0:T(8,128)} %merge_own.1.sum_ref, f32[1,1024]{1,0:T(1,128)} %bitcast.60), custom_call_target="tpu_custom_call" | custom-call | tf_op jit(solution)/shard_map/merge_other/pallas_call | solution.py:239
  157.8 3.8 %all-to-all-start.3 = ((bf16[4,64,1024]{2,1,0:T(8,128)(2,1)}), bf16[4,64,1024]{2,1,0:T(8,128)(2,1)S(1)}, u32[]{:S(2)}, u32[]{:S(2)}) async-start(bf16[4,64,1024]{2,1,0:T(8,128)(2,1)} %get-tuple-element.21), calls=%async_computation.3 | async-start | bytes 1048576 | tf_op jit(solution)/shard_map/all_to_all | solution.py:432
  162.5 7.2 %all-to-all-done.3 = bf16[4,64,1024]{2,1,0:T(8,128)(2,1)S(1)} async-done(((bf16[4,64,1024]{2,1,0:T(8,128)(2,1)}), bf16[4,64,1024]{2,1,0:T(8,128)(2,1)S(1)}, u32[]{:S(2)}, u32[]{:S(2)}) %all-to-all-start.3) | async-done | bytes 524320 | tf_op jit(solution)/shard_map/all_to_all | solution.py:432
  169.7 1.8 select.11
  171.5 7.9 %all-to-all-start.4 = ((bf16[32,160,128]{2,1,0:T(8,128)(2,1)}), bf16[32,160,128]{2,1,0:T(8,128)(2,1)S(1)}, u32[]{:S(2)}, u32[]{:S(2)}) async-start(bf16[32,160,128]{2,1,0:T(8,128)(2,1)} %bitcast.23), calls=%async_computation.4 | async-start | bytes 2621440 | tf_op jit(solution)/shard_map/all_to_all | solution.py:434
  181.4 1.5 fusion.14
  183.6 28.7 %all-to-all-done.4 = bf16[32,160,128]{2,1,0:T(8,128)(2,1)S(1)} async-done(((bf16[32,160,128]{2,1,0:T(8,128)(2,1)}), bf16[32,160,128]{2,1,0:T(8,128)(2,1)S(1)}, u32[]{:S(2)}, u32[]{:S(2)}) %all-to-all-start.4) | async-done | bytes 1310752 | tf_op jit(solution)/shard_map/all_to_all | solution.py:434
  212.3 1.1 copy-done.1
  213.4 4.4 %expert.1 = bf16[5120,128]{1,0:T(8,128)(2,1)} custom-call(bf16[5120,128]{1,0:T(8,128)(2,1)S(1)} %bitcast.43, bf16[1024,768]{1,0:T(8,128)(2,1)S(1)} %pad_maximum_fusion.win_ref, bf16[384,1024]{1,0:T(8,128)(2,1)S(1)} %copy-done.1), custom_call_target="tpu_custom_call" | custom-call | tf_op jit(solution)/shard_map/expert/pallas_call | solution.py:295
  217.8 7.3 %all-to-all-start.5 = ((bf16[32,160,128]{2,1,0:T(8,128)(2,1)}), bf16[32,160,128]{2,1,0:T(8,128)(2,1)S(1)}, u32[]{:S(2)}, u32[]{:S(2)}) async-start(bf16[32,160,128]{2,1,0:T(8,128)(2,1)} %bitcast.25), calls=%async_computation.5 | async-start | bytes 2621440 | tf_op jit(solution)/shard_map/all_to_all | solution.py:438
  226.5 34.2 %all-to-all-done.5 = bf16[32,160,128]{2,1,0:T(8,128)(2,1)S(1)} async-done(((bf16[32,160,128]{2,1,0:T(8,128)(2,1)}), bf16[32,160,128]{2,1,0:T(8,128)(2,1)S(1)}, u32[]{:S(2)}, u32[]{:S(2)}) %all-to-all-start.5) | async-done | bytes 1310752 | tf_op jit(solution)/shard_map/all_to_all | solution.py:438
  261.5 17.2 %all_to_all.36 = bf16[4,64,1024]{2,1,0:T(8,128)(2,1)S(1)} all-to-all(bf16[4,64,1024]{2,1,0:T(8,128)(2,1)S(1)} %bitcast.45), channel_id=1, replica_groups=mesh['z'=8,'x'=4,'y2'=4,'y1'=2,'dp'=2] {'x'}, dimensions={0} | all-to-all | bytes 1048576 | tf_op jit(solution)/shard_map/all_to_all | solution.py:442
  (72 shorter events, 12.4 us)
Async XLA Ops:
  6.5 33.0 %copy-start = (bf16[256,1024]{1,0:T(8,128)(2,1)S(1)}, bf16[256,1024]{1,0:T(8,128)(2,1)}, u32[]{:S(2)}) copy-start(bf16[256,1024]{1,0:T(8,128)(2,1)} %param.14) | copy-start | bytes 1572868
  6.5 27.2 %copy-start.10 = (bf16[64,2048]{1,0:T(8,128)(2,1)S(1)}, bf16[64,2048]{1,0:T(8,128)(2,1)}, u32[]{:S(2)}) copy-start(bf16[64,2048]{1,0:T(8,128)(2,1)} %param.11) | copy-start | bytes 786436
  6.5 67.0 %all-gather.4.cloned.1.call-start = ((), (), s32[]{:S(2)}) async-start(), calls=%async_computation.7 | async-start | bytes 2359296 | tf_op jit(solution)/shard_map/all_gather | solution.py:375
  34.9 32.6 %copy-start.5 = (bf16[1,1024,384]{2,1,0:T(8,128)(2,1)S(1)}, bf16[1,1024,384]{2,1,0:T(8,128)(2,1)}, u32[]{:S(2)}) copy-start(bf16[1,1024,384]{2,1,0:T(8,128)(2,1)} %param.18) | copy-start | bytes 2359300
  34.9 35.0 %copy-start.6 = (bf16[1,192,1024]{2,1,0:T(8,128)(2,1)S(1)}, bf16[1,192,1024]{2,1,0:T(8,128)(2,1)}, u32[]{:S(2)}) copy-start(bf16[1,192,1024]{2,1,0:T(8,128)(2,1)} %param.19) | copy-start | bytes 1179652
  35.0 32.5 %all-to-all-start.1 = ((bf16[32,64,256]{2,1,0:T(8,128)(2,1)}), bf16[32,64,256]{2,1,0:T(8,128)(2,1)S(1)}, u32[]{:S(2)}, u32[]{:S(2)}) async-start(bf16[32,64,256]{2,1,0:T(8,128)(2,1)} %bitcast.4), calls=%async_computation.1 | async-start | bytes 2097152 | tf_op jit(solution)/shard_map/all_to_all | solution.py:382
  39.5 91.6 %all-gather.6.cloned.1.call-start = ((), (), s32[]{:S(2)}) async-start(), calls=%async_computation.8 | async-start | bytes 2359296 | tf_op jit(solution)/shard_map/all_gather | solution.py:388
  67.5 46.2 %collective-permute-start = (bf16[1024,384]{1,0:T(8,128)(2,1)S(1)}, bf16[1024,384]{1,0:T(8,128)(2,1)}, u32[]{:S(2)}, u32[]{:S(2)}) collective-permute-start(bf16[1024,384]{1,0:T(8,128)(2,1)S(1)} %bitcast.50), channel_id=1, source_target_pairs={{0,2},{2,0},{1,3},{3,1},{4,6},{6,4},{5,7},{7,5},{8,10},{10,8},{9,1... | collective-permute-start | bytes 2359304 | tf_op jit(solution)/shard_map/ppermute | solution.py:391
  70.0 35.3 %copy-start.2 = (s32[3]{0:T(128)}, s32[3]{0:T(128)S(1)}, u32[]{:S(2)}) copy-start(s32[3]{0:T(128)S(1)} %pad_add_fusion.pos_ref) | copy-start | bytes 40
  70.0 43.8 %collective-permute-start.1 = (bf16[192,1024]{1,0:T(8,128)(2,1)S(1)}, bf16[192,1024]{1,0:T(8,128)(2,1)S(1)}, u32[]{:S(2)}, u32[]{:S(2)}) collective-permute-start(bf16[192,1024]{1,0:T(8,128)(2,1)S(1)} %bitcast.55), channel_id=1, source_target_pairs={{0,2},{2,0},{1,3},{3,1},{4,6},{6,4},{5,7},{7,5},{8,10},{10,8},{9,1... | collective-permute-start | bytes 1179656 | tf_op jit(solution)/shard_map/ppermute | solution.py:392
  73.5 1.6 copy-start.3
  105.3 29.0 %copy-start.11 = (s32[64,8]{0,1:T(8,128)S(1)}, s32[64,8]{0,1:T(8,128)}, u32[]{:S(2)}) copy-start(s32[64,8]{0,1:T(8,128)} %param.17) | copy-start | bytes 6148
  105.3 29.0 %copy-start.12 = (s32[64,8]{0,1:T(8,128)S(1)}, s32[64,8]{0,1:T(8,128)}, u32[]{:S(2)}) copy-start(s32[64,8]{0,1:T(8,128)} %param.16) | copy-start | bytes 6148
  105.3 41.5 %all-to-all-start.2 = ((bf16[32,136,128]{2,1,0:T(8,128)(2,1)}), bf16[32,136,128]{2,1,0:T(8,128)(2,1)S(1)}, u32[]{:S(2)}, u32[]{:S(2)}) async-start(bf16[32,136,128]{2,1,0:T(8,128)(2,1)} %bitcast.11), calls=%async_computation.2 | async-start | bytes 2228224 | tf_op jit(solution)/shard_map/all_to_all | solution.py:395
  113.8 38.9 %copy-start.7 = (bf16[192,1024]{1,0:T(8,128)(2,1)}, bf16[192,1024]{1,0:T(8,128)(2,1)S(1)}, u32[]{:S(2)}) copy-start(bf16[192,1024]{1,0:T(8,128)(2,1)S(1)} %collective-permute-done.1) | copy-start | bytes 1179652
  131.1 21.6 %collective-permute-start.2 = (bf16[1024,1024]{1,0:T(8,128)(2,1)}, bf16[1024,1024]{1,0:T(8,128)(2,1)}, u32[]{:S(2)}, u32[]{:S(2)}) collective-permute-start(bf16[1024,1024]{1,0:T(8,128)(2,1)} %all-gather.6.cloned.1.call-done.w_ref), channel_id=1, source_target_pairs={{0,1},{1,0},{2,3},{3,2},{4,5},{5,4},{6,7},{7,6},{8,9},{9,8},{10,11... | collective-permute-start | bytes 6291464 | tf_op jit(solution)/shard_map/ppermute | solution.py:399
  146.8 1.1 copy-start.4
  157.8 11.9 %all-to-all-start.3 = ((bf16[4,64,1024]{2,1,0:T(8,128)(2,1)}), bf16[4,64,1024]{2,1,0:T(8,128)(2,1)S(1)}, u32[]{:S(2)}, u32[]{:S(2)}) async-start(bf16[4,64,1024]{2,1,0:T(8,128)(2,1)} %get-tuple-element.21), calls=%async_computation.3 | async-start | bytes 1048576 | tf_op jit(solution)/shard_map/all_to_all | solution.py:432
  171.5 40.8 %all-to-all-start.4 = ((bf16[32,160,128]{2,1,0:T(8,128)(2,1)}), bf16[32,160,128]{2,1,0:T(8,128)(2,1)S(1)}, u32[]{:S(2)}, u32[]{:S(2)}) async-start(bf16[32,160,128]{2,1,0:T(8,128)(2,1)} %bitcast.23), calls=%async_computation.4 | async-start | bytes 2621440 | tf_op jit(solution)/shard_map/all_to_all | solution.py:434
  179.4 1.0 copy-start.8
  212.3 1.1 copy-start.1
  217.8 42.9 %all-to-all-start.5 = ((bf16[32,160,128]{2,1,0:T(8,128)(2,1)}), bf16[32,160,128]{2,1,0:T(8,128)(2,1)S(1)}, u32[]{:S(2)}, u32[]{:S(2)}) async-start(bf16[32,160,128]{2,1,0:T(8,128)(2,1)} %bitcast.25), calls=%async_computation.5 | async-start | bytes 2621440 | tf_op jit(solution)/shard_map/all_to_all | solution.py:438
  260.7 18.1 %copy-start.9 = (f32[64,1024]{1,0:T(8,128)S(1)}, f32[64,1024]{1,0:T(8,128)}, u32[]{:S(2)}) copy-start(f32[64,1024]{1,0:T(8,128)} %get-tuple-element.19) | copy-start | bytes 786436
Sparse Core Ops, SparseCore 0:
  33.8 38.6 all-gather.3
  74.6 56.4 all-gather.5

commit v5 on v4

--- a/solution.py
+++ b/solution.py
@@ -19,7 +19,9 @@
 SWAP = [(0, 1), (1, 0)]
 
 
-def flash_kernel(pos_ref, q_ref, kv_ref, o_ref, vt_ref, bias_ref, acc_ref, m_ref, top_ref):
+def flash_kernel(
+    pos_ref, q_ref, b0, b1, b2, b3, b4, b5, b6, b7, b8, o_ref, kv_ref, vt_ref, bias_ref, acc_ref, m_ref, top_ref
+):
     block = pl.program_id(0)
     own_x = pos_ref[0]
     own_y = pos_ref[1]
@@ -35,6 +37,10 @@
             lax.broadcasted_iota(jnp.int32, (HD, HD), 0)
             == lax.broadcasted_iota(jnp.int32, (HD, HD), 1)
         ).astype(BF)
+        for far, ref in ((0, b0), (7, b1), (6, b2), (5, b3), (1, b4), (2, b5), (3, b6)):
+            kv_ref[(own_y + far) % 8] = ref[...]
+        kv_ref[(own_y + 4) % 8, 0:2] = b7[...]
+        kv_ref[(own_y + 4) % 8, 2:4] = b8[...]
         for c in range(8):
             v = kv_ref[4 * (c % 2) : 4 * (c % 2) + 4, c // 2, :, HD : 2 * HD].reshape(512, HD)
             turned = lax.dot_general(eye, v, (((1,), (1,)), ((), ())), preferred_element_type=F32)
@@ -143,10 +149,11 @@
             grid=(4,),
             in_specs=[
                 pl.BlockSpec((1, 8, 64, 256), lambda i, s: (i, 0, 0, 0)),
-                pl.BlockSpec((8, 4, 128, 256), lambda i, s: (0, 0, 0, 0)),
-            ],
+            ]
+            + [pl.BlockSpec(block.shape, lambda i, s: (0, 0, 0)) for block in key_values],
             out_specs=pl.BlockSpec((1, 8, HD + STAT, 128), lambda i, s: (i, 0, 0, 0)),
             scratch_shapes=[
+                pltpu.VMEM((8, 4, 128, 2 * HD), BF),
                 pltpu.VMEM((8, HD + 16, 512), BF),
                 pltpu.VMEM((512, 1024), F32),
                 pltpu.VMEM((HD + 16, 1024), F32),
@@ -160,7 +167,7 @@
             flops=4 * 4096 * 2560 * HD, bytes_accessed=5 << 20, transcendentals=4096 * 2560
         ),
         name="flash",
-    )(position, queries, key_values)
+    )(position, queries, *key_values)
 
 
 def merged_heads(pos_ref, parts_ref, second):
@@ -372,9 +379,15 @@
         32, 16, 2 * HD
     )
     key_value = lax.all_to_all(key_value, ("x", "z"), split_axis=0, concat_axis=0, tiled=True)
-    key_values = lax.all_gather(
-        key_value.reshape(512, 2 * HD), ("y2", "y1"), axis=0, tiled=True
-    ).reshape(8, 4, 128, 2 * HD)
+    up = [(i, (i + 1) % 8) for i in range(8)]
+    down = [(i, (i - 1) % 8) for i in range(8)]
+    ups, downs = [key_value.reshape(4, 128, 2 * HD)], [key_value.reshape(4, 128, 2 * HD)]
+    for _ in range(3):
+        ups.append(lax.ppermute(ups[-1], ("y2", "y1"), up))
+        downs.append(lax.ppermute(downs[-1], ("y2", "y1"), down))
+    key_values = ups + downs[1:]
+    key_values.append(lax.ppermute(ups[3][0:2], ("y2", "y1"), up))
+    key_values.append(lax.ppermute(downs[3][2:4], ("y2", "y1"), down))
 
     query = queries.reshape(tokens, 8, 2 * HD).transpose(1, 0, 2)
     query = jnp.broadcast_to(query[None], (4, 8, tokens, 2 * HD)).reshape(32, tokens, 2 * HD)
@@ -384,20 +397,17 @@
     )
 
     head_weight = lax.dynamic_slice_in_dim(output_weight, own_core * HD, HD, 0)
-    head_weight, _ = lax.optimization_barrier((head_weight, query))
     gathered = lax.all_gather(head_weight, "z", axis=0, tiled=True)
-
-    own_in, own_out, _ = lax.optimization_barrier((expert_in[0], expert_out[0], query))
-    other_in = lax.ppermute(own_in, "y1", SWAP)
-    other_out = lax.ppermute(own_out, "y1", SWAP)
 
     shards = flash(position, query, key_values)
     parts = lax.all_to_all(
         shards.reshape(32, HD + STAT, 128), ("x", "z"), split_axis=0, concat_axis=0, tiled=True
     ).reshape(4, 8, HD + STAT, 128)
-    gathered, other_in, other_out = lax.optimization_barrier((gathered, other_in, other_out))
+    gathered, own_in, own_out = lax.optimization_barrier((gathered, expert_in[0], expert_out[0]))
     gathered_other = lax.ppermute(gathered, "dp", SWAP)
-    listing = after(jnp.concatenate([routes, gate_levels], axis=1), other_out)
+    other_in = lax.ppermute(own_in, "y1", SWAP)
+    other_out = lax.ppermute(own_out, "y1", SWAP)
+    listing = after(jnp.concatenate([routes, gate_levels], axis=1), gathered)
     listing = lax.all_gather(listing, "x", axis=0, tiled=True).reshape(4, tokens, 16)
     named, levels = listing[:, :, 0:8], listing[:, :, 8:16]
     local_expert = jnp.arange(32, dtype=jnp.int32)
@@ -420,15 +430,16 @@
     shares = jnp.where(back, gates[:, :, :, None, None], 0.0).astype(BF)
     shares = shares.reshape(4 * tokens, 32 * 4 * CAP)
 
+    hidden, spread = merge(
+        position, parts, gathered, gathered_other, residual, norm_gain.reshape(1, width)
+    )
+
+    spread, other_in, other_out = lax.optimization_barrier((spread, other_in, other_out))
     half = own_in.shape[1] // 2
     weight_in = jnp.concatenate(
         [own_in[:, :half], other_in[:, :half], own_in[:, half:], other_in[:, half:]], axis=1
     )
     weight_out = jnp.concatenate([own_out, other_out], axis=0)
-    hidden, spread = merge(
-        position, parts, gathered, gathered_other, residual, norm_gain.reshape(1, width)
-    )
-
     spread = lax.all_to_all(spread, "x", split_axis=0, concat_axis=0, tiled=True)
     outgoing = select(chosen, spread.reshape(4 * tokens, width))
     arrived = lax.all_to_all(

time: 288 us -> 307 us (1.066)
  the two profiles are of different devices: /device:TPU:24 before, /device:TPU:2 now
where the time goes in v5:
time: 307 us; the launch traced here: 306 us
  starting transfers between devices  95.9 us (31%)
  waiting for transfers between devices  95 us (31%)
  Pallas kernels  47.2 us (15%)
  blocking collectives  35.3 us (11%)
  between operations  14.5 us (5%)
  local copies, waits for them, and re-layouts  13.5 us (4%)
  other arithmetic  3.94 us (1%)
    all_to_all x1, waiting for transfers between devices, local(): lax.all_to_all(done.reshape(32, 4 * CAP * 8, 128), ('z', 'y2'), split_axi...  37.6 us
    pallas_call x1, Pallas kernels, flash(): pl.pallas_call(flash_kernel, grid_spec=pltpu.PrefetchScalarGridSpec(num_s...  30.3 us
    all_to_all x1, waiting for transfers between devices, local(): lax.all_to_all(outgoing.reshape(32, 4 * CAP * 8, 128), ('z', 'y2'), split...  29.2 us
    all_to_all x1, blocking collectives, local(): lax.all_to_all(sums.reshape(4, tokens, width), 'x', split_axis=0, concat_...  22.7 us
    all_to_all x1, starting transfers between devices, local(): lax.all_to_all(outgoing.reshape(32, 4 * CAP * 8, 128), ('z', 'y2'), split...  19.3 us
    ppermute x3, starting transfers between devices, local(): downs.append(lax.ppermute(downs[-1], ('y2', 'y1'), down))  14.6 us
    all_to_all x1, starting transfers between devices, local(): lax.all_to_all(key_value, ('x', 'z'), split_axis=0, concat_axis=0, tiled=...  13.5 us
    all_gather x1, blocking collectives, local(): lax.all_gather(listing, 'x', axis=0, tiled=True).reshape(4, tokens, 16)  12.6 us
  transfers between devices with their start and end apart: 18, of which 9 were waited for; matrix products, arithmetic and copies ran while one was open for 4% of the time, Pallas kernels for 13%

profile of v5, /device:TPU:2, one launch (start us, length us, event | category | flops | bytes accessed | tf_op | source)
XLA Modules:
  0.0 305.5 jit_solution(17524619713402789487)
XLA Ops:
  10.6 13.5 %all-to-all-start = ((bf16[32,16,256]{2,1,0:T(8,128)(2,1)}), bf16[32,16,256]{2,1,0:T(8,128)(2,1)S(1)}, u32[]{:S(2)}, u32[]{:S(2)}) async-start(bf16[32,16,256]{2,1,0:T(8,128)(2,1)} %bitcast.7), calls=%async_computation | async-start | bytes 524288 | tf_op jit(solution)/shard_map/all_to_all | solution.py:381
  24.2 11.2 %all-to-all-done = bf16[32,16,256]{2,1,0:T(8,128)(2,1)S(1)} async-done(((bf16[32,16,256]{2,1,0:T(8,128)(2,1)}), bf16[32,16,256]{2,1,0:T(8,128)(2,1)S(1)}, u32[]{:S(2)}, u32[]{:S(2)}) %all-to-all-start) | async-done | bytes 262176 | tf_op jit(solution)/shard_map/all_to_all | solution.py:381
  36.4 6.2 %all-to-all-start.1 = ((bf16[32,64,256]{2,1,0:T(8,128)(2,1)}), bf16[32,64,256]{2,1,0:T(8,128)(2,1)S(1)}, u32[]{:S(2)}, u32[]{:S(2)}) async-start(bf16[32,64,256]{2,1,0:T(8,128)(2,1)} %bitcast.4), calls=%async_computation.1 | async-start | bytes 2097152 | tf_op jit(solution)/shard_map/all_to_all | solution.py:395
  42.6 3.5 %collective-permute-start = (bf16[4,128,256]{2,1,0:T(8,128)(2,1)S(1)}, bf16[4,128,256]{2,1,0:T(8,128)(2,1)S(1)}, u32[]{:S(2)}, u32[]{:S(2)}) collective-permute-start(bf16[4,128,256]{2,1,0:T(8,128)(2,1)S(1)} %bitcast.46), channel_id=1, source_target_pairs={{0,2},{2,4},{4,6},{6,8},{8,10},{10,12},{12,14},{14,0},{1,3},{3,5},... | collective-permute-start | bytes 786440 | tf_op jit(solution)/shard_map/ppermute | solution.py:386
  46.2 4.3 %collective-permute-start.3 = (bf16[4,128,256]{2,1,0:T(8,128)(2,1)S(1)}, bf16[4,128,256]{2,1,0:T(8,128)(2,1)S(1)}, u32[]{:S(2)}, u32[]{:S(2)}) collective-permute-start(bf16[4,128,256]{2,1,0:T(8,128)(2,1)S(1)} %bitcast.47), channel_id=1, source_target_pairs={{0,14},{2,0},{4,2},{6,4},{8,6},{10,8},{12,10},{14,12},{1,15},{3,1}... | collective-permute-start | bytes 786440 | tf_op jit(solution)/shard_map/ppermute | solution.py:387
  50.5 2.4 collective-permute-done.b1
  54.8 5.1 %collective-permute-start.4 = (bf16[4,128,256]{2,1,0:T(8,128)(2,1)S(1)}, bf16[4,128,256]{2,1,0:T(8,128)(2,1)S(1)}, u32[]{:S(2)}, u32[]{:S(2)}) collective-permute-start(bf16[4,128,256]{2,1,0:T(8,128)(2,1)S(1)} %collective-permute-done.3.b4), channel_id=1, source_target_pairs={{0,14},{2,0},{4,2},{6,4},{8,6},{10,8},{12,10},{14,12},{1,15},{3,1}... | collective-permute-start | bytes 786440 | tf_op jit(solution)/shard_map/ppermute | solution.py:387
  64.3 5.1 %collective-permute-start.5 = (bf16[4,128,256]{2,1,0:T(8,128)(2,1)S(1)}, bf16[4,128,256]{2,1,0:T(8,128)(2,1)S(1)}, u32[]{:S(2)}, u32[]{:S(2)}) collective-permute-start(bf16[4,128,256]{2,1,0:T(8,128)(2,1)S(1)} %collective-permute-done.4.b5), channel_id=1, source_target_pairs={{0,14},{2,0},{4,2},{6,4},{8,6},{10,8},{12,10},{14,12},{1,15},{3,1}... | collective-permute-start | bytes 786440 | tf_op jit(solution)/shard_map/ppermute | solution.py:387
  75.1 5.1 %collective-permute-start.7 = (bf16[2,128,256]{2,1,0:T(8,128)(2,1)}, bf16[2,128,256]{2,1,0:T(8,128)(2,1)}, u32[]{:S(2)}, u32[]{:S(2)}) collective-permute-start(bf16[2,128,256]{2,1,0:T(8,128)(2,1)} %slice.53), channel_id=1, source_target_pairs={{0,14},{2,0},{4,2},{6,4},{8,6},{10,8},{12,10},{14,12},{1,15},{3,1}... | collective-permute-start | bytes 393224 | tf_op jit(solution)/shard_map/ppermute | solution.py:390
  83.0 30.3 %flash.1 = bf16[4,8,136,128]{3,2,1,0:T(8,128)(2,1)} custom-call(s32[3]{0:T(128)S(1)} %pad_add_fusion.pos_ref, bf16[4,8,64,256]{3,2,1,0:T(8,128)(2,1)S(1)} %bitcast.45, bf16[4,128,256]{2,1,0:T(8,128)(2,1)S(1)} %bitcast.48, bf16[4,128,256]{2,1,0:T(8,128)(2,1)S(1)} %collective-permute-done.b1, bf16[4,128,256]{2,1,0:T(8,128)(2,1)S(1)} %collective-permute-done.1.b2, ...), custom_call_target="tpu_custom_call" | custom-call | flops 5368709120 | bytes 5242880 | tf_op jit(solution)/shard_map/flash/pallas_call | solution.py:145
  113.4 8.4 %all-to-all-start.2 = ((bf16[32,136,128]{2,1,0:T(8,128)(2,1)}), bf16[32,136,128]{2,1,0:T(8,128)(2,1)S(1)}, u32[]{:S(2)}, u32[]{:S(2)}) async-start(bf16[32,136,128]{2,1,0:T(8,128)(2,1)} %bitcast.10), calls=%async_computation.2 | async-start | bytes 2228224 | tf_op jit(solution)/shard_map/all_to_all | solution.py:403
  125.1 3.3 %collective-permute-start.9 = (bf16[1024,384]{1,0:T(8,128)(2,1)S(1)}, bf16[1024,384]{1,0:T(8,128)(2,1)}, u32[]{:S(2)}, u32[]{:S(2)}) collective-permute-start(bf16[1024,384]{1,0:T(8,128)(2,1)S(1)} %bitcast.51), channel_id=1, source_target_pairs={{0,2},{2,0},{1,3},{3,1},{4,6},{6,4},{5,7},{7,5},{8,10},{10,8},{9,1... | collective-permute-start | bytes 2359304 | tf_op jit(solution)/shard_map/ppermute | solution.py:408
  128.4 2.5 collective-permute-start.10
  131.6 12.6 %all-gather = s32[4,64,16]{1,2,0:T(8,128)S(1)} all-gather(s32[1,64,16]{1,2,0:T(8,128)S(1)} %fusion.5), channel_id=1, replica_groups=mesh['z'=8,'x'=4,'y2'=4,'y1'=2,'dp'=2] {'x'}, dimensions={0}, use_global_device_ids=true | all-gather | bytes 20480 | tf_op jit(solution)/shard_map/all_gather | solution.py:411
  145.7 4.8 %merge_own.1.sum_ref = f32[64,1024]{1,0:T(8,128)} custom-call(s32[3]{0:T(128)} %copy-done.2, bf16[4,8,136,128]{3,2,1,0:T(8,128)(2,1)} %bitcast.49, bf16[1024,1024]{1,0:T(8,128)(2,1)} %all-gather.3.cloned.1.call-done.w_ref, bf16[64,1024]{1,0:T(8,128)(2,1)} %res_ref.1), custom_call_target="tpu_custom_call" | custom-call | tf_op jit(solution)/shard_map/merge_own/pallas_call | solution.py:235
  150.4 5.1 %merge_other.1 = (f32[64,1024]{1,0:T(8,128)}, bf16[4,64,1024]{2,1,0:T(8,128)(2,1)}) custom-call(s32[3]{0:T(128)} %copy-done.2, bf16[4,8,136,128]{3,2,1,0:T(8,128)(2,1)} %bitcast.50, bf16[1024,1024]{1,0:T(8,128)(2,1)} %collective-permute-done.8.w_ref, f32[64,1024]{1,0:T(8,128)} %merge_own.1.sum_ref, f32[1,1024]{1,0:T(1,128)} %bitcast.59), custom_call_target="tpu_custom_call" | custom-call | tf_op jit(solution)/shard_map/merge_other/pallas_call | solution.py:246
  155.6 4.5 %all-to-all-start.3 = ((bf16[4,64,1024]{2,1,0:T(8,128)(2,1)}), bf16[4,64,1024]{2,1,0:T(8,128)(2,1)S(1)}, u32[]{:S(2)}, u32[]{:S(2)}) async-start(bf16[4,64,1024]{2,1,0:T(8,128)(2,1)} %get-tuple-element.20), calls=%async_computation.3 | async-start | bytes 1048576 | tf_op jit(solution)/shard_map/all_to_all | solution.py:443
  161.0 7.0 %all-to-all-done.3 = bf16[4,64,1024]{2,1,0:T(8,128)(2,1)S(1)} async-done(((bf16[4,64,1024]{2,1,0:T(8,128)(2,1)}), bf16[4,64,1024]{2,1,0:T(8,128)(2,1)S(1)}, u32[]{:S(2)}, u32[]{:S(2)}) %all-to-all-start.3) | async-done | bytes 524320 | tf_op jit(solution)/shard_map/all_to_all | solution.py:443
  169.8 19.3 %all-to-all-start.4 = ((bf16[32,160,128]{2,1,0:T(8,128)(2,1)}), bf16[32,160,128]{2,1,0:T(8,128)(2,1)S(1)}, u32[]{:S(2)}, u32[]{:S(2)}) async-start(bf16[32,160,128]{2,1,0:T(8,128)(2,1)} %bitcast.22), calls=%async_computation.4 | async-start | bytes 2621440 | tf_op jit(solution)/shard_map/all_to_all | solution.py:445
  193.4 29.2 %all-to-all-done.4 = bf16[32,160,128]{2,1,0:T(8,128)(2,1)S(1)} async-done(((bf16[32,160,128]{2,1,0:T(8,128)(2,1)}), bf16[32,160,128]{2,1,0:T(8,128)(2,1)S(1)}, u32[]{:S(2)}, u32[]{:S(2)}) %all-to-all-start.4) | async-done | bytes 1310752 | tf_op jit(solution)/shard_map/all_to_all | solution.py:445
  223.6 4.4 %expert.1 = bf16[5120,128]{1,0:T(8,128)(2,1)} custom-call(bf16[5120,128]{1,0:T(8,128)(2,1)S(1)} %bitcast.42, bf16[1024,768]{1,0:T(8,128)(2,1)S(1)} %pad_maximum_fusion.win_ref, bf16[384,1024]{1,0:T(8,128)(2,1)S(1)} %copy-done.1), custom_call_target="tpu_custom_call" | custom-call | tf_op jit(solution)/shard_map/expert/pallas_call | solution.py:302
  228.0 7.3 %all-to-all-start.5 = ((bf16[32,160,128]{2,1,0:T(8,128)(2,1)}), bf16[32,160,128]{2,1,0:T(8,128)(2,1)S(1)}, u32[]{:S(2)}, u32[]{:S(2)}) async-start(bf16[32,160,128]{2,1,0:T(8,128)(2,1)} %bitcast.24), calls=%async_computation.5 | async-start | bytes 2621440 | tf_op jit(solution)/shard_map/all_to_all | solution.py:449
  236.7 37.6 %all-to-all-done.5 = bf16[32,160,128]{2,1,0:T(8,128)(2,1)S(1)} async-done(((bf16[32,160,128]{2,1,0:T(8,128)(2,1)}), bf16[32,160,128]{2,1,0:T(8,128)(2,1)S(1)}, u32[]{:S(2)}, u32[]{:S(2)}) %all-to-all-start.5) | async-done | bytes 1310752 | tf_op jit(solution)/shard_map/all_to_all | solution.py:449
  275.1 22.7 %all_to_all.35 = bf16[4,64,1024]{2,1,0:T(8,128)(2,1)S(1)} all-to-all(bf16[4,64,1024]{2,1,0:T(8,128)(2,1)S(1)} %bitcast.44), channel_id=1, replica_groups=mesh['z'=8,'x'=4,'y2'=4,'y1'=2,'dp'=2] {'x'}, dimensions={0} | all-to-all | bytes 1048576 | tf_op jit(solution)/shard_map/all_to_all | solution.py:453
  (86 shorter events, 35.5 us)
Async XLA Ops:
  6.5 17.5 %copy-start.9 = (bf16[64,2048]{1,0:T(8,128)(2,1)S(1)}, bf16[64,2048]{1,0:T(8,128)(2,1)}, u32[]{:S(2)}) copy-start(bf16[64,2048]{1,0:T(8,128)(2,1)} %param.11) | copy-start | bytes 786436
  6.5 115.3 %all-gather.3.cloned.1.call-start = ((), (), s32[]{:S(2)}) async-start(), calls=%async_computation.7 | async-start | bytes 2359296 | tf_op jit(solution)/shard_map/all_gather | solution.py:400
  10.6 24.8 %all-to-all-start = ((bf16[32,16,256]{2,1,0:T(8,128)(2,1)}), bf16[32,16,256]{2,1,0:T(8,128)(2,1)S(1)}, u32[]{:S(2)}, u32[]{:S(2)}) async-start(bf16[32,16,256]{2,1,0:T(8,128)(2,1)} %bitcast.7), calls=%async_computation | async-start | bytes 524288 | tf_op jit(solution)/shard_map/all_to_all | solution.py:381
  36.4 46.6 %all-to-all-start.1 = ((bf16[32,64,256]{2,1,0:T(8,128)(2,1)}), bf16[32,64,256]{2,1,0:T(8,128)(2,1)S(1)}, u32[]{:S(2)}, u32[]{:S(2)}) async-start(bf16[32,64,256]{2,1,0:T(8,128)(2,1)} %bitcast.4), calls=%async_computation.1 | async-start | bytes 2097152 | tf_op jit(solution)/shard_map/all_to_all | solution.py:395
  42.6 10.3 %collective-permute-start = (bf16[4,128,256]{2,1,0:T(8,128)(2,1)S(1)}, bf16[4,128,256]{2,1,0:T(8,128)(2,1)S(1)}, u32[]{:S(2)}, u32[]{:S(2)}) collective-permute-start(bf16[4,128,256]{2,1,0:T(8,128)(2,1)S(1)} %bitcast.46), channel_id=1, source_target_pairs={{0,2},{2,4},{4,6},{6,8},{8,10},{10,12},{12,14},{14,0},{1,3},{3,5},... | collective-permute-start | bytes 786440 | tf_op jit(solution)/shard_map/ppermute | solution.py:386
  46.2 8.6 %collective-permute-start.3 = (bf16[4,128,256]{2,1,0:T(8,128)(2,1)S(1)}, bf16[4,128,256]{2,1,0:T(8,128)(2,1)S(1)}, u32[]{:S(2)}, u32[]{:S(2)}) collective-permute-start(bf16[4,128,256]{2,1,0:T(8,128)(2,1)S(1)} %bitcast.47), channel_id=1, source_target_pairs={{0,14},{2,0},{4,2},{6,4},{8,6},{10,8},{12,10},{14,12},{1,15},{3,1}... | collective-permute-start | bytes 786440 | tf_op jit(solution)/shard_map/ppermute | solution.py:387
  52.9 9.5 %collective-permute-start.1 = (bf16[4,128,256]{2,1,0:T(8,128)(2,1)S(1)}, bf16[4,128,256]{2,1,0:T(8,128)(2,1)S(1)}, u32[]{:S(2)}, u32[]{:S(2)}) collective-permute-start(bf16[4,128,256]{2,1,0:T(8,128)(2,1)S(1)} %collective-permute-done.b1), channel_id=1, source_target_pairs={{0,2},{2,4},{4,6},{6,8},{8,10},{10,12},{12,14},{14,0},{1,3},{3,5},... | collective-permute-start | bytes 786440 | tf_op jit(solution)/shard_map/ppermute | solution.py:386
  54.8 9.5 %collective-permute-start.4 = (bf16[4,128,256]{2,1,0:T(8,128)(2,1)S(1)}, bf16[4,128,256]{2,1,0:T(8,128)(2,1)S(1)}, u32[]{:S(2)}, u32[]{:S(2)}) collective-permute-start(bf16[4,128,256]{2,1,0:T(8,128)(2,1)S(1)} %collective-permute-done.3.b4), channel_id=1, source_target_pairs={{0,14},{2,0},{4,2},{6,4},{8,6},{10,8},{12,10},{14,12},{1,15},{3,1}... | collective-permute-start | bytes 786440 | tf_op jit(solution)/shard_map/ppermute | solution.py:387
  62.4 9.5 %collective-permute-start.2 = (bf16[4,128,256]{2,1,0:T(8,128)(2,1)S(1)}, bf16[4,128,256]{2,1,0:T(8,128)(2,1)S(1)}, u32[]{:S(2)}, u32[]{:S(2)}) collective-permute-start(bf16[4,128,256]{2,1,0:T(8,128)(2,1)S(1)} %collective-permute-done.1.b2), channel_id=1, source_target_pairs={{0,2},{2,4},{4,6},{6,8},{8,10},{10,12},{12,14},{14,0},{1,3},{3,5},... | collective-permute-start | bytes 786440 | tf_op jit(solution)/shard_map/ppermute | solution.py:386
  64.3 10.1 %collective-permute-start.5 = (bf16[4,128,256]{2,1,0:T(8,128)(2,1)S(1)}, bf16[4,128,256]{2,1,0:T(8,128)(2,1)S(1)}, u32[]{:S(2)}, u32[]{:S(2)}) collective-permute-start(bf16[4,128,256]{2,1,0:T(8,128)(2,1)S(1)} %collective-permute-done.4.b5), channel_id=1, source_target_pairs={{0,14},{2,0},{4,2},{6,4},{8,6},{10,8},{12,10},{14,12},{1,15},{3,1}... | collective-permute-start | bytes 786440 | tf_op jit(solution)/shard_map/ppermute | solution.py:387
  72.5 8.3 %collective-permute-start.6 = (bf16[2,128,256]{2,1,0:T(8,128)(2,1)}, bf16[2,128,256]{2,1,0:T(8,128)(2,1)S(1)}, u32[]{:S(2)}, u32[]{:S(2)}) collective-permute-start(bf16[2,128,256]{2,1,0:T(8,128)(2,1)} %slice.52), channel_id=1, source_target_pairs={{0,2},{2,4},{4,6},{6,8},{8,10},{10,12},{12,14},{14,0},{1,3},{3,5},... | collective-permute-start | bytes 393224 | tf_op jit(solution)/shard_map/ppermute | solution.py:389
  75.1 7.9 %collective-permute-start.7 = (bf16[2,128,256]{2,1,0:T(8,128)(2,1)}, bf16[2,128,256]{2,1,0:T(8,128)(2,1)}, u32[]{:S(2)}, u32[]{:S(2)}) collective-permute-start(bf16[2,128,256]{2,1,0:T(8,128)(2,1)} %slice.53), channel_id=1, source_target_pairs={{0,14},{2,0},{4,2},{6,4},{8,6},{10,8},{12,10},{14,12},{1,15},{3,1}... | collective-permute-start | bytes 393224 | tf_op jit(solution)/shard_map/ppermute | solution.py:390
  80.3 33.0 %copy-start.2 = (s32[3]{0:T(128)}, s32[3]{0:T(128)S(1)}, u32[]{:S(2)}) copy-start(s32[3]{0:T(128)S(1)} %pad_add_fusion.pos_ref) | copy-start | bytes 40
  113.4 15.0 %copy-start.5 = (bf16[1,192,1024]{2,1,0:T(8,128)(2,1)S(1)}, bf16[1,192,1024]{2,1,0:T(8,128)(2,1)}, u32[]{:S(2)}) copy-start(bf16[1,192,1024]{2,1,0:T(8,128)(2,1)} %param.19) | copy-start | bytes 1179652
  113.4 18.2 %copy-start.10 = (s32[64,8]{0,1:T(8,128)S(1)}, s32[64,8]{0,1:T(8,128)}, u32[]{:S(2)}) copy-start(s32[64,8]{0,1:T(8,128)} %param.17) | copy-start | bytes 6148
  113.4 18.2 %copy-start.11 = (s32[64,8]{0,1:T(8,128)S(1)}, s32[64,8]{0,1:T(8,128)}, u32[]{:S(2)}) copy-start(s32[64,8]{0,1:T(8,128)} %param.16) | copy-start | bytes 6148
  113.4 31.3 %all-to-all-start.2 = ((bf16[32,136,128]{2,1,0:T(8,128)(2,1)}), bf16[32,136,128]{2,1,0:T(8,128)(2,1)S(1)}, u32[]{:S(2)}, u32[]{:S(2)}) async-start(bf16[32,136,128]{2,1,0:T(8,128)(2,1)} %bitcast.10), calls=%async_computation.2 | async-start | bytes 2228224 | tf_op jit(solution)/shard_map/all_to_all | solution.py:403
  121.8 28.6 %collective-permute-start.8 = (bf16[1024,1024]{1,0:T(8,128)(2,1)}, bf16[1024,1024]{1,0:T(8,128)(2,1)}, u32[]{:S(2)}, u32[]{:S(2)}) collective-permute-start(bf16[1024,1024]{1,0:T(8,128)(2,1)} %all-gather.3.cloned.1.call-done.w_ref), channel_id=1, source_target_pairs={{0,1},{1,0},{2,3},{3,2},{4,5},{5,4},{6,7},{7,6},{8,9},{9,8},{10,11... | collective-permute-start | bytes 6291464 | tf_op jit(solution)/shard_map/ppermute | solution.py:407
  125.1 30.5 %collective-permute-start.9 = (bf16[1024,384]{1,0:T(8,128)(2,1)S(1)}, bf16[1024,384]{1,0:T(8,128)(2,1)}, u32[]{:S(2)}, u32[]{:S(2)}) collective-permute-start(bf16[1024,384]{1,0:T(8,128)(2,1)S(1)} %bitcast.51), channel_id=1, source_target_pairs={{0,2},{2,0},{1,3},{3,1},{4,6},{6,4},{5,7},{7,5},{8,10},{10,8},{9,1... | collective-permute-start | bytes 2359304 | tf_op jit(solution)/shard_map/ppermute | solution.py:408
  128.4 27.2 %collective-permute-start.10 = (bf16[192,1024]{1,0:T(8,128)(2,1)S(1)}, bf16[192,1024]{1,0:T(8,128)(2,1)S(1)}, u32[]{:S(2)}, u32[]{:S(2)}) collective-permute-start(bf16[192,1024]{1,0:T(8,128)(2,1)S(1)} %bitcast.54), channel_id=1, source_target_pairs={{0,2},{2,0},{1,3},{3,1},{4,6},{6,4},{5,7},{7,5},{8,10},{10,8},{9,1... | collective-permute-start | bytes 1179656 | tf_op jit(solution)/shard_map/ppermute | solution.py:409
  155.6 12.4 %all-to-all-start.3 = ((bf16[4,64,1024]{2,1,0:T(8,128)(2,1)}), bf16[4,64,1024]{2,1,0:T(8,128)(2,1)S(1)}, u32[]{:S(2)}, u32[]{:S(2)}) async-start(bf16[4,64,1024]{2,1,0:T(8,128)(2,1)} %get-tuple-element.20), calls=%async_computation.3 | async-start | bytes 1048576 | tf_op jit(solution)/shard_map/all_to_all | solution.py:443
  169.8 52.7 %all-to-all-start.4 = ((bf16[32,160,128]{2,1,0:T(8,128)(2,1)}), bf16[32,160,128]{2,1,0:T(8,128)(2,1)S(1)}, u32[]{:S(2)}, u32[]{:S(2)}) async-start(bf16[32,160,128]{2,1,0:T(8,128)(2,1)} %bitcast.22), calls=%async_computation.4 | async-start | bytes 2621440 | tf_op jit(solution)/shard_map/all_to_all | solution.py:445
  228.0 46.3 %all-to-all-start.5 = ((bf16[32,160,128]{2,1,0:T(8,128)(2,1)}), bf16[32,160,128]{2,1,0:T(8,128)(2,1)S(1)}, u32[]{:S(2)}, u32[]{:S(2)}) async-start(bf16[32,160,128]{2,1,0:T(8,128)(2,1)} %bitcast.24), calls=%async_computation.5 | async-start | bytes 2621440 | tf_op jit(solution)/shard_map/all_to_all | solution.py:449
  274.3 23.6 %copy-start.8 = (f32[64,1024]{1,0:T(8,128)S(1)}, f32[64,1024]{1,0:T(8,128)}, u32[]{:S(2)}) copy-start(f32[64,1024]{1,0:T(8,128)} %get-tuple-element.16) | copy-start | bytes 786436
  (6 other events, 20.4 us)
Sparse Core Ops, SparseCore 0:
  9.4 68.1 all-gather.2

commit v6 on v5

--- a/solution.py
+++ b/solution.py
@@ -38,9 +38,9 @@
             == lax.broadcasted_iota(jnp.int32, (HD, HD), 1)
         ).astype(BF)
         for far, ref in ((0, b0), (7, b1), (6, b2), (5, b3), (1, b4), (2, b5), (3, b6)):
-            kv_ref[(own_y + far) % 8] = ref[...]
-        kv_ref[(own_y + 4) % 8, 0:2] = b7[...]
-        kv_ref[(own_y + 4) % 8, 2:4] = b8[...]
+            kv_ref[(own_y + far) % 8] = ref[0:512, :].reshape(4, 128, 2 * HD)
+        kv_ref[(own_y + 4) % 8, 0:2] = b7[...].reshape(2, 128, 2 * HD)
+        kv_ref[(own_y + 4) % 8, 2:4] = b8[0:256, :].reshape(2, 128, 2 * HD)
         for c in range(8):
             v = kv_ref[4 * (c % 2) : 4 * (c % 2) + 4, c // 2, :, HD : 2 * HD].reshape(512, HD)
             turned = lax.dot_general(eye, v, (((1,), (1,)), ((), ())), preferred_element_type=F32)
@@ -150,7 +150,7 @@
             in_specs=[
                 pl.BlockSpec((1, 8, 64, 256), lambda i, s: (i, 0, 0, 0)),
             ]
-            + [pl.BlockSpec(block.shape, lambda i, s: (0, 0, 0)) for block in key_values],
+            + [pl.BlockSpec(block.shape, lambda i, s: (0, 0)) for block in key_values],
             out_specs=pl.BlockSpec((1, 8, HD + STAT, 128), lambda i, s: (i, 0, 0, 0)),
             scratch_shapes=[
                 pltpu.VMEM((8, 4, 128, 2 * HD), BF),
@@ -170,7 +170,8 @@
     )(position, queries, *key_values)
 
 
-def merged_heads(pos_ref, parts_ref, second):
+def merge_kernel(parts_ref, w_ref, res_ref, gain_ref, hidden_ref, normed_ref):
+    step = pl.program_id(0)
     found = []
     for c in range(2):
         levels = []
@@ -184,29 +185,12 @@
         for x in range(1, 4):
             mixed = mixed + parts_ref[x, c, 0:HD, :].astype(F32) * (shares[x] * inverse)
         rows = mixed.T.astype(BF)
-        found.append(jnp.where((pos_ref[2] == 0) != second, rows[0:64], rows[64:128]))
-    return jnp.concatenate(found, axis=1)
-
-
-def merge_own_kernel(pos_ref, parts_ref, w_ref, res_ref, o_ref):
-    part = jnp.dot(merged_heads(pos_ref, parts_ref, False), w_ref[...], preferred_element_type=F32)
-
-    @pl.when(pl.program_id(0) == 0)
-    def _():
-        o_ref[...] = res_ref[...].astype(F32) + part
-
-    @pl.when(pl.program_id(0) > 0)
-    def _():
-        o_ref[...] = o_ref[...] + part
-
-
-def merge_other_kernel(pos_ref, parts_ref, w_ref, sum_ref, gain_ref, hidden_ref, normed_ref):
-    step = pl.program_id(0)
-    part = jnp.dot(merged_heads(pos_ref, parts_ref, True), w_ref[...], preferred_element_type=F32)
+        found += [rows[0:64], rows[64:128]]
+    part = jnp.dot(jnp.concatenate(found, axis=1), w_ref[...], preferred_element_type=F32)
 
     @pl.when(step == 0)
     def _():
-        hidden_ref[...] = sum_ref[...] + part
+        hidden_ref[...] = res_ref[...].astype(F32) + part
 
     @pl.when(step > 0)
     def _():
@@ -217,46 +201,29 @@
         hidden = hidden_ref[...]
         mean_square = jnp.mean(hidden * hidden, axis=1, keepdims=True)
         normed = (hidden * lax.rsqrt(mean_square + 1e-6) * gain_ref[...]).astype(BF)
-        for x in range(4):
-            normed_ref[x] = normed
-
-
-def merge_specs(tokens, width):
-    return [
-        pl.BlockSpec((4, 2, HD + STAT, 128), lambda c, s: (0, c, 0, 0)),
-        pl.BlockSpec((256, width), lambda c, s: (c, 0)),
-        pl.BlockSpec((tokens, width), lambda c, s: (0, 0)),
-    ]
-
-
-def merge(position, parts, weight, weight_other, residual, gain):
+        for i in range(4):
+            normed_ref[i] = normed
+
+
+def merge(parts, weight, residual, gain):
     tokens, width = residual.shape
-    whole = pl.BlockSpec((tokens, width), lambda c, s: (0, 0))
-    half_sum = pl.pallas_call(
-        merge_own_kernel,
-        grid_spec=pltpu.PrefetchScalarGridSpec(
-            num_scalar_prefetch=1,
-            grid=(4,),
-            in_specs=merge_specs(tokens, width),
-            out_specs=whole,
-        ),
-        out_shape=jax.ShapeDtypeStruct((tokens, width), F32),
-        name="merge_own",
-    )(position, parts, weight, residual)
+    whole = pl.BlockSpec((tokens, width), lambda c: (0, 0))
     return pl.pallas_call(
-        merge_other_kernel,
-        grid_spec=pltpu.PrefetchScalarGridSpec(
-            num_scalar_prefetch=1,
-            grid=(4,),
-            in_specs=merge_specs(tokens, width) + [pl.BlockSpec((1, width), lambda c, s: (0, 0))],
-            out_specs=[whole, pl.BlockSpec((4, tokens, width), lambda c, s: (0, 0, 0))],
-        ),
+        merge_kernel,
+        grid=(4,),
+        in_specs=[
+            pl.BlockSpec((4, 2, HD + STAT, 128), lambda c: (0, c, 0, 0)),
+            pl.BlockSpec((512, width), lambda c: (c, 0)),
+            whole,
+            pl.BlockSpec((1, width), lambda c: (0, 0)),
+        ],
+        out_specs=[whole, pl.BlockSpec((4, tokens, width), lambda c: (0, 0, 0))],
         out_shape=[
             jax.ShapeDtypeStruct((tokens, width), F32),
             jax.ShapeDtypeStruct((4, tokens, width), BF),
         ],
-        name="merge_other",
-    )(position, parts, weight_other, half_sum, gain)
+        name="merge",
+    )(parts, weight, residual, gain)
 
 
 def select_kernel(sel_ref, x_ref, o_ref, tmp_ref):
@@ -343,11 +310,6 @@
     )(gates, rows)
 
 
-def after(value, other):
-    first = other[(0,) * other.ndim]
-    return value + jnp.where(first > 1 << 30, 1, 0).astype(value.dtype)
-
-
 def local(
     residual,
     queries,
@@ -362,9 +324,9 @@
 ):
     tokens, width = residual.shape
     own_x = lax.axis_index("x")
-    own_y = lax.axis_index("y2") * 2 + lax.axis_index("y1")
-    own_core = lax.axis_index("dp")
-    position = jnp.stack([own_x, own_y, own_core]).astype(jnp.int32)
+    own_y2 = lax.axis_index("y2")
+    own_y = own_y2 * 2 + lax.axis_index("y1")
+    position = jnp.stack([own_x, own_y]).astype(jnp.int32)
 
     key_value = jnp.stack(
         [
@@ -379,15 +341,18 @@
         32, 16, 2 * HD
     )
     key_value = lax.all_to_all(key_value, ("x", "z"), split_axis=0, concat_axis=0, tiled=True)
+    listing = jnp.concatenate([routes.T, gate_levels.T], axis=0).astype(BF)
+    listing = jnp.pad(listing, ((0, 0), (0, 2 * HD - tokens)))
+    block = jnp.concatenate([key_value.reshape(512, 2 * HD), listing], axis=0)
     up = [(i, (i + 1) % 8) for i in range(8)]
     down = [(i, (i - 1) % 8) for i in range(8)]
-    ups, downs = [key_value.reshape(4, 128, 2 * HD)], [key_value.reshape(4, 128, 2 * HD)]
+    ups, downs = [block], [block]
     for _ in range(3):
         ups.append(lax.ppermute(ups[-1], ("y2", "y1"), up))
         downs.append(lax.ppermute(downs[-1], ("y2", "y1"), down))
     key_values = ups + downs[1:]
-    key_values.append(lax.ppermute(ups[3][0:2], ("y2", "y1"), up))
-    key_values.append(lax.ppermute(downs[3][2:4], ("y2", "y1"), down))
+    key_values.append(lax.ppermute(ups[3][0:256], ("y2", "y1"), up))
+    key_values.append(lax.ppermute(downs[3][256:528], ("y2", "y1"), down))
 
     query = queries.reshape(tokens, 8, 2 * HD).transpose(1, 0, 2)
     query = jnp.broadcast_to(query[None], (4, 8, tokens, 2 * HD)).reshape(32, tokens, 2 * HD)
@@ -396,42 +361,38 @@
         4, 8, tokens, 2 * HD
     )
 
-    head_weight = lax.dynamic_slice_in_dim(output_weight, own_core * HD, HD, 0)
-    gathered = lax.all_gather(head_weight, "z", axis=0, tiled=True)
+    whole_weight = lax.all_gather(output_weight, "z", axis=0, tiled=True)
 
     shards = flash(position, query, key_values)
     parts = lax.all_to_all(
         shards.reshape(32, HD + STAT, 128), ("x", "z"), split_axis=0, concat_axis=0, tiled=True
     ).reshape(4, 8, HD + STAT, 128)
-    gathered, own_in, own_out = lax.optimization_barrier((gathered, expert_in[0], expert_out[0]))
-    gathered_other = lax.ppermute(gathered, "dp", SWAP)
+    whole_weight, own_in, own_out = lax.optimization_barrier(
+        (whole_weight, expert_in[0], expert_out[0])
+    )
     other_in = lax.ppermute(own_in, "y1", SWAP)
     other_out = lax.ppermute(own_out, "y1", SWAP)
-    listing = after(jnp.concatenate([routes, gate_levels], axis=1), gathered)
-    listing = lax.all_gather(listing, "x", axis=0, tiled=True).reshape(4, tokens, 16)
-    named, levels = listing[:, :, 0:8], listing[:, :, 8:16]
-    local_expert = jnp.arange(32, dtype=jnp.int32)
-    wanted = (local_expert // 4) * 16 + own_x * 4 + local_expert % 4
-    match = named[:, :, :, None] == wanted
+    turned = [ups[0][512:], ups[2][512:], key_values[8][256:], downs[2][512:]]
+    listing = lax.dynamic_slice_in_dim(
+        jnp.stack([turned[k][:, :tokens] for k in (3, 2, 1, 0, 3, 2, 1)]), 3 - own_y2, 4, 0
+    ).astype(jnp.int32)
+    named, levels = listing[:, None, 0:8], listing[:, None, 8:16]
+    q = jnp.arange(32, dtype=jnp.int32)
+    match = named == ((q % 8) * 16 + (q // 8) * 4 + own_y2)[None, :, None, None]
     hits = jnp.any(match, axis=2)
-    gates = jnp.sum(jnp.where(match, levels[:, :, :, None], 0), axis=2).astype(F32) / 256.0
-    before = jnp.tril(jnp.ones((tokens, tokens), BF), -1)
-    ranks = jnp.einsum(
-        "ab,sbq->saq", before, hits.astype(BF), preferred_element_type=F32
-    ).astype(jnp.int32)
-    ranks = jnp.where(hits, ranks, -1)
-    slots = jnp.arange(CAP, dtype=jnp.int32)
-    same = jnp.eye(4, dtype=jnp.bool_)
-    placed = (ranks.transpose(2, 0, 1)[:, None, None, :, :] == slots[None, None, :, None, None]) & (
-        same[None, :, None, :, None]
-    )
+    gates = jnp.sum(jnp.where(match, levels, 0), axis=2).astype(F32) / 256.0
+    before = jnp.triu(jnp.ones((tokens, tokens), BF), 1)
+    ranks = jnp.einsum("sqb,ba->sqa", hits.astype(BF), before, preferred_element_type=F32)
+    ranks = jnp.where(hits, ranks.astype(jnp.int32), -1)
+    slots = jnp.arange(CAP, dtype=jnp.int32)[None, None, :, None, None]
+    same = jnp.eye(4, dtype=jnp.bool_)[None, :, None, :, None]
+    placed = (ranks.transpose(1, 0, 2)[:, None, None] == slots) & same
     chosen = placed.astype(BF).reshape(32 * 4 * CAP, 4 * tokens)
-    back = (ranks[:, :, :, None, None] == slots) & same[:, None, None, :, None]
-    shares = jnp.where(back, gates[:, :, :, None, None], 0.0).astype(BF)
-    shares = shares.reshape(4 * tokens, 32 * 4 * CAP)
+    shares = jnp.where(placed, gates.transpose(1, 0, 2)[:, None, None], 0.0).astype(BF)
+    shares = shares.reshape(32 * 4 * CAP, 4 * tokens).T
 
     hidden, spread = merge(
-        position, parts, gathered, gathered_other, residual, norm_gain.reshape(1, width)
+        parts, whole_weight, residual, norm_gain.reshape(1, width)
     )
 
     spread, other_in, other_out = lax.optimization_barrier((spread, other_in, other_out))
@@ -440,18 +401,18 @@
         [own_in[:, :half], other_in[:, :half], own_in[:, half:], other_in[:, half:]], axis=1
     )
     weight_out = jnp.concatenate([own_out, other_out], axis=0)
-    spread = lax.all_to_all(spread, "x", split_axis=0, concat_axis=0, tiled=True)
+    spread = lax.all_to_all(spread, "y2", split_axis=0, concat_axis=0, tiled=True)
     outgoing = select(chosen, spread.reshape(4 * tokens, width))
     arrived = lax.all_to_all(
-        outgoing.reshape(32, 4 * CAP * 8, 128), ("z", "y2"), split_axis=0, concat_axis=0, tiled=True
+        outgoing.reshape(32, 4 * CAP * 8, 128), ("x", "z"), split_axis=0, concat_axis=0, tiled=True
     )
     done = expert(arrived.reshape(-1, 128), weight_in, weight_out)
     answers = lax.all_to_all(
-        done.reshape(32, 4 * CAP * 8, 128), ("z", "y2"), split_axis=0, concat_axis=0, tiled=True
+        done.reshape(32, 4 * CAP * 8, 128), ("x", "z"), split_axis=0, concat_axis=0, tiled=True
     )
     sums = gather(shares, answers.reshape(-1, 128))
     sums = lax.all_to_all(
-        sums.reshape(4, tokens, width), "x", split_axis=0, concat_axis=0, tiled=True
+        sums.reshape(4, tokens, width), "y2", split_axis=0, concat_axis=0, tiled=True
     )
     return hidden + jnp.sum(sums.astype(F32), axis=0)
 

time: 307 us -> 274 us (0.89)
  the two profiles are of different devices: /device:TPU:2 before, /device:TPU:64 now
where the time goes in v6:
time: 274 us; the launch traced here: 273 us
  waiting for transfers between devices  102 us (37%)
  starting transfers between devices  84.7 us (31%)
  Pallas kernels  40.7 us (15%)
  blocking collectives  17.4 us (6%)
  between operations  13.9 us (5%)
  local copies, waits for them, and re-layouts  10.5 us (4%)
  other arithmetic  4.09 us (1%)
    pallas_call x1, Pallas kernels, flash(): pl.pallas_call(flash_kernel, grid_spec=pltpu.PrefetchScalarGridSpec(num_s...  29.4 us
    all_to_all x1, waiting for transfers between devices, local(): lax.all_to_all(done.reshape(32, 4 * CAP * 8, 128), ('x', 'z'), split_axis...  25.2 us
    all_to_all x1, waiting for transfers between devices, local(): lax.all_to_all(outgoing.reshape(32, 4 * CAP * 8, 128), ('x', 'z'), split_...  22.8 us
    all_to_all x1, waiting for transfers between devices, local(): lax.all_to_all(shards.reshape(32, HD + STAT, 128), ('x', 'z'), split_axis...  18.9 us
    all_to_all x1, blocking collectives, local(): lax.all_to_all(sums.reshape(4, tokens, width), 'y2', split_axis=0, concat...  17.4 us
    ppermute x3, starting transfers between devices, local(): downs.append(lax.ppermute(downs[-1], ('y2', 'y1'), down))  16.9 us
    all_to_all x1, starting transfers between devices, local(): lax.all_to_all(key_value, ('x', 'z'), split_axis=0, concat_axis=0, tiled=...  12.6 us
    all_to_all x1, waiting for transfers between devices, local(): lax.all_to_all(key_value, ('x', 'z'), split_axis=0, concat_axis=0, tiled=...  12.1 us
  transfers between devices with their start and end apart: 17, of which 9 were waited for; matrix products, arithmetic and copies ran while one was open for 4% of the time, Pallas kernels for 13%

profile of v6, /device:TPU:64, one launch (start us, length us, event | category | flops | bytes accessed | tf_op | source)
XLA Modules:
  0.0 273.0 jit_solution(5998525650415417669)
XLA Ops:
  9.5 12.6 %all-to-all-start = ((bf16[32,16,256]{2,1,0:T(8,128)(2,1)}), bf16[32,16,256]{2,1,0:T(8,128)(2,1)S(1)}, u32[]{:S(2)}, u32[]{:S(2)}) async-start(bf16[32,16,256]{2,1,0:T(8,128)(2,1)} %bitcast.6), calls=%async_computation | async-start | bytes 524288 | tf_op jit(solution)/shard_map/all_to_all | solution.py:343
  22.2 12.1 %all-to-all-done = bf16[32,16,256]{2,1,0:T(8,128)(2,1)S(1)} async-done(((bf16[32,16,256]{2,1,0:T(8,128)(2,1)}), bf16[32,16,256]{2,1,0:T(8,128)(2,1)S(1)}, u32[]{:S(2)}, u32[]{:S(2)}) %all-to-all-start) | async-done | bytes 262176 | tf_op jit(solution)/shard_map/all_to_all | solution.py:343
  35.5 4.6 %all-to-all-start.1 = ((bf16[32,64,256]{2,1,0:T(8,128)(2,1)}), bf16[32,64,256]{2,1,0:T(8,128)(2,1)S(1)}, u32[]{:S(2)}, u32[]{:S(2)}) async-start(bf16[32,64,256]{2,1,0:T(8,128)(2,1)} %bitcast.3), calls=%async_computation.1 | async-start | bytes 2097152 | tf_op jit(solution)/shard_map/all_to_all | solution.py:360
  40.2 5.7 %collective-permute-start.3 = (bf16[528,256]{1,0:T(8,128)(2,1)S(1)}, bf16[528,256]{1,0:T(8,128)(2,1)S(1)}, u32[]{:S(2)}, u32[]{:S(2)}) collective-permute-start(bf16[528,256]{1,0:T(8,128)(2,1)S(1)} %pad_maximum_fusion.2.b0), channel_id=1, source_target_pairs={{0,14},{2,0},{4,2},{6,4},{8,6},{10,8},{12,10},{14,12},{1,15},{3,1}... | collective-permute-start | bytes 811016 | tf_op jit(solution)/shard_map/ppermute | solution.py:352
  47.8 2.0 collective-permute-done.3.b4
  49.9 5.6 %collective-permute-start.4 = (bf16[528,256]{1,0:T(8,128)(2,1)S(1)}, bf16[528,256]{1,0:T(8,128)(2,1)S(1)}, u32[]{:S(2)}, u32[]{:S(2)}) collective-permute-start(bf16[528,256]{1,0:T(8,128)(2,1)S(1)} %collective-permute-done.3.b4), channel_id=1, source_target_pairs={{0,14},{2,0},{4,2},{6,4},{8,6},{10,8},{12,10},{14,12},{1,15},{3,1}... | collective-permute-start | bytes 811016 | tf_op jit(solution)/shard_map/ppermute | solution.py:352
  57.4 2.0 collective-permute-done.4.b5
  59.4 5.6 %collective-permute-start.5 = (bf16[528,256]{1,0:T(8,128)(2,1)S(1)}, bf16[528,256]{1,0:T(8,128)(2,1)S(1)}, u32[]{:S(2)}, u32[]{:S(2)}) collective-permute-start(bf16[528,256]{1,0:T(8,128)(2,1)S(1)} %collective-permute-done.4.b5), channel_id=1, source_target_pairs={{0,14},{2,0},{4,2},{6,4},{8,6},{10,8},{12,10},{14,12},{1,15},{3,1}... | collective-permute-start | bytes 811016 | tf_op jit(solution)/shard_map/ppermute | solution.py:352
  66.9 2.0 collective-permute-done.5.b6
  69.0 5.6 %collective-permute-start.7 = (bf16[272,256]{1,0:T(8,128)(2,1)S(1)}, bf16[272,256]{1,0:T(8,128)(2,1)S(1)}, u32[]{:S(2)}, u32[]{:S(2)}) collective-permute-start(bf16[272,256]{1,0:T(8,128)(2,1)S(1)} %slice.71), channel_id=1, source_target_pairs={{0,14},{2,0},{4,2},{6,4},{8,6},{10,8},{12,10},{14,12},{1,15},{3,1}... | collective-permute-start | bytes 417800 | tf_op jit(solution)/shard_map/ppermute | solution.py:355
  76.6 6.1 %collective-permute-done.6.b7 = bf16[256,256]{1,0:T(8,128)(2,1)S(1)} collective-permute-done((bf16[256,256]{1,0:T(8,128)(2,1)S(1)}, bf16[256,256]{1,0:T(8,128)(2,1)S(1)}, u32[]{:S(2)}, u32[]{:S(2)}) %collective-permute-start.6) | collective-permute-done | bytes 131104 | tf_op jit(solution)/shard_map/ppermute | solution.py:354
  82.7 29.4 %flash.1 = bf16[4,8,136,128]{3,2,1,0:T(8,128)(2,1)} custom-call(s32[2]{0:T(128)S(1)} %pad_add_fusion.pos_ref, bf16[4,8,64,256]{3,2,1,0:T(8,128)(2,1)S(1)} %bitcast.66, bf16[528,256]{1,0:T(8,128)(2,1)S(1)} %pad_maximum_fusion.2.b0, bf16[528,256]{1,0:T(8,128)(2,1)S(1)} %collective-permute-done.b1, bf16[528,256]{1,0:T(8,128)(2,1)S(1)} %collective-permute-done.1.b2, ...), custom_call_target="tpu_custom_call" | custom-call | flops 5368709120 | bytes 5242880 | tf_op jit(solution)/shard_map/flash/pallas_call | solution.py:145
  112.1 8.4 %all-to-all-start.2 = ((bf16[32,136,128]{2,1,0:T(8,128)(2,1)}), bf16[32,136,128]{2,1,0:T(8,128)(2,1)S(1)}, u32[]{:S(2)}, u32[]{:S(2)}) async-start(bf16[32,136,128]{2,1,0:T(8,128)(2,1)} %bitcast.11), calls=%async_computation.2 | async-start | bytes 2228224 | tf_op jit(solution)/shard_map/all_to_all | solution.py:367
  122.6 3.9 %collective-permute-start.9 = (bf16[192,1024]{1,0:T(8,128)(2,1)S(1)}, bf16[192,1024]{1,0:T(8,128)(2,1)S(1)}, u32[]{:S(2)}, u32[]{:S(2)}) collective-permute-start(bf16[192,1024]{1,0:T(8,128)(2,1)S(1)} %bitcast.72), channel_id=1, source_target_pairs={{0,2},{2,0},{1,3},{3,1},{4,6},{6,4},{5,7},{7,5},{8,10},{10,8},{9,1... | collective-permute-start | bytes 1179656 | tf_op jit(solution)/shard_map/ppermute | solution.py:374
  126.5 18.9 %all-to-all-done.2 = bf16[32,136,128]{2,1,0:T(8,128)(2,1)S(1)} async-done(((bf16[32,136,128]{2,1,0:T(8,128)(2,1)}), bf16[32,136,128]{2,1,0:T(8,128)(2,1)S(1)}, u32[]{:S(2)}, u32[]{:S(2)}) %all-to-all-start.2) | async-done | bytes 1114144 | tf_op jit(solution)/shard_map/all_to_all | solution.py:367
  146.4 5.1 %merge.1 = (f32[64,1024]{1,0:T(8,128)}, bf16[4,64,1024]{2,1,0:T(8,128)(2,1)}) custom-call(bf16[4,8,136,128]{3,2,1,0:T(8,128)(2,1)} %bitcast.67, bf16[2048,1024]{1,0:T(8,128)(2,1)} %all-gather.2.cloned.1.call-done.w_ref, bf16[64,1024]{1,0:T(8,128)(2,1)} %res_ref.1, f32[1,1024]{1,0:T(1,128)} %bitcast.77), custom_call_target="tpu_custom_call" | custom-call | tf_op jit(solution)/shard_map/merge/pallas_call | solution.py:211
  151.5 12.0 %all-to-all-start.3 = ((bf16[4,64,1024]{2,1,0:T(8,128)(2,1)}), bf16[4,64,1024]{2,1,0:T(8,128)(2,1)S(1)}, u32[]{:S(2)}, u32[]{:S(2)}) async-start(bf16[4,64,1024]{2,1,0:T(8,128)(2,1)} %get-tuple-element.20), calls=%async_computation.3 | async-start | bytes 1048576 | tf_op jit(solution)/shard_map/all_to_all | solution.py:404
  164.8 9.7 %all-to-all-done.3 = bf16[4,64,1024]{2,1,0:T(8,128)(2,1)S(1)} async-done(((bf16[4,64,1024]{2,1,0:T(8,128)(2,1)}), bf16[4,64,1024]{2,1,0:T(8,128)(2,1)S(1)}, u32[]{:S(2)}, u32[]{:S(2)}) %all-to-all-start.3) | async-done | bytes 524320 | tf_op jit(solution)/shard_map/all_to_all | solution.py:404
  176.3 6.0 %all-to-all-start.4 = ((bf16[32,160,128]{2,1,0:T(8,128)(2,1)}), bf16[32,160,128]{2,1,0:T(8,128)(2,1)S(1)}, u32[]{:S(2)}, u32[]{:S(2)}) async-start(bf16[32,160,128]{2,1,0:T(8,128)(2,1)} %bitcast.26), calls=%async_computation.4 | async-start | bytes 2621440 | tf_op jit(solution)/shard_map/all_to_all | solution.py:406
  186.6 22.8 %all-to-all-done.4 = bf16[32,160,128]{2,1,0:T(8,128)(2,1)S(1)} async-done(((bf16[32,160,128]{2,1,0:T(8,128)(2,1)}), bf16[32,160,128]{2,1,0:T(8,128)(2,1)S(1)}, u32[]{:S(2)}, u32[]{:S(2)}) %all-to-all-start.4) | async-done | bytes 1310752 | tf_op jit(solution)/shard_map/all_to_all | solution.py:406
  210.6 3.6 %expert.1 = bf16[5120,128]{1,0:T(8,128)(2,1)S(1)} custom-call(bf16[5120,128]{1,0:T(8,128)(2,1)S(1)} %bitcast.61, bf16[1024,768]{1,0:T(8,128)(2,1)S(1)} %pad_maximum_fusion.win_ref, bf16[384,1024]{1,0:T(8,128)(2,1)S(1)} %copy-done.1), custom_call_target="tpu_custom_call" | custom-call | tf_op jit(solution)/shard_map/expert/pallas_call | solution.py:269
  215.3 5.2 %all-to-all-start.5 = ((bf16[32,160,128]{2,1,0:T(8,128)(2,1)}), bf16[32,160,128]{2,1,0:T(8,128)(2,1)S(1)}, u32[]{:S(2)}, u32[]{:S(2)}) async-start(bf16[32,160,128]{2,1,0:T(8,128)(2,1)} %bitcast.62), calls=%async_computation.5 | async-start | bytes 2621440 | tf_op jit(solution)/shard_map/all_to_all | solution.py:410
  221.9 25.2 %all-to-all-done.5 = bf16[32,160,128]{2,1,0:T(8,128)(2,1)S(1)} async-done(((bf16[32,160,128]{2,1,0:T(8,128)(2,1)}), bf16[32,160,128]{2,1,0:T(8,128)(2,1)S(1)}, u32[]{:S(2)}, u32[]{:S(2)}) %all-to-all-start.5) | async-done | bytes 1310752 | tf_op jit(solution)/shard_map/all_to_all | solution.py:410
  247.9 17.4 %all_to_all.35 = bf16[4,64,1024]{2,1,0:T(8,128)(2,1)S(1)} all-to-all(bf16[4,64,1024]{2,1,0:T(8,128)(2,1)S(1)} %bitcast.64), channel_id=1, replica_groups=mesh['z'=8,'x'=4,'y2'=4,'y1'=2,'dp'=2] {'y2'}, dimensions={0} | all-to-all | bytes 1048576 | tf_op jit(solution)/shard_map/all_to_all | solution.py:414
  (85 shorter events, 27.6 us)
Async XLA Ops:
  6.5 15.6 %copy-start.9 = (bf16[64,2048]{1,0:T(8,128)(2,1)S(1)}, bf16[64,2048]{1,0:T(8,128)(2,1)}, u32[]{:S(2)}) copy-start(bf16[64,2048]{1,0:T(8,128)(2,1)} %param.11) | copy-start | bytes 786436
  6.5 114.1 %all-gather.2.cloned.1.call-start = ((), (), s32[]{:S(2)}) async-start(), calls=%async_computation.7 | async-start | bytes 4718592 | tf_op jit(solution)/shard_map/all_gather | solution.py:364
  9.5 24.9 %all-to-all-start = ((bf16[32,16,256]{2,1,0:T(8,128)(2,1)}), bf16[32,16,256]{2,1,0:T(8,128)(2,1)S(1)}, u32[]{:S(2)}, u32[]{:S(2)}) async-start(bf16[32,16,256]{2,1,0:T(8,128)(2,1)} %bitcast.6), calls=%async_computation | async-start | bytes 524288 | tf_op jit(solution)/shard_map/all_to_all | solution.py:343
  22.2 17.9 %copy-start.10 = (s32[64,8]{0,1:T(8,128)S(1)}, s32[64,8]{0,1:T(8,128)}, u32[]{:S(2)}) copy-start(s32[64,8]{0,1:T(8,128)} %param.17) | copy-start | bytes 6148
  22.2 17.9 %copy-start.11 = (s32[64,8]{0,1:T(8,128)S(1)}, s32[64,8]{0,1:T(8,128)}, u32[]{:S(2)}) copy-start(s32[64,8]{0,1:T(8,128)} %param.16) | copy-start | bytes 6148
  35.5 47.1 %all-to-all-start.1 = ((bf16[32,64,256]{2,1,0:T(8,128)(2,1)}), bf16[32,64,256]{2,1,0:T(8,128)(2,1)S(1)}, u32[]{:S(2)}, u32[]{:S(2)}) async-start(bf16[32,64,256]{2,1,0:T(8,128)(2,1)} %bitcast.3), calls=%async_computation.1 | async-start | bytes 2097152 | tf_op jit(solution)/shard_map/all_to_all | solution.py:360
  40.2 9.7 %collective-permute-start.3 = (bf16[528,256]{1,0:T(8,128)(2,1)S(1)}, bf16[528,256]{1,0:T(8,128)(2,1)S(1)}, u32[]{:S(2)}, u32[]{:S(2)}) collective-permute-start(bf16[528,256]{1,0:T(8,128)(2,1)S(1)} %pad_maximum_fusion.2.b0), channel_id=1, source_target_pairs={{0,14},{2,0},{4,2},{6,4},{8,6},{10,8},{12,10},{14,12},{1,15},{3,1}... | collective-permute-start | bytes 811016 | tf_op jit(solution)/shard_map/ppermute | solution.py:352
  45.9 9.6 %collective-permute-start = (bf16[528,256]{1,0:T(8,128)(2,1)S(1)}, bf16[528,256]{1,0:T(8,128)(2,1)S(1)}, u32[]{:S(2)}, u32[]{:S(2)}) collective-permute-start(bf16[528,256]{1,0:T(8,128)(2,1)S(1)} %pad_maximum_fusion.2.b0), channel_id=1, source_target_pairs={{0,2},{2,4},{4,6},{6,8},{8,10},{10,12},{12,14},{14,0},{1,3},{3,5},... | collective-permute-start | bytes 811016 | tf_op jit(solution)/shard_map/ppermute | solution.py:351
  49.9 9.6 %collective-permute-start.4 = (bf16[528,256]{1,0:T(8,128)(2,1)S(1)}, bf16[528,256]{1,0:T(8,128)(2,1)S(1)}, u32[]{:S(2)}, u32[]{:S(2)}) collective-permute-start(bf16[528,256]{1,0:T(8,128)(2,1)S(1)} %collective-permute-done.3.b4), channel_id=1, source_target_pairs={{0,14},{2,0},{4,2},{6,4},{8,6},{10,8},{12,10},{14,12},{1,15},{3,1}... | collective-permute-start | bytes 811016 | tf_op jit(solution)/shard_map/ppermute | solution.py:352
  55.5 9.6 %collective-permute-start.1 = (bf16[528,256]{1,0:T(8,128)(2,1)S(1)}, bf16[528,256]{1,0:T(8,128)(2,1)S(1)}, u32[]{:S(2)}, u32[]{:S(2)}) collective-permute-start(bf16[528,256]{1,0:T(8,128)(2,1)S(1)} %collective-permute-done.b1), channel_id=1, source_target_pairs={{0,2},{2,4},{4,6},{6,8},{8,10},{10,12},{12,14},{14,0},{1,3},{3,5},... | collective-permute-start | bytes 811016 | tf_op jit(solution)/shard_map/ppermute | solution.py:351
  59.4 9.6 %collective-permute-start.5 = (bf16[528,256]{1,0:T(8,128)(2,1)S(1)}, bf16[528,256]{1,0:T(8,128)(2,1)S(1)}, u32[]{:S(2)}, u32[]{:S(2)}) collective-permute-start(bf16[528,256]{1,0:T(8,128)(2,1)S(1)} %collective-permute-done.4.b5), channel_id=1, source_target_pairs={{0,14},{2,0},{4,2},{6,4},{8,6},{10,8},{12,10},{14,12},{1,15},{3,1}... | collective-permute-start | bytes 811016 | tf_op jit(solution)/shard_map/ppermute | solution.py:352
  65.0 9.6 %collective-permute-start.2 = (bf16[528,256]{1,0:T(8,128)(2,1)S(1)}, bf16[528,256]{1,0:T(8,128)(2,1)S(1)}, u32[]{:S(2)}, u32[]{:S(2)}) collective-permute-start(bf16[528,256]{1,0:T(8,128)(2,1)S(1)} %collective-permute-done.1.b2), channel_id=1, source_target_pairs={{0,2},{2,4},{4,6},{6,8},{8,10},{10,12},{12,14},{14,0},{1,3},{3,5},... | collective-permute-start | bytes 811016 | tf_op jit(solution)/shard_map/ppermute | solution.py:351
  69.0 13.7 %collective-permute-start.7 = (bf16[272,256]{1,0:T(8,128)(2,1)S(1)}, bf16[272,256]{1,0:T(8,128)(2,1)S(1)}, u32[]{:S(2)}, u32[]{:S(2)}) collective-permute-start(bf16[272,256]{1,0:T(8,128)(2,1)S(1)} %slice.71), channel_id=1, source_target_pairs={{0,14},{2,0},{4,2},{6,4},{8,6},{10,8},{12,10},{14,12},{1,15},{3,1}... | collective-permute-start | bytes 417800 | tf_op jit(solution)/shard_map/ppermute | solution.py:355
  74.6 8.1 %collective-permute-start.6 = (bf16[256,256]{1,0:T(8,128)(2,1)S(1)}, bf16[256,256]{1,0:T(8,128)(2,1)S(1)}, u32[]{:S(2)}, u32[]{:S(2)}) collective-permute-start(bf16[256,256]{1,0:T(8,128)(2,1)S(1)} %slice.70), channel_id=1, source_target_pairs={{0,2},{2,4},{4,6},{6,8},{8,10},{10,12},{12,14},{14,0},{1,3},{3,5},... | collective-permute-start | bytes 393224 | tf_op jit(solution)/shard_map/ppermute | solution.py:354
  112.1 8.5 %copy-start.3 = (bf16[1,1024,384]{2,1,0:T(8,128)(2,1)S(1)}, bf16[1,1024,384]{2,1,0:T(8,128)(2,1)}, u32[]{:S(2)}) copy-start(bf16[1,1024,384]{2,1,0:T(8,128)(2,1)} %param.18) | copy-start | bytes 2359300
  112.1 10.5 %copy-start.4 = (bf16[1,192,1024]{2,1,0:T(8,128)(2,1)S(1)}, bf16[1,192,1024]{2,1,0:T(8,128)(2,1)}, u32[]{:S(2)}) copy-start(bf16[1,192,1024]{2,1,0:T(8,128)(2,1)} %param.19) | copy-start | bytes 1179652
  112.1 33.3 %all-to-all-start.2 = ((bf16[32,136,128]{2,1,0:T(8,128)(2,1)}), bf16[32,136,128]{2,1,0:T(8,128)(2,1)S(1)}, u32[]{:S(2)}, u32[]{:S(2)}) async-start(bf16[32,136,128]{2,1,0:T(8,128)(2,1)} %bitcast.11), calls=%async_computation.2 | async-start | bytes 2228224 | tf_op jit(solution)/shard_map/all_to_all | solution.py:367
  120.6 30.9 %collective-permute-start.8 = (bf16[1024,384]{1,0:T(8,128)(2,1)S(1)}, bf16[1024,384]{1,0:T(8,128)(2,1)}, u32[]{:S(2)}, u32[]{:S(2)}) collective-permute-start(bf16[1024,384]{1,0:T(8,128)(2,1)S(1)} %bitcast.68), channel_id=1, source_target_pairs={{0,2},{2,0},{1,3},{3,1},{4,6},{6,4},{5,7},{7,5},{8,10},{10,8},{9,1... | collective-permute-start | bytes 2359304 | tf_op jit(solution)/shard_map/ppermute | solution.py:373
  122.6 28.9 %collective-permute-start.9 = (bf16[192,1024]{1,0:T(8,128)(2,1)S(1)}, bf16[192,1024]{1,0:T(8,128)(2,1)S(1)}, u32[]{:S(2)}, u32[]{:S(2)}) collective-permute-start(bf16[192,1024]{1,0:T(8,128)(2,1)S(1)} %bitcast.72), channel_id=1, source_target_pairs={{0,2},{2,0},{1,3},{3,1},{4,6},{6,4},{5,7},{7,5},{8,10},{10,8},{9,1... | collective-permute-start | bytes 1179656 | tf_op jit(solution)/shard_map/ppermute | solution.py:374
  151.5 13.3 %copy-start.6 = (bf16[192,1024]{1,0:T(8,128)(2,1)}, bf16[192,1024]{1,0:T(8,128)(2,1)S(1)}, u32[]{:S(2)}) copy-start(bf16[192,1024]{1,0:T(8,128)(2,1)S(1)} %collective-permute-done.9) | copy-start | bytes 1179652
  151.5 23.0 %all-to-all-start.3 = ((bf16[4,64,1024]{2,1,0:T(8,128)(2,1)}), bf16[4,64,1024]{2,1,0:T(8,128)(2,1)S(1)}, u32[]{:S(2)}, u32[]{:S(2)}) async-start(bf16[4,64,1024]{2,1,0:T(8,128)(2,1)} %get-tuple-element.20), calls=%async_computation.3 | async-start | bytes 1048576 | tf_op jit(solution)/shard_map/all_to_all | solution.py:404
  176.3 33.2 %all-to-all-start.4 = ((bf16[32,160,128]{2,1,0:T(8,128)(2,1)}), bf16[32,160,128]{2,1,0:T(8,128)(2,1)S(1)}, u32[]{:S(2)}, u32[]{:S(2)}) async-start(bf16[32,160,128]{2,1,0:T(8,128)(2,1)} %bitcast.26), calls=%async_computation.4 | async-start | bytes 2621440 | tf_op jit(solution)/shard_map/all_to_all | solution.py:406
  215.3 31.8 %all-to-all-start.5 = ((bf16[32,160,128]{2,1,0:T(8,128)(2,1)}), bf16[32,160,128]{2,1,0:T(8,128)(2,1)S(1)}, u32[]{:S(2)}, u32[]{:S(2)}) async-start(bf16[32,160,128]{2,1,0:T(8,128)(2,1)} %bitcast.62), calls=%async_computation.5 | async-start | bytes 2621440 | tf_op jit(solution)/shard_map/all_to_all | solution.py:410
  247.1 18.3 %copy-start.8 = (f32[64,1024]{1,0:T(8,128)S(1)}, f32[64,1024]{1,0:T(8,128)}, u32[]{:S(2)}) copy-start(f32[64,1024]{1,0:T(8,128)} %get-tuple-element.16) | copy-start | bytes 786436
  (5 other events, 5.3 us)
Sparse Core Ops, SparseCore 0:
  9.4 83.1 all-gather.1

commit v7 on v6

--- a/solution.py
+++ b/solution.py
@@ -20,7 +20,7 @@
 
 
 def flash_kernel(
-    pos_ref, q_ref, b0, b1, b2, b3, b4, b5, b6, b7, b8, o_ref, kv_ref, vt_ref, bias_ref, acc_ref, m_ref, top_ref
+    pos_ref, q_ref, b0, b1, b2, b3, b4, b5, b6, b7, o_ref, kv_ref, vt_ref, bias_ref, acc_ref, m_ref, top_ref
 ):
     block = pl.program_id(0)
     own_x = pos_ref[0]
@@ -37,10 +37,8 @@
             lax.broadcasted_iota(jnp.int32, (HD, HD), 0)
             == lax.broadcasted_iota(jnp.int32, (HD, HD), 1)
         ).astype(BF)
-        for far, ref in ((0, b0), (7, b1), (6, b2), (5, b3), (1, b4), (2, b5), (3, b6)):
+        for far, ref in enumerate((b0, b5, b6, b7, b4, b3, b2, b1)):
             kv_ref[(own_y + far) % 8] = ref[0:512, :].reshape(4, 128, 2 * HD)
-        kv_ref[(own_y + 4) % 8, 0:2] = b7[...].reshape(2, 128, 2 * HD)
-        kv_ref[(own_y + 4) % 8, 2:4] = b8[0:256, :].reshape(2, 128, 2 * HD)
         for c in range(8):
             v = kv_ref[4 * (c % 2) : 4 * (c % 2) + 4, c // 2, :, HD : 2 * HD].reshape(512, HD)
             turned = lax.dot_general(eye, v, (((1,), (1,)), ((), ())), preferred_element_type=F32)
@@ -310,6 +308,39 @@
     )(gates, rows)
 
 
+def pack_kv_kernel(k_ref, v_ref, o_ref):
+    for g in range(2):
+        lanes = slice(g * HD, (g + 1) * HD)
+        both = jnp.concatenate([k_ref[:, lanes], v_ref[:, lanes]], axis=1)
+        for x in range(4):
+            for i in range(4):
+                o_ref[x * 8 + g * 4 + i] = both[16 * x : 16 * x + 16]
+
+
+def pack_kv(keys, values):
+    return pl.pallas_call(
+        pack_kv_kernel,
+        out_shape=jax.ShapeDtypeStruct((32, 16, 2 * HD), BF),
+        name="pack_kv",
+    )(keys, values)
+
+
+def pack_q_kernel(q_ref, o_ref):
+    for z in range(8):
+        piece = q_ref[:, z * 2 * HD : (z + 1) * 2 * HD]
+        for x in range(4):
+            o_ref[x * 8 + z] = piece
+
+
+def pack_q(queries):
+    return pl.pallas_call(
+        pack_q_kernel,
+        out_shape=jax.ShapeDtypeStruct((32, queries.shape[0], 2 * HD), BF),
+        cost_estimate=pl.CostEstimate(flops=0, bytes_accessed=5 << 18, transcendentals=0),
+        name="pack_q",
+    )(queries)
+
+
 def local(
     residual,
     queries,
@@ -328,18 +359,7 @@
     own_y = own_y2 * 2 + lax.axis_index("y1")
     position = jnp.stack([own_x, own_y]).astype(jnp.int32)
 
-    key_value = jnp.stack(
-        [
-            jnp.concatenate(
-                [key_vectors[:, g : g + HD], value_vectors[:, g : g + HD]], axis=1
-            ).reshape(4, 16, 2 * HD)
-            for g in (0, HD)
-        ],
-        axis=1,
-    )
-    key_value = jnp.broadcast_to(key_value[:, :, None], (4, 2, 4, 16, 2 * HD)).reshape(
-        32, 16, 2 * HD
-    )
+    key_value = pack_kv(key_vectors, value_vectors)
     key_value = lax.all_to_all(key_value, ("x", "z"), split_axis=0, concat_axis=0, tiled=True)
     listing = jnp.concatenate([routes.T, gate_levels.T], axis=0).astype(BF)
     listing = jnp.pad(listing, ((0, 0), (0, 2 * HD - tokens)))
@@ -347,17 +367,13 @@
     up = [(i, (i + 1) % 8) for i in range(8)]
     down = [(i, (i - 1) % 8) for i in range(8)]
     ups, downs = [block], [block]
-    for _ in range(3):
+    for step in range(4):
         ups.append(lax.ppermute(ups[-1], ("y2", "y1"), up))
-        downs.append(lax.ppermute(downs[-1], ("y2", "y1"), down))
+        if step < 3:
+            downs.append(lax.ppermute(downs[-1], ("y2", "y1"), down))
     key_values = ups + downs[1:]
-    key_values.append(lax.ppermute(ups[3][0:256], ("y2", "y1"), up))
-    key_values.append(lax.ppermute(downs[3][256:528], ("y2", "y1"), down))
-
-    query = queries.reshape(tokens, 8, 2 * HD).transpose(1, 0, 2)
-    query = jnp.broadcast_to(query[None], (4, 8, tokens, 2 * HD)).reshape(32, tokens, 2 * HD)
-    query, _ = lax.optimization_barrier((query, key_value))
-    query = lax.all_to_all(query, ("x", "z"), split_axis=0, concat_axis=0, tiled=True).reshape(
+
+    query = lax.all_to_all(pack_q(queries), ("x", "z"), split_axis=0, concat_axis=0, tiled=True).reshape(
         4, 8, tokens, 2 * HD
     )
 
@@ -372,7 +388,7 @@
     )
     other_in = lax.ppermute(own_in, "y1", SWAP)
     other_out = lax.ppermute(own_out, "y1", SWAP)
-    turned = [ups[0][512:], ups[2][512:], key_values[8][256:], downs[2][512:]]
+    turned = [ups[0][512:], ups[2][512:], ups[4][512:], downs[2][512:]]
     listing = lax.dynamic_slice_in_dim(
         jnp.stack([turned[k][:, :tokens] for k in (3, 2, 1, 0, 3, 2, 1)]), 3 - own_y2, 4, 0
     ).astype(jnp.int32)

time: 274 us -> 277 us (1.011)
  the two profiles are of different devices: /device:TPU:64 before, /device:TPU:8 now
where the time goes in v7:
time: 277 us; the launch traced here: 276 us
  waiting for transfers between devices  115 us (42%)
  starting transfers between devices  74.5 us (27%)
  Pallas kernels  45.2 us (16%)
  blocking collectives  15.7 us (6%)
  between operations  13.8 us (5%)
  local copies, waits for them, and re-layouts  7.15 us (3%)
  other arithmetic  4.1 us (1%)
    pallas_call x1, Pallas kernels, flash(): pl.pallas_call(flash_kernel, grid_spec=pltpu.PrefetchScalarGridSpec(num_s...  30.4 us
    all_to_all x1, waiting for transfers between devices, local(): lax.all_to_all(done.reshape(32, 4 * CAP * 8, 128), ('x', 'z'), split_axis...  28.5 us
    all_to_all x1, waiting for transfers between devices, local(): lax.all_to_all(outgoing.reshape(32, 4 * CAP * 8, 128), ('x', 'z'), split_...  27.7 us
    all_to_all x1, waiting for transfers between devices, local(): lax.all_to_all(shards.reshape(32, HD + STAT, 128), ('x', 'z'), split_axis...  21.3 us
    all_to_all x1, blocking collectives, local(): lax.all_to_all(sums.reshape(4, tokens, width), 'y2', split_axis=0, concat...  15.7 us
    ppermute x4, waiting for transfers between devices, local(): ups.append(lax.ppermute(ups[-1], ('y2', 'y1'), up))  14.4 us
    all_to_all x1, starting transfers between devices, local(): lax.all_to_all(key_value, ('x', 'z'), split_axis=0, concat_axis=0, tiled=...  13.2 us
    all_to_all x1, starting transfers between devices, local(): lax.all_to_all(spread, 'y2', split_axis=0, concat_axis=0, tiled=True)  12.8 us
  transfers between devices with their start and end apart: 16, of which 12 were waited for; matrix products, arithmetic and copies ran while one was open for 2% of the time, Pallas kernels for 14%

profile of v7, /device:TPU:8, one launch (start us, length us, event | category | flops | bytes accessed | tf_op | source)
XLA Modules:
  0.0 276.1 jit_solution(17340331802071611972)
XLA Ops:
  8.8 13.2 %all-to-all-start.1 = ((bf16[32,16,256]{2,1,0:T(8,128)(2,1)}), bf16[32,16,256]{2,1,0:T(8,128)(2,1)S(1)}, u32[]{:S(2)}, u32[]{:S(2)}) async-start(bf16[32,16,256]{2,1,0:T(8,128)(2,1)} %pack_kv.1), calls=%async_computation.1 | async-start | bytes 524288 | tf_op jit(solution)/shard_map/all_to_all | solution.py:363
  24.0 10.4 %all-to-all-done.1 = bf16[32,16,256]{2,1,0:T(8,128)(2,1)S(1)} async-done(((bf16[32,16,256]{2,1,0:T(8,128)(2,1)}), bf16[32,16,256]{2,1,0:T(8,128)(2,1)S(1)}, u32[]{:S(2)}, u32[]{:S(2)}) %all-to-all-start.1) | async-done | bytes 262176 | tf_op jit(solution)/shard_map/all_to_all | solution.py:363
  34.4 4.4 %all-to-all-start = ((bf16[32,64,256]{2,1,0:T(8,128)(2,1)}), bf16[32,64,256]{2,1,0:T(8,128)(2,1)S(1)}, u32[]{:S(2)}, u32[]{:S(2)}) async-start(bf16[32,64,256]{2,1,0:T(8,128)(2,1)} %pack_q.1), calls=%async_computation | async-start | bytes 2097152 | tf_op jit(solution)/shard_map/all_to_all | solution.py:376
  38.9 3.5 %collective-permute-start = (bf16[528,256]{1,0:T(8,128)(2,1)S(1)}, bf16[528,256]{1,0:T(8,128)(2,1)S(1)}, u32[]{:S(2)}, u32[]{:S(2)}) collective-permute-start(bf16[528,256]{1,0:T(8,128)(2,1)S(1)} %pad_maximum_fusion.2.b0), channel_id=1, source_target_pairs={{0,2},{2,4},{4,6},{6,8},{8,10},{10,12},{12,14},{14,0},{1,3},{3,5},... | collective-permute-start | bytes 811016 | tf_op jit(solution)/shard_map/ppermute | solution.py:371
  44.7 3.1 %collective-permute-done.b1 = bf16[528,256]{1,0:T(8,128)(2,1)S(1)} collective-permute-done((bf16[528,256]{1,0:T(8,128)(2,1)S(1)}, bf16[528,256]{1,0:T(8,128)(2,1)S(1)}, u32[]{:S(2)}, u32[]{:S(2)}) %collective-permute-start) | collective-permute-done | bytes 270368 | tf_op jit(solution)/shard_map/ppermute | solution.py:371
  47.8 3.5 %collective-permute-start.1 = (bf16[528,256]{1,0:T(8,128)(2,1)S(1)}, bf16[528,256]{1,0:T(8,128)(2,1)S(1)}, u32[]{:S(2)}, u32[]{:S(2)}) collective-permute-start(bf16[528,256]{1,0:T(8,128)(2,1)S(1)} %collective-permute-done.b1), channel_id=1, source_target_pairs={{0,2},{2,4},{4,6},{6,8},{8,10},{10,12},{12,14},{14,0},{1,3},{3,5},... | collective-permute-start | bytes 811016 | tf_op jit(solution)/shard_map/ppermute | solution.py:371
  53.9 2.8 %collective-permute-done.1.b2 = bf16[528,256]{1,0:T(8,128)(2,1)S(1)} collective-permute-done((bf16[528,256]{1,0:T(8,128)(2,1)S(1)}, bf16[528,256]{1,0:T(8,128)(2,1)S(1)}, u32[]{:S(2)}, u32[]{:S(2)}) %collective-permute-start.1) | collective-permute-done | bytes 270368 | tf_op jit(solution)/shard_map/ppermute | solution.py:371
  56.7 3.0 %collective-permute-start.2 = (bf16[528,256]{1,0:T(8,128)(2,1)S(1)}, bf16[528,256]{1,0:T(8,128)(2,1)S(1)}, u32[]{:S(2)}, u32[]{:S(2)}) collective-permute-start(bf16[528,256]{1,0:T(8,128)(2,1)S(1)} %collective-permute-done.1.b2), channel_id=1, source_target_pairs={{0,2},{2,4},{4,6},{6,8},{8,10},{10,12},{12,14},{14,0},{1,3},{3,5},... | collective-permute-start | bytes 811016 | tf_op jit(solution)/shard_map/ppermute | solution.py:371
  60.1 3.4 %collective-permute-start.6 = (bf16[528,256]{1,0:T(8,128)(2,1)S(1)}, bf16[528,256]{1,0:T(8,128)(2,1)S(1)}, u32[]{:S(2)}, u32[]{:S(2)}) collective-permute-start(bf16[528,256]{1,0:T(8,128)(2,1)S(1)} %collective-permute-done.5.b6), channel_id=1, source_target_pairs={{0,14},{2,0},{4,2},{6,4},{8,6},{10,8},{12,10},{14,12},{1,15},{3,1}... | collective-permute-start | bytes 811016 | tf_op jit(solution)/shard_map/ppermute | solution.py:373
  66.0 2.6 collective-permute-start.3
  69.6 5.9 %collective-permute-done.3.b4 = bf16[528,256]{1,0:T(8,128)(2,1)S(1)} collective-permute-done((bf16[528,256]{1,0:T(8,128)(2,1)S(1)}, bf16[528,256]{1,0:T(8,128)(2,1)S(1)}, u32[]{:S(2)}, u32[]{:S(2)}) %collective-permute-start.3) | collective-permute-done | bytes 270368 | tf_op jit(solution)/shard_map/ppermute | solution.py:371
  77.1 30.4 %flash.1 = bf16[4,8,136,128]{3,2,1,0:T(8,128)(2,1)} custom-call(s32[2]{0:T(128)S(1)} %pad_add_fusion.pos_ref, bf16[4,8,64,256]{3,2,1,0:T(8,128)(2,1)S(1)} %bitcast.58, bf16[528,256]{1,0:T(8,128)(2,1)S(1)} %pad_maximum_fusion.2.b0, bf16[528,256]{1,0:T(8,128)(2,1)S(1)} %collective-permute-done.b1, bf16[528,256]{1,0:T(8,128)(2,1)S(1)} %collective-permute-done.1.b2, ...), custom_call_target="tpu_custom_call" | custom-call | flops 5368709120 | bytes 5242880 | tf_op jit(solution)/shard_map/flash/pallas_call | solution.py:143
  107.5 6.5 %all-to-all-start.2 = ((bf16[32,136,128]{2,1,0:T(8,128)(2,1)}), bf16[32,136,128]{2,1,0:T(8,128)(2,1)S(1)}, u32[]{:S(2)}, u32[]{:S(2)}) async-start(bf16[32,136,128]{2,1,0:T(8,128)(2,1)} %bitcast.6), calls=%async_computation.2 | async-start | bytes 2228224 | tf_op jit(solution)/shard_map/all_to_all | solution.py:383
  114.1 4.1 %collective-permute-start.7 = (bf16[1024,384]{1,0:T(8,128)(2,1)S(1)}, bf16[1024,384]{1,0:T(8,128)(2,1)S(1)}, u32[]{:S(2)}, u32[]{:S(2)}) collective-permute-start(bf16[1024,384]{1,0:T(8,128)(2,1)S(1)} %bitcast.60), channel_id=1, source_target_pairs={{0,2},{2,0},{1,3},{3,1},{4,6},{6,4},{5,7},{7,5},{8,10},{10,8},{9,1... | collective-permute-start | bytes 2359304 | tf_op jit(solution)/shard_map/ppermute | solution.py:389
  120.2 21.3 %all-to-all-done.2 = bf16[32,136,128]{2,1,0:T(8,128)(2,1)S(1)} async-done(((bf16[32,136,128]{2,1,0:T(8,128)(2,1)}), bf16[32,136,128]{2,1,0:T(8,128)(2,1)S(1)}, u32[]{:S(2)}, u32[]{:S(2)}) %all-to-all-start.2) | async-done | bytes 1114144 | tf_op jit(solution)/shard_map/all_to_all | solution.py:383
  142.6 5.0 %merge.1 = (f32[64,1024]{1,0:T(8,128)}, bf16[4,64,1024]{2,1,0:T(8,128)(2,1)}) custom-call(bf16[4,8,136,128]{3,2,1,0:T(8,128)(2,1)} %bitcast.59, bf16[2048,1024]{1,0:T(8,128)(2,1)} %all-gather.2.cloned.1.call-done.w_ref, bf16[64,1024]{1,0:T(8,128)(2,1)} %res_ref.1, f32[1,1024]{1,0:T(1,128)} %bitcast.65), custom_call_target="tpu_custom_call" | custom-call | tf_op jit(solution)/shard_map/merge/pallas_call | solution.py:209
  148.4 12.8 %all-to-all-start.3 = ((bf16[4,64,1024]{2,1,0:T(8,128)(2,1)}), bf16[4,64,1024]{2,1,0:T(8,128)(2,1)S(1)}, u32[]{:S(2)}, u32[]{:S(2)}) async-start(bf16[4,64,1024]{2,1,0:T(8,128)(2,1)} %get-tuple-element.18), calls=%async_computation.3 | async-start | bytes 1048576 | tf_op jit(solution)/shard_map/all_to_all | solution.py:420
  163.2 9.6 %all-to-all-done.3 = bf16[4,64,1024]{2,1,0:T(8,128)(2,1)S(1)} async-done(((bf16[4,64,1024]{2,1,0:T(8,128)(2,1)}), bf16[4,64,1024]{2,1,0:T(8,128)(2,1)S(1)}, u32[]{:S(2)}, u32[]{:S(2)}) %all-to-all-start.3) | async-done | bytes 524320 | tf_op jit(solution)/shard_map/all_to_all | solution.py:420
  174.5 5.5 %all-to-all-start.4 = ((bf16[32,160,128]{2,1,0:T(8,128)(2,1)}), bf16[32,160,128]{2,1,0:T(8,128)(2,1)S(1)}, u32[]{:S(2)}, u32[]{:S(2)}) async-start(bf16[32,160,128]{2,1,0:T(8,128)(2,1)} %bitcast.21), calls=%async_computation.4 | async-start | bytes 2621440 | tf_op jit(solution)/shard_map/all_to_all | solution.py:422
  183.2 27.7 %all-to-all-done.4 = bf16[32,160,128]{2,1,0:T(8,128)(2,1)S(1)} async-done(((bf16[32,160,128]{2,1,0:T(8,128)(2,1)}), bf16[32,160,128]{2,1,0:T(8,128)(2,1)S(1)}, u32[]{:S(2)}, u32[]{:S(2)}) %all-to-all-start.4) | async-done | bytes 1310752 | tf_op jit(solution)/shard_map/all_to_all | solution.py:422
  212.0 3.6 %expert.1 = bf16[5120,128]{1,0:T(8,128)(2,1)S(1)} custom-call(bf16[5120,128]{1,0:T(8,128)(2,1)S(1)} %bitcast.53, bf16[1024,768]{1,0:T(8,128)(2,1)S(1)} %pad_maximum_fusion.win_ref, bf16[384,1024]{1,0:T(8,128)(2,1)S(1)} %copy-done.1), custom_call_target="tpu_custom_call" | custom-call | tf_op jit(solution)/shard_map/expert/pallas_call | solution.py:267
  216.8 5.2 %all-to-all-start.5 = ((bf16[32,160,128]{2,1,0:T(8,128)(2,1)}), bf16[32,160,128]{2,1,0:T(8,128)(2,1)S(1)}, u32[]{:S(2)}, u32[]{:S(2)}) async-start(bf16[32,160,128]{2,1,0:T(8,128)(2,1)} %bitcast.54), calls=%async_computation.5 | async-start | bytes 2621440 | tf_op jit(solution)/shard_map/all_to_all | solution.py:426
  223.3 28.5 %all-to-all-done.5 = bf16[32,160,128]{2,1,0:T(8,128)(2,1)S(1)} async-done(((bf16[32,160,128]{2,1,0:T(8,128)(2,1)}), bf16[32,160,128]{2,1,0:T(8,128)(2,1)S(1)}, u32[]{:S(2)}, u32[]{:S(2)}) %all-to-all-start.5) | async-done | bytes 1310752 | tf_op jit(solution)/shard_map/all_to_all | solution.py:426
  252.7 15.7 %all_to_all.35 = bf16[4,64,1024]{2,1,0:T(8,128)(2,1)S(1)} all-to-all(bf16[4,64,1024]{2,1,0:T(8,128)(2,1)S(1)} %bitcast.56), channel_id=1, replica_groups=mesh['z'=8,'x'=4,'y2'=4,'y1'=2,'dp'=2] {'y2'}, dimensions={0} | all-to-all | bytes 1048576 | tf_op jit(solution)/shard_map/all_to_all | solution.py:430
  (74 shorter events, 30.4 us)
Async XLA Ops:
  6.5 107.6 %all-gather.2.cloned.1.call-start = ((), (), s32[]{:S(2)}) async-start(), calls=%async_computation.7 | async-start | bytes 4718592 | tf_op jit(solution)/shard_map/all_gather | solution.py:380
  8.8 25.6 %all-to-all-start.1 = ((bf16[32,16,256]{2,1,0:T(8,128)(2,1)}), bf16[32,16,256]{2,1,0:T(8,128)(2,1)S(1)}, u32[]{:S(2)}, u32[]{:S(2)}) async-start(bf16[32,16,256]{2,1,0:T(8,128)(2,1)} %pack_kv.1), calls=%async_computation.1 | async-start | bytes 524288 | tf_op jit(solution)/shard_map/all_to_all | solution.py:363
  21.9 16.9 %copy-start.10 = (s32[64,8]{0,1:T(8,128)S(1)}, s32[64,8]{0,1:T(8,128)}, u32[]{:S(2)}) copy-start(s32[64,8]{0,1:T(8,128)} %param.17) | copy-start | bytes 6148
  21.9 16.9 %copy-start.11 = (s32[64,8]{0,1:T(8,128)S(1)}, s32[64,8]{0,1:T(8,128)}, u32[]{:S(2)}) copy-start(s32[64,8]{0,1:T(8,128)} %param.16) | copy-start | bytes 6148
  34.4 42.7 %all-to-all-start = ((bf16[32,64,256]{2,1,0:T(8,128)(2,1)}), bf16[32,64,256]{2,1,0:T(8,128)(2,1)S(1)}, u32[]{:S(2)}, u32[]{:S(2)}) async-start(bf16[32,64,256]{2,1,0:T(8,128)(2,1)} %pack_q.1), calls=%async_computation | async-start | bytes 2097152 | tf_op jit(solution)/shard_map/all_to_all | solution.py:376
  38.9 9.0 %collective-permute-start = (bf16[528,256]{1,0:T(8,128)(2,1)S(1)}, bf16[528,256]{1,0:T(8,128)(2,1)S(1)}, u32[]{:S(2)}, u32[]{:S(2)}) collective-permute-start(bf16[528,256]{1,0:T(8,128)(2,1)S(1)} %pad_maximum_fusion.2.b0), channel_id=1, source_target_pairs={{0,2},{2,4},{4,6},{6,8},{8,10},{10,12},{12,14},{14,0},{1,3},{3,5},... | collective-permute-start | bytes 811016 | tf_op jit(solution)/shard_map/ppermute | solution.py:371
  42.4 8.9 %collective-permute-start.4 = (bf16[528,256]{1,0:T(8,128)(2,1)S(1)}, bf16[528,256]{1,0:T(8,128)(2,1)S(1)}, u32[]{:S(2)}, u32[]{:S(2)}) collective-permute-start(bf16[528,256]{1,0:T(8,128)(2,1)S(1)} %pad_maximum_fusion.2.b0), channel_id=1, source_target_pairs={{0,14},{2,0},{4,2},{6,4},{8,6},{10,8},{12,10},{14,12},{1,15},{3,1}... | collective-permute-start | bytes 811016 | tf_op jit(solution)/shard_map/ppermute | solution.py:373
  47.8 8.9 %collective-permute-start.1 = (bf16[528,256]{1,0:T(8,128)(2,1)S(1)}, bf16[528,256]{1,0:T(8,128)(2,1)S(1)}, u32[]{:S(2)}, u32[]{:S(2)}) collective-permute-start(bf16[528,256]{1,0:T(8,128)(2,1)S(1)} %collective-permute-done.b1), channel_id=1, source_target_pairs={{0,2},{2,4},{4,6},{6,8},{8,10},{10,12},{12,14},{14,0},{1,3},{3,5},... | collective-permute-start | bytes 811016 | tf_op jit(solution)/shard_map/ppermute | solution.py:371
  51.3 8.7 %collective-permute-start.5 = (bf16[528,256]{1,0:T(8,128)(2,1)S(1)}, bf16[528,256]{1,0:T(8,128)(2,1)S(1)}, u32[]{:S(2)}, u32[]{:S(2)}) collective-permute-start(bf16[528,256]{1,0:T(8,128)(2,1)S(1)} %collective-permute-done.4.b5), channel_id=1, source_target_pairs={{0,14},{2,0},{4,2},{6,4},{8,6},{10,8},{12,10},{14,12},{1,15},{3,1}... | collective-permute-start | bytes 811016 | tf_op jit(solution)/shard_map/ppermute | solution.py:373
  56.7 9.3 %collective-permute-start.2 = (bf16[528,256]{1,0:T(8,128)(2,1)S(1)}, bf16[528,256]{1,0:T(8,128)(2,1)S(1)}, u32[]{:S(2)}, u32[]{:S(2)}) collective-permute-start(bf16[528,256]{1,0:T(8,128)(2,1)S(1)} %collective-permute-done.1.b2), channel_id=1, source_target_pairs={{0,2},{2,4},{4,6},{6,8},{8,10},{10,12},{12,14},{14,0},{1,3},{3,5},... | collective-permute-start | bytes 811016 | tf_op jit(solution)/shard_map/ppermute | solution.py:371
  60.1 9.5 %collective-permute-start.6 = (bf16[528,256]{1,0:T(8,128)(2,1)S(1)}, bf16[528,256]{1,0:T(8,128)(2,1)S(1)}, u32[]{:S(2)}, u32[]{:S(2)}) collective-permute-start(bf16[528,256]{1,0:T(8,128)(2,1)S(1)} %collective-permute-done.5.b6), channel_id=1, source_target_pairs={{0,14},{2,0},{4,2},{6,4},{8,6},{10,8},{12,10},{14,12},{1,15},{3,1}... | collective-permute-start | bytes 811016 | tf_op jit(solution)/shard_map/ppermute | solution.py:373
  66.0 9.6 %collective-permute-start.3 = (bf16[528,256]{1,0:T(8,128)(2,1)S(1)}, bf16[528,256]{1,0:T(8,128)(2,1)S(1)}, u32[]{:S(2)}, u32[]{:S(2)}) collective-permute-start(bf16[528,256]{1,0:T(8,128)(2,1)S(1)} %collective-permute-done.2.b3), channel_id=1, source_target_pairs={{0,2},{2,4},{4,6},{6,8},{8,10},{10,12},{12,14},{14,0},{1,3},{3,5},... | collective-permute-start | bytes 811016 | tf_op jit(solution)/shard_map/ppermute | solution.py:371
  107.5 6.6 %copy-start.3 = (bf16[1,1024,384]{2,1,0:T(8,128)(2,1)S(1)}, bf16[1,1024,384]{2,1,0:T(8,128)(2,1)}, u32[]{:S(2)}) copy-start(bf16[1,1024,384]{2,1,0:T(8,128)(2,1)} %param.18) | copy-start | bytes 2359300
  107.5 34.1 %all-to-all-start.2 = ((bf16[32,136,128]{2,1,0:T(8,128)(2,1)}), bf16[32,136,128]{2,1,0:T(8,128)(2,1)S(1)}, u32[]{:S(2)}, u32[]{:S(2)}) async-start(bf16[32,136,128]{2,1,0:T(8,128)(2,1)} %bitcast.6), calls=%async_computation.2 | async-start | bytes 2228224 | tf_op jit(solution)/shard_map/all_to_all | solution.py:383
  114.1 33.6 %collective-permute-start.7 = (bf16[1024,384]{1,0:T(8,128)(2,1)S(1)}, bf16[1024,384]{1,0:T(8,128)(2,1)S(1)}, u32[]{:S(2)}, u32[]{:S(2)}) collective-permute-start(bf16[1024,384]{1,0:T(8,128)(2,1)S(1)} %bitcast.60), channel_id=1, source_target_pairs={{0,2},{2,0},{1,3},{3,1},{4,6},{6,4},{5,7},{7,5},{8,10},{10,8},{9,1... | collective-permute-start | bytes 2359304 | tf_op jit(solution)/shard_map/ppermute | solution.py:389
  118.3 29.4 %collective-permute-start.8 = (bf16[192,1024]{1,0:T(8,128)(2,1)}, bf16[192,1024]{1,0:T(8,128)(2,1)S(1)}, u32[]{:S(2)}, u32[]{:S(2)}) collective-permute-start(bf16[192,1024]{1,0:T(8,128)(2,1)} %bitcast.63), channel_id=1, source_target_pairs={{0,2},{2,0},{1,3},{3,1},{4,6},{6,4},{5,7},{7,5},{8,10},{10,8},{9,1... | collective-permute-start | bytes 1179656 | tf_op jit(solution)/shard_map/ppermute | solution.py:390
  148.4 24.3 %all-to-all-start.3 = ((bf16[4,64,1024]{2,1,0:T(8,128)(2,1)}), bf16[4,64,1024]{2,1,0:T(8,128)(2,1)S(1)}, u32[]{:S(2)}, u32[]{:S(2)}) async-start(bf16[4,64,1024]{2,1,0:T(8,128)(2,1)} %get-tuple-element.18), calls=%async_computation.3 | async-start | bytes 1048576 | tf_op jit(solution)/shard_map/all_to_all | solution.py:420
  174.5 36.3 %all-to-all-start.4 = ((bf16[32,160,128]{2,1,0:T(8,128)(2,1)}), bf16[32,160,128]{2,1,0:T(8,128)(2,1)S(1)}, u32[]{:S(2)}, u32[]{:S(2)}) async-start(bf16[32,160,128]{2,1,0:T(8,128)(2,1)} %bitcast.21), calls=%async_computation.4 | async-start | bytes 2621440 | tf_op jit(solution)/shard_map/all_to_all | solution.py:422
  180.1 1.1 copy-start.8
  210.9 1.1 copy-start.1
  215.7 1.1 copy-start
  216.8 5.5 %copy-start.5 = (pred[32,5,4,64]{3,2,1,0:T(4,128)(4,1)S(1)}, pred[32,5,4,64]{3,2,1,0:T(4,128)(4,1)}, u32[]{:S(2)}) copy-start(pred[32,5,4,64]{3,2,1,0:T(4,128)(4,1)} %copy-done.4) | copy-start | bytes 122884
  216.8 35.1 %all-to-all-start.5 = ((bf16[32,160,128]{2,1,0:T(8,128)(2,1)}), bf16[32,160,128]{2,1,0:T(8,128)(2,1)S(1)}, u32[]{:S(2)}, u32[]{:S(2)}) async-start(bf16[32,160,128]{2,1,0:T(8,128)(2,1)} %bitcast.54), calls=%async_computation.5 | async-start | bytes 2621440 | tf_op jit(solution)/shard_map/all_to_all | solution.py:426
  251.9 16.6 %copy-start.9 = (f32[64,1024]{1,0:T(8,128)S(1)}, f32[64,1024]{1,0:T(8,128)}, u32[]{:S(2)}) copy-start(f32[64,1024]{1,0:T(8,128)} %get-tuple-element.14) | copy-start | bytes 786436
  (4 other events, 3.4 us)
Sparse Core Ops, SparseCore 0:
  9.4 85.3 all-gather.1

commit v8 on v7

--- a/solution.py
+++ b/solution.py
@@ -135,8 +135,8 @@
     stats = jnp.where(pick == 0, first, jnp.where(pick == 1, second, jnp.where(pick == 2, third, 0.0)))
     stats = stats.astype(BF)
     for i in range(8):
-        o_ref[0, i, 0:HD, :] = out[:, i * 128 : (i + 1) * 128]
-        o_ref[0, i, HD : HD + STAT, :] = stats[:, i * 128 : (i + 1) * 128]
+        o_ref[i, 0, 0:HD, :] = out[:, i * 128 : (i + 1) * 128]
+        o_ref[i, 0, HD : HD + STAT, :] = stats[:, i * 128 : (i + 1) * 128]
 
 
 def flash(position, queries, key_values):
@@ -149,7 +149,7 @@
                 pl.BlockSpec((1, 8, 64, 256), lambda i, s: (i, 0, 0, 0)),
             ]
             + [pl.BlockSpec(block.shape, lambda i, s: (0, 0)) for block in key_values],
-            out_specs=pl.BlockSpec((1, 8, HD + STAT, 128), lambda i, s: (i, 0, 0, 0)),
+            out_specs=pl.BlockSpec((8, 1, HD + STAT, 128), lambda i, s: (0, i, 0, 0)),
             scratch_shapes=[
                 pltpu.VMEM((8, 4, 128, 2 * HD), BF),
                 pltpu.VMEM((8, HD + 16, 512), BF),
@@ -159,7 +159,7 @@
                 pltpu.VMEM((8, 1024), F32),
             ],
         ),
-        out_shape=jax.ShapeDtypeStruct((4, 8, HD + STAT, 128), BF),
+        out_shape=jax.ShapeDtypeStruct((8, 4, HD + STAT, 128), BF),
         compiler_params=pltpu.CompilerParams(vmem_limit_bytes=40 * 1024 * 1024),
         cost_estimate=pl.CostEstimate(
             flops=4 * 4096 * 2560 * HD, bytes_accessed=5 << 20, transcendentals=4096 * 2560
@@ -174,14 +174,14 @@
     for c in range(2):
         levels = []
         for x in range(4):
-            st = parts_ref[x, c, HD : HD + STAT, :].astype(F32)
+            st = parts_ref[c, x, HD : HD + STAT, :].astype(F32)
             levels.append(st[0:1] + st[1:2] + st[2:3])
         top = jnp.maximum(jnp.maximum(levels[0], levels[1]), jnp.maximum(levels[2], levels[3]))
         shares = [jnp.exp2(level - top) for level in levels]
         inverse = 1.0 / (shares[0] + shares[1] + shares[2] + shares[3])
-        mixed = parts_ref[0, c, 0:HD, :].astype(F32) * (shares[0] * inverse)
+        mixed = parts_ref[c, 0, 0:HD, :].astype(F32) * (shares[0] * inverse)
         for x in range(1, 4):
-            mixed = mixed + parts_ref[x, c, 0:HD, :].astype(F32) * (shares[x] * inverse)
+            mixed = mixed + parts_ref[c, x, 0:HD, :].astype(F32) * (shares[x] * inverse)
         rows = mixed.T.astype(BF)
         found += [rows[0:64], rows[64:128]]
     part = jnp.dot(jnp.concatenate(found, axis=1), w_ref[...], preferred_element_type=F32)
@@ -210,7 +210,7 @@
         merge_kernel,
         grid=(4,),
         in_specs=[
-            pl.BlockSpec((4, 2, HD + STAT, 128), lambda c: (0, c, 0, 0)),
+            pl.BlockSpec((2, 4, HD + STAT, 128), lambda c: (c, 0, 0, 0)),
             pl.BlockSpec((512, width), lambda c: (c, 0)),
             whole,
             pl.BlockSpec((1, width), lambda c: (0, 0)),
@@ -381,12 +381,9 @@
 
     shards = flash(position, query, key_values)
     parts = lax.all_to_all(
-        shards.reshape(32, HD + STAT, 128), ("x", "z"), split_axis=0, concat_axis=0, tiled=True
-    ).reshape(4, 8, HD + STAT, 128)
-    whole_weight, own_in, own_out = lax.optimization_barrier(
-        (whole_weight, expert_in[0], expert_out[0])
-    )
-    other_in = lax.ppermute(own_in, "y1", SWAP)
+        shards.reshape(32, HD + STAT, 128), ("z", "x"), split_axis=0, concat_axis=0, tiled=True
+    ).reshape(8, 4, HD + STAT, 128)
+    whole_weight, own_out = lax.optimization_barrier((whole_weight, expert_out[0]))
     other_out = lax.ppermute(own_out, "y1", SWAP)
     turned = [ups[0][512:], ups[2][512:], ups[4][512:], downs[2][512:]]
     listing = lax.dynamic_slice_in_dim(
@@ -394,7 +391,7 @@
     ).astype(jnp.int32)
     named, levels = listing[:, None, 0:8], listing[:, None, 8:16]
     q = jnp.arange(32, dtype=jnp.int32)
-    match = named == ((q % 8) * 16 + (q // 8) * 4 + own_y2)[None, :, None, None]
+    match = named == ((q // 4) * 16 + (q % 4) * 4 + own_y2)[None, :, None, None]
     hits = jnp.any(match, axis=2)
     gates = jnp.sum(jnp.where(match, levels, 0), axis=2).astype(F32) / 256.0
     before = jnp.triu(jnp.ones((tokens, tokens), BF), 1)
@@ -411,20 +408,22 @@
         parts, whole_weight, residual, norm_gain.reshape(1, width)
     )
 
-    spread, other_in, other_out = lax.optimization_barrier((spread, other_in, other_out))
+    spread, other_out = lax.optimization_barrier((spread, other_out))
+    spread = lax.all_to_all(spread, "y2", split_axis=0, concat_axis=0, tiled=True)
+    outgoing = select(chosen, spread.reshape(4 * tokens, width))
+    outgoing, own_in = lax.optimization_barrier((outgoing, expert_in[0]))
+    other_in = lax.ppermute(own_in, "y1", SWAP)
     half = own_in.shape[1] // 2
     weight_in = jnp.concatenate(
         [own_in[:, :half], other_in[:, :half], own_in[:, half:], other_in[:, half:]], axis=1
     )
     weight_out = jnp.concatenate([own_out, other_out], axis=0)
-    spread = lax.all_to_all(spread, "y2", split_axis=0, concat_axis=0, tiled=True)
-    outgoing = select(chosen, spread.reshape(4 * tokens, width))
     arrived = lax.all_to_all(
-        outgoing.reshape(32, 4 * CAP * 8, 128), ("x", "z"), split_axis=0, concat_axis=0, tiled=True
+        outgoing.reshape(32, 4 * CAP * 8, 128), ("z", "x"), split_axis=0, concat_axis=0, tiled=True
     )
     done = expert(arrived.reshape(-1, 128), weight_in, weight_out)
     answers = lax.all_to_all(
-        done.reshape(32, 4 * CAP * 8, 128), ("x", "z"), split_axis=0, concat_axis=0, tiled=True
+        done.reshape(32, 4 * CAP * 8, 128), ("z", "x"), split_axis=0, concat_axis=0, tiled=True
     )
     sums = gather(shares, answers.reshape(-1, 128))
     sums = lax.all_to_all(

time: 277 us -> 279 us (level)
  the two profiles are of different devices: /device:TPU:8 before, /device:TPU:4 now
where the time goes in v8:
time: 279 us; the launch traced here: 278 us
  waiting for transfers between devices  109 us (39%)
  starting transfers between devices  96.1 us (34%)
  Pallas kernels  29.1 us (10%)
  blocking collectives  19.2 us (7%)
  between operations  13.8 us (5%)
  local copies, waits for them, and re-layouts  5.72 us (2%)
  other arithmetic  4.08 us (1%)
    all_to_all x1, waiting for transfers between devices, local(): lax.all_to_all(done.reshape(32, 4 * CAP * 8, 128), ('z', 'x'), split_axis...  26.7 us
    all_to_all x1, starting transfers between devices, local(): lax.all_to_all(shards.reshape(32, HD + STAT, 128), ('z', 'x'), split_axis...  23.6 us
    all_to_all x1, waiting for transfers between devices, local(): lax.all_to_all(shards.reshape(32, HD + STAT, 128), ('z', 'x'), split_axis...  23.1 us
    all_to_all x1, blocking collectives, local(): lax.all_to_all(sums.reshape(4, tokens, width), 'y2', split_axis=0, concat...  19.2 us
    ppermute x4, waiting for transfers between devices, local(): ups.append(lax.ppermute(ups[-1], ('y2', 'y1'), up))  15.6 us
    pallas_call x1, Pallas kernels, flash(): pl.pallas_call(flash_kernel, grid_spec=pltpu.PrefetchScalarGridSpec(num_s...  14.3 us
    ppermute x3, starting transfers between devices, local(): downs.append(lax.ppermute(downs[-1], ('y2', 'y1'), down))  14.1 us
    all_to_all x1, starting transfers between devices, local(): lax.all_to_all(spread, 'y2', split_axis=0, concat_axis=0, tiled=True)  13.9 us
  transfers between devices with their start and end apart: 16, of which 10 were waited for; matrix products, arithmetic and copies ran while one was open for 2% of the time, Pallas kernels for 8%

profile of v8, /device:TPU:4, one launch (start us, length us, event | category | flops | bytes accessed | tf_op | source)
XLA Modules:
  0.0 277.6 jit_solution(7034871441890263683)
XLA Ops:
  8.8 13.4 %all-to-all-start.1 = ((bf16[32,16,256]{2,1,0:T(8,128)(2,1)}), bf16[32,16,256]{2,1,0:T(8,128)(2,1)S(1)}, u32[]{:S(2)}, u32[]{:S(2)}) async-start(bf16[32,16,256]{2,1,0:T(8,128)(2,1)} %pack_kv.1), calls=%async_computation.1 | async-start | bytes 524288 | tf_op jit(solution)/shard_map/all_to_all | solution.py:363
  24.3 8.6 %all-to-all-done.1 = bf16[32,16,256]{2,1,0:T(8,128)(2,1)S(1)} async-done(((bf16[32,16,256]{2,1,0:T(8,128)(2,1)}), bf16[32,16,256]{2,1,0:T(8,128)(2,1)S(1)}, u32[]{:S(2)}, u32[]{:S(2)}) %all-to-all-start.1) | async-done | bytes 262176 | tf_op jit(solution)/shard_map/all_to_all | solution.py:363
  32.8 6.2 %all-to-all-start = ((bf16[32,64,256]{2,1,0:T(8,128)(2,1)}), bf16[32,64,256]{2,1,0:T(8,128)(2,1)S(1)}, u32[]{:S(2)}, u32[]{:S(2)}) async-start(bf16[32,64,256]{2,1,0:T(8,128)(2,1)} %pack_q.1), calls=%async_computation | async-start | bytes 2097152 | tf_op jit(solution)/shard_map/all_to_all | solution.py:376
  39.2 3.5 %collective-permute-start = (bf16[528,256]{1,0:T(8,128)(2,1)S(1)}, bf16[528,256]{1,0:T(8,128)(2,1)S(1)}, u32[]{:S(2)}, u32[]{:S(2)}) collective-permute-start(bf16[528,256]{1,0:T(8,128)(2,1)S(1)} %pad_maximum_fusion.2.b0), channel_id=1, source_target_pairs={{0,2},{2,4},{4,6},{6,8},{8,10},{10,12},{12,14},{14,0},{1,3},{3,5},... | collective-permute-start | bytes 811016 | tf_op jit(solution)/shard_map/ppermute | solution.py:371
  42.6 3.8 %collective-permute-start.4 = (bf16[528,256]{1,0:T(8,128)(2,1)S(1)}, bf16[528,256]{1,0:T(8,128)(2,1)S(1)}, u32[]{:S(2)}, u32[]{:S(2)}) collective-permute-start(bf16[528,256]{1,0:T(8,128)(2,1)S(1)} %pad_maximum_fusion.2.b0), channel_id=1, source_target_pairs={{0,14},{2,0},{4,2},{6,4},{8,6},{10,8},{12,10},{14,12},{1,15},{3,1}... | collective-permute-start | bytes 811016 | tf_op jit(solution)/shard_map/ppermute | solution.py:373
  46.5 3.1 %collective-permute-done.b1 = bf16[528,256]{1,0:T(8,128)(2,1)S(1)} collective-permute-done((bf16[528,256]{1,0:T(8,128)(2,1)S(1)}, bf16[528,256]{1,0:T(8,128)(2,1)S(1)}, u32[]{:S(2)}, u32[]{:S(2)}) %collective-permute-start) | collective-permute-done | bytes 270368 | tf_op jit(solution)/shard_map/ppermute | solution.py:371
  51.5 5.1 %collective-permute-start.5 = (bf16[528,256]{1,0:T(8,128)(2,1)S(1)}, bf16[528,256]{1,0:T(8,128)(2,1)S(1)}, u32[]{:S(2)}, u32[]{:S(2)}) collective-permute-start(bf16[528,256]{1,0:T(8,128)(2,1)S(1)} %collective-permute-done.4.b5), channel_id=1, source_target_pairs={{0,14},{2,0},{4,2},{6,4},{8,6},{10,8},{12,10},{14,12},{1,15},{3,1}... | collective-permute-start | bytes 811016 | tf_op jit(solution)/shard_map/ppermute | solution.py:373
  56.6 2.5 collective-permute-done.1.b2
  61.0 5.1 %collective-permute-start.6 = (bf16[528,256]{1,0:T(8,128)(2,1)S(1)}, bf16[528,256]{1,0:T(8,128)(2,1)S(1)}, u32[]{:S(2)}, u32[]{:S(2)}) collective-permute-start(bf16[528,256]{1,0:T(8,128)(2,1)S(1)} %collective-permute-done.5.b6), channel_id=1, source_target_pairs={{0,14},{2,0},{4,2},{6,4},{8,6},{10,8},{12,10},{14,12},{1,15},{3,1}... | collective-permute-start | bytes 811016 | tf_op jit(solution)/shard_map/ppermute | solution.py:373
  66.2 2.5 collective-permute-done.2.b3
  70.7 7.5 %collective-permute-done.3.b4 = bf16[528,256]{1,0:T(8,128)(2,1)S(1)} collective-permute-done((bf16[528,256]{1,0:T(8,128)(2,1)S(1)}, bf16[528,256]{1,0:T(8,128)(2,1)S(1)}, u32[]{:S(2)}, u32[]{:S(2)}) %collective-permute-start.3) | collective-permute-done | bytes 270368 | tf_op jit(solution)/shard_map/ppermute | solution.py:371
  78.2 14.3 %flash.1 = bf16[8,4,136,128]{3,2,1,0:T(8,128)(2,1)} custom-call(s32[2]{0:T(128)S(1)} %pad_add_fusion.pos_ref, bf16[4,8,64,256]{3,2,1,0:T(8,128)(2,1)S(1)} %bitcast.58, bf16[528,256]{1,0:T(8,128)(2,1)S(1)} %pad_maximum_fusion.2.b0, bf16[528,256]{1,0:T(8,128)(2,1)S(1)} %collective-permute-done.b1, bf16[528,256]{1,0:T(8,128)(2,1)S(1)} %collective-permute-done.1.b2, ...), custom_call_target="tpu_custom_call" | custom-call | flops 5368709120 | bytes 5242880 | tf_op jit(solution)/shard_map/flash/pallas_call | solution.py:143
  92.5 23.6 %all-to-all-start.2 = ((bf16[32,136,128]{2,1,0:T(8,128)(2,1)}), bf16[32,136,128]{2,1,0:T(8,128)(2,1)S(1)}, u32[]{:S(2)}, u32[]{:S(2)}) async-start(bf16[32,136,128]{2,1,0:T(8,128)(2,1)} %bitcast.6), calls=%async_computation.2 | async-start | bytes 2228224 | tf_op jit(solution)/shard_map/all_to_all | solution.py:383
  118.2 23.1 %all-to-all-done.2 = bf16[32,136,128]{2,1,0:T(8,128)(2,1)S(1)} async-done(((bf16[32,136,128]{2,1,0:T(8,128)(2,1)}), bf16[32,136,128]{2,1,0:T(8,128)(2,1)S(1)}, u32[]{:S(2)}, u32[]{:S(2)}) %all-to-all-start.2) | async-done | bytes 1114144 | tf_op jit(solution)/shard_map/all_to_all | solution.py:383
  142.4 5.0 %merge.1 = (f32[64,1024]{1,0:T(8,128)}, bf16[4,64,1024]{2,1,0:T(8,128)(2,1)}) custom-call(bf16[8,4,136,128]{3,2,1,0:T(8,128)(2,1)} %bitcast.59, bf16[2048,1024]{1,0:T(8,128)(2,1)} %all-gather.2.cloned.1.call-done.w_ref, bf16[64,1024]{1,0:T(8,128)(2,1)} %res_ref.1, f32[1,1024]{1,0:T(1,128)} %bitcast.65), custom_call_target="tpu_custom_call" | custom-call | tf_op jit(solution)/shard_map/merge/pallas_call | solution.py:209
  148.2 13.9 %all-to-all-start.3 = ((bf16[4,64,1024]{2,1,0:T(8,128)(2,1)}), bf16[4,64,1024]{2,1,0:T(8,128)(2,1)S(1)}, u32[]{:S(2)}, u32[]{:S(2)}) async-start(bf16[4,64,1024]{2,1,0:T(8,128)(2,1)} %get-tuple-element.17), calls=%async_computation.3 | async-start | bytes 1048576 | tf_op jit(solution)/shard_map/all_to_all | solution.py:412
  163.4 11.1 %all-to-all-done.3 = bf16[4,64,1024]{2,1,0:T(8,128)(2,1)S(1)} async-done(((bf16[4,64,1024]{2,1,0:T(8,128)(2,1)}), bf16[4,64,1024]{2,1,0:T(8,128)(2,1)S(1)}, u32[]{:S(2)}, u32[]{:S(2)}) %all-to-all-start.3) | async-done | bytes 524320 | tf_op jit(solution)/shard_map/all_to_all | solution.py:412
  176.3 6.0 %all-to-all-start.4 = ((bf16[32,160,128]{2,1,0:T(8,128)(2,1)}), bf16[32,160,128]{2,1,0:T(8,128)(2,1)S(1)}, u32[]{:S(2)}, u32[]{:S(2)}) async-start(bf16[32,160,128]{2,1,0:T(8,128)(2,1)} %bitcast.21), calls=%async_computation.4 | async-start | bytes 2621440 | tf_op jit(solution)/shard_map/all_to_all | solution.py:421
  185.8 11.8 %collective-permute-done.8 = bf16[1024,384]{1,0:T(8,128)(2,1)S(1)} collective-permute-done((bf16[1024,384]{1,0:T(8,128)(2,1)S(1)}, bf16[1024,384]{1,0:T(8,128)(2,1)S(1)}, u32[]{:S(2)}, u32[]{:S(2)}) %collective-permute-start.8) | collective-permute-done | bytes 786464 | tf_op jit(solution)/shard_map/ppermute | solution.py:415
  198.6 11.6 %all-to-all-done.4 = bf16[32,160,128]{2,1,0:T(8,128)(2,1)S(1)} async-done(((bf16[32,160,128]{2,1,0:T(8,128)(2,1)}), bf16[32,160,128]{2,1,0:T(8,128)(2,1)S(1)}, u32[]{:S(2)}, u32[]{:S(2)}) %all-to-all-start.4) | async-done | bytes 1310752 | tf_op jit(solution)/shard_map/all_to_all | solution.py:421
  211.4 3.6 %expert.1 = bf16[5120,128]{1,0:T(8,128)(2,1)S(1)} custom-call(bf16[5120,128]{1,0:T(8,128)(2,1)S(1)} %bitcast.53, bf16[1024,768]{1,0:T(8,128)(2,1)S(1)} %pad_maximum_fusion.win_ref, bf16[384,1024]{1,0:T(8,128)(2,1)S(1)} %copy-done.1), custom_call_target="tpu_custom_call" | custom-call | tf_op jit(solution)/shard_map/expert/pallas_call | solution.py:267
  216.2 5.6 %all-to-all-start.5 = ((bf16[32,160,128]{2,1,0:T(8,128)(2,1)}), bf16[32,160,128]{2,1,0:T(8,128)(2,1)S(1)}, u32[]{:S(2)}, u32[]{:S(2)}) async-start(bf16[32,160,128]{2,1,0:T(8,128)(2,1)} %bitcast.54), calls=%async_computation.5 | async-start | bytes 2621440 | tf_op jit(solution)/shard_map/all_to_all | solution.py:425
  223.1 26.7 %all-to-all-done.5 = bf16[32,160,128]{2,1,0:T(8,128)(2,1)S(1)} async-done(((bf16[32,160,128]{2,1,0:T(8,128)(2,1)}), bf16[32,160,128]{2,1,0:T(8,128)(2,1)S(1)}, u32[]{:S(2)}, u32[]{:S(2)}) %all-to-all-start.5) | async-done | bytes 1310752 | tf_op jit(solution)/shard_map/all_to_all | solution.py:425
  250.6 19.2 %all_to_all.35 = bf16[4,64,1024]{2,1,0:T(8,128)(2,1)S(1)} all-to-all(bf16[4,64,1024]{2,1,0:T(8,128)(2,1)S(1)} %bitcast.56), channel_id=1, replica_groups=mesh['z'=8,'x'=4,'y2'=4,'y1'=2,'dp'=2] {'y2'}, dimensions={0} | all-to-all | bytes 1048576 | tf_op jit(solution)/shard_map/all_to_all | solution.py:429
  (70 shorter events, 26.7 us)
Async XLA Ops:
  6.5 109.6 %all-gather.2.cloned.1.call-start = ((), (), s32[]{:S(2)}) async-start(), calls=%async_computation.7 | async-start | bytes 4718592 | tf_op jit(solution)/shard_map/all_gather | solution.py:380
  8.8 24.1 %all-to-all-start.1 = ((bf16[32,16,256]{2,1,0:T(8,128)(2,1)}), bf16[32,16,256]{2,1,0:T(8,128)(2,1)S(1)}, u32[]{:S(2)}, u32[]{:S(2)}) async-start(bf16[32,16,256]{2,1,0:T(8,128)(2,1)} %pack_kv.1), calls=%async_computation.1 | async-start | bytes 524288 | tf_op jit(solution)/shard_map/all_to_all | solution.py:363
  22.2 16.9 %copy-start.8 = (s32[64,8]{0,1:T(8,128)S(1)}, s32[64,8]{0,1:T(8,128)}, u32[]{:S(2)}) copy-start(s32[64,8]{0,1:T(8,128)} %param.17) | copy-start | bytes 6148
  22.2 16.9 %copy-start.9 = (s32[64,8]{0,1:T(8,128)S(1)}, s32[64,8]{0,1:T(8,128)}, u32[]{:S(2)}) copy-start(s32[64,8]{0,1:T(8,128)} %param.16) | copy-start | bytes 6148
  32.8 45.4 %all-to-all-start = ((bf16[32,64,256]{2,1,0:T(8,128)(2,1)}), bf16[32,64,256]{2,1,0:T(8,128)(2,1)S(1)}, u32[]{:S(2)}, u32[]{:S(2)}) async-start(bf16[32,64,256]{2,1,0:T(8,128)(2,1)} %pack_q.1), calls=%async_computation | async-start | bytes 2097152 | tf_op jit(solution)/shard_map/all_to_all | solution.py:376
  39.2 10.4 %collective-permute-start = (bf16[528,256]{1,0:T(8,128)(2,1)S(1)}, bf16[528,256]{1,0:T(8,128)(2,1)S(1)}, u32[]{:S(2)}, u32[]{:S(2)}) collective-permute-start(bf16[528,256]{1,0:T(8,128)(2,1)S(1)} %pad_maximum_fusion.2.b0), channel_id=1, source_target_pairs={{0,2},{2,4},{4,6},{6,8},{8,10},{10,12},{12,14},{14,0},{1,3},{3,5},... | collective-permute-start | bytes 811016 | tf_op jit(solution)/shard_map/ppermute | solution.py:371
  42.6 8.8 %collective-permute-start.4 = (bf16[528,256]{1,0:T(8,128)(2,1)S(1)}, bf16[528,256]{1,0:T(8,128)(2,1)S(1)}, u32[]{:S(2)}, u32[]{:S(2)}) collective-permute-start(bf16[528,256]{1,0:T(8,128)(2,1)S(1)} %pad_maximum_fusion.2.b0), channel_id=1, source_target_pairs={{0,14},{2,0},{4,2},{6,4},{8,6},{10,8},{12,10},{14,12},{1,15},{3,1}... | collective-permute-start | bytes 811016 | tf_op jit(solution)/shard_map/ppermute | solution.py:373
  49.6 9.6 %collective-permute-start.1 = (bf16[528,256]{1,0:T(8,128)(2,1)S(1)}, bf16[528,256]{1,0:T(8,128)(2,1)S(1)}, u32[]{:S(2)}, u32[]{:S(2)}) collective-permute-start(bf16[528,256]{1,0:T(8,128)(2,1)S(1)} %collective-permute-done.b1), channel_id=1, source_target_pairs={{0,2},{2,4},{4,6},{6,8},{8,10},{10,12},{12,14},{14,0},{1,3},{3,5},... | collective-permute-start | bytes 811016 | tf_op jit(solution)/shard_map/ppermute | solution.py:371
  51.5 9.5 %collective-permute-start.5 = (bf16[528,256]{1,0:T(8,128)(2,1)S(1)}, bf16[528,256]{1,0:T(8,128)(2,1)S(1)}, u32[]{:S(2)}, u32[]{:S(2)}) collective-permute-start(bf16[528,256]{1,0:T(8,128)(2,1)S(1)} %collective-permute-done.4.b5), channel_id=1, source_target_pairs={{0,14},{2,0},{4,2},{6,4},{8,6},{10,8},{12,10},{14,12},{1,15},{3,1}... | collective-permute-start | bytes 811016 | tf_op jit(solution)/shard_map/ppermute | solution.py:373
  59.1 9.6 %collective-permute-start.2 = (bf16[528,256]{1,0:T(8,128)(2,1)S(1)}, bf16[528,256]{1,0:T(8,128)(2,1)S(1)}, u32[]{:S(2)}, u32[]{:S(2)}) collective-permute-start(bf16[528,256]{1,0:T(8,128)(2,1)S(1)} %collective-permute-done.1.b2), channel_id=1, source_target_pairs={{0,2},{2,4},{4,6},{6,8},{8,10},{10,12},{12,14},{14,0},{1,3},{3,5},... | collective-permute-start | bytes 811016 | tf_op jit(solution)/shard_map/ppermute | solution.py:371
  61.0 9.6 %collective-permute-start.6 = (bf16[528,256]{1,0:T(8,128)(2,1)S(1)}, bf16[528,256]{1,0:T(8,128)(2,1)S(1)}, u32[]{:S(2)}, u32[]{:S(2)}) collective-permute-start(bf16[528,256]{1,0:T(8,128)(2,1)S(1)} %collective-permute-done.5.b6), channel_id=1, source_target_pairs={{0,14},{2,0},{4,2},{6,4},{8,6},{10,8},{12,10},{14,12},{1,15},{3,1}... | collective-permute-start | bytes 811016 | tf_op jit(solution)/shard_map/ppermute | solution.py:373
  68.7 9.6 %collective-permute-start.3 = (bf16[528,256]{1,0:T(8,128)(2,1)S(1)}, bf16[528,256]{1,0:T(8,128)(2,1)S(1)}, u32[]{:S(2)}, u32[]{:S(2)}) collective-permute-start(bf16[528,256]{1,0:T(8,128)(2,1)S(1)} %collective-permute-done.2.b3), channel_id=1, source_target_pairs={{0,2},{2,4},{4,6},{6,8},{8,10},{10,12},{12,14},{14,0},{1,3},{3,5},... | collective-permute-start | bytes 811016 | tf_op jit(solution)/shard_map/ppermute | solution.py:371
  92.5 23.7 %copy-start.4 = (bf16[1,192,1024]{2,1,0:T(8,128)(2,1)S(1)}, bf16[1,192,1024]{2,1,0:T(8,128)(2,1)}, u32[]{:S(2)}) copy-start(bf16[1,192,1024]{2,1,0:T(8,128)(2,1)} %param.19) | copy-start | bytes 1179652
  92.5 48.8 %all-to-all-start.2 = ((bf16[32,136,128]{2,1,0:T(8,128)(2,1)}), bf16[32,136,128]{2,1,0:T(8,128)(2,1)S(1)}, u32[]{:S(2)}, u32[]{:S(2)}) async-start(bf16[32,136,128]{2,1,0:T(8,128)(2,1)} %bitcast.6), calls=%async_computation.2 | async-start | bytes 2228224 | tf_op jit(solution)/shard_map/all_to_all | solution.py:383
  116.2 31.2 %collective-permute-start.7 = (bf16[192,1024]{1,0:T(8,128)(2,1)S(1)}, bf16[192,1024]{1,0:T(8,128)(2,1)S(1)}, u32[]{:S(2)}, u32[]{:S(2)}) collective-permute-start(bf16[192,1024]{1,0:T(8,128)(2,1)S(1)} %bitcast.63), channel_id=1, source_target_pairs={{0,2},{2,0},{1,3},{3,1},{4,6},{6,4},{5,7},{7,5},{8,10},{10,8},{9,1... | collective-permute-start | bytes 1179656 | tf_op jit(solution)/shard_map/ppermute | solution.py:387
  148.2 26.3 %all-to-all-start.3 = ((bf16[4,64,1024]{2,1,0:T(8,128)(2,1)}), bf16[4,64,1024]{2,1,0:T(8,128)(2,1)S(1)}, u32[]{:S(2)}, u32[]{:S(2)}) async-start(bf16[4,64,1024]{2,1,0:T(8,128)(2,1)} %get-tuple-element.17), calls=%async_computation.3 | async-start | bytes 1048576 | tf_op jit(solution)/shard_map/all_to_all | solution.py:412
  176.3 6.0 %copy-start.3 = (bf16[1,1024,384]{2,1,0:T(8,128)(2,1)S(1)}, bf16[1,1024,384]{2,1,0:T(8,128)(2,1)}, u32[]{:S(2)}) copy-start(bf16[1,1024,384]{2,1,0:T(8,128)(2,1)} %param.18) | copy-start | bytes 2359300
  176.3 8.3 %copy-start.6 = (bf16[192,1024]{1,0:T(8,128)(2,1)S(1)}, bf16[192,1024]{1,0:T(8,128)(2,1)}, u32[]{:S(2)}) copy-start(bf16[192,1024]{1,0:T(8,128)(2,1)} %copy-done.5) | copy-start | bytes 1179652
  176.3 34.0 %all-to-all-start.4 = ((bf16[32,160,128]{2,1,0:T(8,128)(2,1)}), bf16[32,160,128]{2,1,0:T(8,128)(2,1)S(1)}, u32[]{:S(2)}, u32[]{:S(2)}) async-start(bf16[32,160,128]{2,1,0:T(8,128)(2,1)} %bitcast.21), calls=%async_computation.4 | async-start | bytes 2621440 | tf_op jit(solution)/shard_map/all_to_all | solution.py:421
  182.3 15.3 %collective-permute-start.8 = (bf16[1024,384]{1,0:T(8,128)(2,1)S(1)}, bf16[1024,384]{1,0:T(8,128)(2,1)S(1)}, u32[]{:S(2)}, u32[]{:S(2)}) collective-permute-start(bf16[1024,384]{1,0:T(8,128)(2,1)S(1)} %bitcast.60), channel_id=1, source_target_pairs={{0,2},{2,0},{1,3},{3,1},{4,6},{6,4},{5,7},{7,5},{8,10},{10,8},{9,1... | collective-permute-start | bytes 2359304 | tf_op jit(solution)/shard_map/ppermute | solution.py:415
  210.3 1.1 copy-start.1
  215.1 1.1 copy-start
  216.2 33.7 %all-to-all-start.5 = ((bf16[32,160,128]{2,1,0:T(8,128)(2,1)}), bf16[32,160,128]{2,1,0:T(8,128)(2,1)S(1)}, u32[]{:S(2)}, u32[]{:S(2)}) async-start(bf16[32,160,128]{2,1,0:T(8,128)(2,1)} %bitcast.54), calls=%async_computation.5 | async-start | bytes 2621440 | tf_op jit(solution)/shard_map/all_to_all | solution.py:425
  249.8 20.1 %copy-start.7 = (f32[64,1024]{1,0:T(8,128)S(1)}, f32[64,1024]{1,0:T(8,128)}, u32[]{:S(2)}) copy-start(f32[64,1024]{1,0:T(8,128)} %get-tuple-element.14) | copy-start | bytes 786436
  (2 other events, 1.8 us)
Sparse Core Ops, SparseCore 0:
  9.4 85.4 all-gather.1

commit v9 on v7

--- a/solution.py
+++ b/solution.py
@@ -16,7 +16,8 @@
 NEG = -1e30
 LOW = -1e29
 STAT = 8
-SWAP = [(0, 1), (1, 0)]
+SWAP = [(i, i ^ 1) for i in range(8)]
+CLASSES = [[0, 2, 5, 7], [1, 3, 4, 6]]
 
 
 def flash_kernel(
@@ -355,8 +356,8 @@
 ):
     tokens, width = residual.shape
     own_x = lax.axis_index("x")
-    own_y2 = lax.axis_index("y2")
-    own_y = own_y2 * 2 + lax.axis_index("y1")
+    own_y = lax.axis_index("y")
+    own_y2 = own_y // 2
     position = jnp.stack([own_x, own_y]).astype(jnp.int32)
 
     key_value = pack_kv(key_vectors, value_vectors)
@@ -368,9 +369,9 @@
     down = [(i, (i - 1) % 8) for i in range(8)]
     ups, downs = [block], [block]
     for step in range(4):
-        ups.append(lax.ppermute(ups[-1], ("y2", "y1"), up))
+        ups.append(lax.ppermute(ups[-1], "y", up))
         if step < 3:
-            downs.append(lax.ppermute(downs[-1], ("y2", "y1"), down))
+            downs.append(lax.ppermute(downs[-1], "y", down))
     key_values = ups + downs[1:]
 
     query = lax.all_to_all(pack_q(queries), ("x", "z"), split_axis=0, concat_axis=0, tiled=True).reshape(
@@ -386,11 +387,12 @@
     whole_weight, own_in, own_out = lax.optimization_barrier(
         (whole_weight, expert_in[0], expert_out[0])
     )
-    other_in = lax.ppermute(own_in, "y1", SWAP)
-    other_out = lax.ppermute(own_out, "y1", SWAP)
-    turned = [ups[0][512:], ups[2][512:], ups[4][512:], downs[2][512:]]
-    listing = lax.dynamic_slice_in_dim(
-        jnp.stack([turned[k][:, :tokens] for k in (3, 2, 1, 0, 3, 2, 1)]), 3 - own_y2, 4, 0
+    other_in = lax.ppermute(own_in, "y", SWAP)
+    other_out = lax.ppermute(own_out, "y", SWAP)
+    ringed = jnp.stack([part[512:, :tokens] for part in [block, *downs[1:], ups[4], ups[3], ups[2], ups[1]]])
+    members = jnp.where((own_y % 2) == own_y // 4, jnp.array(CLASSES[0]), jnp.array(CLASSES[1]))
+    listing = jnp.stack(
+        [lax.dynamic_index_in_dim(ringed, (members[i] - own_y) & 7, 0, False) for i in range(4)]
     ).astype(jnp.int32)
     named, levels = listing[:, None, 0:8], listing[:, None, 8:16]
     q = jnp.arange(32, dtype=jnp.int32)
@@ -417,7 +419,9 @@
         [own_in[:, :half], other_in[:, :half], own_in[:, half:], other_in[:, half:]], axis=1
     )
     weight_out = jnp.concatenate([own_out, other_out], axis=0)
-    spread = lax.all_to_all(spread, "y2", split_axis=0, concat_axis=0, tiled=True)
+    spread = lax.all_to_all(
+        spread, "y", split_axis=0, concat_axis=0, axis_index_groups=CLASSES, tiled=True
+    )
     outgoing = select(chosen, spread.reshape(4 * tokens, width))
     arrived = lax.all_to_all(
         outgoing.reshape(32, 4 * CAP * 8, 128), ("x", "z"), split_axis=0, concat_axis=0, tiled=True
@@ -428,15 +432,20 @@
     )
     sums = gather(shares, answers.reshape(-1, 128))
     sums = lax.all_to_all(
-        sums.reshape(4, tokens, width), "y2", split_axis=0, concat_axis=0, tiled=True
+        sums.reshape(4, tokens, width),
+        "y",
+        split_axis=0,
+        concat_axis=0,
+        axis_index_groups=CLASSES,
+        tiled=True,
     )
     return hidden + jnp.sum(sums.astype(F32), axis=0)
 
 
 def solution(mesh):
-    fine = Mesh(mesh.devices.reshape(8, 4, 4, 2, 2), ("z", "x", "y2", "y1", "dp"))
-    rows = P(("dp", "x", "y2", "y1", "z"), None)
-    halves = P(("z", "x", "y2", "y1"), None, None)
+    fine = Mesh(mesh.devices.reshape(8, 4, 8, 2), ("z", "x", "y", "dp"))
+    rows = P(("dp", "x", "y", "z"), None)
+    halves = P(("z", "x", "y"), None, None)
     return jax.shard_map(
         local,
         mesh=fine,

time: 277 us -> 279 us (level)
  waiting for transfers between devices: 115 us -> 107 us
  blocking collectives: 15.7 us -> 22.3 us
    all_to_all x1, blocking collectives: 15.7 us -> 22.3 us  [local(): lax.all_to_all(sums.reshape(4, tokens, width), 'y', split_axis=0, concat_...]
    all_to_all x1, waiting for transfers between devices: 27.7 us -> 24.6 us  [local(): lax.all_to_all(outgoing.reshape(32, 4 * CAP * 8, 128), ('x', 'z'), split_...]
where the time goes in v9:
time: 279 us; the launch traced here: 278 us
  waiting for transfers between devices  107 us (38%)
  starting transfers between devices  75.9 us (27%)
  Pallas kernels  45.2 us (16%)
  blocking collectives  22.3 us (8%)
  between operations  16.3 us (6%)
  local copies, waits for them, and re-layouts  7.22 us (3%)
  other arithmetic  4.09 us (1%)
    pallas_call x1, Pallas kernels, flash(): pl.pallas_call(flash_kernel, grid_spec=pltpu.PrefetchScalarGridSpec(num_s...  30.4 us
    all_to_all x1, waiting for transfers between devices, local(): lax.all_to_all(done.reshape(32, 4 * CAP * 8, 128), ('x', 'z'), split_axis...  25.9 us
    all_to_all x1, waiting for transfers between devices, local(): lax.all_to_all(outgoing.reshape(32, 4 * CAP * 8, 128), ('x', 'z'), split_...  24.6 us
    all_to_all x1, blocking collectives, local(): lax.all_to_all(sums.reshape(4, tokens, width), 'y', split_axis=0, concat_...  22.3 us
    all_to_all x1, waiting for transfers between devices, local(): lax.all_to_all(shards.reshape(32, HD + STAT, 128), ('x', 'z'), split_axis...  18.9 us
    ppermute x4, waiting for transfers between devices, local(): ups.append(lax.ppermute(ups[-1], 'y', up))  14.3 us
    all_to_all x1, starting transfers between devices, local(): lax.all_to_all(key_value, ('x', 'z'), split_axis=0, concat_axis=0, tiled=...  13.2 us
    ppermute x4, starting transfers between devices, local(): ups.append(lax.ppermute(ups[-1], 'y', up))  12.6 us
  transfers between devices with their start and end apart: 16, of which 12 were waited for; matrix products, arithmetic and copies ran while one was open for 2% of the time, Pallas kernels for 14%

profile of v9, /device:TPU:8, one launch (start us, length us, event | category | flops | bytes accessed | tf_op | source)
XLA Modules:
  0.0 277.6 jit_solution(10626774608270405092)
XLA Ops:
  8.8 13.2 %all-to-all-start.1 = ((bf16[32,16,256]{2,1,0:T(8,128)(2,1)}), bf16[32,16,256]{2,1,0:T(8,128)(2,1)S(1)}, u32[]{:S(2)}, u32[]{:S(2)}) async-start(bf16[32,16,256]{2,1,0:T(8,128)(2,1)} %pack_kv.1), calls=%async_computation.1 | async-start | bytes 524288 | tf_op jit(solution)/shard_map/all_to_all | solution.py:364
  24.0 10.4 %all-to-all-done.1 = bf16[32,16,256]{2,1,0:T(8,128)(2,1)S(1)} async-done(((bf16[32,16,256]{2,1,0:T(8,128)(2,1)}), bf16[32,16,256]{2,1,0:T(8,128)(2,1)S(1)}, u32[]{:S(2)}, u32[]{:S(2)}) %all-to-all-start.1) | async-done | bytes 262176 | tf_op jit(solution)/shard_map/all_to_all | solution.py:364
  34.4 4.4 %all-to-all-start = ((bf16[32,64,256]{2,1,0:T(8,128)(2,1)}), bf16[32,64,256]{2,1,0:T(8,128)(2,1)S(1)}, u32[]{:S(2)}, u32[]{:S(2)}) async-start(bf16[32,64,256]{2,1,0:T(8,128)(2,1)} %pack_q.1), calls=%async_computation | async-start | bytes 2097152 | tf_op jit(solution)/shard_map/all_to_all | solution.py:377
  38.9 3.5 %collective-permute-start = (bf16[528,256]{1,0:T(8,128)(2,1)S(1)}, bf16[528,256]{1,0:T(8,128)(2,1)S(1)}, u32[]{:S(2)}, u32[]{:S(2)}) collective-permute-start(bf16[528,256]{1,0:T(8,128)(2,1)S(1)} %pad_maximum_fusion.2.b0), channel_id=1, source_target_pairs={{0,2},{2,4},{4,6},{6,8},{8,10},{10,12},{12,14},{14,0},{1,3},{3,5},... | collective-permute-start | bytes 811016 | tf_op jit(solution)/shard_map/ppermute | solution.py:372
  44.7 3.1 %collective-permute-done.b1 = bf16[528,256]{1,0:T(8,128)(2,1)S(1)} collective-permute-done((bf16[528,256]{1,0:T(8,128)(2,1)S(1)}, bf16[528,256]{1,0:T(8,128)(2,1)S(1)}, u32[]{:S(2)}, u32[]{:S(2)}) %collective-permute-start) | collective-permute-done | bytes 270368 | tf_op jit(solution)/shard_map/ppermute | solution.py:372
  47.8 3.5 %collective-permute-start.1 = (bf16[528,256]{1,0:T(8,128)(2,1)S(1)}, bf16[528,256]{1,0:T(8,128)(2,1)S(1)}, u32[]{:S(2)}, u32[]{:S(2)}) collective-permute-start(bf16[528,256]{1,0:T(8,128)(2,1)S(1)} %collective-permute-done.b1), channel_id=1, source_target_pairs={{0,2},{2,4},{4,6},{6,8},{8,10},{10,12},{12,14},{14,0},{1,3},{3,5},... | collective-permute-start | bytes 811016 | tf_op jit(solution)/shard_map/ppermute | solution.py:372
  53.9 2.8 %collective-permute-done.1.b2 = bf16[528,256]{1,0:T(8,128)(2,1)S(1)} collective-permute-done((bf16[528,256]{1,0:T(8,128)(2,1)S(1)}, bf16[528,256]{1,0:T(8,128)(2,1)S(1)}, u32[]{:S(2)}, u32[]{:S(2)}) %collective-permute-start.1) | collective-permute-done | bytes 270368 | tf_op jit(solution)/shard_map/ppermute | solution.py:372
  56.7 3.0 %collective-permute-start.2 = (bf16[528,256]{1,0:T(8,128)(2,1)S(1)}, bf16[528,256]{1,0:T(8,128)(2,1)S(1)}, u32[]{:S(2)}, u32[]{:S(2)}) collective-permute-start(bf16[528,256]{1,0:T(8,128)(2,1)S(1)} %collective-permute-done.1.b2), channel_id=1, source_target_pairs={{0,2},{2,4},{4,6},{6,8},{8,10},{10,12},{12,14},{14,0},{1,3},{3,5},... | collective-permute-start | bytes 811016 | tf_op jit(solution)/shard_map/ppermute | solution.py:372
  60.1 3.5 %collective-permute-start.6 = (bf16[528,256]{1,0:T(8,128)(2,1)S(1)}, bf16[528,256]{1,0:T(8,128)(2,1)S(1)}, u32[]{:S(2)}, u32[]{:S(2)}) collective-permute-start(bf16[528,256]{1,0:T(8,128)(2,1)S(1)} %collective-permute-done.5.b6), channel_id=1, source_target_pairs={{0,14},{2,0},{4,2},{6,4},{8,6},{10,8},{12,10},{14,12},{1,15},{3,1}... | collective-permute-start | bytes 811016 | tf_op jit(solution)/shard_map/ppermute | solution.py:374
  66.0 2.6 collective-permute-start.3
  69.6 5.9 %collective-permute-done.3.b4 = bf16[528,256]{1,0:T(8,128)(2,1)S(1)} collective-permute-done((bf16[528,256]{1,0:T(8,128)(2,1)S(1)}, bf16[528,256]{1,0:T(8,128)(2,1)S(1)}, u32[]{:S(2)}, u32[]{:S(2)}) %collective-permute-start.3) | collective-permute-done | bytes 270368 | tf_op jit(solution)/shard_map/ppermute | solution.py:372
  77.1 30.4 %flash.1 = bf16[4,8,136,128]{3,2,1,0:T(8,128)(2,1)} custom-call(s32[2]{0:T(128)S(1)} %pad_add_fusion.pos_ref, bf16[4,8,64,256]{3,2,1,0:T(8,128)(2,1)S(1)} %bitcast.72, bf16[528,256]{1,0:T(8,128)(2,1)S(1)} %pad_maximum_fusion.2.b0, bf16[528,256]{1,0:T(8,128)(2,1)S(1)} %collective-permute-done.b1, bf16[528,256]{1,0:T(8,128)(2,1)S(1)} %collective-permute-done.1.b2, ...), custom_call_target="tpu_custom_call" | custom-call | flops 5368709120 | bytes 5242880 | tf_op jit(solution)/shard_map/flash/pallas_call | solution.py:144
  107.5 6.4 %all-to-all-start.2 = ((bf16[32,136,128]{2,1,0:T(8,128)(2,1)}), bf16[32,136,128]{2,1,0:T(8,128)(2,1)S(1)}, u32[]{:S(2)}, u32[]{:S(2)}) async-start(bf16[32,136,128]{2,1,0:T(8,128)(2,1)} %bitcast.6), calls=%async_computation.2 | async-start | bytes 2228224 | tf_op jit(solution)/shard_map/all_to_all | solution.py:384
  116.3 4.2 %collective-permute-start.7 = (bf16[1024,384]{1,0:T(8,128)(2,1)}, bf16[1024,384]{1,0:T(8,128)(2,1)S(1)}, u32[]{:S(2)}, u32[]{:S(2)}) collective-permute-start(bf16[1024,384]{1,0:T(8,128)(2,1)} %bitcast.74), channel_id=1, source_target_pairs={{0,2},{2,0},{4,6},{6,4},{8,10},{10,8},{12,14},{14,12},{1,3},{3,1},... | collective-permute-start | bytes 2359304 | tf_op jit(solution)/shard_map/ppermute | solution.py:390
  122.5 18.9 %all-to-all-done.2 = bf16[32,136,128]{2,1,0:T(8,128)(2,1)S(1)} async-done(((bf16[32,136,128]{2,1,0:T(8,128)(2,1)}), bf16[32,136,128]{2,1,0:T(8,128)(2,1)S(1)}, u32[]{:S(2)}, u32[]{:S(2)}) %all-to-all-start.2) | async-done | bytes 1114144 | tf_op jit(solution)/shard_map/all_to_all | solution.py:384
  142.5 5.0 %merge.1 = (f32[64,1024]{1,0:T(8,128)}, bf16[4,64,1024]{2,1,0:T(8,128)(2,1)}) custom-call(bf16[4,8,136,128]{3,2,1,0:T(8,128)(2,1)} %bitcast.73, bf16[2048,1024]{1,0:T(8,128)(2,1)} %all-gather.2.cloned.1.call-done.w_ref, bf16[64,1024]{1,0:T(8,128)(2,1)} %res_ref.1, f32[1,1024]{1,0:T(1,128)} %bitcast.79), custom_call_target="tpu_custom_call" | custom-call | tf_op jit(solution)/shard_map/merge/pallas_call | solution.py:210
  148.3 12.5 %all-to-all-start.3 = ((bf16[4,64,1024]{2,1,0:T(8,128)(2,1)}), bf16[4,64,1024]{2,1,0:T(8,128)(2,1)S(1)}, u32[]{:S(2)}, u32[]{:S(2)}) async-start(bf16[4,64,1024]{2,1,0:T(8,128)(2,1)} %get-tuple-element.18), calls=%async_computation.3 | async-start | bytes 1048576 | tf_op jit(solution)/shard_map/all_to_all | solution.py:422
  162.1 9.7 %all-to-all-done.3 = bf16[4,64,1024]{2,1,0:T(8,128)(2,1)S(1)} async-done(((bf16[4,64,1024]{2,1,0:T(8,128)(2,1)}), bf16[4,64,1024]{2,1,0:T(8,128)(2,1)S(1)}, u32[]{:S(2)}, u32[]{:S(2)}) %all-to-all-start.3) | async-done | bytes 524320 | tf_op jit(solution)/shard_map/all_to_all | solution.py:422
  173.5 6.8 %all-to-all-start.4 = ((bf16[32,160,128]{2,1,0:T(8,128)(2,1)}), bf16[32,160,128]{2,1,0:T(8,128)(2,1)S(1)}, u32[]{:S(2)}, u32[]{:S(2)}) async-start(bf16[32,160,128]{2,1,0:T(8,128)(2,1)} %bitcast.29), calls=%async_computation.4 | async-start | bytes 2621440 | tf_op jit(solution)/shard_map/all_to_all | solution.py:426
  183.5 24.6 %all-to-all-done.4 = bf16[32,160,128]{2,1,0:T(8,128)(2,1)S(1)} async-done(((bf16[32,160,128]{2,1,0:T(8,128)(2,1)}), bf16[32,160,128]{2,1,0:T(8,128)(2,1)S(1)}, u32[]{:S(2)}, u32[]{:S(2)}) %all-to-all-start.4) | async-done | bytes 1310752 | tf_op jit(solution)/shard_map/all_to_all | solution.py:426
  209.2 3.7 %expert.1 = bf16[5120,128]{1,0:T(8,128)(2,1)S(1)} custom-call(bf16[5120,128]{1,0:T(8,128)(2,1)S(1)} %bitcast.67, bf16[1024,768]{1,0:T(8,128)(2,1)S(1)} %pad_maximum_fusion.win_ref, bf16[384,1024]{1,0:T(8,128)(2,1)S(1)} %copy-done.1), custom_call_target="tpu_custom_call" | custom-call | tf_op jit(solution)/shard_map/expert/pallas_call | solution.py:268
  214.0 5.7 %all-to-all-start.5 = ((bf16[32,160,128]{2,1,0:T(8,128)(2,1)}), bf16[32,160,128]{2,1,0:T(8,128)(2,1)S(1)}, u32[]{:S(2)}, u32[]{:S(2)}) async-start(bf16[32,160,128]{2,1,0:T(8,128)(2,1)} %bitcast.68), calls=%async_computation.5 | async-start | bytes 2621440 | tf_op jit(solution)/shard_map/all_to_all | solution.py:430
  221.0 25.9 %all-to-all-done.5 = bf16[32,160,128]{2,1,0:T(8,128)(2,1)S(1)} async-done(((bf16[32,160,128]{2,1,0:T(8,128)(2,1)}), bf16[32,160,128]{2,1,0:T(8,128)(2,1)S(1)}, u32[]{:S(2)}, u32[]{:S(2)}) %all-to-all-start.5) | async-done | bytes 1310752 | tf_op jit(solution)/shard_map/all_to_all | solution.py:430
  247.7 22.3 %all_to_all.35 = bf16[4,64,1024]{2,1,0:T(8,128)(2,1)S(1)} all-to-all(bf16[4,64,1024]{2,1,0:T(8,128)(2,1)S(1)} %bitcast.70), channel_id=1, replica_groups={{0,4,10,14},{2,6,8,12},{1,5,11,15},{3,7,9,13},{16,20,26,30},{18,22,24,2..., dimensions={0} | all-to-all | bytes 1048576 | tf_op jit(solution)/shard_map/all_to_all | solution.py:434
  (78 shorter events, 29.7 us)
Async XLA Ops:
  6.5 109.8 %all-gather.2.cloned.1.call-start = ((), (), s32[]{:S(2)}) async-start(), calls=%async_computation.7 | async-start | bytes 4718592 | tf_op jit(solution)/shard_map/all_gather | solution.py:381
  8.8 25.6 %all-to-all-start.1 = ((bf16[32,16,256]{2,1,0:T(8,128)(2,1)}), bf16[32,16,256]{2,1,0:T(8,128)(2,1)S(1)}, u32[]{:S(2)}, u32[]{:S(2)}) async-start(bf16[32,16,256]{2,1,0:T(8,128)(2,1)} %pack_kv.1), calls=%async_computation.1 | async-start | bytes 524288 | tf_op jit(solution)/shard_map/all_to_all | solution.py:364
  21.9 16.9 %copy-start.8 = (s32[64,8]{0,1:T(8,128)S(1)}, s32[64,8]{0,1:T(8,128)}, u32[]{:S(2)}) copy-start(s32[64,8]{0,1:T(8,128)} %param.19) | copy-start | bytes 6148
  21.9 16.9 %copy-start.9 = (s32[64,8]{0,1:T(8,128)S(1)}, s32[64,8]{0,1:T(8,128)}, u32[]{:S(2)}) copy-start(s32[64,8]{0,1:T(8,128)} %param.18) | copy-start | bytes 6148
  24.0 35.7 %copy-start.10 = (s32[4]{0:T(128)S(1)}, s32[4]{0:T(128)}, u32[]{:S(2)}) copy-start(s32[4]{0:T(128)} %constant.107.clone) | copy-start | bytes 52
  24.0 35.7 %copy-start.11 = (s32[4]{0:T(128)S(1)}, s32[4]{0:T(128)}, u32[]{:S(2)}) copy-start(s32[4]{0:T(128)} %constant.108.clone) | copy-start | bytes 52
  34.4 42.7 %all-to-all-start = ((bf16[32,64,256]{2,1,0:T(8,128)(2,1)}), bf16[32,64,256]{2,1,0:T(8,128)(2,1)S(1)}, u32[]{:S(2)}, u32[]{:S(2)}) async-start(bf16[32,64,256]{2,1,0:T(8,128)(2,1)} %pack_q.1), calls=%async_computation | async-start | bytes 2097152 | tf_op jit(solution)/shard_map/all_to_all | solution.py:377
  38.9 9.0 %collective-permute-start = (bf16[528,256]{1,0:T(8,128)(2,1)S(1)}, bf16[528,256]{1,0:T(8,128)(2,1)S(1)}, u32[]{:S(2)}, u32[]{:S(2)}) collective-permute-start(bf16[528,256]{1,0:T(8,128)(2,1)S(1)} %pad_maximum_fusion.2.b0), channel_id=1, source_target_pairs={{0,2},{2,4},{4,6},{6,8},{8,10},{10,12},{12,14},{14,0},{1,3},{3,5},... | collective-permute-start | bytes 811016 | tf_op jit(solution)/shard_map/ppermute | solution.py:372
  42.4 8.9 %collective-permute-start.4 = (bf16[528,256]{1,0:T(8,128)(2,1)S(1)}, bf16[528,256]{1,0:T(8,128)(2,1)S(1)}, u32[]{:S(2)}, u32[]{:S(2)}) collective-permute-start(bf16[528,256]{1,0:T(8,128)(2,1)S(1)} %pad_maximum_fusion.2.b0), channel_id=1, source_target_pairs={{0,14},{2,0},{4,2},{6,4},{8,6},{10,8},{12,10},{14,12},{1,15},{3,1}... | collective-permute-start | bytes 811016 | tf_op jit(solution)/shard_map/ppermute | solution.py:374
  47.8 8.9 %collective-permute-start.1 = (bf16[528,256]{1,0:T(8,128)(2,1)S(1)}, bf16[528,256]{1,0:T(8,128)(2,1)S(1)}, u32[]{:S(2)}, u32[]{:S(2)}) collective-permute-start(bf16[528,256]{1,0:T(8,128)(2,1)S(1)} %collective-permute-done.b1), channel_id=1, source_target_pairs={{0,2},{2,4},{4,6},{6,8},{8,10},{10,12},{12,14},{14,0},{1,3},{3,5},... | collective-permute-start | bytes 811016 | tf_op jit(solution)/shard_map/ppermute | solution.py:372
  51.3 8.7 %collective-permute-start.5 = (bf16[528,256]{1,0:T(8,128)(2,1)S(1)}, bf16[528,256]{1,0:T(8,128)(2,1)S(1)}, u32[]{:S(2)}, u32[]{:S(2)}) collective-permute-start(bf16[528,256]{1,0:T(8,128)(2,1)S(1)} %collective-permute-done.4.b5), channel_id=1, source_target_pairs={{0,14},{2,0},{4,2},{6,4},{8,6},{10,8},{12,10},{14,12},{1,15},{3,1}... | collective-permute-start | bytes 811016 | tf_op jit(solution)/shard_map/ppermute | solution.py:374
  56.7 9.3 %collective-permute-start.2 = (bf16[528,256]{1,0:T(8,128)(2,1)S(1)}, bf16[528,256]{1,0:T(8,128)(2,1)S(1)}, u32[]{:S(2)}, u32[]{:S(2)}) collective-permute-start(bf16[528,256]{1,0:T(8,128)(2,1)S(1)} %collective-permute-done.1.b2), channel_id=1, source_target_pairs={{0,2},{2,4},{4,6},{6,8},{8,10},{10,12},{12,14},{14,0},{1,3},{3,5},... | collective-permute-start | bytes 811016 | tf_op jit(solution)/shard_map/ppermute | solution.py:372
  60.1 9.5 %collective-permute-start.6 = (bf16[528,256]{1,0:T(8,128)(2,1)S(1)}, bf16[528,256]{1,0:T(8,128)(2,1)S(1)}, u32[]{:S(2)}, u32[]{:S(2)}) collective-permute-start(bf16[528,256]{1,0:T(8,128)(2,1)S(1)} %collective-permute-done.5.b6), channel_id=1, source_target_pairs={{0,14},{2,0},{4,2},{6,4},{8,6},{10,8},{12,10},{14,12},{1,15},{3,1}... | collective-permute-start | bytes 811016 | tf_op jit(solution)/shard_map/ppermute | solution.py:374
  66.0 9.6 %collective-permute-start.3 = (bf16[528,256]{1,0:T(8,128)(2,1)S(1)}, bf16[528,256]{1,0:T(8,128)(2,1)S(1)}, u32[]{:S(2)}, u32[]{:S(2)}) collective-permute-start(bf16[528,256]{1,0:T(8,128)(2,1)S(1)} %collective-permute-done.2.b3), channel_id=1, source_target_pairs={{0,2},{2,4},{4,6},{6,8},{8,10},{10,12},{12,14},{14,0},{1,3},{3,5},... | collective-permute-start | bytes 811016 | tf_op jit(solution)/shard_map/ppermute | solution.py:372
  107.5 34.0 %all-to-all-start.2 = ((bf16[32,136,128]{2,1,0:T(8,128)(2,1)}), bf16[32,136,128]{2,1,0:T(8,128)(2,1)S(1)}, u32[]{:S(2)}, u32[]{:S(2)}) async-start(bf16[32,136,128]{2,1,0:T(8,128)(2,1)} %bitcast.6), calls=%async_computation.2 | async-start | bytes 2228224 | tf_op jit(solution)/shard_map/all_to_all | solution.py:384
  116.3 31.2 %collective-permute-start.7 = (bf16[1024,384]{1,0:T(8,128)(2,1)}, bf16[1024,384]{1,0:T(8,128)(2,1)S(1)}, u32[]{:S(2)}, u32[]{:S(2)}) collective-permute-start(bf16[1024,384]{1,0:T(8,128)(2,1)} %bitcast.74), channel_id=1, source_target_pairs={{0,2},{2,0},{4,6},{6,4},{8,10},{10,8},{12,14},{14,12},{1,3},{3,1},... | collective-permute-start | bytes 2359304 | tf_op jit(solution)/shard_map/ppermute | solution.py:390
  120.5 27.0 %collective-permute-start.8 = (bf16[192,1024]{1,0:T(8,128)(2,1)}, bf16[192,1024]{1,0:T(8,128)(2,1)S(1)}, u32[]{:S(2)}, u32[]{:S(2)}) collective-permute-start(bf16[192,1024]{1,0:T(8,128)(2,1)} %bitcast.77), channel_id=1, source_target_pairs={{0,2},{2,0},{4,6},{6,4},{8,10},{10,8},{12,14},{14,12},{1,3},{3,1},... | collective-permute-start | bytes 1179656 | tf_op jit(solution)/shard_map/ppermute | solution.py:391
  148.3 23.5 %all-to-all-start.3 = ((bf16[4,64,1024]{2,1,0:T(8,128)(2,1)}), bf16[4,64,1024]{2,1,0:T(8,128)(2,1)S(1)}, u32[]{:S(2)}, u32[]{:S(2)}) async-start(bf16[4,64,1024]{2,1,0:T(8,128)(2,1)} %get-tuple-element.18), calls=%async_computation.3 | async-start | bytes 1048576 | tf_op jit(solution)/shard_map/all_to_all | solution.py:422
  173.5 6.8 %copy-start.3 = (bf16[1,1024,384]{2,1,0:T(8,128)(2,1)S(1)}, bf16[1,1024,384]{2,1,0:T(8,128)(2,1)}, u32[]{:S(2)}) copy-start(bf16[1,1024,384]{2,1,0:T(8,128)(2,1)} %param.20) | copy-start | bytes 2359300
  173.5 34.5 %all-to-all-start.4 = ((bf16[32,160,128]{2,1,0:T(8,128)(2,1)}), bf16[32,160,128]{2,1,0:T(8,128)(2,1)S(1)}, u32[]{:S(2)}, u32[]{:S(2)}) async-start(bf16[32,160,128]{2,1,0:T(8,128)(2,1)} %bitcast.29), calls=%async_computation.4 | async-start | bytes 2621440 | tf_op jit(solution)/shard_map/all_to_all | solution.py:426
  180.4 1.1 copy-start.6
  208.1 1.1 copy-start.1
  214.0 32.9 %all-to-all-start.5 = ((bf16[32,160,128]{2,1,0:T(8,128)(2,1)}), bf16[32,160,128]{2,1,0:T(8,128)(2,1)S(1)}, u32[]{:S(2)}, u32[]{:S(2)}) async-start(bf16[32,160,128]{2,1,0:T(8,128)(2,1)} %bitcast.68), calls=%async_computation.5 | async-start | bytes 2621440 | tf_op jit(solution)/shard_map/all_to_all | solution.py:430
  246.9 23.1 %copy-start.7 = (f32[64,1024]{1,0:T(8,128)S(1)}, f32[64,1024]{1,0:T(8,128)}, u32[]{:S(2)}) copy-start(f32[64,1024]{1,0:T(8,128)} %get-tuple-element.14) | copy-start | bytes 786436
  (4 other events, 3.9 us)
Sparse Core Ops, SparseCore 0:
  9.4 85.3 all-gather.1

commit v10 on v9

--- a/solution.py
+++ b/solution.py
@@ -17,7 +17,7 @@
 LOW = -1e29
 STAT = 8
 SWAP = [(i, i ^ 1) for i in range(8)]
-CLASSES = [[0, 2, 5, 7], [1, 3, 4, 6]]
+CLASSES = [[z * 8 + y for z in range(8) for y in ys] for ys in ((0, 2, 5, 7), (1, 3, 4, 6))]
 
 
 def flash_kernel(
@@ -39,7 +39,7 @@
             == lax.broadcasted_iota(jnp.int32, (HD, HD), 1)
         ).astype(BF)
         for far, ref in enumerate((b0, b5, b6, b7, b4, b3, b2, b1)):
-            kv_ref[(own_y + far) % 8] = ref[0:512, :].reshape(4, 128, 2 * HD)
+            kv_ref[(own_y + far) % 8] = ref[...].reshape(4, 128, 2 * HD)
         for c in range(8):
             v = kv_ref[4 * (c % 2) : 4 * (c % 2) + 4, c // 2, :, HD : 2 * HD].reshape(512, HD)
             turned = lax.dot_general(eye, v, (((1,), (1,)), ((), ())), preferred_element_type=F32)
@@ -326,20 +326,30 @@
     )(keys, values)
 
 
-def pack_q_kernel(q_ref, o_ref):
+def pack_q_kernel(q_ref, routes_ref, levels_ref, o_ref):
+    tokens = q_ref.shape[0]
+    listing = jnp.concatenate(
+        [
+            routes_ref[...].astype(F32),
+            levels_ref[...].astype(F32),
+            jnp.zeros((8, 2 * HD - 2 * tokens), F32),
+        ],
+        axis=1,
+    ).astype(BF)
     for z in range(8):
         piece = q_ref[:, z * 2 * HD : (z + 1) * 2 * HD]
         for x in range(4):
-            o_ref[x * 8 + z] = piece
-
-
-def pack_q(queries):
+            o_ref[x * 8 + z, 0:tokens] = piece
+            o_ref[x * 8 + z, tokens : tokens + 8] = listing
+
+
+def pack_q(queries, routes, levels):
     return pl.pallas_call(
         pack_q_kernel,
-        out_shape=jax.ShapeDtypeStruct((32, queries.shape[0], 2 * HD), BF),
+        out_shape=jax.ShapeDtypeStruct((32, queries.shape[0] + 8, 2 * HD), BF),
         cost_estimate=pl.CostEstimate(flops=0, bytes_accessed=5 << 18, transcendentals=0),
         name="pack_q",
-    )(queries)
+    )(queries, routes, levels)
 
 
 def local(
@@ -357,14 +367,11 @@
     tokens, width = residual.shape
     own_x = lax.axis_index("x")
     own_y = lax.axis_index("y")
-    own_y2 = own_y // 2
     position = jnp.stack([own_x, own_y]).astype(jnp.int32)
 
     key_value = pack_kv(key_vectors, value_vectors)
     key_value = lax.all_to_all(key_value, ("x", "z"), split_axis=0, concat_axis=0, tiled=True)
-    listing = jnp.concatenate([routes.T, gate_levels.T], axis=0).astype(BF)
-    listing = jnp.pad(listing, ((0, 0), (0, 2 * HD - tokens)))
-    block = jnp.concatenate([key_value.reshape(512, 2 * HD), listing], axis=0)
+    block = key_value.reshape(512, 2 * HD)
     up = [(i, (i + 1) % 8) for i in range(8)]
     down = [(i, (i - 1) % 8) for i in range(8)]
     ups, downs = [block], [block]
@@ -374,9 +381,9 @@
             downs.append(lax.ppermute(downs[-1], "y", down))
     key_values = ups + downs[1:]
 
-    query = lax.all_to_all(pack_q(queries), ("x", "z"), split_axis=0, concat_axis=0, tiled=True).reshape(
-        4, 8, tokens, 2 * HD
-    )
+    query = lax.all_to_all(
+        pack_q(queries, routes.T, gate_levels.T), ("x", "z"), split_axis=0, concat_axis=0, tiled=True
+    ).reshape(4, 8, tokens + 8, 2 * HD)
 
     whole_weight = lax.all_gather(output_weight, "z", axis=0, tiled=True)
 
@@ -389,14 +396,11 @@
     )
     other_in = lax.ppermute(own_in, "y", SWAP)
     other_out = lax.ppermute(own_out, "y", SWAP)
-    ringed = jnp.stack([part[512:, :tokens] for part in [block, *downs[1:], ups[4], ups[3], ups[2], ups[1]]])
-    members = jnp.where((own_y % 2) == own_y // 4, jnp.array(CLASSES[0]), jnp.array(CLASSES[1]))
-    listing = jnp.stack(
-        [lax.dynamic_index_in_dim(ringed, (members[i] - own_y) & 7, 0, False) for i in range(4)]
-    ).astype(jnp.int32)
-    named, levels = listing[:, None, 0:8], listing[:, None, 8:16]
+    listing = lax.dynamic_index_in_dim(query, lax.axis_index("z"), 1, False)[:, tokens:]
+    listing = listing.astype(jnp.int32)
+    named, levels = listing[:, None, :, 0:tokens], listing[:, None, :, tokens : 2 * tokens]
     q = jnp.arange(32, dtype=jnp.int32)
-    match = named == ((q % 8) * 16 + (q // 8) * 4 + own_y2)[None, :, None, None]
+    match = named == ((q // 4) * 16 + own_x * 4 + q % 4)[None, :, None, None]
     hits = jnp.any(match, axis=2)
     gates = jnp.sum(jnp.where(match, levels, 0), axis=2).astype(F32) / 256.0
     before = jnp.triu(jnp.ones((tokens, tokens), BF), 1)
@@ -420,23 +424,24 @@
     )
     weight_out = jnp.concatenate([own_out, other_out], axis=0)
     spread = lax.all_to_all(
-        spread, "y", split_axis=0, concat_axis=0, axis_index_groups=CLASSES, tiled=True
+        spread, "x", split_axis=0, concat_axis=0, tiled=True
     )
     outgoing = select(chosen, spread.reshape(4 * tokens, width))
     arrived = lax.all_to_all(
-        outgoing.reshape(32, 4 * CAP * 8, 128), ("x", "z"), split_axis=0, concat_axis=0, tiled=True
+        outgoing.reshape(32, 4 * CAP * 8, 128), ("z", "y"), split_axis=0, concat_axis=0,
+        axis_index_groups=CLASSES, tiled=True,
     )
     done = expert(arrived.reshape(-1, 128), weight_in, weight_out)
     answers = lax.all_to_all(
-        done.reshape(32, 4 * CAP * 8, 128), ("x", "z"), split_axis=0, concat_axis=0, tiled=True
+        done.reshape(32, 4 * CAP * 8, 128), ("z", "y"), split_axis=0, concat_axis=0,
+        axis_index_groups=CLASSES, tiled=True,
     )
     sums = gather(shares, answers.reshape(-1, 128))
     sums = lax.all_to_all(
         sums.reshape(4, tokens, width),
-        "y",
+        "x",
         split_axis=0,
         concat_axis=0,
-        axis_index_groups=CLASSES,
         tiled=True,
     )
     return hidden + jnp.sum(sums.astype(F32), axis=0)

time: 279 us -> 281 us (level)
  the two profiles are of different devices: /device:TPU:8 before, /device:TPU:16 now
where the time goes in v10:
time: 281 us; the launch traced here: 280 us
  waiting for transfers between devices  115 us (41%)
  starting transfers between devices  78.6 us (28%)
  Pallas kernels  45.3 us (16%)
  between operations  13.7 us (5%)
  blocking collectives  11.7 us (4%)
  local copies, waits for them, and re-layouts  8.47 us (3%)
  other arithmetic  6.84 us (2%)
    all_to_all x1, waiting for transfers between devices, local(): lax.all_to_all(done.reshape(32, 4 * CAP * 8, 128), ('z', 'y'), split_axis...  33.7 us
    pallas_call x1, Pallas kernels, flash(): pl.pallas_call(flash_kernel, grid_spec=pltpu.PrefetchScalarGridSpec(num_s...  30.5 us
    all_to_all x1, waiting for transfers between devices, local(): lax.all_to_all(outgoing.reshape(32, 4 * CAP * 8, 128), ('z', 'y'), split_...  27.5 us
    all_to_all x1, waiting for transfers between devices, local(): lax.all_to_all(shards.reshape(32, HD + STAT, 128), ('x', 'z'), split_axis...  18.8 us
    ppermute x4, starting transfers between devices, local(): ups.append(lax.ppermute(ups[-1], 'y', up))  17.8 us
    all_to_all x1, starting transfers between devices, local(): lax.all_to_all(outgoing.reshape(32, 4 * CAP * 8, 128), ('z', 'y'), split_...  15.4 us
    all_to_all x1, starting transfers between devices, local(): lax.all_to_all(key_value, ('x', 'z'), split_axis=0, concat_axis=0, tiled=...  13.2 us
    all_to_all x1, blocking collectives, local(): lax.all_to_all(sums.reshape(4, tokens, width), 'x', split_axis=0, concat_...  11.7 us
  transfers between devices with their start and end apart: 16, of which 13 were waited for; matrix products, arithmetic and copies ran while one was open for 3% of the time, Pallas kernels for 14%

profile of v10, /device:TPU:16, one launch (start us, length us, event | category | flops | bytes accessed | tf_op | source)
XLA Modules:
  0.0 279.9 jit_solution(4768830174915066235)
XLA Ops:
  8.8 13.2 %all-to-all-start.1 = ((bf16[32,16,256]{2,1,0:T(8,128)(2,1)}), bf16[32,16,256]{2,1,0:T(8,128)(2,1)S(1)}, u32[]{:S(2)}, u32[]{:S(2)}) async-start(bf16[32,16,256]{2,1,0:T(8,128)(2,1)} %pack_kv.1), calls=%async_computation.1 | async-start | bytes 524288 | tf_op jit(solution)/shard_map/all_to_all | solution.py:373
  24.0 10.4 %all-to-all-done.1 = bf16[32,16,256]{2,1,0:T(8,128)(2,1)S(1)} async-done(((bf16[32,16,256]{2,1,0:T(8,128)(2,1)}), bf16[32,16,256]{2,1,0:T(8,128)(2,1)S(1)}, u32[]{:S(2)}, u32[]{:S(2)}) %all-to-all-start.1) | async-done | bytes 262176 | tf_op jit(solution)/shard_map/all_to_all | solution.py:373
  34.4 4.4 %all-to-all-start = ((bf16[32,72,256]{2,1,0:T(8,128)(2,1)}), bf16[32,72,256]{2,1,0:T(8,128)(2,1)S(1)}, u32[]{:S(2)}, u32[]{:S(2)}) async-start(bf16[32,72,256]{2,1,0:T(8,128)(2,1)} %pack_q.1), calls=%async_computation | async-start | bytes 2359296 | tf_op jit(solution)/shard_map/all_to_all | solution.py:384
  38.8 3.5 %collective-permute-start = (bf16[512,256]{1,0:T(8,128)(2,1)S(1)}, bf16[512,256]{1,0:T(8,128)(2,1)S(1)}, u32[]{:S(2)}, u32[]{:S(2)}) collective-permute-start(bf16[512,256]{1,0:T(8,128)(2,1)S(1)} %bitcast.36), channel_id=1, source_target_pairs={{0,2},{2,4},{4,6},{6,8},{8,10},{10,12},{12,14},{14,0},{1,3},{3,5},... | collective-permute-start | bytes 786440 | tf_op jit(solution)/shard_map/ppermute | solution.py:379
  44.7 2.9 %collective-permute-done.b1 = bf16[512,256]{1,0:T(8,128)(2,1)S(1)} collective-permute-done((bf16[512,256]{1,0:T(8,128)(2,1)S(1)}, bf16[512,256]{1,0:T(8,128)(2,1)S(1)}, u32[]{:S(2)}, u32[]{:S(2)}) %collective-permute-start) | collective-permute-done | bytes 262176 | tf_op jit(solution)/shard_map/ppermute | solution.py:379
  47.6 3.8 %collective-permute-start.1 = (bf16[512,256]{1,0:T(8,128)(2,1)S(1)}, bf16[512,256]{1,0:T(8,128)(2,1)S(1)}, u32[]{:S(2)}, u32[]{:S(2)}) collective-permute-start(bf16[512,256]{1,0:T(8,128)(2,1)S(1)} %collective-permute-done.b1), channel_id=1, source_target_pairs={{0,2},{2,4},{4,6},{6,8},{8,10},{10,12},{12,14},{14,0},{1,3},{3,5},... | collective-permute-start | bytes 786440 | tf_op jit(solution)/shard_map/ppermute | solution.py:379
  55.8 5.0 %collective-permute-start.2 = (bf16[512,256]{1,0:T(8,128)(2,1)S(1)}, bf16[512,256]{1,0:T(8,128)(2,1)S(1)}, u32[]{:S(2)}, u32[]{:S(2)}) collective-permute-start(bf16[512,256]{1,0:T(8,128)(2,1)S(1)} %collective-permute-done.1.b2), channel_id=1, source_target_pairs={{0,2},{2,4},{4,6},{6,8},{8,10},{10,12},{12,14},{14,0},{1,3},{3,5},... | collective-permute-start | bytes 786440 | tf_op jit(solution)/shard_map/ppermute | solution.py:379
  64.7 5.6 %collective-permute-start.3 = (bf16[512,256]{1,0:T(8,128)(2,1)S(1)}, bf16[512,256]{1,0:T(8,128)(2,1)S(1)}, u32[]{:S(2)}, u32[]{:S(2)}) collective-permute-start(bf16[512,256]{1,0:T(8,128)(2,1)S(1)} %collective-permute-done.2.b3), channel_id=1, source_target_pairs={{0,2},{2,4},{4,6},{6,8},{8,10},{10,12},{12,14},{14,0},{1,3},{3,5},... | collective-permute-start | bytes 786440 | tf_op jit(solution)/shard_map/ppermute | solution.py:379
  70.8 3.4 %collective-permute-done.3.b4 = bf16[512,256]{1,0:T(8,128)(2,1)S(1)} collective-permute-done((bf16[512,256]{1,0:T(8,128)(2,1)S(1)}, bf16[512,256]{1,0:T(8,128)(2,1)S(1)}, u32[]{:S(2)}, u32[]{:S(2)}) %collective-permute-start.3) | collective-permute-done | bytes 262176 | tf_op jit(solution)/shard_map/ppermute | solution.py:379
  74.2 7.2 %all-to-all-done = bf16[32,72,256]{2,1,0:T(8,128)(2,1)S(1)} async-done(((bf16[32,72,256]{2,1,0:T(8,128)(2,1)}), bf16[32,72,256]{2,1,0:T(8,128)(2,1)S(1)}, u32[]{:S(2)}, u32[]{:S(2)}) %all-to-all-start) | async-done | bytes 1179680 | tf_op jit(solution)/shard_map/all_to_all | solution.py:384
  81.3 30.5 %flash.1 = bf16[4,8,136,128]{3,2,1,0:T(8,128)(2,1)} custom-call(s32[2]{0:T(128)S(1)} %pad_add_fusion.pos_ref, bf16[4,8,72,256]{3,2,1,0:T(8,128)(2,1)S(1)} %bitcast.33, bf16[512,256]{1,0:T(8,128)(2,1)S(1)} %bitcast.38, bf16[512,256]{1,0:T(8,128)(2,1)S(1)} %collective-permute-done.b1, bf16[512,256]{1,0:T(8,128)(2,1)S(1)} %collective-permute-done.1.b2, ...), custom_call_target="tpu_custom_call" | custom-call | flops 5368709120 | bytes 5242880 | tf_op jit(solution)/shard_map/flash/pallas_call | solution.py:144
  111.8 5.5 %all-to-all-start.2 = ((bf16[32,136,128]{2,1,0:T(8,128)(2,1)}), bf16[32,136,128]{2,1,0:T(8,128)(2,1)S(1)}, u32[]{:S(2)}, u32[]{:S(2)}) async-start(bf16[32,136,128]{2,1,0:T(8,128)(2,1)} %bitcast.6), calls=%async_computation.2 | async-start | bytes 2228224 | tf_op jit(solution)/shard_map/all_to_all | solution.py:391
  118.6 3.5 %collective-permute-start.7 = (bf16[1024,384]{1,0:T(8,128)(2,1)S(1)}, bf16[1024,384]{1,0:T(8,128)(2,1)S(1)}, u32[]{:S(2)}, u32[]{:S(2)}) collective-permute-start(bf16[1024,384]{1,0:T(8,128)(2,1)S(1)} %bitcast.40), channel_id=1, source_target_pairs={{0,2},{2,0},{4,6},{6,4},{8,10},{10,8},{12,14},{14,12},{1,3},{3,1},... | collective-permute-start | bytes 2359304 | tf_op jit(solution)/shard_map/ppermute | solution.py:397
  122.8 2.4 collective-permute-start.8
  126.9 18.8 %all-to-all-done.2 = bf16[32,136,128]{2,1,0:T(8,128)(2,1)S(1)} async-done(((bf16[32,136,128]{2,1,0:T(8,128)(2,1)}), bf16[32,136,128]{2,1,0:T(8,128)(2,1)S(1)}, u32[]{:S(2)}, u32[]{:S(2)}) %all-to-all-start.2) | async-done | bytes 1114144 | tf_op jit(solution)/shard_map/all_to_all | solution.py:391
  146.8 5.0 %merge.1 = (f32[64,1024]{1,0:T(8,128)}, bf16[4,64,1024]{2,1,0:T(8,128)(2,1)}) custom-call(bf16[4,8,136,128]{3,2,1,0:T(8,128)(2,1)} %bitcast.39, bf16[2048,1024]{1,0:T(8,128)(2,1)} %all-gather.2.cloned.1.call-done.w_ref, bf16[64,1024]{1,0:T(8,128)(2,1)} %res_ref.1, f32[1,1024]{1,0:T(1,128)} %bitcast.46), custom_call_target="tpu_custom_call" | custom-call | tf_op jit(solution)/shard_map/merge/pallas_call | solution.py:210
  152.8 3.5 %all-to-all-start.3 = ((bf16[4,64,1024]{2,1,0:T(8,128)(2,1)}), bf16[4,64,1024]{2,1,0:T(8,128)(2,1)S(1)}, u32[]{:S(2)}, u32[]{:S(2)}) async-start(bf16[4,64,1024]{2,1,0:T(8,128)(2,1)} %get-tuple-element.18), calls=%async_computation.3 | async-start | bytes 1048576 | tf_op jit(solution)/shard_map/all_to_all | solution.py:426
  158.7 5.7 %all-to-all-done.3 = bf16[4,64,1024]{2,1,0:T(8,128)(2,1)S(1)} async-done(((bf16[4,64,1024]{2,1,0:T(8,128)(2,1)}), bf16[4,64,1024]{2,1,0:T(8,128)(2,1)S(1)}, u32[]{:S(2)}, u32[]{:S(2)}) %all-to-all-start.3) | async-done | bytes 524320 | tf_op jit(solution)/shard_map/all_to_all | solution.py:426
  166.1 15.4 %all-to-all-start.4 = ((bf16[32,160,128]{2,1,0:T(8,128)(2,1)}), bf16[32,160,128]{2,1,0:T(8,128)(2,1)S(1)}, u32[]{:S(2)}, u32[]{:S(2)}) async-start(bf16[32,160,128]{2,1,0:T(8,128)(2,1)} %bitcast.17), calls=%async_computation.4 | async-start | bytes 2621440 | tf_op jit(solution)/shard_map/all_to_all | solution.py:430
  184.5 27.5 %all-to-all-done.4 = bf16[32,160,128]{2,1,0:T(8,128)(2,1)S(1)} async-done(((bf16[32,160,128]{2,1,0:T(8,128)(2,1)}), bf16[32,160,128]{2,1,0:T(8,128)(2,1)S(1)}, u32[]{:S(2)}, u32[]{:S(2)}) %all-to-all-start.4) | async-done | bytes 1310752 | tf_op jit(solution)/shard_map/all_to_all | solution.py:430
  213.1 3.7 %expert.1 = bf16[5120,128]{1,0:T(8,128)(2,1)S(1)} custom-call(bf16[5120,128]{1,0:T(8,128)(2,1)S(1)} %bitcast.29, bf16[1024,768]{1,0:T(8,128)(2,1)S(1)} %pad_maximum_fusion.win_ref, bf16[384,1024]{1,0:T(8,128)(2,1)S(1)} %copy-done.1), custom_call_target="tpu_custom_call" | custom-call | tf_op jit(solution)/shard_map/expert/pallas_call | solution.py:268
  217.8 6.8 %all-to-all-start.5 = ((bf16[32,160,128]{2,1,0:T(8,128)(2,1)}), bf16[32,160,128]{2,1,0:T(8,128)(2,1)S(1)}, u32[]{:S(2)}, u32[]{:S(2)}) async-start(bf16[32,160,128]{2,1,0:T(8,128)(2,1)} %bitcast.30), calls=%async_computation.5 | async-start | bytes 2621440 | tf_op jit(solution)/shard_map/all_to_all | solution.py:435
  226.1 33.7 %all-to-all-done.5 = bf16[32,160,128]{2,1,0:T(8,128)(2,1)S(1)} async-done(((bf16[32,160,128]{2,1,0:T(8,128)(2,1)}), bf16[32,160,128]{2,1,0:T(8,128)(2,1)S(1)}, u32[]{:S(2)}, u32[]{:S(2)}) %all-to-all-start.5) | async-done | bytes 1310752 | tf_op jit(solution)/shard_map/all_to_all | solution.py:435
  260.5 11.7 %all_to_all.35 = bf16[4,64,1024]{2,1,0:T(8,128)(2,1)S(1)} all-to-all(bf16[4,64,1024]{2,1,0:T(8,128)(2,1)S(1)} %bitcast.32), channel_id=1, replica_groups=mesh['z'=8,'x'=4,'y'=8,'dp'=2] {'x'}, dimensions={0} | all-to-all | bytes 1048576 | tf_op jit(solution)/shard_map/all_to_all | solution.py:440
  (73 shorter events, 33.4 us)
Async XLA Ops:
  6.5 112.1 %all-gather.2.cloned.1.call-start = ((), (), s32[]{:S(2)}) async-start(), calls=%async_computation.7 | async-start | bytes 4718592 | tf_op jit(solution)/shard_map/all_gather | solution.py:388
  8.8 25.6 %all-to-all-start.1 = ((bf16[32,16,256]{2,1,0:T(8,128)(2,1)}), bf16[32,16,256]{2,1,0:T(8,128)(2,1)S(1)}, u32[]{:S(2)}, u32[]{:S(2)}) async-start(bf16[32,16,256]{2,1,0:T(8,128)(2,1)} %pack_kv.1), calls=%async_computation.1 | async-start | bytes 524288 | tf_op jit(solution)/shard_map/all_to_all | solution.py:373
  34.4 46.9 %all-to-all-start = ((bf16[32,72,256]{2,1,0:T(8,128)(2,1)}), bf16[32,72,256]{2,1,0:T(8,128)(2,1)S(1)}, u32[]{:S(2)}, u32[]{:S(2)}) async-start(bf16[32,72,256]{2,1,0:T(8,128)(2,1)} %pack_q.1), calls=%async_computation | async-start | bytes 2359296 | tf_op jit(solution)/shard_map/all_to_all | solution.py:384
  38.8 8.8 %collective-permute-start = (bf16[512,256]{1,0:T(8,128)(2,1)S(1)}, bf16[512,256]{1,0:T(8,128)(2,1)S(1)}, u32[]{:S(2)}, u32[]{:S(2)}) collective-permute-start(bf16[512,256]{1,0:T(8,128)(2,1)S(1)} %bitcast.36), channel_id=1, source_target_pairs={{0,2},{2,4},{4,6},{6,8},{8,10},{10,12},{12,14},{14,0},{1,3},{3,5},... | collective-permute-start | bytes 786440 | tf_op jit(solution)/shard_map/ppermute | solution.py:379
  42.3 9.5 %collective-permute-start.4 = (bf16[512,256]{1,0:T(8,128)(2,1)S(1)}, bf16[512,256]{1,0:T(8,128)(2,1)S(1)}, u32[]{:S(2)}, u32[]{:S(2)}) collective-permute-start(bf16[512,256]{1,0:T(8,128)(2,1)S(1)} %bitcast.37), channel_id=1, source_target_pairs={{0,14},{2,0},{4,2},{6,4},{8,6},{10,8},{12,10},{14,12},{1,15},{3,1}... | collective-permute-start | bytes 786440 | tf_op jit(solution)/shard_map/ppermute | solution.py:381
  47.6 8.3 %collective-permute-start.1 = (bf16[512,256]{1,0:T(8,128)(2,1)S(1)}, bf16[512,256]{1,0:T(8,128)(2,1)S(1)}, u32[]{:S(2)}, u32[]{:S(2)}) collective-permute-start(bf16[512,256]{1,0:T(8,128)(2,1)S(1)} %collective-permute-done.b1), channel_id=1, source_target_pairs={{0,2},{2,4},{4,6},{6,8},{8,10},{10,12},{12,14},{14,0},{1,3},{3,5},... | collective-permute-start | bytes 786440 | tf_op jit(solution)/shard_map/ppermute | solution.py:379
  51.8 9.5 %collective-permute-start.5 = (bf16[512,256]{1,0:T(8,128)(2,1)S(1)}, bf16[512,256]{1,0:T(8,128)(2,1)S(1)}, u32[]{:S(2)}, u32[]{:S(2)}) collective-permute-start(bf16[512,256]{1,0:T(8,128)(2,1)S(1)} %collective-permute-done.4.b5), channel_id=1, source_target_pairs={{0,14},{2,0},{4,2},{6,4},{8,6},{10,8},{12,10},{14,12},{1,15},{3,1}... | collective-permute-start | bytes 786440 | tf_op jit(solution)/shard_map/ppermute | solution.py:381
  55.8 8.9 %collective-permute-start.2 = (bf16[512,256]{1,0:T(8,128)(2,1)S(1)}, bf16[512,256]{1,0:T(8,128)(2,1)S(1)}, u32[]{:S(2)}, u32[]{:S(2)}) collective-permute-start(bf16[512,256]{1,0:T(8,128)(2,1)S(1)} %collective-permute-done.1.b2), channel_id=1, source_target_pairs={{0,2},{2,4},{4,6},{6,8},{8,10},{10,12},{12,14},{14,0},{1,3},{3,5},... | collective-permute-start | bytes 786440 | tf_op jit(solution)/shard_map/ppermute | solution.py:379
  61.3 9.5 %collective-permute-start.6 = (bf16[512,256]{1,0:T(8,128)(2,1)S(1)}, bf16[512,256]{1,0:T(8,128)(2,1)S(1)}, u32[]{:S(2)}, u32[]{:S(2)}) collective-permute-start(bf16[512,256]{1,0:T(8,128)(2,1)S(1)} %collective-permute-done.5.b6), channel_id=1, source_target_pairs={{0,14},{2,0},{4,2},{6,4},{8,6},{10,8},{12,10},{14,12},{1,15},{3,1}... | collective-permute-start | bytes 786440 | tf_op jit(solution)/shard_map/ppermute | solution.py:381
  64.7 9.5 %collective-permute-start.3 = (bf16[512,256]{1,0:T(8,128)(2,1)S(1)}, bf16[512,256]{1,0:T(8,128)(2,1)S(1)}, u32[]{:S(2)}, u32[]{:S(2)}) collective-permute-start(bf16[512,256]{1,0:T(8,128)(2,1)S(1)} %collective-permute-done.2.b3), channel_id=1, source_target_pairs={{0,2},{2,4},{4,6},{6,8},{8,10},{10,12},{12,14},{14,0},{1,3},{3,5},... | collective-permute-start | bytes 786440 | tf_op jit(solution)/shard_map/ppermute | solution.py:379
  111.8 6.8 %copy-start.3 = (bf16[1,1024,384]{2,1,0:T(8,128)(2,1)S(1)}, bf16[1,1024,384]{2,1,0:T(8,128)(2,1)}, u32[]{:S(2)}) copy-start(bf16[1,1024,384]{2,1,0:T(8,128)(2,1)} %param.18) | copy-start | bytes 2359300
  111.8 11.0 %copy-start.6 = (bf16[1,192,1024]{2,1,0:T(8,128)(2,1)S(1)}, bf16[1,192,1024]{2,1,0:T(8,128)(2,1)}, u32[]{:S(2)}) copy-start(bf16[1,192,1024]{2,1,0:T(8,128)(2,1)} %param.19) | copy-start | bytes 1179652
  111.8 34.0 %all-to-all-start.2 = ((bf16[32,136,128]{2,1,0:T(8,128)(2,1)}), bf16[32,136,128]{2,1,0:T(8,128)(2,1)S(1)}, u32[]{:S(2)}, u32[]{:S(2)}) async-start(bf16[32,136,128]{2,1,0:T(8,128)(2,1)} %bitcast.6), calls=%async_computation.2 | async-start | bytes 2228224 | tf_op jit(solution)/shard_map/all_to_all | solution.py:391
  117.9 7.9 %copy-start.13 = (s32[32]{0:T(128)}, s32[32]{0:T(128)S(1)}, u32[]{:S(2)}) copy-start(s32[32]{0:T(128)S(1)} %fusion.9) | copy-start | bytes 388
  118.6 33.2 %collective-permute-start.7 = (bf16[1024,384]{1,0:T(8,128)(2,1)S(1)}, bf16[1024,384]{1,0:T(8,128)(2,1)S(1)}, u32[]{:S(2)}, u32[]{:S(2)}) collective-permute-start(bf16[1024,384]{1,0:T(8,128)(2,1)S(1)} %bitcast.40), channel_id=1, source_target_pairs={{0,2},{2,0},{4,6},{6,4},{8,10},{10,8},{12,14},{14,12},{1,3},{3,1},... | collective-permute-start | bytes 2359304 | tf_op jit(solution)/shard_map/ppermute | solution.py:397
  122.8 29.0 %collective-permute-start.8 = (bf16[192,1024]{1,0:T(8,128)(2,1)S(1)}, bf16[192,1024]{1,0:T(8,128)(2,1)S(1)}, u32[]{:S(2)}, u32[]{:S(2)}) collective-permute-start(bf16[192,1024]{1,0:T(8,128)(2,1)S(1)} %bitcast.42), channel_id=1, source_target_pairs={{0,2},{2,0},{4,6},{6,4},{8,10},{10,8},{12,14},{14,12},{1,3},{3,1},... | collective-permute-start | bytes 1179656 | tf_op jit(solution)/shard_map/ppermute | solution.py:398
  125.9 26.0 %copy-start.10 = (s32[4,8,64]{2,1,0:T(8,128)}, s32[4,8,64]{2,1,0:T(8,128)S(1)}, u32[]{:S(2)}) copy-start(s32[4,8,64]{2,1,0:T(8,128)S(1)} %get-tuple-element.25) | copy-start | bytes 24580
  152.8 11.5 %all-to-all-start.3 = ((bf16[4,64,1024]{2,1,0:T(8,128)(2,1)}), bf16[4,64,1024]{2,1,0:T(8,128)(2,1)S(1)}, u32[]{:S(2)}, u32[]{:S(2)}) async-start(bf16[4,64,1024]{2,1,0:T(8,128)(2,1)} %get-tuple-element.18), calls=%async_computation.3 | async-start | bytes 1048576 | tf_op jit(solution)/shard_map/all_to_all | solution.py:426
  166.1 45.9 %all-to-all-start.4 = ((bf16[32,160,128]{2,1,0:T(8,128)(2,1)}), bf16[32,160,128]{2,1,0:T(8,128)(2,1)S(1)}, u32[]{:S(2)}, u32[]{:S(2)}) async-start(bf16[32,160,128]{2,1,0:T(8,128)(2,1)} %bitcast.17), calls=%async_computation.4 | async-start | bytes 2621440 | tf_op jit(solution)/shard_map/all_to_all | solution.py:430
  217.8 6.8 %copy-start.12 = (s32[4,8,64]{2,1,0:T(8,128)S(1)}, s32[4,8,64]{2,1,0:T(8,128)}, u32[]{:S(2)}) copy-start(s32[4,8,64]{2,1,0:T(8,128)} %get-tuple-element.26) | copy-start | bytes 24580
  217.8 6.8 %copy-start.14 = (s32[32]{0:T(128)S(1)}, s32[32]{0:T(128)}, u32[]{:S(2)}) copy-start(s32[32]{0:T(128)} %copy-done.13) | copy-start | bytes 388
  217.8 7.1 %copy-start.15 = (pred[4,4]{1,0:T(4,128)(4,1)S(1)}, pred[4,4]{1,0:T(4,128)(4,1)}, u32[]{:S(2)}) copy-start(pred[4,4]{1,0:T(4,128)(4,1)} %iota_compare_fusion.2) | copy-start | bytes 52
  217.8 41.9 %all-to-all-start.5 = ((bf16[32,160,128]{2,1,0:T(8,128)(2,1)}), bf16[32,160,128]{2,1,0:T(8,128)(2,1)S(1)}, u32[]{:S(2)}, u32[]{:S(2)}) async-start(bf16[32,160,128]{2,1,0:T(8,128)(2,1)} %bitcast.30), calls=%async_computation.5 | async-start | bytes 2621440 | tf_op jit(solution)/shard_map/all_to_all | solution.py:435
  259.7 12.6 %copy-start.9 = (f32[64,1024]{1,0:T(8,128)S(1)}, f32[64,1024]{1,0:T(8,128)}, u32[]{:S(2)}) copy-start(f32[64,1024]{1,0:T(8,128)} %get-tuple-element.14) | copy-start | bytes 786436
  (8 other events, 18.3 us)
Sparse Core Ops, SparseCore 0:
  9.4 88.1 all-gather.1

commit v11 on v7

--- a/solution.py
+++ b/solution.py
@@ -220,6 +220,7 @@
             jax.ShapeDtypeStruct((tokens, width), F32),
             jax.ShapeDtypeStruct((4, tokens, width), BF),
         ],
+        compiler_params=pltpu.CompilerParams(vmem_limit_bytes=48 * 1024 * 1024),
         name="merge",
     )(parts, weight, residual, gain)
 
@@ -240,7 +241,7 @@
         select_kernel,
         out_shape=jax.ShapeDtypeStruct((count * 8, 128), BF),
         scratch_shapes=[pltpu.VMEM((count * 8, 128), F32)],
-        compiler_params=pltpu.CompilerParams(vmem_limit_bytes=40 * 1024 * 1024),
+        compiler_params=pltpu.CompilerParams(vmem_limit_bytes=14 * 1024 * 1024),
         name="select",
     )(chosen, tokens)
 
@@ -275,7 +276,7 @@
         out_specs=pl.BlockSpec((block, 128), lambda i: (i, 0)),
         out_shape=jax.ShapeDtypeStruct((total, 128), BF),
         scratch_shapes=[pltpu.VMEM((block, 128), F32)],
-        compiler_params=pltpu.CompilerParams(vmem_limit_bytes=40 * 1024 * 1024),
+        compiler_params=pltpu.CompilerParams(vmem_limit_bytes=14 * 1024 * 1024),
         name="expert",
     )(rows_in, weight_in, weight_out)
 
@@ -303,7 +304,7 @@
         gather_kernel,
         out_shape=jax.ShapeDtypeStruct((gates.shape[0], 1024), BF),
         scratch_shapes=[pltpu.VMEM((count * 8, 128), F32)],
-        compiler_params=pltpu.CompilerParams(vmem_limit_bytes=40 * 1024 * 1024),
+        compiler_params=pltpu.CompilerParams(vmem_limit_bytes=14 * 1024 * 1024),
         name="gather",
     )(gates, rows)
 

time: 277 us -> 275 us (level)
  transfers between devices with their start and end apart: 16 -> 16, of which waited for: 12 -> 12; matrix products, arithmetic and copies ran while one was open for 2% -> 3% of each run, Pallas kernels for 14% -> 14%
where the time goes in v11:
time: 275 us; the launch traced here: 274 us
  waiting for transfers between devices  114 us (41%)
  starting transfers between devices  74.4 us (27%)
  Pallas kernels  45 us (16%)
  blocking collectives  15.7 us (6%)
  between operations  13.8 us (5%)
  local copies, waits for them, and re-layouts  5.83 us (2%)
  other arithmetic  5.07 us (2%)
    pallas_call x1, Pallas kernels, flash(): pl.pallas_call(flash_kernel, grid_spec=pltpu.PrefetchScalarGridSpec(num_s...  30.4 us
    all_to_all x1, waiting for transfers between devices, local(): lax.all_to_all(done.reshape(32, 4 * CAP * 8, 128), ('x', 'z'), split_axis...  28.6 us
    all_to_all x1, waiting for transfers between devices, local(): lax.all_to_all(outgoing.reshape(32, 4 * CAP * 8, 128), ('x', 'z'), split_...  25.6 us
    all_to_all x1, waiting for transfers between devices, local(): lax.all_to_all(shards.reshape(32, HD + STAT, 128), ('x', 'z'), split_axis...  21.3 us
    all_to_all x1, blocking collectives, local(): lax.all_to_all(sums.reshape(4, tokens, width), 'y2', split_axis=0, concat...  15.7 us
    ppermute x4, waiting for transfers between devices, local(): ups.append(lax.ppermute(ups[-1], ('y2', 'y1'), up))  14.4 us
    all_to_all x1, starting transfers between devices, local(): lax.all_to_all(key_value, ('x', 'z'), split_axis=0, concat_axis=0, tiled=...  13.2 us
    all_to_all x1, starting transfers between devices, local(): lax.all_to_all(spread, 'y2', split_axis=0, concat_axis=0, tiled=True)  12.8 us
  transfers between devices with their start and end apart: 16, of which 12 were waited for; matrix products, arithmetic and copies ran while one was open for 3% of the time, Pallas kernels for 14%

profile of v11, /device:TPU:8, one launch (start us, length us, event | category | flops | bytes accessed | tf_op | source)
XLA Modules:
  0.0 273.9 jit_solution(8835985786819384583)
XLA Ops:
  8.8 13.2 %all-to-all-start.1 = ((bf16[32,16,256]{2,1,0:T(8,128)(2,1)}), bf16[32,16,256]{2,1,0:T(8,128)(2,1)S(1)}, u32[]{:S(2)}, u32[]{:S(2)}) async-start(bf16[32,16,256]{2,1,0:T(8,128)(2,1)} %pack_kv.1), calls=%async_computation.1 | async-start | bytes 524288 | tf_op jit(solution)/shard_map/all_to_all | solution.py:364
  24.0 10.4 %all-to-all-done.1 = bf16[32,16,256]{2,1,0:T(8,128)(2,1)S(1)} async-done(((bf16[32,16,256]{2,1,0:T(8,128)(2,1)}), bf16[32,16,256]{2,1,0:T(8,128)(2,1)S(1)}, u32[]{:S(2)}, u32[]{:S(2)}) %all-to-all-start.1) | async-done | bytes 262176 | tf_op jit(solution)/shard_map/all_to_all | solution.py:364
  34.4 4.4 %all-to-all-start = ((bf16[32,64,256]{2,1,0:T(8,128)(2,1)}), bf16[32,64,256]{2,1,0:T(8,128)(2,1)S(1)}, u32[]{:S(2)}, u32[]{:S(2)}) async-start(bf16[32,64,256]{2,1,0:T(8,128)(2,1)} %pack_q.1), calls=%async_computation | async-start | bytes 2097152 | tf_op jit(solution)/shard_map/all_to_all | solution.py:377
  38.9 3.5 %collective-permute-start = (bf16[528,256]{1,0:T(8,128)(2,1)S(1)}, bf16[528,256]{1,0:T(8,128)(2,1)S(1)}, u32[]{:S(2)}, u32[]{:S(2)}) collective-permute-start(bf16[528,256]{1,0:T(8,128)(2,1)S(1)} %pad_maximum_fusion.2.b0), channel_id=1, source_target_pairs={{0,2},{2,4},{4,6},{6,8},{8,10},{10,12},{12,14},{14,0},{1,3},{3,5},... | collective-permute-start | bytes 811016 | tf_op jit(solution)/shard_map/ppermute | solution.py:372
  44.7 3.1 %collective-permute-done.b1 = bf16[528,256]{1,0:T(8,128)(2,1)S(1)} collective-permute-done((bf16[528,256]{1,0:T(8,128)(2,1)S(1)}, bf16[528,256]{1,0:T(8,128)(2,1)S(1)}, u32[]{:S(2)}, u32[]{:S(2)}) %collective-permute-start) | collective-permute-done | bytes 270368 | tf_op jit(solution)/shard_map/ppermute | solution.py:372
  47.8 3.5 %collective-permute-start.1 = (bf16[528,256]{1,0:T(8,128)(2,1)S(1)}, bf16[528,256]{1,0:T(8,128)(2,1)S(1)}, u32[]{:S(2)}, u32[]{:S(2)}) collective-permute-start(bf16[528,256]{1,0:T(8,128)(2,1)S(1)} %collective-permute-done.b1), channel_id=1, source_target_pairs={{0,2},{2,4},{4,6},{6,8},{8,10},{10,12},{12,14},{14,0},{1,3},{3,5},... | collective-permute-start | bytes 811016 | tf_op jit(solution)/shard_map/ppermute | solution.py:372
  53.9 2.8 %collective-permute-done.1.b2 = bf16[528,256]{1,0:T(8,128)(2,1)S(1)} collective-permute-done((bf16[528,256]{1,0:T(8,128)(2,1)S(1)}, bf16[528,256]{1,0:T(8,128)(2,1)S(1)}, u32[]{:S(2)}, u32[]{:S(2)}) %collective-permute-start.1) | collective-permute-done | bytes 270368 | tf_op jit(solution)/shard_map/ppermute | solution.py:372
  56.7 3.0 %collective-permute-start.2 = (bf16[528,256]{1,0:T(8,128)(2,1)S(1)}, bf16[528,256]{1,0:T(8,128)(2,1)S(1)}, u32[]{:S(2)}, u32[]{:S(2)}) collective-permute-start(bf16[528,256]{1,0:T(8,128)(2,1)S(1)} %collective-permute-done.1.b2), channel_id=1, source_target_pairs={{0,2},{2,4},{4,6},{6,8},{8,10},{10,12},{12,14},{14,0},{1,3},{3,5},... | collective-permute-start | bytes 811016 | tf_op jit(solution)/shard_map/ppermute | solution.py:372
  60.1 3.4 %collective-permute-start.6 = (bf16[528,256]{1,0:T(8,128)(2,1)S(1)}, bf16[528,256]{1,0:T(8,128)(2,1)S(1)}, u32[]{:S(2)}, u32[]{:S(2)}) collective-permute-start(bf16[528,256]{1,0:T(8,128)(2,1)S(1)} %collective-permute-done.5.b6), channel_id=1, source_target_pairs={{0,14},{2,0},{4,2},{6,4},{8,6},{10,8},{12,10},{14,12},{1,15},{3,1}... | collective-permute-start | bytes 811016 | tf_op jit(solution)/shard_map/ppermute | solution.py:374
  66.0 2.6 collective-permute-start.3
  69.6 5.9 %collective-permute-done.3.b4 = bf16[528,256]{1,0:T(8,128)(2,1)S(1)} collective-permute-done((bf16[528,256]{1,0:T(8,128)(2,1)S(1)}, bf16[528,256]{1,0:T(8,128)(2,1)S(1)}, u32[]{:S(2)}, u32[]{:S(2)}) %collective-permute-start.3) | collective-permute-done | bytes 270368 | tf_op jit(solution)/shard_map/ppermute | solution.py:372
  77.1 30.4 %flash.1 = bf16[4,8,136,128]{3,2,1,0:T(8,128)(2,1)} custom-call(s32[2]{0:T(128)S(1)} %pad_add_fusion.pos_ref, bf16[4,8,64,256]{3,2,1,0:T(8,128)(2,1)S(1)} %bitcast.59, bf16[528,256]{1,0:T(8,128)(2,1)S(1)} %pad_maximum_fusion.2.b0, bf16[528,256]{1,0:T(8,128)(2,1)S(1)} %collective-permute-done.b1, bf16[528,256]{1,0:T(8,128)(2,1)S(1)} %collective-permute-done.1.b2, ...), custom_call_target="tpu_custom_call" | custom-call | flops 5368709120 | bytes 5242880 | tf_op jit(solution)/shard_map/flash/pallas_call | solution.py:143
  107.5 6.5 %all-to-all-start.2 = ((bf16[32,136,128]{2,1,0:T(8,128)(2,1)}), bf16[32,136,128]{2,1,0:T(8,128)(2,1)S(1)}, u32[]{:S(2)}, u32[]{:S(2)}) async-start(bf16[32,136,128]{2,1,0:T(8,128)(2,1)} %bitcast.6), calls=%async_computation.2 | async-start | bytes 2228224 | tf_op jit(solution)/shard_map/all_to_all | solution.py:384
  114.1 4.1 %collective-permute-start.7 = (bf16[1024,384]{1,0:T(8,128)(2,1)S(1)}, bf16[1024,384]{1,0:T(8,128)(2,1)}, u32[]{:S(2)}, u32[]{:S(2)}) collective-permute-start(bf16[1024,384]{1,0:T(8,128)(2,1)S(1)} %bitcast.61), channel_id=1, source_target_pairs={{0,2},{2,0},{1,3},{3,1},{4,6},{6,4},{5,7},{7,5},{8,10},{10,8},{9,1... | collective-permute-start | bytes 2359304 | tf_op jit(solution)/shard_map/ppermute | solution.py:390
  120.3 21.3 %all-to-all-done.2 = bf16[32,136,128]{2,1,0:T(8,128)(2,1)S(1)} async-done(((bf16[32,136,128]{2,1,0:T(8,128)(2,1)}), bf16[32,136,128]{2,1,0:T(8,128)(2,1)S(1)}, u32[]{:S(2)}, u32[]{:S(2)}) %all-to-all-start.2) | async-done | bytes 1114144 | tf_op jit(solution)/shard_map/all_to_all | solution.py:384
  141.6 4.8 %merge.1 = (f32[64,1024]{1,0:T(8,128)S(1)}, bf16[4,64,1024]{2,1,0:T(8,128)(2,1)}) custom-call(bf16[4,8,136,128]{3,2,1,0:T(8,128)(2,1)S(1)} %bitcast.55, bf16[2048,1024]{1,0:T(8,128)(2,1)} %all-gather.2.cloned.1.call-done.w_ref, bf16[64,1024]{1,0:T(8,128)(2,1)S(1)} %copy-done.2, f32[1,1024]{1,0:T(1,128)S(1)} %bitcast.60), custom_call_target="tpu_custom_call" | custom-call | tf_op jit(solution)/shard_map/merge/pallas_call | solution.py:209
  146.4 12.8 %all-to-all-start.3 = ((bf16[4,64,1024]{2,1,0:T(8,128)(2,1)}), bf16[4,64,1024]{2,1,0:T(8,128)(2,1)S(1)}, u32[]{:S(2)}, u32[]{:S(2)}) async-start(bf16[4,64,1024]{2,1,0:T(8,128)(2,1)} %get-tuple-element.18), calls=%async_computation.3 | async-start | bytes 1048576 | tf_op jit(solution)/shard_map/all_to_all | solution.py:421
  160.5 10.2 %all-to-all-done.3 = bf16[4,64,1024]{2,1,0:T(8,128)(2,1)S(1)} async-done(((bf16[4,64,1024]{2,1,0:T(8,128)(2,1)}), bf16[4,64,1024]{2,1,0:T(8,128)(2,1)S(1)}, u32[]{:S(2)}, u32[]{:S(2)}) %all-to-all-start.3) | async-done | bytes 524320 | tf_op jit(solution)/shard_map/all_to_all | solution.py:421
  172.5 5.5 %all-to-all-start.4 = ((bf16[32,160,128]{2,1,0:T(8,128)(2,1)}), bf16[32,160,128]{2,1,0:T(8,128)(2,1)S(1)}, u32[]{:S(2)}, u32[]{:S(2)}) async-start(bf16[32,160,128]{2,1,0:T(8,128)(2,1)} %bitcast.21), calls=%async_computation.4 | async-start | bytes 2621440 | tf_op jit(solution)/shard_map/all_to_all | solution.py:423
  183.2 25.6 %all-to-all-done.4 = bf16[32,160,128]{2,1,0:T(8,128)(2,1)S(1)} async-done(((bf16[32,160,128]{2,1,0:T(8,128)(2,1)}), bf16[32,160,128]{2,1,0:T(8,128)(2,1)S(1)}, u32[]{:S(2)}, u32[]{:S(2)}) %all-to-all-start.4) | async-done | bytes 1310752 | tf_op jit(solution)/shard_map/all_to_all | solution.py:423
  210.0 3.7 %expert.1 = bf16[5120,128]{1,0:T(8,128)(2,1)S(1)} custom-call(bf16[5120,128]{1,0:T(8,128)(2,1)S(1)} %bitcast.53, bf16[1024,768]{1,0:T(8,128)(2,1)S(1)} %pad_maximum_fusion.win_ref, bf16[384,1024]{1,0:T(8,128)(2,1)S(1)} %copy-done.1), custom_call_target="tpu_custom_call" | custom-call | tf_op jit(solution)/shard_map/expert/pallas_call | solution.py:268
  214.7 5.1 %all-to-all-start.5 = ((bf16[32,160,128]{2,1,0:T(8,128)(2,1)}), bf16[32,160,128]{2,1,0:T(8,128)(2,1)S(1)}, u32[]{:S(2)}, u32[]{:S(2)}) async-start(bf16[32,160,128]{2,1,0:T(8,128)(2,1)} %bitcast.54), calls=%async_computation.5 | async-start | bytes 2621440 | tf_op jit(solution)/shard_map/all_to_all | solution.py:427
  221.2 28.6 %all-to-all-done.5 = bf16[32,160,128]{2,1,0:T(8,128)(2,1)S(1)} async-done(((bf16[32,160,128]{2,1,0:T(8,128)(2,1)}), bf16[32,160,128]{2,1,0:T(8,128)(2,1)S(1)}, u32[]{:S(2)}, u32[]{:S(2)}) %all-to-all-start.5) | async-done | bytes 1310752 | tf_op jit(solution)/shard_map/all_to_all | solution.py:427
  250.5 15.7 %all_to_all.35 = bf16[4,64,1024]{2,1,0:T(8,128)(2,1)S(1)} all-to-all(bf16[4,64,1024]{2,1,0:T(8,128)(2,1)S(1)} %bitcast.57), channel_id=1, replica_groups=mesh['z'=8,'x'=4,'y2'=4,'y1'=2,'dp'=2] {'y2'}, dimensions={0} | all-to-all | bytes 1048576 | tf_op jit(solution)/shard_map/all_to_all | solution.py:431
  (68 shorter events, 30.0 us)
Async XLA Ops:
  6.5 107.6 %all-gather.2.cloned.1.call-start = ((), (), s32[]{:S(2)}) async-start(), calls=%async_computation.7 | async-start | bytes 4718592 | tf_op jit(solution)/shard_map/all_gather | solution.py:381
  8.8 25.6 %all-to-all-start.1 = ((bf16[32,16,256]{2,1,0:T(8,128)(2,1)}), bf16[32,16,256]{2,1,0:T(8,128)(2,1)S(1)}, u32[]{:S(2)}, u32[]{:S(2)}) async-start(bf16[32,16,256]{2,1,0:T(8,128)(2,1)} %pack_kv.1), calls=%async_computation.1 | async-start | bytes 524288 | tf_op jit(solution)/shard_map/all_to_all | solution.py:364
  21.9 16.9 %copy-start.7 = (s32[64,8]{0,1:T(8,128)S(1)}, s32[64,8]{0,1:T(8,128)}, u32[]{:S(2)}) copy-start(s32[64,8]{0,1:T(8,128)} %param.17) | copy-start | bytes 6148
  21.9 16.9 %copy-start.8 = (s32[64,8]{0,1:T(8,128)S(1)}, s32[64,8]{0,1:T(8,128)}, u32[]{:S(2)}) copy-start(s32[64,8]{0,1:T(8,128)} %param.16) | copy-start | bytes 6148
  34.4 42.7 %all-to-all-start = ((bf16[32,64,256]{2,1,0:T(8,128)(2,1)}), bf16[32,64,256]{2,1,0:T(8,128)(2,1)S(1)}, u32[]{:S(2)}, u32[]{:S(2)}) async-start(bf16[32,64,256]{2,1,0:T(8,128)(2,1)} %pack_q.1), calls=%async_computation | async-start | bytes 2097152 | tf_op jit(solution)/shard_map/all_to_all | solution.py:377
  38.9 9.0 %collective-permute-start = (bf16[528,256]{1,0:T(8,128)(2,1)S(1)}, bf16[528,256]{1,0:T(8,128)(2,1)S(1)}, u32[]{:S(2)}, u32[]{:S(2)}) collective-permute-start(bf16[528,256]{1,0:T(8,128)(2,1)S(1)} %pad_maximum_fusion.2.b0), channel_id=1, source_target_pairs={{0,2},{2,4},{4,6},{6,8},{8,10},{10,12},{12,14},{14,0},{1,3},{3,5},... | collective-permute-start | bytes 811016 | tf_op jit(solution)/shard_map/ppermute | solution.py:372
  42.4 8.9 %collective-permute-start.4 = (bf16[528,256]{1,0:T(8,128)(2,1)S(1)}, bf16[528,256]{1,0:T(8,128)(2,1)S(1)}, u32[]{:S(2)}, u32[]{:S(2)}) collective-permute-start(bf16[528,256]{1,0:T(8,128)(2,1)S(1)} %pad_maximum_fusion.2.b0), channel_id=1, source_target_pairs={{0,14},{2,0},{4,2},{6,4},{8,6},{10,8},{12,10},{14,12},{1,15},{3,1}... | collective-permute-start | bytes 811016 | tf_op jit(solution)/shard_map/ppermute | solution.py:374
  47.8 8.9 %collective-permute-start.1 = (bf16[528,256]{1,0:T(8,128)(2,1)S(1)}, bf16[528,256]{1,0:T(8,128)(2,1)S(1)}, u32[]{:S(2)}, u32[]{:S(2)}) collective-permute-start(bf16[528,256]{1,0:T(8,128)(2,1)S(1)} %collective-permute-done.b1), channel_id=1, source_target_pairs={{0,2},{2,4},{4,6},{6,8},{8,10},{10,12},{12,14},{14,0},{1,3},{3,5},... | collective-permute-start | bytes 811016 | tf_op jit(solution)/shard_map/ppermute | solution.py:372
  51.3 8.7 %collective-permute-start.5 = (bf16[528,256]{1,0:T(8,128)(2,1)S(1)}, bf16[528,256]{1,0:T(8,128)(2,1)S(1)}, u32[]{:S(2)}, u32[]{:S(2)}) collective-permute-start(bf16[528,256]{1,0:T(8,128)(2,1)S(1)} %collective-permute-done.4.b5), channel_id=1, source_target_pairs={{0,14},{2,0},{4,2},{6,4},{8,6},{10,8},{12,10},{14,12},{1,15},{3,1}... | collective-permute-start | bytes 811016 | tf_op jit(solution)/shard_map/ppermute | solution.py:374
  56.7 9.3 %collective-permute-start.2 = (bf16[528,256]{1,0:T(8,128)(2,1)S(1)}, bf16[528,256]{1,0:T(8,128)(2,1)S(1)}, u32[]{:S(2)}, u32[]{:S(2)}) collective-permute-start(bf16[528,256]{1,0:T(8,128)(2,1)S(1)} %collective-permute-done.1.b2), channel_id=1, source_target_pairs={{0,2},{2,4},{4,6},{6,8},{8,10},{10,12},{12,14},{14,0},{1,3},{3,5},... | collective-permute-start | bytes 811016 | tf_op jit(solution)/shard_map/ppermute | solution.py:372
  60.1 9.5 %collective-permute-start.6 = (bf16[528,256]{1,0:T(8,128)(2,1)S(1)}, bf16[528,256]{1,0:T(8,128)(2,1)S(1)}, u32[]{:S(2)}, u32[]{:S(2)}) collective-permute-start(bf16[528,256]{1,0:T(8,128)(2,1)S(1)} %collective-permute-done.5.b6), channel_id=1, source_target_pairs={{0,14},{2,0},{4,2},{6,4},{8,6},{10,8},{12,10},{14,12},{1,15},{3,1}... | collective-permute-start | bytes 811016 | tf_op jit(solution)/shard_map/ppermute | solution.py:374
  66.0 9.6 %collective-permute-start.3 = (bf16[528,256]{1,0:T(8,128)(2,1)S(1)}, bf16[528,256]{1,0:T(8,128)(2,1)S(1)}, u32[]{:S(2)}, u32[]{:S(2)}) collective-permute-start(bf16[528,256]{1,0:T(8,128)(2,1)S(1)} %collective-permute-done.2.b3), channel_id=1, source_target_pairs={{0,2},{2,4},{4,6},{6,8},{8,10},{10,12},{12,14},{14,0},{1,3},{3,5},... | collective-permute-start | bytes 811016 | tf_op jit(solution)/shard_map/ppermute | solution.py:372
  107.5 6.7 %copy-start.4 = (bf16[1,1024,384]{2,1,0:T(8,128)(2,1)S(1)}, bf16[1,1024,384]{2,1,0:T(8,128)(2,1)}, u32[]{:S(2)}) copy-start(bf16[1,1024,384]{2,1,0:T(8,128)(2,1)} %param.18) | copy-start | bytes 2359300
  107.5 10.8 %copy-start.5 = (bf16[1,192,1024]{2,1,0:T(8,128)(2,1)S(1)}, bf16[1,192,1024]{2,1,0:T(8,128)(2,1)}, u32[]{:S(2)}) copy-start(bf16[1,192,1024]{2,1,0:T(8,128)(2,1)} %param.19) | copy-start | bytes 1179652
  107.5 34.1 %copy-start.2 = (bf16[64,1024]{1,0:T(8,128)(2,1)S(1)}, bf16[64,1024]{1,0:T(8,128)(2,1)}, u32[]{:S(2)}) copy-start(bf16[64,1024]{1,0:T(8,128)(2,1)} %res_ref.1) | copy-start | bytes 393220
  107.5 34.1 %copy-start.3 = (f32[1024]{0:T(1024)S(1)}, f32[1024]{0:T(1024)}, u32[]{:S(2)}) copy-start(f32[1024]{0:T(1024)} %param.15) | copy-start | bytes 12292
  107.5 34.1 %all-to-all-start.2 = ((bf16[32,136,128]{2,1,0:T(8,128)(2,1)}), bf16[32,136,128]{2,1,0:T(8,128)(2,1)S(1)}, u32[]{:S(2)}, u32[]{:S(2)}) async-start(bf16[32,136,128]{2,1,0:T(8,128)(2,1)} %bitcast.6), calls=%async_computation.2 | async-start | bytes 2228224 | tf_op jit(solution)/shard_map/all_to_all | solution.py:384
  114.1 32.3 %collective-permute-start.7 = (bf16[1024,384]{1,0:T(8,128)(2,1)S(1)}, bf16[1024,384]{1,0:T(8,128)(2,1)}, u32[]{:S(2)}, u32[]{:S(2)}) collective-permute-start(bf16[1024,384]{1,0:T(8,128)(2,1)S(1)} %bitcast.61), channel_id=1, source_target_pairs={{0,2},{2,0},{1,3},{3,1},{4,6},{6,4},{5,7},{7,5},{8,10},{10,8},{9,1... | collective-permute-start | bytes 2359304 | tf_op jit(solution)/shard_map/ppermute | solution.py:390
  118.3 28.1 %collective-permute-start.8 = (bf16[192,1024]{1,0:T(8,128)(2,1)S(1)}, bf16[192,1024]{1,0:T(8,128)(2,1)}, u32[]{:S(2)}, u32[]{:S(2)}) collective-permute-start(bf16[192,1024]{1,0:T(8,128)(2,1)S(1)} %bitcast.64), channel_id=1, source_target_pairs={{0,2},{2,0},{1,3},{3,1},{4,6},{6,4},{5,7},{7,5},{8,10},{10,8},{9,1... | collective-permute-start | bytes 1179656 | tf_op jit(solution)/shard_map/ppermute | solution.py:391
  146.4 24.3 %all-to-all-start.3 = ((bf16[4,64,1024]{2,1,0:T(8,128)(2,1)}), bf16[4,64,1024]{2,1,0:T(8,128)(2,1)S(1)}, u32[]{:S(2)}, u32[]{:S(2)}) async-start(bf16[4,64,1024]{2,1,0:T(8,128)(2,1)} %get-tuple-element.18), calls=%async_computation.3 | async-start | bytes 1048576 | tf_op jit(solution)/shard_map/all_to_all | solution.py:421
  172.5 36.4 %all-to-all-start.4 = ((bf16[32,160,128]{2,1,0:T(8,128)(2,1)}), bf16[32,160,128]{2,1,0:T(8,128)(2,1)S(1)}, u32[]{:S(2)}, u32[]{:S(2)}) async-start(bf16[32,160,128]{2,1,0:T(8,128)(2,1)} %bitcast.21), calls=%async_computation.4 | async-start | bytes 2621440 | tf_op jit(solution)/shard_map/all_to_all | solution.py:423
  208.9 1.1 copy-start.1
  213.7 1.1 copy-start
  214.7 35.0 %all-to-all-start.5 = ((bf16[32,160,128]{2,1,0:T(8,128)(2,1)}), bf16[32,160,128]{2,1,0:T(8,128)(2,1)S(1)}, u32[]{:S(2)}, u32[]{:S(2)}) async-start(bf16[32,160,128]{2,1,0:T(8,128)(2,1)} %bitcast.54), calls=%async_computation.5 | async-start | bytes 2621440 | tf_op jit(solution)/shard_map/all_to_all | solution.py:427
  (1 other events, 1.0 us)
Sparse Core Ops, SparseCore 0:
  9.4 85.3 all-gather.1

commit v12 on v11

--- a/solution.py
+++ b/solution.py
@@ -276,7 +276,7 @@
         out_specs=pl.BlockSpec((block, 128), lambda i: (i, 0)),
         out_shape=jax.ShapeDtypeStruct((total, 128), BF),
         scratch_shapes=[pltpu.VMEM((block, 128), F32)],
-        compiler_params=pltpu.CompilerParams(vmem_limit_bytes=14 * 1024 * 1024),
+        compiler_params=pltpu.CompilerParams(vmem_limit_bytes=52 * 1024 * 1024),
         name="expert",
     )(rows_in, weight_in, weight_out)
 

time: 275 us -> 276 us (level)
  no operation moved by 1% of the time
where the time goes in v12:
time: 276 us; the launch traced here: 275 us
  waiting for transfers between devices  115 us (42%)
  starting transfers between devices  74.4 us (27%)
  Pallas kernels  47.4 us (17%)
  blocking collectives  15.7 us (6%)
  between operations  13.8 us (5%)
  other arithmetic  5.34 us (2%)
  local copies, waits for them, and re-layouts  3.98 us (1%)
    pallas_call x1, Pallas kernels, flash(): pl.pallas_call(flash_kernel, grid_spec=pltpu.PrefetchScalarGridSpec(num_s...  30.4 us
    all_to_all x1, waiting for transfers between devices, local(): lax.all_to_all(done.reshape(32, 4 * CAP * 8, 128), ('x', 'z'), split_axis...  28.6 us
    all_to_all x1, waiting for transfers between devices, local(): lax.all_to_all(outgoing.reshape(32, 4 * CAP * 8, 128), ('x', 'z'), split_...  26.1 us
    all_to_all x1, waiting for transfers between devices, local(): lax.all_to_all(shards.reshape(32, HD + STAT, 128), ('x', 'z'), split_axis...  21.3 us
    all_to_all x1, blocking collectives, local(): lax.all_to_all(sums.reshape(4, tokens, width), 'y2', split_axis=0, concat...  15.7 us
    ppermute x4, waiting for transfers between devices, local(): ups.append(lax.ppermute(ups[-1], ('y2', 'y1'), up))  14.4 us
    all_to_all x1, starting transfers between devices, local(): lax.all_to_all(key_value, ('x', 'z'), split_axis=0, concat_axis=0, tiled=...  13.2 us
    all_to_all x1, starting transfers between devices, local(): lax.all_to_all(spread, 'y2', split_axis=0, concat_axis=0, tiled=True)  12.8 us
  transfers between devices with their start and end apart: 16, of which 12 were waited for; matrix products, arithmetic and copies ran while one was open for 3% of the time, Pallas kernels for 14%

profile of v12, /device:TPU:8, one launch (start us, length us, event | category | flops | bytes accessed | tf_op | source)
XLA Modules:
  0.0 275.2 jit_solution(5020800711953193218)
XLA Ops:
  8.8 13.2 %all-to-all-start.1 = ((bf16[32,16,256]{2,1,0:T(8,128)(2,1)}), bf16[32,16,256]{2,1,0:T(8,128)(2,1)S(1)}, u32[]{:S(2)}, u32[]{:S(2)}) async-start(bf16[32,16,256]{2,1,0:T(8,128)(2,1)} %pack_kv.1), calls=%async_computation.1 | async-start | bytes 524288 | tf_op jit(solution)/shard_map/all_to_all | solution.py:364
  24.0 10.4 %all-to-all-done.1 = bf16[32,16,256]{2,1,0:T(8,128)(2,1)S(1)} async-done(((bf16[32,16,256]{2,1,0:T(8,128)(2,1)}), bf16[32,16,256]{2,1,0:T(8,128)(2,1)S(1)}, u32[]{:S(2)}, u32[]{:S(2)}) %all-to-all-start.1) | async-done | bytes 262176 | tf_op jit(solution)/shard_map/all_to_all | solution.py:364
  34.4 4.4 %all-to-all-start = ((bf16[32,64,256]{2,1,0:T(8,128)(2,1)}), bf16[32,64,256]{2,1,0:T(8,128)(2,1)S(1)}, u32[]{:S(2)}, u32[]{:S(2)}) async-start(bf16[32,64,256]{2,1,0:T(8,128)(2,1)} %pack_q.1), calls=%async_computation | async-start | bytes 2097152 | tf_op jit(solution)/shard_map/all_to_all | solution.py:377
  38.9 3.5 %collective-permute-start = (bf16[528,256]{1,0:T(8,128)(2,1)S(1)}, bf16[528,256]{1,0:T(8,128)(2,1)S(1)}, u32[]{:S(2)}, u32[]{:S(2)}) collective-permute-start(bf16[528,256]{1,0:T(8,128)(2,1)S(1)} %pad_maximum_fusion.2.b0), channel_id=1, source_target_pairs={{0,2},{2,4},{4,6},{6,8},{8,10},{10,12},{12,14},{14,0},{1,3},{3,5},... | collective-permute-start | bytes 811016 | tf_op jit(solution)/shard_map/ppermute | solution.py:372
  44.7 3.1 %collective-permute-done.b1 = bf16[528,256]{1,0:T(8,128)(2,1)S(1)} collective-permute-done((bf16[528,256]{1,0:T(8,128)(2,1)S(1)}, bf16[528,256]{1,0:T(8,128)(2,1)S(1)}, u32[]{:S(2)}, u32[]{:S(2)}) %collective-permute-start) | collective-permute-done | bytes 270368 | tf_op jit(solution)/shard_map/ppermute | solution.py:372
  47.8 3.5 %collective-permute-start.1 = (bf16[528,256]{1,0:T(8,128)(2,1)S(1)}, bf16[528,256]{1,0:T(8,128)(2,1)S(1)}, u32[]{:S(2)}, u32[]{:S(2)}) collective-permute-start(bf16[528,256]{1,0:T(8,128)(2,1)S(1)} %collective-permute-done.b1), channel_id=1, source_target_pairs={{0,2},{2,4},{4,6},{6,8},{8,10},{10,12},{12,14},{14,0},{1,3},{3,5},... | collective-permute-start | bytes 811016 | tf_op jit(solution)/shard_map/ppermute | solution.py:372
  53.9 2.8 %collective-permute-done.1.b2 = bf16[528,256]{1,0:T(8,128)(2,1)S(1)} collective-permute-done((bf16[528,256]{1,0:T(8,128)(2,1)S(1)}, bf16[528,256]{1,0:T(8,128)(2,1)S(1)}, u32[]{:S(2)}, u32[]{:S(2)}) %collective-permute-start.1) | collective-permute-done | bytes 270368 | tf_op jit(solution)/shard_map/ppermute | solution.py:372
  56.7 3.0 %collective-permute-start.2 = (bf16[528,256]{1,0:T(8,128)(2,1)S(1)}, bf16[528,256]{1,0:T(8,128)(2,1)S(1)}, u32[]{:S(2)}, u32[]{:S(2)}) collective-permute-start(bf16[528,256]{1,0:T(8,128)(2,1)S(1)} %collective-permute-done.1.b2), channel_id=1, source_target_pairs={{0,2},{2,4},{4,6},{6,8},{8,10},{10,12},{12,14},{14,0},{1,3},{3,5},... | collective-permute-start | bytes 811016 | tf_op jit(solution)/shard_map/ppermute | solution.py:372
  60.1 3.4 %collective-permute-start.6 = (bf16[528,256]{1,0:T(8,128)(2,1)S(1)}, bf16[528,256]{1,0:T(8,128)(2,1)S(1)}, u32[]{:S(2)}, u32[]{:S(2)}) collective-permute-start(bf16[528,256]{1,0:T(8,128)(2,1)S(1)} %collective-permute-done.5.b6), channel_id=1, source_target_pairs={{0,14},{2,0},{4,2},{6,4},{8,6},{10,8},{12,10},{14,12},{1,15},{3,1}... | collective-permute-start | bytes 811016 | tf_op jit(solution)/shard_map/ppermute | solution.py:374
  66.0 2.6 collective-permute-start.3
  69.6 5.9 %collective-permute-done.3.b4 = bf16[528,256]{1,0:T(8,128)(2,1)S(1)} collective-permute-done((bf16[528,256]{1,0:T(8,128)(2,1)S(1)}, bf16[528,256]{1,0:T(8,128)(2,1)S(1)}, u32[]{:S(2)}, u32[]{:S(2)}) %collective-permute-start.3) | collective-permute-done | bytes 270368 | tf_op jit(solution)/shard_map/ppermute | solution.py:372
  77.1 30.4 %flash.1 = bf16[4,8,136,128]{3,2,1,0:T(8,128)(2,1)} custom-call(s32[2]{0:T(128)S(1)} %pad_add_fusion.pos_ref, bf16[4,8,64,256]{3,2,1,0:T(8,128)(2,1)S(1)} %bitcast.57, bf16[528,256]{1,0:T(8,128)(2,1)S(1)} %pad_maximum_fusion.2.b0, bf16[528,256]{1,0:T(8,128)(2,1)S(1)} %collective-permute-done.b1, bf16[528,256]{1,0:T(8,128)(2,1)S(1)} %collective-permute-done.1.b2, ...), custom_call_target="tpu_custom_call" | custom-call | flops 5368709120 | bytes 5242880 | tf_op jit(solution)/shard_map/flash/pallas_call | solution.py:143
  107.5 6.5 %all-to-all-start.2 = ((bf16[32,136,128]{2,1,0:T(8,128)(2,1)}), bf16[32,136,128]{2,1,0:T(8,128)(2,1)S(1)}, u32[]{:S(2)}, u32[]{:S(2)}) async-start(bf16[32,136,128]{2,1,0:T(8,128)(2,1)} %bitcast.6), calls=%async_computation.2 | async-start | bytes 2228224 | tf_op jit(solution)/shard_map/all_to_all | solution.py:384
  114.1 4.1 %collective-permute-start.7 = (bf16[1024,384]{1,0:T(8,128)(2,1)S(1)}, bf16[1024,384]{1,0:T(8,128)(2,1)}, u32[]{:S(2)}, u32[]{:S(2)}) collective-permute-start(bf16[1024,384]{1,0:T(8,128)(2,1)S(1)} %bitcast.61), channel_id=1, source_target_pairs={{0,2},{2,0},{1,3},{3,1},{4,6},{6,4},{5,7},{7,5},{8,10},{10,8},{9,1... | collective-permute-start | bytes 2359304 | tf_op jit(solution)/shard_map/ppermute | solution.py:390
  120.3 21.3 %all-to-all-done.2 = bf16[32,136,128]{2,1,0:T(8,128)(2,1)S(1)} async-done(((bf16[32,136,128]{2,1,0:T(8,128)(2,1)}), bf16[32,136,128]{2,1,0:T(8,128)(2,1)S(1)}, u32[]{:S(2)}, u32[]{:S(2)}) %all-to-all-start.2) | async-done | bytes 1114144 | tf_op jit(solution)/shard_map/all_to_all | solution.py:384
  141.6 4.8 %merge.1 = (f32[64,1024]{1,0:T(8,128)S(1)}, bf16[4,64,1024]{2,1,0:T(8,128)(2,1)}) custom-call(bf16[4,8,136,128]{3,2,1,0:T(8,128)(2,1)S(1)} %bitcast.53, bf16[2048,1024]{1,0:T(8,128)(2,1)} %all-gather.2.cloned.1.call-done.w_ref, bf16[64,1024]{1,0:T(8,128)(2,1)S(1)} %copy-done, f32[1,1024]{1,0:T(1,128)S(1)} %bitcast.58), custom_call_target="tpu_custom_call" | custom-call | tf_op jit(solution)/shard_map/merge/pallas_call | solution.py:209
  146.4 12.8 %all-to-all-start.3 = ((bf16[4,64,1024]{2,1,0:T(8,128)(2,1)}), bf16[4,64,1024]{2,1,0:T(8,128)(2,1)S(1)}, u32[]{:S(2)}, u32[]{:S(2)}) async-start(bf16[4,64,1024]{2,1,0:T(8,128)(2,1)} %get-tuple-element.18), calls=%async_computation.3 | async-start | bytes 1048576 | tf_op jit(solution)/shard_map/all_to_all | solution.py:421
  160.5 10.2 %all-to-all-done.3 = bf16[4,64,1024]{2,1,0:T(8,128)(2,1)S(1)} async-done(((bf16[4,64,1024]{2,1,0:T(8,128)(2,1)}), bf16[4,64,1024]{2,1,0:T(8,128)(2,1)S(1)}, u32[]{:S(2)}, u32[]{:S(2)}) %all-to-all-start.3) | async-done | bytes 524320 | tf_op jit(solution)/shard_map/all_to_all | solution.py:421
  172.5 5.5 %all-to-all-start.4 = ((bf16[32,160,128]{2,1,0:T(8,128)(2,1)}), bf16[32,160,128]{2,1,0:T(8,128)(2,1)S(1)}, u32[]{:S(2)}, u32[]{:S(2)}) async-start(bf16[32,160,128]{2,1,0:T(8,128)(2,1)} %bitcast.21), calls=%async_computation.4 | async-start | bytes 2621440 | tf_op jit(solution)/shard_map/all_to_all | solution.py:423
  182.8 26.1 %all-to-all-done.4 = bf16[32,160,128]{2,1,0:T(8,128)(2,1)S(1)} async-done(((bf16[32,160,128]{2,1,0:T(8,128)(2,1)}), bf16[32,160,128]{2,1,0:T(8,128)(2,1)S(1)}, u32[]{:S(2)}, u32[]{:S(2)}) %all-to-all-start.4) | async-done | bytes 1310752 | tf_op jit(solution)/shard_map/all_to_all | solution.py:423
  209.9 6.1 %expert.1 = bf16[5120,128]{1,0:T(8,128)(2,1)} custom-call(bf16[5120,128]{1,0:T(8,128)(2,1)} %bitcast.59, bf16[1024,768]{1,0:T(8,128)(2,1)} %pad_maximum_fusion.win_ref, bf16[384,1024]{1,0:T(8,128)(2,1)S(1)} %pad_maximum_fusion.1.wout_ref), custom_call_target="tpu_custom_call" | custom-call | tf_op jit(solution)/shard_map/expert/pallas_call | solution.py:268
  216.0 5.1 %all-to-all-start.5 = ((bf16[32,160,128]{2,1,0:T(8,128)(2,1)}), bf16[32,160,128]{2,1,0:T(8,128)(2,1)S(1)}, u32[]{:S(2)}, u32[]{:S(2)}) async-start(bf16[32,160,128]{2,1,0:T(8,128)(2,1)} %bitcast.60), calls=%async_computation.5 | async-start | bytes 2621440 | tf_op jit(solution)/shard_map/all_to_all | solution.py:427
  222.5 28.6 %all-to-all-done.5 = bf16[32,160,128]{2,1,0:T(8,128)(2,1)S(1)} async-done(((bf16[32,160,128]{2,1,0:T(8,128)(2,1)}), bf16[32,160,128]{2,1,0:T(8,128)(2,1)S(1)}, u32[]{:S(2)}, u32[]{:S(2)}) %all-to-all-start.5) | async-done | bytes 1310752 | tf_op jit(solution)/shard_map/all_to_all | solution.py:427
  251.8 15.7 %all_to_all.35 = bf16[4,64,1024]{2,1,0:T(8,128)(2,1)S(1)} all-to-all(bf16[4,64,1024]{2,1,0:T(8,128)(2,1)S(1)} %bitcast.55), channel_id=1, replica_groups=mesh['z'=8,'x'=4,'y2'=4,'y1'=2,'dp'=2] {'y2'}, dimensions={0} | all-to-all | bytes 1048576 | tf_op jit(solution)/shard_map/all_to_all | solution.py:431
  (64 shorter events, 28.4 us)
Async XLA Ops:
  6.5 107.6 %all-gather.2.cloned.1.call-start = ((), (), s32[]{:S(2)}) async-start(), calls=%async_computation.7 | async-start | bytes 4718592 | tf_op jit(solution)/shard_map/all_gather | solution.py:381
  8.8 25.6 %all-to-all-start.1 = ((bf16[32,16,256]{2,1,0:T(8,128)(2,1)}), bf16[32,16,256]{2,1,0:T(8,128)(2,1)S(1)}, u32[]{:S(2)}, u32[]{:S(2)}) async-start(bf16[32,16,256]{2,1,0:T(8,128)(2,1)} %pack_kv.1), calls=%async_computation.1 | async-start | bytes 524288 | tf_op jit(solution)/shard_map/all_to_all | solution.py:364
  21.9 16.9 %copy-start.5 = (s32[64,8]{0,1:T(8,128)S(1)}, s32[64,8]{0,1:T(8,128)}, u32[]{:S(2)}) copy-start(s32[64,8]{0,1:T(8,128)} %param.17) | copy-start | bytes 6148
  21.9 16.9 %copy-start.6 = (s32[64,8]{0,1:T(8,128)S(1)}, s32[64,8]{0,1:T(8,128)}, u32[]{:S(2)}) copy-start(s32[64,8]{0,1:T(8,128)} %param.16) | copy-start | bytes 6148
  34.4 42.7 %all-to-all-start = ((bf16[32,64,256]{2,1,0:T(8,128)(2,1)}), bf16[32,64,256]{2,1,0:T(8,128)(2,1)S(1)}, u32[]{:S(2)}, u32[]{:S(2)}) async-start(bf16[32,64,256]{2,1,0:T(8,128)(2,1)} %pack_q.1), calls=%async_computation | async-start | bytes 2097152 | tf_op jit(solution)/shard_map/all_to_all | solution.py:377
  38.9 9.0 %collective-permute-start = (bf16[528,256]{1,0:T(8,128)(2,1)S(1)}, bf16[528,256]{1,0:T(8,128)(2,1)S(1)}, u32[]{:S(2)}, u32[]{:S(2)}) collective-permute-start(bf16[528,256]{1,0:T(8,128)(2,1)S(1)} %pad_maximum_fusion.2.b0), channel_id=1, source_target_pairs={{0,2},{2,4},{4,6},{6,8},{8,10},{10,12},{12,14},{14,0},{1,3},{3,5},... | collective-permute-start | bytes 811016 | tf_op jit(solution)/shard_map/ppermute | solution.py:372
  42.4 8.9 %collective-permute-start.4 = (bf16[528,256]{1,0:T(8,128)(2,1)S(1)}, bf16[528,256]{1,0:T(8,128)(2,1)S(1)}, u32[]{:S(2)}, u32[]{:S(2)}) collective-permute-start(bf16[528,256]{1,0:T(8,128)(2,1)S(1)} %pad_maximum_fusion.2.b0), channel_id=1, source_target_pairs={{0,14},{2,0},{4,2},{6,4},{8,6},{10,8},{12,10},{14,12},{1,15},{3,1}... | collective-permute-start | bytes 811016 | tf_op jit(solution)/shard_map/ppermute | solution.py:374
  47.8 8.9 %collective-permute-start.1 = (bf16[528,256]{1,0:T(8,128)(2,1)S(1)}, bf16[528,256]{1,0:T(8,128)(2,1)S(1)}, u32[]{:S(2)}, u32[]{:S(2)}) collective-permute-start(bf16[528,256]{1,0:T(8,128)(2,1)S(1)} %collective-permute-done.b1), channel_id=1, source_target_pairs={{0,2},{2,4},{4,6},{6,8},{8,10},{10,12},{12,14},{14,0},{1,3},{3,5},... | collective-permute-start | bytes 811016 | tf_op jit(solution)/shard_map/ppermute | solution.py:372
  51.3 8.7 %collective-permute-start.5 = (bf16[528,256]{1,0:T(8,128)(2,1)S(1)}, bf16[528,256]{1,0:T(8,128)(2,1)S(1)}, u32[]{:S(2)}, u32[]{:S(2)}) collective-permute-start(bf16[528,256]{1,0:T(8,128)(2,1)S(1)} %collective-permute-done.4.b5), channel_id=1, source_target_pairs={{0,14},{2,0},{4,2},{6,4},{8,6},{10,8},{12,10},{14,12},{1,15},{3,1}... | collective-permute-start | bytes 811016 | tf_op jit(solution)/shard_map/ppermute | solution.py:374
  56.7 9.3 %collective-permute-start.2 = (bf16[528,256]{1,0:T(8,128)(2,1)S(1)}, bf16[528,256]{1,0:T(8,128)(2,1)S(1)}, u32[]{:S(2)}, u32[]{:S(2)}) collective-permute-start(bf16[528,256]{1,0:T(8,128)(2,1)S(1)} %collective-permute-done.1.b2), channel_id=1, source_target_pairs={{0,2},{2,4},{4,6},{6,8},{8,10},{10,12},{12,14},{14,0},{1,3},{3,5},... | collective-permute-start | bytes 811016 | tf_op jit(solution)/shard_map/ppermute | solution.py:372
  60.1 9.5 %collective-permute-start.6 = (bf16[528,256]{1,0:T(8,128)(2,1)S(1)}, bf16[528,256]{1,0:T(8,128)(2,1)S(1)}, u32[]{:S(2)}, u32[]{:S(2)}) collective-permute-start(bf16[528,256]{1,0:T(8,128)(2,1)S(1)} %collective-permute-done.5.b6), channel_id=1, source_target_pairs={{0,14},{2,0},{4,2},{6,4},{8,6},{10,8},{12,10},{14,12},{1,15},{3,1}... | collective-permute-start | bytes 811016 | tf_op jit(solution)/shard_map/ppermute | solution.py:374
  66.0 9.6 %collective-permute-start.3 = (bf16[528,256]{1,0:T(8,128)(2,1)S(1)}, bf16[528,256]{1,0:T(8,128)(2,1)S(1)}, u32[]{:S(2)}, u32[]{:S(2)}) collective-permute-start(bf16[528,256]{1,0:T(8,128)(2,1)S(1)} %collective-permute-done.2.b3), channel_id=1, source_target_pairs={{0,2},{2,4},{4,6},{6,8},{8,10},{10,12},{12,14},{14,0},{1,3},{3,5},... | collective-permute-start | bytes 811016 | tf_op jit(solution)/shard_map/ppermute | solution.py:372
  107.5 6.7 %copy-start.3 = (bf16[1,1024,384]{2,1,0:T(8,128)(2,1)S(1)}, bf16[1,1024,384]{2,1,0:T(8,128)(2,1)}, u32[]{:S(2)}) copy-start(bf16[1,1024,384]{2,1,0:T(8,128)(2,1)} %param.18) | copy-start | bytes 2359300
  107.5 10.8 %copy-start.4 = (bf16[1,192,1024]{2,1,0:T(8,128)(2,1)S(1)}, bf16[1,192,1024]{2,1,0:T(8,128)(2,1)}, u32[]{:S(2)}) copy-start(bf16[1,192,1024]{2,1,0:T(8,128)(2,1)} %param.19) | copy-start | bytes 1179652
  107.5 34.1 %copy-start = (bf16[64,1024]{1,0:T(8,128)(2,1)S(1)}, bf16[64,1024]{1,0:T(8,128)(2,1)}, u32[]{:S(2)}) copy-start(bf16[64,1024]{1,0:T(8,128)(2,1)} %res_ref.1) | copy-start | bytes 393220
  107.5 34.1 %copy-start.1 = (f32[1024]{0:T(1024)S(1)}, f32[1024]{0:T(1024)}, u32[]{:S(2)}) copy-start(f32[1024]{0:T(1024)} %param.15) | copy-start | bytes 12292
  107.5 34.1 %all-to-all-start.2 = ((bf16[32,136,128]{2,1,0:T(8,128)(2,1)}), bf16[32,136,128]{2,1,0:T(8,128)(2,1)S(1)}, u32[]{:S(2)}, u32[]{:S(2)}) async-start(bf16[32,136,128]{2,1,0:T(8,128)(2,1)} %bitcast.6), calls=%async_computation.2 | async-start | bytes 2228224 | tf_op jit(solution)/shard_map/all_to_all | solution.py:384
  114.1 32.3 %collective-permute-start.7 = (bf16[1024,384]{1,0:T(8,128)(2,1)S(1)}, bf16[1024,384]{1,0:T(8,128)(2,1)}, u32[]{:S(2)}, u32[]{:S(2)}) collective-permute-start(bf16[1024,384]{1,0:T(8,128)(2,1)S(1)} %bitcast.61), channel_id=1, source_target_pairs={{0,2},{2,0},{1,3},{3,1},{4,6},{6,4},{5,7},{7,5},{8,10},{10,8},{9,1... | collective-permute-start | bytes 2359304 | tf_op jit(solution)/shard_map/ppermute | solution.py:390
  118.3 28.1 %collective-permute-start.8 = (bf16[192,1024]{1,0:T(8,128)(2,1)S(1)}, bf16[192,1024]{1,0:T(8,128)(2,1)}, u32[]{:S(2)}, u32[]{:S(2)}) collective-permute-start(bf16[192,1024]{1,0:T(8,128)(2,1)S(1)} %bitcast.64), channel_id=1, source_target_pairs={{0,2},{2,0},{1,3},{3,1},{4,6},{6,4},{5,7},{7,5},{8,10},{10,8},{9,1... | collective-permute-start | bytes 1179656 | tf_op jit(solution)/shard_map/ppermute | solution.py:391
  146.4 24.3 %all-to-all-start.3 = ((bf16[4,64,1024]{2,1,0:T(8,128)(2,1)}), bf16[4,64,1024]{2,1,0:T(8,128)(2,1)S(1)}, u32[]{:S(2)}, u32[]{:S(2)}) async-start(bf16[4,64,1024]{2,1,0:T(8,128)(2,1)} %get-tuple-element.18), calls=%async_computation.3 | async-start | bytes 1048576 | tf_op jit(solution)/shard_map/all_to_all | solution.py:421
  172.5 36.3 %all-to-all-start.4 = ((bf16[32,160,128]{2,1,0:T(8,128)(2,1)}), bf16[32,160,128]{2,1,0:T(8,128)(2,1)S(1)}, u32[]{:S(2)}, u32[]{:S(2)}) async-start(bf16[32,160,128]{2,1,0:T(8,128)(2,1)} %bitcast.21), calls=%async_computation.4 | async-start | bytes 2621440 | tf_op jit(solution)/shard_map/all_to_all | solution.py:423
  208.9 1.1 copy-start.2
  216.0 35.0 %all-to-all-start.5 = ((bf16[32,160,128]{2,1,0:T(8,128)(2,1)}), bf16[32,160,128]{2,1,0:T(8,128)(2,1)S(1)}, u32[]{:S(2)}, u32[]{:S(2)}) async-start(bf16[32,160,128]{2,1,0:T(8,128)(2,1)} %bitcast.60), calls=%async_computation.5 | async-start | bytes 2621440 | tf_op jit(solution)/shard_map/all_to_all | solution.py:427
Sparse Core Ops, SparseCore 0:
  9.4 85.3 all-gather.1
